TPU v7x, 256 devices: a whole 4x4x8 slice. The times are simulated.
256 devices in a mesh: atoms: 32 (over x, z_lo, core), blk: 8 (over z_hi, y).
Axes of the slice: x: 4, y: 4, z: 8 (z_hi: 2, z_lo: 4; z = z_hi * 4 + z_lo), core: 2. Of those that a mesh axis runs over, the one named last changes fastest.
Arguments:
- desc: bfloat16 [524288, 768], P(('atoms', 'blk')), may hold values from -6 to 6
- species: int32 [524288], P(('atoms', 'blk')), may hold values from 0 to 1
- atom_cfg: int32 [524288], P(('atoms', 'blk')), may hold values from 0 to 255
- slot: int32 [256], replicated, may hold values from 0 to 255, each once
- weights: float32 [256], P('atoms'), may hold values from 0.25 to 4
Outputs:
- normal_matrix: float32 [1536, 1536], P('blk')
- config_rows: float32 [256, 1536], P('atoms', 'blk')
All inputs are finite; a program needn't handle non-finite values.
Results may differ from a plain program's by a relative error of at most 0.0003.
Values sent between devices are 32-bit elements; how exact they have to be, the bound alone decides.
No kernel may reach another device: no remote copies, remote signals or barrier semaphores. Data moves between devices by JAX's collectives and lax.ppermute only.
A program may use at most 64 MiB of HBM per device.

v0:
```python
import math

import jax
import jax.numpy as jnp
from jax import lax
from jax.sharding import PartitionSpec as P


def shards(desc, species, atom_cfg, slot, weights):
    rows_here = desc.shape[0]
    width = desc.shape[1]
    columns = 2 * width
    n_blk = lax.axis_size("blk")
    n_owners = lax.axis_size("atoms")
    configs = slot.shape[0]
    cfg_here = weights.shape[0]
    band = columns // n_blk
    first_row = lax.axis_index("blk") * band
    scale = 1.0 / math.sqrt(rows_here * n_blk / cfg_here)
    keys = jnp.take(slot, atom_cfg) * 2 + species
    targets = 0 * 2 + lax.iota(jnp.int32, 2 * configs)
    onehot = (keys[None, :] == targets[:, None]).astype(jnp.bfloat16)
    partial_sums = jnp.dot(onehot, desc, preferred_element_type=jnp.float32)
    local_sums = partial_sums.reshape(configs, columns)
    by_cols = lax.psum_scatter(local_sums, "blk", scatter_dimension=1, tiled=True)
    own_cols = lax.psum_scatter(by_cols, "atoms", scatter_dimension=0, tiled=True) * scale
    full_rows = lax.all_gather(own_cols, "blk", axis=1, tiled=True)
    weighted = lax.dynamic_slice_in_dim(full_rows * weights[:, None], first_row, band, 1)
    cfg_part = (
        lax.dot_general(
            weighted,
            full_rows,
            (((0,), (0,)), ((), ())),
            precision=lax.Precision.HIGHEST,
            preferred_element_type=jnp.float32,
        )
        / configs
    )
    first_mask = (species == 0).astype(jnp.bfloat16)[:, None]
    design = jnp.concatenate([desc * first_mask, desc * (1 - first_mask)], 1)
    atom_part = lax.psum_scatter(
        lax.dot_general(
            design, design, (((0,), (0,)), ((), ())), preferred_element_type=jnp.float32
        ),
        "blk",
        scatter_dimension=0,
        tiled=True,
    )
    total = cfg_part + atom_part / (rows_here * n_owners)
    normal_matrix = lax.psum(total, "atoms")
    return (normal_matrix, own_cols)


def solution(mesh):
    return jax.shard_map(
        shards,
        mesh=mesh,
        in_specs=(
            P(("atoms", "blk"), None),
            P(("atoms", "blk")),
            P(("atoms", "blk")),
            P(),
            P("atoms"),
        ),
        out_specs=(P("blk", None), P("atoms", "blk")),
        check_vma=False,
    )
```

profile of v0, /device:TPU:1, one launch (start us, length us, event | category | flops | bytes accessed | tf_op | source)
XLA Modules:
  0.0 749.0 jit_solution(13732062544771604484)
XLA Ops:
  7.2 0.0 copy-start
  7.2 0.0 reduce-scatter.10.cloned.1.call-start
  7.2 0.7 fusion.7
  7.9 0.0 copy-done
  7.9 0.0 copy-start.3
  7.9 0.0 copy-start.4
  7.9 0.0 copy-start.1
  8.0 13.2 %gather_fusion = s32[2048]{0:T(1024)S(1)} fusion(s32[256]{0:T(256)S(1)} %copy-done, s32[2048]{0:T(1024)S(1)} %fusion.7), kind=kCustom, calls=%fused_computation | custom fusion | bytes 24576 | tf_op jit(solution)/shard_map/jit(_take)/gather | solution.py:20
  21.2 0.0 copy-done.3
  21.2 0.0 copy-done.4
  21.2 0.0 copy-done.1
  21.2 3.1 fusion.4
  24.3 1.7 reshape.17
  26.1 1.6 copy.9
  27.7 0.0 reduce-scatter.10.cloned.1.call-update
  27.7 0.0 reduce-scatter.6.cloned.1.call-start
  27.8 3.4 broadcast_multiply_fusion.1
  31.2 89.3 %reduce-scatter.10.cloned.1.call-done = f32[192,256]{1,0:T(8,128)} async-done(((f32[1536,256]{1,0:T(8,128)}), f32[192,256]{1,0:T(8,128)}) %reduce-scatter.10.cloned.1.call-update) | async-done | bytes 196624
  120.5 1.8 copy.10
  122.3 0.0 reduce-scatter.6.cloned.1.call-update
  122.3 0.0 reduce-scatter.8.cloned.1.call-start
  122.3 14.5 %fusion = f32[1536,1536]{1,0:T(8,128)} fusion(bf16[2048,768]{1,0:T(8,128)(2,1)} %get-tuple-element.5, bf16[2048,768]{1,0:T(8,128)(2,1)S(1)} %get-tuple-element.4), kind=kOutput, calls=%fused_computation.1 | convolution fusion | flops 9676259328 | bytes 15728640 | tf_op jit(solution)/shard_map/dot_general | solution.py:42
  136.8 0.0 copy-start.5
  136.8 0.0 reduce-scatter.8.cloned.1.call-update
  136.8 0.0 all-reduce.2.cloned.1.call-start
  136.9 122.9 %reduce-scatter.6.cloned.1.call-done = f32[8,192]{1,0:T(8,128)} async-done(((f32[256,192]{1,0:T(8,128)}), f32[8,192]{1,0:T(8,128)}) %reduce-scatter.6.cloned.1.call-update) | async-done | bytes 6160 | tf_op jit(solution)/shard_map/reduce_scatter | solution.py:26
  259.9 0.0 copy-start.2
  259.9 0.8 fusion.13
  260.6 37.9 %all-gather = f32[8,192,8]{1,2,0:T(8,128)S(1)} all-gather(f32[1,192,8]{1,2,0:T(8,128)S(1)} %fusion.13), channel_id=1, replica_groups=mesh['atoms'=32,'blk'=8] {'blk'}, dimensions={0}, use_global_device_ids=true | all-gather | bytes 55296 | tf_op jit(solution)/shard_map/all_gather | solution.py:27
  298.6 0.1 reshape.28
  298.7 168.7 %reduce-scatter.8.cloned.1.call-done = f32[192,1536]{1,0:T(8,128)} async-done(((f32[1536,1536]{1,0:T(8,128)}), f32[192,1536]{1,0:T(8,128)}) %reduce-scatter.8.cloned.1.call-update) | async-done | bytes 1179664 | tf_op jit(solution)/shard_map/reduce_scatter | solution.py:41
  467.4 0.0 copy-done.5
  467.4 3.6 fusion.5
  471.0 0.0 all-reduce.2.cloned.1.call-update
  471.0 0.0 copy-done.2
  471.0 0.6 broadcast_multiply_fusion.2
  471.6 268.5 %all-reduce.2.cloned.1.call-done = f32[192,1536]{1,0:T(8,128)} async-done(((f32[192,1536]{1,0:T(8,128)}), f32[192,1536]{1,0:T(8,128)}) %all-reduce.2.cloned.1.call-update) | async-done | bytes 1179664 | tf_op jit(solution)/shard_map/psum | solution.py:50
  740.1 2.4 copy.12
  (3 shorter events, 0.0 us)
Async XLA Ops:
  7.2 0.8 copy-start
  7.2 113.3 %reduce-scatter.10.cloned.1.call-start = ((), (), s32[]{:S(2)}) async-start(), calls=%async_computation.6 | async-start | bytes 1769472
  7.9 13.2 %copy-start.3 = (s32[2048]{0:T(1024)S(1)}, s32[2048]{0:T(1024)}, u32[]{:S(2)}) copy-start(s32[2048]{0:T(1024)} %param.7) | copy-start | bytes 24580
  7.9 13.2 %copy-start.4 = (s32[2048]{0:T(1024)S(1)}, s32[2048]{0:T(1024)}, u32[]{:S(2)}) copy-start(s32[2048]{0:T(1024)} %param.6) | copy-start | bytes 24580
  7.9 13.3 %copy-start.1 = (bf16[2048,768]{1,0:T(8,128)(2,1)S(1)}, bf16[2048,768]{1,0:T(8,128)(2,1)}, u32[]{:S(2)}) copy-start(bf16[2048,768]{1,0:T(8,128)(2,1)} %param.5) | copy-start | bytes 9437188
  27.7 232.1 %reduce-scatter.6.cloned.1.call-start = ((), (), s32[]{:S(2)}) async-start(), calls=%async_computation.3 | async-start | bytes 270336 | tf_op jit(solution)/shard_map/reduce_scatter | solution.py:26
  122.3 345.1 %reduce-scatter.8.cloned.1.call-start = ((), (), s32[]{:S(2)}) async-start(), calls=%async_computation.4 | async-start | bytes 10616832 | tf_op jit(solution)/shard_map/reduce_scatter | solution.py:41
  136.8 330.6 %copy-start.5 = (f32[8]{0:T(128)S(1)}, f32[8]{0:T(128)}, u32[]{:S(2)}) copy-start(f32[8]{0:T(128)} %param.9) | copy-start | bytes 100
  136.8 603.3 %all-reduce.2.cloned.1.call-start = ((), (), s32[]{:S(2)}) async-start(), calls=%async_computation.5 | async-start | bytes 2359296 | tf_op jit(solution)/shard_map/psum | solution.py:50
  259.9 211.1 %copy-start.2 = (f32[8,192]{1,0:T(8,128)S(1)}, f32[8,192]{1,0:T(8,128)}, u32[]{:S(2)}) copy-start(f32[8,192]{1,0:T(8,128)} %reduce-scatter.6.cloned.1.call-done) | copy-start | bytes 18436
Sparse Core Ops, SparseCore 0:
  27.8 92.6 reduce-scatter.9
  123.6 136.2 reduce-scatter.5
  264.6 202.7 reduce-scatter.7
  471.1 268.9 all-reduce.1
where the time goes:
time: 750 us; the launch traced here: 749 us
  waiting for transfers between devices  650 us (87%)
  blocking collectives  37.9 us (5%)
  matrix products  21.2 us (3%)
  local copies, waits for them, and re-layouts  20.8 us (3%)
  between operations  13.9 us (2%)
    psum x1, waiting for transfers between devices, shards(): normal_matrix = lax.psum(total, 'atoms')  269 us
    reduce_scatter x1, waiting for transfers between devices, shards(): lax.psum_scatter(lax.dot_general(design, design, (((0,), (0,)), ((), ()))...  169 us
    reduce_scatter x1, waiting for transfers between devices, shards(): lax.psum_scatter(by_cols, 'atoms', scatter_dimension=0, tiled=True) * scale  123 us
    unnamed x5, waiting for transfers between devices  89.4 us
    all_gather x1, blocking collectives, shards(): full_rows = lax.all_gather(own_cols, 'blk', axis=1, tiled=True)  37.9 us
  transfers between devices with their start and end apart: 4, of which 4 were waited for; matrix products, arithmetic and copies ran while one was open for 3% of the time, Pallas kernels for 0%

commit v1 on v0

v1 whole, which is shorter than its diff:
```python
import math

import jax
import jax.numpy as jnp
from jax import lax
from jax.experimental import pallas as pl
from jax.experimental.pallas import tpu as pltpu
from jax.sharding import Mesh, PartitionSpec as P

AXES = ("x", "l", "c", "h", "y")
SIZES = (4, 4, 2, 2, 4)
TILE = 256
OFF = ((0, 1), (0, 2), (1, 2))
VMEM_LIMIT = 56 << 20


def local_kernel(core_ref, desc_ref, species_ref, cfg_ref, slot_ref, keep_ref, send_ref, turned):
    core = core_ref[0]
    atoms, width = desc_ref.shape
    configs = slot_ref.shape[1]
    turned[...] = desc_ref[...].T
    species = species_ref[...]
    ids = lax.broadcasted_iota(jnp.int32, (configs, atoms), 0)
    member = (cfg_ref[...] == ids).astype(jnp.bfloat16)
    rows = lax.broadcasted_iota(jnp.int32, (configs, configs), 0)
    place = (slot_ref[...] == rows).astype(jnp.bfloat16)
    placed = jnp.dot(place, member, preferred_element_type=jnp.float32).astype(jnp.bfloat16)

    def put(first, second, start, size):
        keep_ref[:, start : start + size, :] = jnp.where(core == 0, first, second)
        send_ref[:, start : start + size, :] = jnp.where(core == 0, second, first)

    for kind in range(2):
        mask = (species == kind).astype(jnp.bfloat16)
        sums = jnp.dot(placed * mask, desc_ref[...], preferred_element_type=jnp.float32)
        for j in range(3):
            tile = sums[:, j * TILE : (j + 1) * TILE].reshape(16, 2, 8, TILE)
            put(tile[:, 0], tile[:, 1], 96 + (kind * 3 + j) * 8, 8)
        tiles = {}
        for i in range(3):
            left = turned[i * TILE : (i + 1) * TILE, :] * mask
            for j in range(i, 3):
                tiles[i, j] = jnp.dot(
                    left, desc_ref[:, j * TILE : (j + 1) * TILE], preferred_element_type=jnp.float32
                ).reshape(16, 16, TILE)
        for b in range(3):
            put(tiles[OFF[b]], tiles[b, b], (kind * 3 + b) * 16, 16)


def add_kernel(a_ref, b_ref, out_ref):
    out_ref[...] = a_ref[...] + b_ref[...]


def plane_kernel(got_ref, out_ref):
    total = got_ref[0]
    for k in range(1, got_ref.shape[0]):
        total = total + got_ref[k]
    for k in range(out_ref.shape[0]):
        half = k % 2
        out_ref[k, :48, :] = total[half * 48 : half * 48 + 48]
        out_ref[k, 48:, :] = total[96:]


def spread_kernel(scale, got_ref, root_ref, out_ref):
    total = got_ref[0]
    for k in range(1, got_ref.shape[0]):
        total = total + got_ref[k]
    gram = total[:48]
    factor = jnp.tile(root_ref[:, :1] * scale, (6, 1))
    rows = total[48:] * factor
    for k in range(out_ref.shape[0]):
        out_ref[k, :48, :] = gram
        out_ref[k, 48:, :] = rows


def final_kernel(norm, pos_ref, mine_ref, other_ref, root_ref, normal_ref, cfg_ref, full, left, gram):
    core, kind, part, owner = pos_ref[0], pos_ref[1], pos_ref[2], pos_ref[3]
    width = gram.shape[1]
    band = left.shape[1]

    def half(which, start, size):
        a = mine_ref[:, start : start + size, :]
        b = other_ref[:, start : start + size, :]
        return jnp.where(core == which, a, b)

    for j in range(6):
        pair = [half(which, 48 + 8 * j, 8)[:, None] for which in range(2)]
        full[:, j * TILE : (j + 1) * TILE] = jnp.concatenate(pair, 1).reshape(256, TILE)

    def off(b):
        return half(0, 16 * b, 16).reshape(TILE, TILE)

    def diag(b):
        return half(1, 16 * b, 16).reshape(TILE, TILE)

    def block(i, j, lo, hi):
        if i == j:
            return diag(i)[lo:hi]
        if i < j:
            return off(OFF.index((i, j)))[lo:hi]
        return off(OFF.index((j, i)))[:, lo:hi].T

    for k in range(4):

        @pl.when(part == k)
        def _():
            cols = slice(k * band, (k + 1) * band)
            shifted = slice(width + k * band, width + (k + 1) * band)
            left[...] = jnp.where(kind == 0, full[:, cols], full[:, shifted])
            own = pl.ds(pl.multiple_of(owner * 8, 8), 8)
            tile = jnp.where(kind == 0, full[own, cols], full[own, shifted])
            cfg_ref[...] = tile / root_ref[:, :1]
            at = k * band
            while at < (k + 1) * band:
                i = at // TILE
                stop = min((i + 1) * TILE, (k + 1) * band)
                for j in range(3):
                    piece = block(i, j, at - i * TILE, stop - i * TILE)
                    gram[at - k * band : stop - k * band, j * TILE : (j + 1) * TILE] = piece
                at = stop

    for s in range(2):
        cols = slice(s * width, (s + 1) * width)
        cross = lax.dot_general(
            left[...],
            full[:, cols],
            (((0,), (0,)), ((), ())),
            precision=lax.Precision.HIGHEST,
            preferred_element_type=jnp.float32,
        )
        extra = jnp.where(kind == s, gram[...] * (1.0 / norm), 0.0)
        normal_ref[:, cols] = cross * (1.0 / full.shape[0]) + extra


def call(kernel, outs, args, scratch=(), scalars=0):
    smem = [pl.BlockSpec(memory_space=pltpu.SMEM)] * scalars
    vmem = [pl.BlockSpec(memory_space=pltpu.VMEM)] * (len(args) - scalars)
    many = isinstance(outs, (list, tuple))
    out_specs = pl.BlockSpec(memory_space=pltpu.VMEM)
    return pl.pallas_call(
        kernel,
        out_shape=outs,
        in_specs=smem + vmem,
        out_specs=[out_specs] * len(outs) if many else out_specs,
        scratch_shapes=list(scratch),
        compiler_params=pltpu.CompilerParams(vmem_limit_bytes=VMEM_LIMIT),
    )(*args)


def exchange(values, axes):
    flat = values.reshape(-1, values.shape[-1])
    return lax.all_to_all(flat, axes, 0, 0, tiled=True).reshape(values.shape)


def shards(desc, species, atom_cfg, slot, weights):
    atoms, width = desc.shape
    configs = slot.shape[0]
    cfg_here = weights.shape[0]
    n_dev = math.prod(SIZES)
    core, kind, part = lax.axis_index("c"), lax.axis_index("h"), lax.axis_index("y")
    owner = (lax.axis_index("x") * 4 + lax.axis_index("l")) * 2 + core
    f32 = jnp.float32

    def shape(*dims):
        return jax.ShapeDtypeStruct(dims, f32)

    root = jnp.broadcast_to(jnp.sqrt(weights)[:, None], (cfg_here, 128))
    swap = [((l * 2 + h) * 4 + y, (y * 2 + h) * 4 + l) for l in range(4) for h in range(2) for y in range(4)]
    root_here = lax.ppermute(root, ("l", "h", "y"), swap)

    keep, send = call(
        local_kernel,
        [shape(16, 144, TILE), shape(16, 144, TILE)],
        [core[None], desc, species[None], atom_cfg[None], slot[None]],
        [pltpu.VMEM((width, atoms), jnp.bfloat16)],
        1,
    )
    flip = [(0, 1), (1, 0)]
    paired = call(add_kernel, shape(16, 144, TILE), [keep, lax.ppermute(send, "c", flip)])
    planes = call(plane_kernel, shape(8, 96, TILE), [exchange(paired, ("x", "y"))])
    scale = 1.0 / math.sqrt(atoms * n_dev / configs)
    spread = call(
        lambda *refs: spread_kernel(scale, *refs),
        shape(16, 96, TILE),
        [exchange(planes, ("l", "h")), root_here],
    )
    mine = exchange(spread, ("x", "y"))
    other = lax.ppermute(mine, "c", flip)
    band = 2 * width // 8
    norm = atoms * n_dev // 8
    normal, rows = call(
        lambda *refs: final_kernel(norm, *refs),
        [shape(band, 2 * width), shape(cfg_here, band)],
        [jnp.stack([core, kind, part, owner]), mine, other, root],
        [
            pltpu.VMEM((configs, 2 * width), f32),
            pltpu.VMEM((configs, band), f32),
            pltpu.VMEM((band, width), f32),
        ],
        1,
    )
    return normal, rows


def solution(mesh):
    fine = Mesh(mesh.devices.reshape(SIZES), AXES)
    return jax.shard_map(
        shards,
        mesh=fine,
        in_specs=(P(AXES, None), P(AXES), P(AXES), P(), P(("x", "l", "c"))),
        out_specs=(P(("h", "y"), None), P(("x", "l", "c"), ("h", "y"))),
        check_vma=False,
    )
```

time: 750 us -> 129 us (0.17)
  waiting for transfers between devices: 650 us -> 24.6 us
  Pallas kernels: 0 us -> 22.9 us
  blocking collectives: 37.9 us -> 60.4 us
  matrix products: 21.2 us -> 0 us
  local copies, waits for them, and re-layouts: 20.8 us -> 3.56 us
  starting transfers between devices: 0.16 us -> 14.9 us
  between operations: 13.9 us -> 0.68 us
    reduce_scatter x2 -> x0, waiting for transfers between devices: 292 us -> none  [the longest x1 169 us: shards(): lax.psum_scatter(lax.dot_general(design, design, (((0,), (0,)), ((), ()))...]
    psum x1 -> x0, waiting for transfers between devices: 269 us -> none  [shards(): normal_matrix = lax.psum(total, 'atoms')]
    unnamed x5 -> x0, waiting for transfers between devices: 89.4 us -> none
    all_to_all x0 -> x2, blocking collectives: none -> 60.4 us  [exchange(): return lax.all_to_all(flat, axes, 0, 0, tiled=True).reshape(values.shape)]
    all_gather x1 -> x0, blocking collectives: 37.9 us -> none  [shards(): full_rows = lax.all_gather(own_cols, 'blk', axis=1, tiled=True)]
    pallas_call x0 -> x5, Pallas kernels: none -> 22.9 us  [call(): pl.pallas_call(kernel, out_shape=outs, in_specs=smem + vmem, out_specs=[o...]
    dot_general x3 -> x0, matrix products: 21.2 us -> none  [the longest x1 14.5 us: shards(): lax.dot_general(design, design, (((0,), (0,)), ((), ())), preferred_eleme...]
    all_to_all x0 -> x1, waiting for transfers between devices: none -> 17.8 us  [exchange(): return lax.all_to_all(flat, axes, 0, 0, tiled=True).reshape(values.shape)]
  transfers between devices with their start and end apart: 4 -> 4, of which waited for: 4 -> 3; matrix products, arithmetic and copies ran while one was open for 3% -> 1% of each run, Pallas kernels for 0% -> 0%
where the time goes in v1:
time: 129 us; the launch traced here: 128 us
  blocking collectives  60.4 us (47%)
  waiting for transfers between devices  24.6 us (19%)
  Pallas kernels  22.9 us (18%)
  starting transfers between devices  14.9 us (12%)
  local copies, waits for them, and re-layouts  3.56 us (3%)
    all_to_all x2, blocking collectives, exchange(): return lax.all_to_all(flat, axes, 0, 0, tiled=True).reshape(values.shape)  60.4 us
    pallas_call x5, Pallas kernels, call(): pl.pallas_call(kernel, out_shape=outs, in_specs=smem + vmem, out_specs=[o...  22.9 us
    all_to_all x1, waiting for transfers between devices, exchange(): return lax.all_to_all(flat, axes, 0, 0, tiled=True).reshape(values.shape)  17.8 us
    all_to_all x1, starting transfers between devices, exchange(): return lax.all_to_all(flat, axes, 0, 0, tiled=True).reshape(values.shape)  8.18 us
    ppermute x1, waiting for transfers between devices, shards(): lax.ppermute(send, 'c', flip)  4.37 us
    unnamed x14, local copies, waits for them, and re-layouts  3.49 us
    ppermute x1, starting transfers between devices, shards(): lax.ppermute(send, 'c', flip)  3.24 us
    ppermute x1, starting transfers between devices, shards(): other = lax.ppermute(mine, 'c', flip)  2.84 us
  transfers between devices with their start and end apart: 4, of which 3 were waited for; matrix products, arithmetic and copies ran while one was open for 1% of the time, Pallas kernels for 0%

profile of v1, /device:TPU:1, one launch (start us, length us, event | category | flops | bytes accessed | tf_op | source)
XLA Modules:
  0.0 127.6 jit_solution(15817869406995390149)
XLA Ops:
  0.6 9.4 %shard_map.68 = (f32[16,144,256]{2,1,0:T(8,128)}, f32[16,144,256]{2,1,0:T(8,128)}) custom-call(s32[1]{0:T(128)} %bitcast.core_ref, bf16[2048,768]{1,0:T(8,128)(2,1)} %desc_ref.1, s32[1,2048]{1,0:T(1,128)} %bitcast.7, s32[1,2048]{1,0:T(1,128)} %bitcast.8, s32[1,256]{1,0:T(1,128)} %bitcast.9), custom_call_target="tpu_custom_call" | custom-call | tf_op jit(solution)/shard_map/pallas_call | solution.py:140
  10.0 3.2 %collective-permute-start = (f32[16,144,256]{2,1,0:T(8,128)}, f32[16,144,256]{2,1,0:T(8,128)S(1)}, u32[]{:S(2)}, u32[]{:S(2)}) collective-permute-start(f32[16,144,256]{2,1,0:T(8,128)} %get-tuple-element.5), channel_id=1, source_target_pairs={{0,8},{8,0},{1,9},{9,1},{2,10},{10,2},{3,11},{11,3},{4,12},{12,4},... | collective-permute-start | bytes 7077896 | tf_op jit(solution)/shard_map/ppermute | solution.py:179
  13.3 4.4 %collective-permute-done.b_ref = f32[16,144,256]{2,1,0:T(8,128)S(1)} collective-permute-done((f32[16,144,256]{2,1,0:T(8,128)}, f32[16,144,256]{2,1,0:T(8,128)S(1)}, u32[]{:S(2)}, u32[]{:S(2)}) %collective-permute-start) | collective-permute-done | bytes 2359328 | tf_op jit(solution)/shard_map/ppermute | solution.py:179
  17.7 0.0 copy-start.2
  17.7 1.4 %copy-done.2 = f32[16,144,256]{2,1,0:T(8,128)} copy-done((f32[16,144,256]{2,1,0:T(8,128)}, f32[16,144,256]{2,1,0:T(8,128)S(1)}, u32[]{:S(2)}) %copy-start.2) | copy-done | bytes 2359320
  19.1 4.0 %shard_map.69 = f32[16,144,256]{2,1,0:T(8,128)} custom-call(f32[16,144,256]{2,1,0:T(8,128)} %get-tuple-element.4.a_ref, f32[16,144,256]{2,1,0:T(8,128)} %copy-done.2), custom_call_target="tpu_custom_call" | custom-call | tf_op jit(solution)/shard_map/pallas_call | solution.py:140
  23.1 35.3 %all_to_all.18.got_ref = f32[16,144,256]{2,1,0:T(8,128)} all-to-all(f32[16,144,256]{2,1,0:T(8,128)} %shard_map.69), channel_id=1, replica_groups=mesh['x'=4,'l'=4,'c'=2,'h'=2,'y'=4] {'x','y'}, dimensions={0} | all-to-all | bytes 4718592 | tf_op jit(solution)/shard_map/all_to_all | solution.py:152
  58.4 0.0 copy-start.6
  58.4 2.7 %shard_map.70 = f32[8,96,256]{2,1,0:T(8,128)} custom-call(f32[16,144,256]{2,1,0:T(8,128)} %all_to_all.18.got_ref), custom_call_target="tpu_custom_call" | custom-call | tf_op jit(solution)/shard_map/pallas_call | solution.py:140
  61.1 8.2 %all-to-all-start.1 = ((f32[8,96,256]{2,1,0:T(8,128)}), f32[8,96,256]{2,1,0:T(8,128)S(1)}, u32[]{:S(2)}, u32[]{:S(2)}) async-start(f32[8,96,256]{2,1,0:T(8,128)} %shard_map.70), calls=%async_computation.1 | async-start | bytes 1572864 | tf_op jit(solution)/shard_map/all_to_all | solution.py:152
  69.3 0.0 copy-done.6
  69.3 0.1 broadcast_in_dim.19.refs_3_
  69.3 0.0 copy-start.4
  69.3 0.7 collective-permute-start.1
  70.0 0.0 collective-permute-done.1.refs_1_
  70.0 0.0 copy-start.5
  70.0 17.8 %all-to-all-done.1.refs_0_ = f32[8,96,256]{2,1,0:T(8,128)S(1)} async-done(((f32[8,96,256]{2,1,0:T(8,128)}), f32[8,96,256]{2,1,0:T(8,128)S(1)}, u32[]{:S(2)}, u32[]{:S(2)}) %all-to-all-start.1) | async-done | bytes 786464 | tf_op jit(solution)/shard_map/all_to_all | solution.py:152
  87.8 0.0 copy-done.5
  87.8 0.0 copy-start.1
  87.8 0.9 copy-done.1
  88.7 2.4 %shard_map.71 = f32[16,96,256]{2,1,0:T(8,128)} custom-call(f32[8,96,256]{2,1,0:T(8,128)} %copy-done.1, f32[8,128]{1,0:T(8,128)} %copy-done.5), custom_call_target="tpu_custom_call" | custom-call | tf_op jit(solution)/shard_map/pallas_call | solution.py:140
  91.2 25.1 %all_to_all.19.refs_1_ = f32[16,96,256]{2,1,0:T(8,128)S(1)} all-to-all(f32[16,96,256]{2,1,0:T(8,128)} %shard_map.71), channel_id=1, replica_groups=mesh['x'=4,'l'=4,'c'=2,'h'=2,'y'=4] {'x','y'}, dimensions={0} | all-to-all | bytes 3145728 | tf_op jit(solution)/shard_map/all_to_all | solution.py:152
  116.3 0.0 copy-start
  116.3 2.8 %collective-permute-start.2 = (f32[16,96,256]{2,1,0:T(8,128)S(1)}, f32[16,96,256]{2,1,0:T(8,128)S(1)}, u32[]{:S(2)}, u32[]{:S(2)}) collective-permute-start(f32[16,96,256]{2,1,0:T(8,128)S(1)} %all_to_all.19.refs_1_), channel_id=1, source_target_pairs={{0,8},{8,0},{1,9},{9,1},{2,10},{10,2},{3,11},{11,3},{4,12},{12,4},... | collective-permute-start | bytes 4718600 | tf_op jit(solution)/shard_map/ppermute | solution.py:188
  119.1 0.6 pad_add_fusion.refs_0_
  119.7 2.4 %collective-permute-done.2.refs_2_ = f32[16,96,256]{2,1,0:T(8,128)S(1)} collective-permute-done((f32[16,96,256]{2,1,0:T(8,128)S(1)}, f32[16,96,256]{2,1,0:T(8,128)S(1)}, u32[]{:S(2)}, u32[]{:S(2)}) %collective-permute-start.2) | collective-permute-done | bytes 1572896 | tf_op jit(solution)/shard_map/ppermute | solution.py:188
  122.1 0.0 copy-done.4
  122.1 0.0 copy-done
  122.1 0.0 copy-start.3
  122.1 1.1 copy-done.3
  123.3 4.3 %shard_map.72 = (f32[192,1536]{1,0:T(8,128)}, f32[8,192]{1,0:T(8,128)}) custom-call(s32[4]{0:T(128)} %pad_add_fusion.refs_0_, f32[16,96,256]{2,1,0:T(8,128)} %copy-done, f32[16,96,256]{2,1,0:T(8,128)} %copy-done.3, f32[8,128]{1,0:T(8,128)} %copy-done.4), custom_call_target="tpu_custom_call" | custom-call | tf_op jit(solution)/shard_map/pallas_call | solution.py:140
  (1 shorter events, 0.0 us)
Async XLA Ops:
  10.0 7.6 %collective-permute-start = (f32[16,144,256]{2,1,0:T(8,128)}, f32[16,144,256]{2,1,0:T(8,128)S(1)}, u32[]{:S(2)}, u32[]{:S(2)}) collective-permute-start(f32[16,144,256]{2,1,0:T(8,128)} %get-tuple-element.5), channel_id=1, source_target_pairs={{0,8},{8,0},{1,9},{9,1},{2,10},{10,2},{3,11},{11,3},{4,12},{12,4},... | collective-permute-start | bytes 7077896 | tf_op jit(solution)/shard_map/ppermute | solution.py:179
  17.7 1.4 %copy-start.2 = (f32[16,144,256]{2,1,0:T(8,128)}, f32[16,144,256]{2,1,0:T(8,128)S(1)}, u32[]{:S(2)}) copy-start(f32[16,144,256]{2,1,0:T(8,128)S(1)} %collective-permute-done.b_ref) | copy-start | bytes 7077892
  58.4 10.9 %copy-start.6 = (f32[8]{0:T(128)S(1)}, f32[8]{0:T(128)}, u32[]{:S(2)}) copy-start(f32[8]{0:T(128)} %param.9) | copy-start | bytes 100
  61.1 26.8 %all-to-all-start.1 = ((f32[8,96,256]{2,1,0:T(8,128)}), f32[8,96,256]{2,1,0:T(8,128)S(1)}, u32[]{:S(2)}, u32[]{:S(2)}) async-start(f32[8,96,256]{2,1,0:T(8,128)} %shard_map.70), calls=%async_computation.1 | async-start | bytes 1572864 | tf_op jit(solution)/shard_map/all_to_all | solution.py:152
  69.3 52.8 %copy-start.4 = (f32[8,128]{1,0:T(8,128)}, f32[8,128]{1,0:T(8,128)S(1)}, u32[]{:S(2)}) copy-start(f32[8,128]{1,0:T(8,128)S(1)} %broadcast_in_dim.19.refs_3_) | copy-start | bytes 12292
  69.3 0.7 collective-permute-start.1
  70.0 17.8 %copy-start.5 = (f32[8,128]{1,0:T(8,128)}, f32[8,128]{1,0:T(8,128)S(1)}, u32[]{:S(2)}) copy-start(f32[8,128]{1,0:T(8,128)S(1)} %collective-permute-done.1.refs_1_) | copy-start | bytes 12292
  87.8 0.9 copy-start.1
  116.3 5.9 %copy-start = (f32[16,96,256]{2,1,0:T(8,128)}, f32[16,96,256]{2,1,0:T(8,128)S(1)}, u32[]{:S(2)}) copy-start(f32[16,96,256]{2,1,0:T(8,128)S(1)} %all_to_all.19.refs_1_) | copy-start | bytes 4718596
  116.3 5.9 %collective-permute-start.2 = (f32[16,96,256]{2,1,0:T(8,128)S(1)}, f32[16,96,256]{2,1,0:T(8,128)S(1)}, u32[]{:S(2)}, u32[]{:S(2)}) collective-permute-start(f32[16,96,256]{2,1,0:T(8,128)S(1)} %all_to_all.19.refs_1_), channel_id=1, source_target_pairs={{0,8},{8,0},{1,9},{9,1},{2,10},{10,2},{3,11},{11,3},{4,12},{12,4},... | collective-permute-start | bytes 4718600 | tf_op jit(solution)/shard_map/ppermute | solution.py:188
  122.1 1.2 copy-start.3

commit v2 on v1

--- a/solution.py
+++ b/solution.py
@@ -14,66 +14,54 @@
 VMEM_LIMIT = 56 << 20
 
 
-def local_kernel(core_ref, desc_ref, species_ref, cfg_ref, slot_ref, keep_ref, send_ref, turned):
+def split(core, first, second, keep_ref, send_ref, start, size):
+    keep_ref[:, start : start + size, :] = jnp.where(core == 0, first, second)
+    send_ref[:, start : start + size, :] = jnp.where(core == 0, second, first)
+
+
+def sums_kernel(core_ref, desc_ref, species_ref, cfg_ref, slot_ref, keep_ref, send_ref):
     core = core_ref[0]
-    atoms, width = desc_ref.shape
+    atoms = desc_ref.shape[0]
     configs = slot_ref.shape[1]
-    turned[...] = desc_ref[...].T
-    species = species_ref[...]
     ids = lax.broadcasted_iota(jnp.int32, (configs, atoms), 0)
     member = (cfg_ref[...] == ids).astype(jnp.bfloat16)
     rows = lax.broadcasted_iota(jnp.int32, (configs, configs), 0)
     place = (slot_ref[...] == rows).astype(jnp.bfloat16)
     placed = jnp.dot(place, member, preferred_element_type=jnp.float32).astype(jnp.bfloat16)
-
-    def put(first, second, start, size):
-        keep_ref[:, start : start + size, :] = jnp.where(core == 0, first, second)
-        send_ref[:, start : start + size, :] = jnp.where(core == 0, second, first)
-
     for kind in range(2):
-        mask = (species == kind).astype(jnp.bfloat16)
+        mask = (species_ref[...] == kind).astype(jnp.bfloat16)
         sums = jnp.dot(placed * mask, desc_ref[...], preferred_element_type=jnp.float32)
         for j in range(3):
             tile = sums[:, j * TILE : (j + 1) * TILE].reshape(16, 2, 8, TILE)
-            put(tile[:, 0], tile[:, 1], 96 + (kind * 3 + j) * 8, 8)
-        tiles = {}
-        for i in range(3):
-            left = turned[i * TILE : (i + 1) * TILE, :] * mask
-            for j in range(i, 3):
-                tiles[i, j] = jnp.dot(
-                    left, desc_ref[:, j * TILE : (j + 1) * TILE], preferred_element_type=jnp.float32
-                ).reshape(16, 16, TILE)
-        for b in range(3):
-            put(tiles[OFF[b]], tiles[b, b], (kind * 3 + b) * 16, 16)
-
-
-def add_kernel(a_ref, b_ref, out_ref):
-    out_ref[...] = a_ref[...] + b_ref[...]
-
-
-def plane_kernel(got_ref, out_ref):
-    total = got_ref[0]
-    for k in range(1, got_ref.shape[0]):
-        total = total + got_ref[k]
-    for k in range(out_ref.shape[0]):
-        half = k % 2
-        out_ref[k, :48, :] = total[half * 48 : half * 48 + 48]
-        out_ref[k, 48:, :] = total[96:]
-
-
-def spread_kernel(scale, got_ref, root_ref, out_ref):
-    total = got_ref[0]
-    for k in range(1, got_ref.shape[0]):
-        total = total + got_ref[k]
-    gram = total[:48]
-    factor = jnp.tile(root_ref[:, :1] * scale, (6, 1))
-    rows = total[48:] * factor
-    for k in range(out_ref.shape[0]):
-        out_ref[k, :48, :] = gram
-        out_ref[k, 48:, :] = rows
-
-
-def final_kernel(norm, pos_ref, mine_ref, other_ref, root_ref, normal_ref, cfg_ref, full, left, gram):
+            split(core, tile[:, 0], tile[:, 1], keep_ref, send_ref, (kind * 3 + j) * 8, 8)
+
+
+def gram_kernel(off_ref, desc_ref, species_ref, out_ref):
+    def tiles(pairs):
+        turned = {}
+        for b, (i, j) in enumerate(pairs):
+            if i not in turned:
+                turned[i] = desc_ref[:, i * TILE : (i + 1) * TILE].T
+            for kind in range(2):
+                mask = (species_ref[...] == kind).astype(jnp.bfloat16)
+                tile = jnp.dot(
+                    turned[i] * mask, desc_ref[:, j * TILE : (j + 1) * TILE], preferred_element_type=jnp.float32
+                )
+                start = (kind * 3 + b) * 16
+                out_ref[:, start : start + 16, :] = tile.reshape(16, 16, TILE)
+
+    @pl.when(off_ref[0] == 1)
+    def _():
+        tiles(OFF)
+
+    @pl.when(off_ref[0] == 0)
+    def _():
+        tiles(((0, 0), (1, 1), (2, 2)))
+
+
+def final_kernel(
+    norm, pos_ref, mine_ref, other_ref, root_ref, normal_ref, cfg_ref, full, left, gram
+):
     core, kind, part, owner = pos_ref[0], pos_ref[1], pos_ref[2], pos_ref[3]
     width = gram.shape[1]
     band = left.shape[1]
@@ -168,23 +156,27 @@
     swap = [((l * 2 + h) * 4 + y, (y * 2 + h) * 4 + l) for l in range(4) for h in range(2) for y in range(4)]
     root_here = lax.ppermute(root, ("l", "h", "y"), swap)
 
-    keep, send = call(
-        local_kernel,
-        [shape(16, 144, TILE), shape(16, 144, TILE)],
+    flip = [(0, 1), (1, 0)]
+    scale = 1.0 / math.sqrt(atoms * n_dev / configs)
+    keep_s, send_s = call(
+        sums_kernel,
+        [shape(16, 48, TILE)] * 2,
         [core[None], desc, species[None], atom_cfg[None], slot[None]],
-        [pltpu.VMEM((width, atoms), jnp.bfloat16)],
-        1,
+        scalars=1,
     )
-    flip = [(0, 1), (1, 0)]
-    paired = call(add_kernel, shape(16, 144, TILE), [keep, lax.ppermute(send, "c", flip)])
-    planes = call(plane_kernel, shape(8, 96, TILE), [exchange(paired, ("x", "y"))])
-    scale = 1.0 / math.sqrt(atoms * n_dev / configs)
-    spread = call(
-        lambda *refs: spread_kernel(scale, *refs),
-        shape(16, 96, TILE),
-        [exchange(planes, ("l", "h")), root_here],
-    )
-    mine = exchange(spread, ("x", "y"))
+    keep_s, send_s, desc = lax.optimization_barrier((keep_s, send_s, desc))
+    send_g = call(gram_kernel, shape(16, 96, TILE), [core[None], desc, species[None]], scalars=1)
+    came_s, root_here = lax.optimization_barrier((lax.ppermute(send_s, "c", flip), root_here))
+    send_g, sums, desc = lax.optimization_barrier((send_g, keep_s + came_s, desc))
+    keep_g = call(gram_kernel, shape(16, 96, TILE), [1 - core[None], desc, species[None]], scalars=1)
+    grams = keep_g + lax.ppermute(send_g, "c", flip)
+    sums = jnp.sum(exchange(sums, ("x", "y")), 0)
+    grams = jnp.sum(exchange(grams, ("x", "y")), 0)
+    planes = jnp.stack([jnp.concatenate([grams[:48], sums]), jnp.concatenate([grams[48:], sums])])
+    planes = jnp.broadcast_to(planes[None], (4, 2, 96, TILE)).reshape(8, 96, TILE)
+    total = jnp.sum(exchange(planes, ("l", "h")), 0)
+    factor = jnp.concatenate([jnp.ones((48, 1), f32), jnp.tile(root_here[:, :1] * scale, (6, 1))])
+    mine = exchange(jnp.broadcast_to(total * factor, (16, 96, TILE)), ("x", "y"))
     other = lax.ppermute(mine, "c", flip)
     band = 2 * width // 8
     norm = atoms * n_dev // 8

time: 129 us -> 129 us (level)
  blocking collectives: 60.4 us -> 25.6 us
  waiting for transfers between devices: 24.6 us -> 44.7 us
  starting transfers between devices: 14.9 us -> 28.4 us
  other arithmetic: 0.6 us -> 5.29 us
  Pallas kernels: 22.9 us -> 19.2 us
    all_to_all x2 -> x1, blocking collectives: 60.4 us -> 25.6 us  [exchange(): return lax.all_to_all(flat, axes, 0, 0, tiled=True).reshape(values.shape)]
    all_to_all x1 -> x3, waiting for transfers between devices: 17.8 us -> 42.2 us  [exchange(): return lax.all_to_all(flat, axes, 0, 0, tiled=True).reshape(values.shape)]
    all_to_all x1 -> x3, starting transfers between devices: 8.18 us -> 21.3 us  [exchange(): return lax.all_to_all(flat, axes, 0, 0, tiled=True).reshape(values.shape)]
    ppermute x1 -> x2, waiting for transfers between devices: 4.37 us -> 0.01 us  [the longest x1 0.01 us: shards(): grams = keep_g + lax.ppermute(send_g, 'c', flip)]
    add x0 -> x2, other arithmetic: none -> 4.26 us  [the longest x1 3.27 us: shards(): grams = keep_g + lax.ppermute(send_g, 'c', flip)]
    pallas_call x5 -> x4, Pallas kernels: 22.9 us -> 19.2 us  [call(): pl.pallas_call(kernel, out_shape=outs, in_specs=smem + vmem, out_specs=[o...]
    unnamed x14 -> x12, local copies, waits for them, and re-layouts: 3.49 us -> 1.85 us
    ppermute x1 -> x2, starting transfers between devices: 3.24 us -> 3.24 us  [the longest x1 3.24 us: shards(): lax.ppermute(send_s, 'c', flip)]
  transfers between devices with their start and end apart: 4 -> 7, of which waited for: 3 -> 4; matrix products, arithmetic and copies ran while one was open for 1% -> 3% of each run, Pallas kernels for 0% -> 8%
where the time goes in v2:
time: 129 us; the launch traced here: 127 us
  waiting for transfers between devices  44.7 us (35%)
  starting transfers between devices  28.4 us (22%)
  blocking collectives  25.6 us (20%)
  Pallas kernels  19.2 us (15%)
  other arithmetic  5.29 us (4%)
  local copies, waits for them, and re-layouts  3.19 us (2%)
    all_to_all x3, waiting for transfers between devices, exchange(): return lax.all_to_all(flat, axes, 0, 0, tiled=True).reshape(values.shape)  42.2 us
    all_to_all x1, blocking collectives, exchange(): return lax.all_to_all(flat, axes, 0, 0, tiled=True).reshape(values.shape)  25.6 us
    all_to_all x3, starting transfers between devices, exchange(): return lax.all_to_all(flat, axes, 0, 0, tiled=True).reshape(values.shape)  21.3 us
    pallas_call x4, Pallas kernels, call(): pl.pallas_call(kernel, out_shape=outs, in_specs=smem + vmem, out_specs=[o...  19.2 us
    add x1, other arithmetic, shards(): grams = keep_g + lax.ppermute(send_g, 'c', flip)  3.27 us
    ppermute x1, starting transfers between devices, shards(): lax.ppermute(send_s, 'c', flip)  3.24 us
    ppermute x1, starting transfers between devices, shards(): other = lax.ppermute(mine, 'c', flip)  3.07 us
  transfers between devices with their start and end apart: 7, of which 4 were waited for; matrix products, arithmetic and copies ran while one was open for 3% of the time, Pallas kernels for 8%

profile of v2, /device:TPU:1, one launch (start us, length us, event | category | flops | bytes accessed | tf_op | source)
XLA Modules:
  0.0 127.1 jit_solution(12140629266587471559)
XLA Ops:
  0.6 0.0 copy-start.5
  0.6 5.2 %shard_map.68 = (f32[16,48,256]{2,1,0:T(8,128)}, f32[16,48,256]{2,1,0:T(8,128)}) custom-call(s32[1]{0:T(128)} %bitcast.core_ref.off_ref, bf16[2048,768]{1,0:T(8,128)(2,1)} %desc_ref.3, s32[1,2048]{1,0:T(1,128)} %bitcast.14, s32[1,2048]{1,0:T(1,128)} %bitcast.17, s32[1,256]{1,0:T(1,128)} %bitcast.18), custom_call_target="tpu_custom_call" | custom-call | tf_op jit(solution)/shard_map/pallas_call | solution.py:128
  5.8 3.2 %collective-permute-start = (f32[16,48,256]{2,1,0:T(8,128)}, f32[16,48,256]{2,1,0:T(8,128)S(1)}, u32[]{:S(2)}, u32[]{:S(2)}) collective-permute-start(f32[16,48,256]{2,1,0:T(8,128)} %get-tuple-element.16), channel_id=1, source_target_pairs={{0,8},{8,0},{1,9},{9,1},{2,10},{10,2},{3,11},{11,3},{4,12},{12,4},... | collective-permute-start | bytes 2359304 | tf_op jit(solution)/shard_map/ppermute | solution.py:169
  9.1 0.0 copy-done.5
  9.1 0.1 broadcast_in_dim.15.refs_3_
  9.1 0.0 copy-start.4
  9.1 0.0 copy-start.3
  9.1 0.8 collective-permute-start.1
  9.9 4.9 %shard_map.69 = f32[16,96,256]{2,1,0:T(8,128)} custom-call(s32[1]{0:T(128)} %bitcast.core_ref.off_ref, bf16[2048,768]{1,0:T(8,128)(2,1)} %desc_ref.3, s32[1,2048]{1,0:T(1,128)} %bitcast.15), custom_call_target="tpu_custom_call" | custom-call | tf_op jit(solution)/shard_map/pallas_call | solution.py:128
  14.8 0.0 copy-done.4
  14.8 0.0 copy-start.1
  14.8 0.0 collective-permute-done.1
  14.8 0.0 collective-permute-done
  14.8 0.0 copy-done.3
  14.8 1.0 add.16
  15.8 0.7 copy-done.1
  16.5 0.0 collective-permute-start.2
  16.5 10.4 %all-to-all-start.1 = ((f32[16,48,256]{2,1,0:T(8,128)}), f32[16,48,256]{2,1,0:T(8,128)S(1)}, u32[]{:S(2)}, u32[]{:S(2)}) async-start(f32[16,48,256]{2,1,0:T(8,128)} %add.16), calls=%async_computation.1 | async-start | bytes 1572864 | tf_op jit(solution)/shard_map/all_to_all | solution.py:140
  26.9 4.9 %shard_map.70 = f32[16,96,256]{2,1,0:T(8,128)} custom-call(s32[1]{0:T(128)S(6)} %sub.3.off_ref, bf16[2048,768]{1,0:T(8,128)(2,1)} %desc_ref.3, s32[1,2048]{1,0:T(1,128)} %bitcast.16), custom_call_target="tpu_custom_call" | custom-call | tf_op jit(solution)/shard_map/pallas_call | solution.py:128
  31.7 0.0 collective-permute-done.2
  31.8 3.3 %add.17 = f32[16,96,256]{2,1,0:T(8,128)} add(f32[16,96,256]{2,1,0:T(8,128)} %shard_map.70, f32[16,96,256]{2,1,0:T(8,128)} %collective-permute-done.2) | non-fusion elementwise | flops 393216 | bytes 4718592 | tf_op jit(solution)/shard_map/add | solution.py:172
  35.0 4.5 %all-to-all-done.1 = f32[16,48,256]{2,1,0:T(8,128)S(1)} async-done(((f32[16,48,256]{2,1,0:T(8,128)}), f32[16,48,256]{2,1,0:T(8,128)S(1)}, u32[]{:S(2)}, u32[]{:S(2)}) %all-to-all-start.1) | async-done | bytes 786464 | tf_op jit(solution)/shard_map/all_to_all | solution.py:140
  39.5 4.6 %all-to-all-start = ((f32[16,96,256]{2,1,0:T(8,128)}), f32[16,96,256]{2,1,0:T(8,128)S(1)}, u32[]{:S(2)}, u32[]{:S(2)}) async-start(f32[16,96,256]{2,1,0:T(8,128)} %add.17), calls=%async_computation | async-start | bytes 3145728 | tf_op jit(solution)/shard_map/all_to_all | solution.py:140
  44.1 0.1 reduce_sum.28
  44.2 20.3 %all-to-all-done = f32[16,96,256]{2,1,0:T(8,128)S(1)} async-done(((f32[16,96,256]{2,1,0:T(8,128)}), f32[16,96,256]{2,1,0:T(8,128)S(1)}, u32[]{:S(2)}, u32[]{:S(2)}) %all-to-all-start) | async-done | bytes 1572896 | tf_op jit(solution)/shard_map/all_to_all | solution.py:140
  64.5 0.1 reduce_sum.27
  64.6 0.9 broadcast_in_dim.16
  65.6 6.3 %all-to-all-start.2 = ((f32[8,96,256]{2,1,0:T(8,128)}), f32[8,96,256]{2,1,0:T(8,128)S(1)}, u32[]{:S(2)}, u32[]{:S(2)}) async-start(f32[8,96,256]{2,1,0:T(8,128)} %bitcast.9), calls=%async_computation.2 | async-start | bytes 1572864 | tf_op jit(solution)/shard_map/all_to_all | solution.py:140
  71.9 0.1 multiply_reduce_fusion
  72.0 0.1 tile.13
  72.1 0.1 pad_bitcast_fusion
  72.2 17.5 %all-to-all-done.2 = f32[8,96,256]{2,1,0:T(8,128)S(1)} async-done(((f32[8,96,256]{2,1,0:T(8,128)}), f32[8,96,256]{2,1,0:T(8,128)S(1)}, u32[]{:S(2)}, u32[]{:S(2)}) %all-to-all-start.2) | async-done | bytes 786464 | tf_op jit(solution)/shard_map/all_to_all | solution.py:140
  89.6 0.1 reduce_sum.29
  89.7 0.1 broadcast_multiply_fusion
  89.8 0.1 broadcast_in_dim.17
  89.9 25.6 %all_to_all.27.refs_1_ = f32[16,96,256]{2,1,0:T(8,128)S(1)} all-to-all(f32[16,96,256]{2,1,0:T(8,128)S(1)} %broadcast_in_dim.17), channel_id=1, replica_groups=mesh['x'=4,'l'=4,'c'=2,'h'=2,'y'=4] {'x','y'}, dimensions={0} | all-to-all | bytes 3145728 | tf_op jit(solution)/shard_map/all_to_all | solution.py:140
  115.5 0.0 copy-start
  115.5 3.1 %collective-permute-start.3 = (f32[16,96,256]{2,1,0:T(8,128)S(1)}, f32[16,96,256]{2,1,0:T(8,128)S(1)}, u32[]{:S(2)}, u32[]{:S(2)}) collective-permute-start(f32[16,96,256]{2,1,0:T(8,128)S(1)} %all_to_all.27.refs_1_), channel_id=1, source_target_pairs={{0,8},{8,0},{1,9},{9,1},{2,10},{10,2},{3,11},{11,3},{4,12},{12,4},... | collective-permute-start | bytes 4718600 | tf_op jit(solution)/shard_map/ppermute | solution.py:180
  118.6 0.6 pad_add_fusion.refs_0_
  119.2 2.4 %collective-permute-done.3.refs_2_ = f32[16,96,256]{2,1,0:T(8,128)S(1)} collective-permute-done((f32[16,96,256]{2,1,0:T(8,128)S(1)}, f32[16,96,256]{2,1,0:T(8,128)S(1)}, u32[]{:S(2)}, u32[]{:S(2)}) %collective-permute-start.3) | collective-permute-done | bytes 1572896 | tf_op jit(solution)/shard_map/ppermute | solution.py:180
  121.7 0.0 copy-done
  121.7 0.0 copy-start.2
  121.7 1.2 copy-done.2
  122.8 4.3 %shard_map.71 = (f32[192,1536]{1,0:T(8,128)}, f32[8,192]{1,0:T(8,128)}) custom-call(s32[4]{0:T(128)} %pad_add_fusion.refs_0_, f32[16,96,256]{2,1,0:T(8,128)} %copy-done, f32[16,96,256]{2,1,0:T(8,128)} %copy-done.2, f32[8,128]{1,0:T(8,128)} %copy-done.4), custom_call_target="tpu_custom_call" | custom-call | tf_op jit(solution)/shard_map/pallas_call | solution.py:128
  (5 shorter events, 0.1 us)
Async XLA Ops:
  0.6 8.4 %copy-start.5 = (f32[8]{0:T(128)S(1)}, f32[8]{0:T(128)}, u32[]{:S(2)}) copy-start(f32[8]{0:T(128)} %param.9) | copy-start | bytes 100
  5.8 9.0 %collective-permute-start = (f32[16,48,256]{2,1,0:T(8,128)}, f32[16,48,256]{2,1,0:T(8,128)S(1)}, u32[]{:S(2)}, u32[]{:S(2)}) collective-permute-start(f32[16,48,256]{2,1,0:T(8,128)} %get-tuple-element.16), channel_id=1, source_target_pairs={{0,8},{8,0},{1,9},{9,1},{2,10},{10,2},{3,11},{11,3},{4,12},{12,4},... | collective-permute-start | bytes 2359304 | tf_op jit(solution)/shard_map/ppermute | solution.py:169
  9.1 5.7 %copy-start.4 = (f32[8,128]{1,0:T(8,128)}, f32[8,128]{1,0:T(8,128)S(1)}, u32[]{:S(2)}) copy-start(f32[8,128]{1,0:T(8,128)S(1)} %broadcast_in_dim.15.refs_3_) | copy-start | bytes 12292
  9.1 5.7 %copy-start.3 = (f32[16,48,256]{2,1,0:T(8,128)S(1)}, f32[16,48,256]{2,1,0:T(8,128)}, u32[]{:S(2)}) copy-start(f32[16,48,256]{2,1,0:T(8,128)} %get-tuple-element.15) | copy-start | bytes 2359300
  9.1 5.7 %collective-permute-start.1 = (f32[8,128]{1,0:T(8,128)S(1)}, f32[8,128]{1,0:T(8,128)S(1)}, u32[]{:S(2)}, u32[]{:S(2)}) collective-permute-start(f32[8,128]{1,0:T(8,128)S(1)} %broadcast_in_dim.15.refs_3_), channel_id=1, source_target_pairs={{0,0},{1,16},{2,32},{3,48},{4,4},{5,20},{6,36},{7,52},{16,1},{17,1... | collective-permute-start | bytes 12296 | tf_op jit(solution)/shard_map/ppermute | solution.py:157
  14.8 1.7 %copy-start.1 = (f32[16,96,256]{2,1,0:T(8,128)S(1)}, f32[16,96,256]{2,1,0:T(8,128)}, u32[]{:S(2)}) copy-start(f32[16,96,256]{2,1,0:T(8,128)} %shard_map.69) | copy-start | bytes 4718596
  16.5 15.2 %collective-permute-start.2 = (f32[16,96,256]{2,1,0:T(8,128)S(1)}, f32[16,96,256]{2,1,0:T(8,128)}, u32[]{:S(2)}, u32[]{:S(2)}) collective-permute-start(f32[16,96,256]{2,1,0:T(8,128)S(1)} %copy-done.1), channel_id=1, source_target_pairs={{0,8},{8,0},{1,9},{9,1},{2,10},{10,2},{3,11},{11,3},{4,12},{12,4},... | collective-permute-start | bytes 4718600 | tf_op jit(solution)/shard_map/ppermute | solution.py:172
  16.5 23.0 %all-to-all-start.1 = ((f32[16,48,256]{2,1,0:T(8,128)}), f32[16,48,256]{2,1,0:T(8,128)S(1)}, u32[]{:S(2)}, u32[]{:S(2)}) async-start(f32[16,48,256]{2,1,0:T(8,128)} %add.16), calls=%async_computation.1 | async-start | bytes 1572864 | tf_op jit(solution)/shard_map/all_to_all | solution.py:140
  39.5 25.0 %all-to-all-start = ((f32[16,96,256]{2,1,0:T(8,128)}), f32[16,96,256]{2,1,0:T(8,128)S(1)}, u32[]{:S(2)}, u32[]{:S(2)}) async-start(f32[16,96,256]{2,1,0:T(8,128)} %add.17), calls=%async_computation | async-start | bytes 3145728 | tf_op jit(solution)/shard_map/all_to_all | solution.py:140
  65.6 24.0 %all-to-all-start.2 = ((f32[8,96,256]{2,1,0:T(8,128)}), f32[8,96,256]{2,1,0:T(8,128)S(1)}, u32[]{:S(2)}, u32[]{:S(2)}) async-start(f32[8,96,256]{2,1,0:T(8,128)} %bitcast.9), calls=%async_computation.2 | async-start | bytes 1572864 | tf_op jit(solution)/shard_map/all_to_all | solution.py:140
  115.5 6.1 %copy-start = (f32[16,96,256]{2,1,0:T(8,128)}, f32[16,96,256]{2,1,0:T(8,128)S(1)}, u32[]{:S(2)}) copy-start(f32[16,96,256]{2,1,0:T(8,128)S(1)} %all_to_all.27.refs_1_) | copy-start | bytes 4718596
  115.5 6.1 %collective-permute-start.3 = (f32[16,96,256]{2,1,0:T(8,128)S(1)}, f32[16,96,256]{2,1,0:T(8,128)S(1)}, u32[]{:S(2)}, u32[]{:S(2)}) collective-permute-start(f32[16,96,256]{2,1,0:T(8,128)S(1)} %all_to_all.27.refs_1_), channel_id=1, source_target_pairs={{0,8},{8,0},{1,9},{9,1},{2,10},{10,2},{3,11},{11,3},{4,12},{12,4},... | collective-permute-start | bytes 4718600 | tf_op jit(solution)/shard_map/ppermute | solution.py:180
  121.7 1.2 copy-start.2

commit v3 on v1

v3 whole, which is shorter than its diff:
```python
import math

import jax
import jax.numpy as jnp
from jax import lax
from jax.experimental import pallas as pl
from jax.experimental.pallas import tpu as pltpu
from jax.sharding import Mesh, PartitionSpec as P

AXES = ("x", "l", "c", "h", "y")
SIZES = (4, 4, 2, 2, 4)
TILE = 256
LANES = 128
PAIRS = ((0, 1), (0, 2), (1, 2), (0, 0), (1, 1), (2, 2))
VMEM_LIMIT = 40 << 20


def local_kernel(core_ref, desc_ref, species_ref, cfg_ref, slot_ref, keep_ref, send_ref):
    core = core_ref[0]
    atoms, width = desc_ref.shape
    configs = slot_ref.shape[1]

    def put(block, first):
        for half in range(block.shape[1] // LANES):
            tile = block[:, half * LANES : (half + 1) * LANES].reshape(16, 2, 8, LANES)
            at = slice((first + half) * 8, (first + half + 1) * 8)
            keep_ref[:, at, :] = jnp.where(core == 0, tile[:, 0], tile[:, 1])
            send_ref[:, at, :] = jnp.where(core == 0, tile[:, 1], tile[:, 0])

    ids = lax.broadcasted_iota(jnp.int32, (configs, atoms), 0)
    member = (cfg_ref[...] == ids).astype(jnp.bfloat16)
    rows = lax.broadcasted_iota(jnp.int32, (configs, configs), 0)
    place = (slot_ref[...] == rows).astype(jnp.bfloat16)
    placed = jnp.dot(place, member, preferred_element_type=jnp.float32).astype(jnp.bfloat16)
    masks = [(species_ref[...] == kind).astype(jnp.bfloat16) for kind in range(2)]
    for kind in range(2):
        put(jnp.dot(placed * masks[kind], desc_ref[...], preferred_element_type=jnp.float32), 24 + kind * 6)
    for i in range(3):
        turned = desc_ref[:, i * TILE : (i + 1) * TILE].T
        for kind in range(2):
            left = turned * masks[kind]
            for j in range(i, 3):
                right = desc_ref[:, j * TILE : (j + 1) * TILE]
                put(
                    jnp.dot(left, right, preferred_element_type=jnp.float32),
                    kind * 12 + PAIRS.index((i, j)) * 2,
                )


def final_kernel(norm, pos_ref, mine_ref, other_ref, root_ref, normal_ref, cfg_ref, full, left, gram):
    core, kind, part, owner = pos_ref[0], pos_ref[1], pos_ref[2], pos_ref[3]
    width = gram.shape[1]
    band = left.shape[1]

    def joined(tile, lo=0, hi=16):
        at = slice(tile * 8, (tile + 1) * 8)
        a, b = mine_ref[lo:hi, at, :], other_ref[lo:hi, at, :]
        pair = [jnp.where(core == which, a, b)[:, None] for which in range(2)]
        return jnp.concatenate(pair, 1).reshape((hi - lo) * 16, LANES)

    for j in range(2 * width // LANES):
        full[:, j * LANES : (j + 1) * LANES] = joined(6 + j)

    def fill(row, col, piece):
        gram[row : row + piece.shape[0], col : col + piece.shape[1]] = piece

    def straight(tiles, lo, hi, row, col):
        for k, tile in enumerate(tiles):
            fill(row, col + k * LANES, joined(tile, lo, hi))

    def band_0():
        straight((4, 5, 0, 1, 2, 3), 0, 12, 0, 0)

    def band_1():
        straight((2, 3, 0, 1, 4, 5), 12, 16, 0, 0)
        fill(64, 0, joined(0).T)
        straight((1, 2, 3, 4), 0, 8, 64, TILE)

    def band_2():
        fill(0, 0, joined(0).T)
        straight((4, 5, 2, 3), 8, 16, 0, TILE)
        fill(128, 0, joined(1).T[:64])
        fill(128, TILE, joined(2).T[:64])
        straight((3, 4), 0, 4, 128, 2 * TILE)

    def band_3():
        fill(0, 0, joined(0).T[64:])
        fill(64, 0, joined(1).T)
        fill(0, TILE, joined(2).T[64:])
        fill(64, TILE, joined(3).T)
        straight((4, 5), 4, 16, 0, 2 * TILE)

    for k, body in enumerate((band_0, band_1, band_2, band_3)):

        @pl.when(part == k)
        def _():
            cols = slice(k * band, (k + 1) * band)
            shifted = slice(width + k * band, width + (k + 1) * band)
            left[...] = jnp.where(kind == 0, full[:, cols], full[:, shifted])
            own = pl.ds(pl.multiple_of(owner * 8, 8), 8)
            tile = jnp.where(kind == 0, full[own, cols], full[own, shifted])
            cfg_ref[...] = tile / root_ref[:, :1]
            body()

    for s in range(2):
        cols = slice(s * width, (s + 1) * width)
        cross = lax.dot_general(
            left[...],
            full[:, cols],
            (((0,), (0,)), ((), ())),
            precision=lax.Precision.HIGHEST,
            preferred_element_type=jnp.float32,
        )
        extra = jnp.where(kind == s, gram[...] * (1.0 / norm), 0.0)
        normal_ref[:, cols] = cross * (1.0 / full.shape[0]) + extra


def call(kernel, outs, args, scratch=(), scalars=0):
    smem = [pl.BlockSpec(memory_space=pltpu.SMEM)] * scalars
    vmem = [pl.BlockSpec(memory_space=pltpu.VMEM)] * (len(args) - scalars)
    return pl.pallas_call(
        kernel,
        out_shape=outs,
        in_specs=smem + vmem,
        out_specs=[pl.BlockSpec(memory_space=pltpu.VMEM)] * len(outs),
        scratch_shapes=list(scratch),
        compiler_params=pltpu.CompilerParams(vmem_limit_bytes=VMEM_LIMIT),
    )(*args)


def exchange(values, axes):
    flat = values.reshape(-1, values.shape[-1])
    return lax.all_to_all(flat, axes, 0, 0, tiled=True).reshape(values.shape)


def needed(grams, owner):
    def pick(*tiles):
        return jnp.concatenate([grams[8 * k : 8 * k + 8] for k in tiles])

    band_1 = jnp.where(owner >= 12, pick(1, 6, 7, 2, 3), pick(8, 9, 4, 5, 5))
    band_2 = jnp.where(owner >= 8, pick(5, 8, 9), pick(10, 11, 11))
    return jnp.stack(
        [
            pick(0, 1, 2, 3, 6, 7),
            jnp.concatenate([pick(0), band_1]),
            jnp.concatenate([pick(1, 2, 4), band_2]),
            pick(2, 3, 4, 5, 10, 11),
        ]
    )


def shards(desc, species, atom_cfg, slot, weights):
    atoms, width = desc.shape
    configs = slot.shape[0]
    cfg_here = weights.shape[0]
    n_dev = math.prod(SIZES)
    x, l, core, kind, part = [lax.axis_index(axis) for axis in AXES]
    f32 = jnp.float32

    root = jnp.broadcast_to(jnp.sqrt(weights)[:, None], (cfg_here, LANES))
    swap = [((a * 2 + h) * 4 + b, (b * 2 + h) * 4 + a) for a in range(4) for h in range(2) for b in range(4)]
    root_here = lax.ppermute(root, ("l", "h", "y"), swap)
    pos = jnp.stack([core, kind, part, (x * 4 + l) * 2 + core])

    flip = [(0, 1), (1, 0)]
    payload = pltpu.VMEM((16, 288, LANES), f32)
    keep, send = call(
        local_kernel,
        [payload, payload],
        [core[None], desc, species[None], atom_cfg[None], slot[None]],
        scalars=1,
    )
    came, root_here, pos = lax.optimization_barrier((lax.ppermute(send, "c", flip), root_here, pos))
    total = jnp.sum(exchange(keep + came, ("x", "y")), 0)
    grams, sums = total[:192].reshape(2, 96, LANES), total[192:]
    planes = jnp.concatenate([grams, jnp.broadcast_to(sums[None], (2, 96, LANES))], 1)
    planes = jnp.broadcast_to(planes[None], (4, 2, 192, LANES)).reshape(8, 192, LANES)
    total = jnp.sum(exchange(planes, ("l", "h")), 0)
    scale = 1.0 / math.sqrt(atoms * n_dev / configs)
    sums = (total[96:].reshape(12, 8, LANES) * (root_here * scale)).reshape(96, LANES)
    bands = needed(total[:96], x * 4 + part)
    spread = jnp.concatenate([bands, jnp.broadcast_to(sums[None], (4, 96, LANES))], 1)
    spread = jnp.broadcast_to(spread[None], (4, 4, 144, LANES)).reshape(16, 144, LANES)
    mine = exchange(spread, ("x", "y"))
    other = lax.ppermute(mine, "c", flip)
    band = 2 * width // 8
    norm = atoms * n_dev // 8
    normal, rows = call(
        lambda *refs: final_kernel(norm, *refs),
        [jax.ShapeDtypeStruct((band, 2 * width), f32), jax.ShapeDtypeStruct((cfg_here, band), f32)],
        [pos] + [pltpu.with_memory_space_constraint(a, pltpu.VMEM) for a in (mine, other)] + [root],
        [
            pltpu.VMEM((configs, 2 * width), f32),
            pltpu.VMEM((configs, band), f32),
            pltpu.VMEM((band, width), f32),
        ],
        1,
    )
    return normal, rows


def solution(mesh):
    fine = Mesh(mesh.devices.reshape(SIZES), AXES)
    return jax.shard_map(
        shards,
        mesh=fine,
        in_specs=(P(AXES, None), P(AXES), P(AXES), P(), P(("x", "l", "c"))),
        out_specs=(P(("h", "y"), None), P(("x", "l", "c"), ("h", "y"))),
        check_vma=False,
    )
```

time: 129 us -> 118 us (0.915)
  Pallas kernels: 22.9 us -> 9.89 us
  other arithmetic: 0.6 us -> 2.22 us
  local copies, waits for them, and re-layouts: 3.56 us -> 5.1 us
  waiting for transfers between devices: 24.6 us -> 23.2 us
    pallas_call x5 -> x2, Pallas kernels: 22.9 us -> 9.89 us  [call(): pl.pallas_call(kernel, out_shape=outs, in_specs=smem + vmem, out_specs=[p...]
    add x0 -> x1, other arithmetic: none -> 1.9 us  [shards(): total = jnp.sum(exchange(keep + came, ('x', 'y')), 0)]
    unnamed x14 -> x10, local copies, waits for them, and re-layouts: 3.49 us -> 3.96 us
  transfers between devices with their start and end apart: 4 -> 4, of which waited for: 3 -> 3; matrix products, arithmetic and copies ran while one was open for 1% -> 0% of each run, Pallas kernels for 0% -> 0%
where the time goes in v3:
time: 118 us; the launch traced here: 116 us
  blocking collectives  59.2 us (50%)
  waiting for transfers between devices  23.2 us (20%)
  starting transfers between devices  15.2 us (13%)
  Pallas kernels  9.89 us (8%)
  local copies, waits for them, and re-layouts  5.1 us (4%)
  other arithmetic  2.22 us (2%)
    all_to_all x2, blocking collectives, exchange(): return lax.all_to_all(flat, axes, 0, 0, tiled=True).reshape(values.shape)  59.2 us
    all_to_all x1, waiting for transfers between devices, exchange(): return lax.all_to_all(flat, axes, 0, 0, tiled=True).reshape(values.shape)  17 us
    pallas_call x2, Pallas kernels, call(): pl.pallas_call(kernel, out_shape=outs, in_specs=smem + vmem, out_specs=[p...  9.89 us
    all_to_all x1, starting transfers between devices, exchange(): return lax.all_to_all(flat, axes, 0, 0, tiled=True).reshape(values.shape)  8.18 us
    unnamed x10, local copies, waits for them, and re-layouts  3.96 us
    ppermute x1, waiting for transfers between devices, shards(): lax.ppermute(send, 'c', flip)  3.67 us
    ppermute x1, starting transfers between devices, shards(): lax.ppermute(send, 'c', flip)  3.24 us
    ppermute x1, starting transfers between devices, shards(): other = lax.ppermute(mine, 'c', flip)  3.07 us
  transfers between devices with their start and end apart: 4, of which 3 were waited for; matrix products, arithmetic and copies ran while one was open for 0% of the time, Pallas kernels for 0%

profile of v3, /device:TPU:1, one launch (start us, length us, event | category | flops | bytes accessed | tf_op | source)
XLA Modules:
  0.0 115.6 jit_solution(16893497444667468484)
XLA Ops:
  0.6 0.0 copy-start.4
  0.6 0.0 copy-start
  0.7 1.9 %copy-done = bf16[2048,768]{1,0:T(8,128)(2,1)S(1)} copy-done((bf16[2048,768]{1,0:T(8,128)(2,1)S(1)}, bf16[2048,768]{1,0:T(8,128)(2,1)}, u32[]{:S(2)}) %copy-start) | copy-done | bytes 3145752
  2.5 0.0 copy-start.1
  2.5 0.7 copy-done.1
  3.2 0.0 copy-start.2
  3.2 0.7 copy-done.2
  3.9 0.0 copy-start.3
  3.9 0.7 copy-done.3
  4.6 6.8 %shard_map.68 = (f32[16,288,128]{2,1,0:T(8,128)S(1)}, f32[16,288,128]{2,1,0:T(8,128)}) custom-call(s32[1]{0:T(128)} %bitcast.core_ref, bf16[2048,768]{1,0:T(8,128)(2,1)S(1)} %copy-done, s32[1,2048]{1,0:T(1,128)S(1)} %bitcast.20, s32[1,2048]{1,0:T(1,128)S(1)} %bitcast.21, s32[1,256]{1,0:T(1,128)S(1)} %bitcast.22), custom_call_target="tpu_custom_call" | custom-call | tf_op jit(solution)/shard_map/pallas_call | solution.py:121
  11.5 3.2 %collective-permute-start = (f32[16,288,128]{2,1,0:T(8,128)}, f32[16,288,128]{2,1,0:T(8,128)}, u32[]{:S(2)}, u32[]{:S(2)}) collective-permute-start(f32[16,288,128]{2,1,0:T(8,128)} %get-tuple-element.7), channel_id=1, source_target_pairs={{0,8},{8,0},{1,9},{9,1},{2,10},{10,2},{3,11},{11,3},{4,12},{12,4},... | collective-permute-start | bytes 7077896 | tf_op jit(solution)/shard_map/ppermute | solution.py:173
  14.7 0.0 copy-done.4
  14.7 0.1 broadcast_in_dim.22.refs_3_
  14.8 0.7 collective-permute-start.1
  15.5 0.1 pad_add_fusion.refs_0_
  15.5 0.0 collective-permute-done.1
  15.5 3.7 %collective-permute-done = f32[16,288,128]{2,1,0:T(8,128)} collective-permute-done((f32[16,288,128]{2,1,0:T(8,128)}, f32[16,288,128]{2,1,0:T(8,128)}, u32[]{:S(2)}, u32[]{:S(2)}) %collective-permute-start) | collective-permute-done | bytes 2359328 | tf_op jit(solution)/shard_map/ppermute | solution.py:173
  19.2 1.9 %add.14 = f32[16,288,128]{2,1,0:T(8,128)S(1)} add(f32[16,288,128]{2,1,0:T(8,128)S(1)} %get-tuple-element.9, f32[16,288,128]{2,1,0:T(8,128)} %collective-permute-done) | non-fusion elementwise | flops 589824 | bytes 7077888 | tf_op jit(solution)/shard_map/add | solution.py:174
  21.1 37.5 %all_to_all.24 = f32[16,288,128]{2,1,0:T(8,128)S(1)} all-to-all(f32[16,288,128]{2,1,0:T(8,128)S(1)} %add.14), channel_id=1, replica_groups=mesh['x'=4,'l'=4,'c'=2,'h'=2,'y'=4] {'x','y'}, dimensions={0} | all-to-all | bytes 4718592 | tf_op jit(solution)/shard_map/all_to_all | solution.py:133
  58.6 0.1 reduce_sum.18
  58.8 0.9 broadcast_in_dim.48
  59.8 8.2 %all-to-all-start.1 = ((f32[8,192,128]{2,1,0:T(8,128)}), f32[8,192,128]{2,1,0:T(8,128)S(1)}, u32[]{:S(2)}, u32[]{:S(2)}) async-start(f32[8,192,128]{2,1,0:T(8,128)} %bitcast.8), calls=%async_computation.1 | async-start | bytes 1572864 | tf_op jit(solution)/shard_map/all_to_all | solution.py:133
  68.0 17.0 %all-to-all-done.1 = f32[8,192,128]{2,1,0:T(8,128)S(1)} async-done(((f32[8,192,128]{2,1,0:T(8,128)}), f32[8,192,128]{2,1,0:T(8,128)S(1)}, u32[]{:S(2)}, u32[]{:S(2)}) %all-to-all-start.1) | async-done | bytes 786464 | tf_op jit(solution)/shard_map/all_to_all | solution.py:133
  85.2 0.1 broadcast_in_dim.50
  85.3 21.7 %all_to_all.25.refs_1_ = f32[16,144,128]{2,1,0:T(8,128)S(1)} all-to-all(f32[16,144,128]{2,1,0:T(8,128)S(1)} %bitcast.23), channel_id=1, replica_groups=mesh['x'=4,'l'=4,'c'=2,'h'=2,'y'=4] {'x','y'}, dimensions={0} | all-to-all | bytes 2359296 | tf_op jit(solution)/shard_map/all_to_all | solution.py:133
  107.0 3.1 %collective-permute-start.2 = (f32[16,144,128]{2,1,0:T(8,128)S(1)}, f32[16,144,128]{2,1,0:T(8,128)S(1)}, u32[]{:S(2)}, u32[]{:S(2)}) collective-permute-start(f32[16,144,128]{2,1,0:T(8,128)S(1)} %all_to_all.25.refs_1_), channel_id=1, source_target_pairs={{0,8},{8,0},{1,9},{9,1},{2,10},{10,2},{3,11},{11,3},{4,12},{12,4},... | collective-permute-start | bytes 3538952 | tf_op jit(solution)/shard_map/ppermute | solution.py:185
  110.1 2.5 %collective-permute-done.2.refs_2_ = f32[16,144,128]{2,1,0:T(8,128)S(1)} collective-permute-done((f32[16,144,128]{2,1,0:T(8,128)S(1)}, f32[16,144,128]{2,1,0:T(8,128)S(1)}, u32[]{:S(2)}, u32[]{:S(2)}) %collective-permute-start.2) | collective-permute-done | bytes 1179680 | tf_op jit(solution)/shard_map/ppermute | solution.py:185
  112.5 3.0 %shard_map.69 = (f32[192,1536]{1,0:T(8,128)}, f32[8,192]{1,0:T(8,128)}) custom-call(s32[4]{0:T(128)S(1)} %pad_add_fusion.refs_0_, f32[16,144,128]{2,1,0:T(8,128)S(1)} %all_to_all.25.refs_1_, f32[16,144,128]{2,1,0:T(8,128)S(1)} %collective-permute-done.2.refs_2_, f32[8,128]{1,0:T(8,128)S(1)} %broadcast_in_dim.22.refs_3_), custom_call_target="tpu_custom_call" | custom-call | tf_op jit(solution)/shard_map/pallas_call | solution.py:121
  (17 shorter events, 0.2 us)
Async XLA Ops:
  0.6 14.1 %copy-start.4 = (f32[8]{0:T(128)S(1)}, f32[8]{0:T(128)}, u32[]{:S(2)}) copy-start(f32[8]{0:T(128)} %param.9) | copy-start | bytes 100
  0.6 1.9 %copy-start = (bf16[2048,768]{1,0:T(8,128)(2,1)S(1)}, bf16[2048,768]{1,0:T(8,128)(2,1)}, u32[]{:S(2)}) copy-start(bf16[2048,768]{1,0:T(8,128)(2,1)} %desc_ref.1) | copy-start | bytes 9437188
  2.5 0.7 copy-start.1
  3.2 0.7 copy-start.2
  3.9 0.7 copy-start.3
  11.5 7.7 %collective-permute-start = (f32[16,288,128]{2,1,0:T(8,128)}, f32[16,288,128]{2,1,0:T(8,128)}, u32[]{:S(2)}, u32[]{:S(2)}) collective-permute-start(f32[16,288,128]{2,1,0:T(8,128)} %get-tuple-element.7), channel_id=1, source_target_pairs={{0,8},{8,0},{1,9},{9,1},{2,10},{10,2},{3,11},{11,3},{4,12},{12,4},... | collective-permute-start | bytes 7077896 | tf_op jit(solution)/shard_map/ppermute | solution.py:173
  14.8 0.8 collective-permute-start.1
  59.8 25.2 %all-to-all-start.1 = ((f32[8,192,128]{2,1,0:T(8,128)}), f32[8,192,128]{2,1,0:T(8,128)S(1)}, u32[]{:S(2)}, u32[]{:S(2)}) async-start(f32[8,192,128]{2,1,0:T(8,128)} %bitcast.8), calls=%async_computation.1 | async-start | bytes 1572864 | tf_op jit(solution)/shard_map/all_to_all | solution.py:133
  107.0 5.5 %collective-permute-start.2 = (f32[16,144,128]{2,1,0:T(8,128)S(1)}, f32[16,144,128]{2,1,0:T(8,128)S(1)}, u32[]{:S(2)}, u32[]{:S(2)}) collective-permute-start(f32[16,144,128]{2,1,0:T(8,128)S(1)} %all_to_all.25.refs_1_), channel_id=1, source_target_pairs={{0,8},{8,0},{1,9},{9,1},{2,10},{10,2},{3,11},{11,3},{4,12},{12,4},... | collective-permute-start | bytes 3538952 | tf_op jit(solution)/shard_map/ppermute | solution.py:185

commit v4 on v3

--- a/solution.py
+++ b/solution.py
@@ -12,13 +12,35 @@
 TILE = 256
 LANES = 128
 PAIRS = ((0, 1), (0, 2), (1, 2), (0, 0), (1, 1), (2, 2))
-VMEM_LIMIT = 40 << 20
-
-
-def local_kernel(core_ref, desc_ref, species_ref, cfg_ref, slot_ref, keep_ref, send_ref):
+
+
+def local_kernel(
+    core_ref,
+    desc_hbm,
+    species_hbm,
+    cfg_hbm,
+    slot_hbm,
+    keep_ref,
+    send_ref,
+    desc_ref,
+    species_ref,
+    cfg_ref,
+    slot_ref,
+    turned,
+    sems,
+):
     core = core_ref[0]
     atoms, width = desc_ref.shape
     configs = slot_ref.shape[1]
+    small = ((cfg_hbm, cfg_ref), (slot_hbm, slot_ref), (species_hbm, species_ref))
+    copies = [pltpu.make_async_copy(a, b, sems.at[k]) for k, (a, b) in enumerate(small)]
+    for i in range(3):
+        cols = slice(i * TILE, (i + 1) * TILE)
+        copies.append(pltpu.make_async_copy(desc_hbm.at[:, cols], desc_ref.at[:, cols], sems.at[3 + i]))
+    for copy in copies:
+        copy.start()
+    for copy in copies[:3]:
+        copy.wait()
 
     def put(block, first):
         for half in range(block.shape[1] // LANES):
@@ -33,18 +55,18 @@
     place = (slot_ref[...] == rows).astype(jnp.bfloat16)
     placed = jnp.dot(place, member, preferred_element_type=jnp.float32).astype(jnp.bfloat16)
     masks = [(species_ref[...] == kind).astype(jnp.bfloat16) for kind in range(2)]
-    for kind in range(2):
-        put(jnp.dot(placed * masks[kind], desc_ref[...], preferred_element_type=jnp.float32), 24 + kind * 6)
-    for i in range(3):
-        turned = desc_ref[:, i * TILE : (i + 1) * TILE].T
+    members = [placed * mask for mask in masks]
+    for j in range(3):
+        copies[3 + j].wait()
+        right = desc_ref[:, j * TILE : (j + 1) * TILE]
         for kind in range(2):
-            left = turned * masks[kind]
-            for j in range(i, 3):
-                right = desc_ref[:, j * TILE : (j + 1) * TILE]
-                put(
-                    jnp.dot(left, right, preferred_element_type=jnp.float32),
-                    kind * 12 + PAIRS.index((i, j)) * 2,
-                )
+            put(jnp.dot(members[kind], right, preferred_element_type=jnp.float32), 24 + kind * 6 + j * 2)
+        turned[j * TILE : (j + 1) * TILE, :] = right.T
+        for i in range(j + 1):
+            for kind in range(2):
+                left = turned[i * TILE : (i + 1) * TILE, :] * masks[kind]
+                block = jnp.dot(left, right, preferred_element_type=jnp.float32)
+                put(block, kind * 12 + PAIRS.index((i, j)) * 2)
 
 
 def final_kernel(norm, pos_ref, mine_ref, other_ref, root_ref, normal_ref, cfg_ref, full, left, gram):
@@ -115,17 +137,17 @@
         normal_ref[:, cols] = cross * (1.0 / full.shape[0]) + extra
 
 
-def call(kernel, outs, args, scratch=(), scalars=0):
-    smem = [pl.BlockSpec(memory_space=pltpu.SMEM)] * scalars
-    vmem = [pl.BlockSpec(memory_space=pltpu.VMEM)] * (len(args) - scalars)
+def call(kernel, outs, args, scratch, space, limit):
+    smem = pl.BlockSpec(memory_space=pltpu.SMEM)
+    held = [pltpu.with_memory_space_constraint(a, space) for a in args[1:]]
     return pl.pallas_call(
         kernel,
         out_shape=outs,
-        in_specs=smem + vmem,
+        in_specs=[smem] + [pl.BlockSpec(memory_space=space)] * len(held),
         out_specs=[pl.BlockSpec(memory_space=pltpu.VMEM)] * len(outs),
         scratch_shapes=list(scratch),
-        compiler_params=pltpu.CompilerParams(vmem_limit_bytes=VMEM_LIMIT),
-    )(*args)
+        compiler_params=pltpu.CompilerParams(vmem_limit_bytes=limit),
+    )(args[0], *held)
 
 
 def exchange(values, axes):
@@ -158,24 +180,34 @@
     f32 = jnp.float32
 
     root = jnp.broadcast_to(jnp.sqrt(weights)[:, None], (cfg_here, LANES))
-    swap = [((a * 2 + h) * 4 + b, (b * 2 + h) * 4 + a) for a in range(4) for h in range(2) for b in range(4)]
-    root_here = lax.ppermute(root, ("l", "h", "y"), swap)
     pos = jnp.stack([core, kind, part, (x * 4 + l) * 2 + core])
 
     flip = [(0, 1), (1, 0)]
     payload = pltpu.VMEM((16, 288, LANES), f32)
+    int_row = pltpu.VMEM((1, atoms), jnp.int32)
     keep, send = call(
         local_kernel,
         [payload, payload],
         [core[None], desc, species[None], atom_cfg[None], slot[None]],
-        scalars=1,
-    )
-    came, root_here, pos = lax.optimization_barrier((lax.ppermute(send, "c", flip), root_here, pos))
+        [
+            pltpu.VMEM((atoms, width), jnp.bfloat16),
+            int_row,
+            int_row,
+            pltpu.VMEM((1, configs), jnp.int32),
+            pltpu.VMEM((width, atoms), jnp.bfloat16),
+            pltpu.SemaphoreType.DMA((6,)),
+        ],
+        pltpu.HBM,
+        24 << 20,
+    )
+    came, root, pos = lax.optimization_barrier((lax.ppermute(send, "c", flip), root, pos))
     total = jnp.sum(exchange(keep + came, ("x", "y")), 0)
     grams, sums = total[:192].reshape(2, 96, LANES), total[192:]
-    planes = jnp.concatenate([grams, jnp.broadcast_to(sums[None], (2, 96, LANES))], 1)
-    planes = jnp.broadcast_to(planes[None], (4, 2, 192, LANES)).reshape(8, 192, LANES)
-    total = jnp.sum(exchange(planes, ("l", "h")), 0)
+    planes = jnp.concatenate([grams, jnp.broadcast_to(jnp.concatenate([sums, root])[None], (2, 104, LANES))], 1)
+    planes = jnp.broadcast_to(planes[None], (4, 2, 200, LANES)).reshape(8, 200, LANES)
+    got = exchange(planes, ("l", "h"))
+    root_here = lax.dynamic_index_in_dim(got, part * 2, 0, False)[192:]
+    total = jnp.sum(got[:, :192], 0)
     scale = 1.0 / math.sqrt(atoms * n_dev / configs)
     sums = (total[96:].reshape(12, 8, LANES) * (root_here * scale)).reshape(96, LANES)
     bands = needed(total[:96], x * 4 + part)
@@ -188,13 +220,14 @@
     normal, rows = call(
         lambda *refs: final_kernel(norm, *refs),
         [jax.ShapeDtypeStruct((band, 2 * width), f32), jax.ShapeDtypeStruct((cfg_here, band), f32)],
-        [pos] + [pltpu.with_memory_space_constraint(a, pltpu.VMEM) for a in (mine, other)] + [root],
+        [pos, mine, other, root],
         [
             pltpu.VMEM((configs, 2 * width), f32),
             pltpu.VMEM((configs, band), f32),
             pltpu.VMEM((band, width), f32),
         ],
-        1,
+        pltpu.VMEM,
+        24 << 20,
     )
     return normal, rows
 

time: 118 us -> 113 us (0.958)
  blocking collectives: 59.2 us -> 54.2 us
  local copies, waits for them, and re-layouts: 5.1 us -> 1.15 us
  waiting for transfers between devices: 23.2 us -> 26.1 us
  Pallas kernels: 9.89 us -> 11.2 us
    all_to_all x2, blocking collectives: 59.2 us -> 54.2 us  [exchange(): return lax.all_to_all(flat, axes, 0, 0, tiled=True).reshape(values.shape)]
    unnamed x10 -> x2, local copies, waits for them, and re-layouts: 3.96 us -> 0.01 us
    all_to_all x1, waiting for transfers between devices: 17 us -> 19.2 us  [exchange(): return lax.all_to_all(flat, axes, 0, 0, tiled=True).reshape(values.shape)]
    pallas_call x2, Pallas kernels: 9.89 us -> 11.2 us  [call(): pl.pallas_call(kernel, out_shape=outs, in_specs=[smem] + [pl.BlockSpec(me...]
  transfers between devices with their start and end apart: 4 -> 3, of which waited for: 3 -> 3; matrix products, arithmetic and copies ran while one was open for 0% -> 0% of each run, Pallas kernels for 0% -> 0%
where the time goes in v4:
time: 113 us; the launch traced here: 111 us
  blocking collectives  54.2 us (48%)
  waiting for transfers between devices  26.1 us (23%)
  starting transfers between devices  14.8 us (13%)
  Pallas kernels  11.2 us (10%)
  other arithmetic  2.24 us (2%)
  local copies, waits for them, and re-layouts  1.15 us (1%)
    all_to_all x2, blocking collectives, exchange(): return lax.all_to_all(flat, axes, 0, 0, tiled=True).reshape(values.shape)  54.2 us
    all_to_all x1, waiting for transfers between devices, exchange(): return lax.all_to_all(flat, axes, 0, 0, tiled=True).reshape(values.shape)  19.2 us
    pallas_call x2, Pallas kernels, call(): pl.pallas_call(kernel, out_shape=outs, in_specs=[smem] + [pl.BlockSpec(me...  11.2 us
    all_to_all x1, starting transfers between devices, exchange(): return lax.all_to_all(flat, axes, 0, 0, tiled=True).reshape(values.shape)  8.19 us
    ppermute x1, waiting for transfers between devices, shards(): lax.ppermute(send, 'c', flip)  4.42 us
    ppermute x1, starting transfers between devices, shards(): other = lax.ppermute(mine, 'c', flip)  3.33 us
    ppermute x1, starting transfers between devices, shards(): lax.ppermute(send, 'c', flip)  3.33 us
    ppermute x1, waiting for transfers between devices, shards(): other = lax.ppermute(mine, 'c', flip)  2.47 us
  transfers between devices with their start and end apart: 3, of which 3 were waited for; matrix products, arithmetic and copies ran while one was open for 0% of the time, Pallas kernels for 0%

profile of v4, /device:TPU:1, one launch (start us, length us, event | category | flops | bytes accessed | tf_op | source)
XLA Modules:
  0.0 110.6 jit_solution(18060683657161041697)
XLA Ops:
  0.6 0.0 copy-start
  0.6 8.1 %shard_map.68 = (f32[16,288,128]{2,1,0:T(8,128)S(1)}, f32[16,288,128]{2,1,0:T(8,128)}) custom-call(s32[1]{0:T(128)} %bitcast.core_ref, bf16[2048,768]{1,0:T(8,128)(2,1)} %desc_hbm.1, s32[1,2048]{1,0:T(1,128)} %bitcast.24, s32[1,2048]{1,0:T(1,128)} %bitcast.25, s32[1,256]{1,0:T(1,128)} %bitcast.26), custom_call_target="tpu_custom_call" | custom-call | tf_op jit(solution)/shard_map/pallas_call | solution.py:143
  8.8 3.3 %collective-permute-start = (f32[16,288,128]{2,1,0:T(8,128)}, f32[16,288,128]{2,1,0:T(8,128)}, u32[]{:S(2)}, u32[]{:S(2)}) collective-permute-start(f32[16,288,128]{2,1,0:T(8,128)} %get-tuple-element.7), channel_id=1, source_target_pairs={{0,8},{8,0},{1,9},{9,1},{2,10},{10,2},{3,11},{11,3},{4,12},{12,4},... | collective-permute-start | bytes 7077896 | tf_op jit(solution)/shard_map/ppermute | solution.py:203
  12.1 0.0 copy-done
  12.1 0.1 pad_add_fusion.refs_0_
  12.2 4.4 %collective-permute-done = f32[16,288,128]{2,1,0:T(8,128)} collective-permute-done((f32[16,288,128]{2,1,0:T(8,128)}, f32[16,288,128]{2,1,0:T(8,128)}, u32[]{:S(2)}, u32[]{:S(2)}) %collective-permute-start) | collective-permute-done | bytes 2359328 | tf_op jit(solution)/shard_map/ppermute | solution.py:203
  16.6 0.1 broadcast_in_dim.22.refs_3_
  16.7 1.9 %add.18 = f32[16,288,128]{2,1,0:T(8,128)S(1)} add(f32[16,288,128]{2,1,0:T(8,128)S(1)} %get-tuple-element.9, f32[16,288,128]{2,1,0:T(8,128)} %collective-permute-done) | non-fusion elementwise | flops 589824 | bytes 7077888 | tf_op jit(solution)/shard_map/add | solution.py:204
  18.6 35.0 %all_to_all.24 = f32[16,288,128]{2,1,0:T(8,128)S(1)} all-to-all(f32[16,288,128]{2,1,0:T(8,128)S(1)} %add.18), channel_id=1, replica_groups=mesh['x'=4,'l'=4,'c'=2,'h'=2,'y'=4] {'x','y'}, dimensions={0} | all-to-all | bytes 4718592 | tf_op jit(solution)/shard_map/all_to_all | solution.py:155
  53.6 0.1 reduce_sum.18
  53.8 0.9 broadcast_in_dim.48
  54.7 8.2 %all-to-all-start.1 = ((f32[8,200,128]{2,1,0:T(8,128)}), f32[8,200,128]{2,1,0:T(8,128)S(1)}, u32[]{:S(2)}, u32[]{:S(2)}) async-start(f32[8,200,128]{2,1,0:T(8,128)} %bitcast.8), calls=%async_computation.1 | async-start | bytes 1638400 | tf_op jit(solution)/shard_map/all_to_all | solution.py:155
  62.9 19.2 %all-to-all-done.1 = f32[8,200,128]{2,1,0:T(8,128)S(1)} async-done(((f32[8,200,128]{2,1,0:T(8,128)}), f32[8,200,128]{2,1,0:T(8,128)S(1)}, u32[]{:S(2)}, u32[]{:S(2)}) %all-to-all-start.1) | async-done | bytes 819232 | tf_op jit(solution)/shard_map/all_to_all | solution.py:155
  82.4 0.1 broadcast_in_dim.50
  82.5 19.2 %all_to_all.25.refs_1_ = f32[16,144,128]{2,1,0:T(8,128)S(1)} all-to-all(f32[16,144,128]{2,1,0:T(8,128)S(1)} %bitcast.22), channel_id=1, replica_groups=mesh['x'=4,'l'=4,'c'=2,'h'=2,'y'=4] {'x','y'}, dimensions={0} | all-to-all | bytes 2359296 | tf_op jit(solution)/shard_map/all_to_all | solution.py:155
  101.7 3.3 %collective-permute-start.1 = (f32[16,144,128]{2,1,0:T(8,128)S(1)}, f32[16,144,128]{2,1,0:T(8,128)S(1)}, u32[]{:S(2)}, u32[]{:S(2)}) collective-permute-start(f32[16,144,128]{2,1,0:T(8,128)S(1)} %all_to_all.25.refs_1_), channel_id=1, source_target_pairs={{0,8},{8,0},{1,9},{9,1},{2,10},{10,2},{3,11},{11,3},{4,12},{12,4},... | collective-permute-start | bytes 3538952 | tf_op jit(solution)/shard_map/ppermute | solution.py:217
  105.1 2.5 %collective-permute-done.1.refs_2_ = f32[16,144,128]{2,1,0:T(8,128)S(1)} collective-permute-done((f32[16,144,128]{2,1,0:T(8,128)S(1)}, f32[16,144,128]{2,1,0:T(8,128)S(1)}, u32[]{:S(2)}, u32[]{:S(2)}) %collective-permute-start.1) | collective-permute-done | bytes 1179680 | tf_op jit(solution)/shard_map/ppermute | solution.py:217
  107.5 3.0 %shard_map.69 = (f32[192,1536]{1,0:T(8,128)}, f32[8,192]{1,0:T(8,128)}) custom-call(s32[4]{0:T(128)S(1)} %pad_add_fusion.refs_0_, f32[16,144,128]{2,1,0:T(8,128)S(1)} %all_to_all.25.refs_1_, f32[16,144,128]{2,1,0:T(8,128)S(1)} %collective-permute-done.1.refs_2_, f32[8,128]{1,0:T(8,128)S(1)} %broadcast_in_dim.22.refs_3_), custom_call_target="tpu_custom_call" | custom-call | tf_op jit(solution)/shard_map/pallas_call | solution.py:143
  (18 shorter events, 0.2 us)
Async XLA Ops:
  0.6 11.5 %copy-start = (f32[8]{0:T(128)S(1)}, f32[8]{0:T(128)}, u32[]{:S(2)}) copy-start(f32[8]{0:T(128)} %param.9) | copy-start | bytes 100
  8.8 7.8 %collective-permute-start = (f32[16,288,128]{2,1,0:T(8,128)}, f32[16,288,128]{2,1,0:T(8,128)}, u32[]{:S(2)}, u32[]{:S(2)}) collective-permute-start(f32[16,288,128]{2,1,0:T(8,128)} %get-tuple-element.7), channel_id=1, source_target_pairs={{0,8},{8,0},{1,9},{9,1},{2,10},{10,2},{3,11},{11,3},{4,12},{12,4},... | collective-permute-start | bytes 7077896 | tf_op jit(solution)/shard_map/ppermute | solution.py:203
  54.7 27.4 %all-to-all-start.1 = ((f32[8,200,128]{2,1,0:T(8,128)}), f32[8,200,128]{2,1,0:T(8,128)S(1)}, u32[]{:S(2)}, u32[]{:S(2)}) async-start(f32[8,200,128]{2,1,0:T(8,128)} %bitcast.8), calls=%async_computation.1 | async-start | bytes 1638400 | tf_op jit(solution)/shard_map/all_to_all | solution.py:155
  101.7 5.8 %collective-permute-start.1 = (f32[16,144,128]{2,1,0:T(8,128)S(1)}, f32[16,144,128]{2,1,0:T(8,128)S(1)}, u32[]{:S(2)}, u32[]{:S(2)}) collective-permute-start(f32[16,144,128]{2,1,0:T(8,128)S(1)} %all_to_all.25.refs_1_), channel_id=1, source_target_pairs={{0,8},{8,0},{1,9},{9,1},{2,10},{10,2},{3,11},{11,3},{4,12},{12,4},... | collective-permute-start | bytes 3538952 | tf_op jit(solution)/shard_map/ppermute | solution.py:217

commit v5 on v4

--- a/solution.py
+++ b/solution.py
@@ -14,7 +14,27 @@
 PAIRS = ((0, 1), (0, 2), (1, 2), (0, 0), (1, 1), (2, 2))
 
 
-def local_kernel(
+def put(core, block, first, keep_ref, send_ref):
+    for half in range(block.shape[1] // LANES):
+        tile = block[:, half * LANES : (half + 1) * LANES].reshape(16, 2, 8, LANES)
+        at = slice((first + half) * 8, (first + half + 1) * 8)
+        keep_ref[:, at, :] = jnp.where(core == 0, tile[:, 0], tile[:, 1])
+        send_ref[:, at, :] = jnp.where(core == 0, tile[:, 1], tile[:, 0])
+
+
+def load(small, desc_hbm, desc_ref, sems):
+    copies = [pltpu.make_async_copy(a, b, sems.at[k]) for k, (a, b) in enumerate(small)]
+    for i in range(3):
+        cols = slice(i * TILE, (i + 1) * TILE)
+        copies.append(pltpu.make_async_copy(desc_hbm.at[:, cols], desc_ref.at[:, cols], sems.at[3 + i]))
+    for copy in copies:
+        copy.start()
+    for copy in copies[:-3]:
+        copy.wait()
+    return copies[-3:]
+
+
+def sums_kernel(
     core_ref,
     desc_hbm,
     species_hbm,
@@ -26,62 +46,57 @@
     species_ref,
     cfg_ref,
     slot_ref,
-    turned,
     sems,
 ):
     core = core_ref[0]
-    atoms, width = desc_ref.shape
+    atoms = desc_ref.shape[0]
     configs = slot_ref.shape[1]
     small = ((cfg_hbm, cfg_ref), (slot_hbm, slot_ref), (species_hbm, species_ref))
-    copies = [pltpu.make_async_copy(a, b, sems.at[k]) for k, (a, b) in enumerate(small)]
-    for i in range(3):
-        cols = slice(i * TILE, (i + 1) * TILE)
-        copies.append(pltpu.make_async_copy(desc_hbm.at[:, cols], desc_ref.at[:, cols], sems.at[3 + i]))
-    for copy in copies:
-        copy.start()
-    for copy in copies[:3]:
-        copy.wait()
-
-    def put(block, first):
-        for half in range(block.shape[1] // LANES):
-            tile = block[:, half * LANES : (half + 1) * LANES].reshape(16, 2, 8, LANES)
-            at = slice((first + half) * 8, (first + half + 1) * 8)
-            keep_ref[:, at, :] = jnp.where(core == 0, tile[:, 0], tile[:, 1])
-            send_ref[:, at, :] = jnp.where(core == 0, tile[:, 1], tile[:, 0])
-
+    blocks = load(small, desc_hbm, desc_ref, sems)
     ids = lax.broadcasted_iota(jnp.int32, (configs, atoms), 0)
     member = (cfg_ref[...] == ids).astype(jnp.bfloat16)
     rows = lax.broadcasted_iota(jnp.int32, (configs, configs), 0)
     place = (slot_ref[...] == rows).astype(jnp.bfloat16)
     placed = jnp.dot(place, member, preferred_element_type=jnp.float32).astype(jnp.bfloat16)
-    masks = [(species_ref[...] == kind).astype(jnp.bfloat16) for kind in range(2)]
-    members = [placed * mask for mask in masks]
+    members = [placed * (species_ref[...] == kind).astype(jnp.bfloat16) for kind in range(2)]
     for j in range(3):
-        copies[3 + j].wait()
+        blocks[j].wait()
         right = desc_ref[:, j * TILE : (j + 1) * TILE]
         for kind in range(2):
-            put(jnp.dot(members[kind], right, preferred_element_type=jnp.float32), 24 + kind * 6 + j * 2)
+            block = jnp.dot(members[kind], right, preferred_element_type=jnp.float32)
+            put(core, block, kind * 6 + j * 2, keep_ref, send_ref)
+
+
+def gram_kernel(core_ref, desc_hbm, species_hbm, keep_ref, send_ref, desc_ref, species_ref, turned, sems):
+    core = core_ref[0]
+    blocks = load(((species_hbm, species_ref),), desc_hbm, desc_ref, sems)
+    masks = [(species_ref[...] == kind).astype(jnp.bfloat16) for kind in range(2)]
+    for j in range(3):
+        blocks[j].wait()
+        right = desc_ref[:, j * TILE : (j + 1) * TILE]
         turned[j * TILE : (j + 1) * TILE, :] = right.T
         for i in range(j + 1):
             for kind in range(2):
                 left = turned[i * TILE : (i + 1) * TILE, :] * masks[kind]
                 block = jnp.dot(left, right, preferred_element_type=jnp.float32)
-                put(block, kind * 12 + PAIRS.index((i, j)) * 2)
-
-
-def final_kernel(norm, pos_ref, mine_ref, other_ref, root_ref, normal_ref, cfg_ref, full, left, gram):
+                put(core, block, kind * 12 + PAIRS.index((i, j)) * 2, keep_ref, send_ref)
+
+
+def final_kernel(
+    norm, pos_ref, sums_ref, other_sums, gram_ref, other_gram, root_ref, normal_ref, cfg_ref, full, left, gram
+):
     core, kind, part, owner = pos_ref[0], pos_ref[1], pos_ref[2], pos_ref[3]
     width = gram.shape[1]
     band = left.shape[1]
 
-    def joined(tile, lo=0, hi=16):
+    def joined(tile, lo=0, hi=16, refs=(gram_ref, other_gram)):
         at = slice(tile * 8, (tile + 1) * 8)
-        a, b = mine_ref[lo:hi, at, :], other_ref[lo:hi, at, :]
+        a, b = [ref[lo:hi, at, :] for ref in refs]
         pair = [jnp.where(core == which, a, b)[:, None] for which in range(2)]
         return jnp.concatenate(pair, 1).reshape((hi - lo) * 16, LANES)
 
     for j in range(2 * width // LANES):
-        full[:, j * LANES : (j + 1) * LANES] = joined(6 + j)
+        full[:, j * LANES : (j + 1) * LANES] = joined(j, refs=(sums_ref, other_sums))
 
     def fill(row, col, piece):
         gram[row : row + piece.shape[0], col : col + piece.shape[1]] = piece
@@ -183,44 +198,60 @@
     pos = jnp.stack([core, kind, part, (x * 4 + l) * 2 + core])
 
     flip = [(0, 1), (1, 0)]
-    payload = pltpu.VMEM((16, 288, LANES), f32)
     int_row = pltpu.VMEM((1, atoms), jnp.int32)
-    keep, send = call(
-        local_kernel,
-        [payload, payload],
+    matrix = pltpu.VMEM((atoms, width), jnp.bfloat16)
+    sems = pltpu.SemaphoreType.DMA((6,))
+
+    def tiles(count):
+        return pltpu.VMEM((16, count * 8, LANES), f32)
+
+    keep_s, send_s = call(
+        sums_kernel,
+        [tiles(12)] * 2,
         [core[None], desc, species[None], atom_cfg[None], slot[None]],
-        [
-            pltpu.VMEM((atoms, width), jnp.bfloat16),
-            int_row,
-            int_row,
-            pltpu.VMEM((1, configs), jnp.int32),
-            pltpu.VMEM((width, atoms), jnp.bfloat16),
-            pltpu.SemaphoreType.DMA((6,)),
-        ],
+        [matrix, int_row, int_row, pltpu.VMEM((1, configs), jnp.int32), sems],
         pltpu.HBM,
         24 << 20,
     )
-    came, root, pos = lax.optimization_barrier((lax.ppermute(send, "c", flip), root, pos))
-    total = jnp.sum(exchange(keep + came, ("x", "y")), 0)
-    grams, sums = total[:192].reshape(2, 96, LANES), total[192:]
-    planes = jnp.concatenate([grams, jnp.broadcast_to(jnp.concatenate([sums, root])[None], (2, 104, LANES))], 1)
-    planes = jnp.broadcast_to(planes[None], (4, 2, 200, LANES)).reshape(8, 200, LANES)
-    got = exchange(planes, ("l", "h"))
-    root_here = lax.dynamic_index_in_dim(got, part * 2, 0, False)[192:]
-    total = jnp.sum(got[:, :192], 0)
+    pair_s, desc, pos, root = lax.optimization_barrier((keep_s + lax.ppermute(send_s, "c", flip), desc, pos, root))
+    keep_g, send_g = call(
+        gram_kernel,
+        [tiles(24)] * 2,
+        [core[None], desc, species[None]],
+        [matrix, int_row, pltpu.VMEM((width, atoms), jnp.bfloat16), sems],
+        pltpu.HBM,
+        24 << 20,
+    )
+    pair_g = keep_g + lax.ppermute(send_g, "c", flip)
+    plane_s = jnp.sum(exchange(pair_s, ("x", "y")), 0)
+    plane_g = jnp.sum(exchange(pair_g, ("x", "y")), 0).reshape(2, 96, LANES)
+
+    place = kind * 4 + l
+
+    def along_z(value, k):
+        pairs = [((z % 4) * 2 + z // 4, ((z + k) % 8 % 4) * 2 + (z + k) % 8 // 4) for z in range(8)]
+        return lax.ppermute(value, ("l", "h"), pairs)
+
+    far = (4, 3, 5, 2, 6, 1, 7)
+    rooted = jnp.concatenate([plane_s, root])
+    got = [(rooted, place)] + [(along_z(rooted, k), (place - k) % 8) for k in far]
+    root_here = sum(jnp.where(source == part, value[96:], 0.0) for value, source in got)
     scale = 1.0 / math.sqrt(atoms * n_dev / configs)
-    sums = (total[96:].reshape(12, 8, LANES) * (root_here * scale)).reshape(96, LANES)
-    bands = needed(total[:96], x * 4 + part)
-    spread = jnp.concatenate([bands, jnp.broadcast_to(sums[None], (4, 96, LANES))], 1)
-    spread = jnp.broadcast_to(spread[None], (4, 4, 144, LANES)).reshape(16, 144, LANES)
-    mine = exchange(spread, ("x", "y"))
-    other = lax.ppermute(mine, "c", flip)
+    sums = sum(value[:96] for value, _ in got).reshape(12, 8, LANES) * (root_here * scale)
+    mine_s = exchange(jnp.broadcast_to(sums.reshape(1, 96, LANES), (16, 96, LANES)), ("x", "y"))
+
+    grams = lax.dynamic_index_in_dim(plane_g, kind, 0, False)
+    for k in far:
+        theirs = lax.dynamic_index_in_dim(plane_g, (place + k) % 8 // 4, 0, False)
+        grams = grams + along_z(theirs, k)
+    bands = needed(grams, x * 4 + part)
+    mine_g = exchange(jnp.broadcast_to(bands[None], (4, 4, 48, LANES)).reshape(16, 48, LANES), ("x", "y"))
     band = 2 * width // 8
     norm = atoms * n_dev // 8
     normal, rows = call(
         lambda *refs: final_kernel(norm, *refs),
         [jax.ShapeDtypeStruct((band, 2 * width), f32), jax.ShapeDtypeStruct((cfg_here, band), f32)],
-        [pos, mine, other, root],
+        [pos, mine_s, lax.ppermute(mine_s, "c", flip), mine_g, lax.ppermute(mine_g, "c", flip), root],
         [
             pltpu.VMEM((configs, 2 * width), f32),
             pltpu.VMEM((configs, band), f32),

time: 113 us -> 111 us (0.982); the launches traced: 111 us -> 110 us
  starting transfers between devices: 14.8 us -> 61.1 us
  blocking collectives: 54.2 us -> 14.3 us
  waiting for transfers between devices: 26.1 us -> 16.1 us
  other arithmetic: 2.24 us -> 5.18 us
    all_to_all x2 -> x1, blocking collectives: 54.2 us -> 14.3 us  [exchange(): return lax.all_to_all(flat, axes, 0, 0, tiled=True).reshape(values.shape)]
    ppermute x2 -> x18, starting transfers between devices: 6.66 us -> 45 us  [the longest x14 32.2 us: along_z(): return lax.ppermute(value, ('l', 'h'), pairs)]
    all_to_all x1 -> x3, waiting for transfers between devices: 19.2 us -> 9.96 us  [exchange(): return lax.all_to_all(flat, axes, 0, 0, tiled=True).reshape(values.shape)]
    all_to_all x1 -> x3, starting transfers between devices: 8.19 us -> 16.1 us  [exchange(): return lax.all_to_all(flat, axes, 0, 0, tiled=True).reshape(values.shape)]
    add x1 -> x3, other arithmetic: 1.9 us -> 3.74 us  [the longest x1 2.73 us: shards(): pair_g = keep_g + lax.ppermute(send_g, 'c', flip)]
    ppermute x2 -> x18, waiting for transfers between devices: 6.89 us -> 6.12 us  [the longest x14 2.94 us: along_z(): return lax.ppermute(value, ('l', 'h'), pairs)]
    pallas_call x2 -> x3, Pallas kernels: 11.2 us -> 11.6 us  [call(): pl.pallas_call(kernel, out_shape=outs, in_specs=[smem] + [pl.BlockSpec(me...]
  transfers between devices with their start and end apart: 3 -> 21, of which waited for: 3 -> 5; matrix products, arithmetic and copies ran while one was open for 0% -> 4% of each run, Pallas kernels for 0% -> 0%
where the time goes in v5:
time: 111 us; the launch traced here: 110 us
  starting transfers between devices  61.1 us (55%)
  waiting for transfers between devices  16.1 us (15%)
  blocking collectives  14.3 us (13%)
  Pallas kernels  11.6 us (10%)
  other arithmetic  5.18 us (5%)
  local copies, waits for them, and re-layouts  1.12 us (1%)
    ppermute x14, starting transfers between devices, along_z(): return lax.ppermute(value, ('l', 'h'), pairs)  32.2 us
    all_to_all x3, starting transfers between devices, exchange(): return lax.all_to_all(flat, axes, 0, 0, tiled=True).reshape(values.shape)  16.1 us
    all_to_all x1, blocking collectives, exchange(): return lax.all_to_all(flat, axes, 0, 0, tiled=True).reshape(values.shape)  14.3 us
    pallas_call x3, Pallas kernels, call(): pl.pallas_call(kernel, out_shape=outs, in_specs=[smem] + [pl.BlockSpec(me...  11.6 us
    all_to_all x3, waiting for transfers between devices, exchange(): return lax.all_to_all(flat, axes, 0, 0, tiled=True).reshape(values.shape)  9.96 us
    ppermute x1, starting transfers between devices, shards(): lax.ppermute(mine_s, 'c', flip)  5.54 us
    ppermute x1, starting transfers between devices, shards(): lax.ppermute(mine_g, 'c', flip)  3.42 us
    ppermute x1, starting transfers between devices, shards(): lax.ppermute(send_s, 'c', flip)  3.33 us
  transfers between devices with their start and end apart: 21, of which 5 were waited for; matrix products, arithmetic and copies ran while one was open for 4% of the time, Pallas kernels for 0%

profile of v5, /device:TPU:1, one launch (start us, length us, event | category | flops | bytes accessed | tf_op | source)
XLA Modules:
  0.0 110.4 jit_solution(7496678639950593926)
XLA Ops:
  0.6 0.0 copy-start
  0.6 3.5 %shard_map.68 = (f32[16,96,128]{2,1,0:T(8,128)S(1)}, f32[16,96,128]{2,1,0:T(8,128)S(1)}) custom-call(s32[1]{0:T(128)} %bitcast.core_ref, bf16[2048,768]{1,0:T(8,128)(2,1)} %desc_hbm.2, s32[1,2048]{1,0:T(1,128)} %bitcast.50, s32[1,2048]{1,0:T(1,128)} %bitcast.52, s32[1,256]{1,0:T(1,128)} %bitcast.53), custom_call_target="tpu_custom_call" | custom-call | tf_op jit(solution)/shard_map/pallas_call | solution.py:158
  4.1 3.3 %collective-permute-start = (f32[16,96,128]{2,1,0:T(8,128)S(1)}, f32[16,96,128]{2,1,0:T(8,128)S(1)}, u32[]{:S(2)}, u32[]{:S(2)}) collective-permute-start(f32[16,96,128]{2,1,0:T(8,128)S(1)} %get-tuple-element.11), channel_id=1, source_target_pairs={{0,8},{8,0},{1,9},{9,1},{2,10},{10,2},{3,11},{11,3},{4,12},{12,4},... | collective-permute-start | bytes 2359304 | tf_op jit(solution)/shard_map/ppermute | solution.py:216
  7.4 0.0 copy-done
  7.4 0.1 pad_add_fusion.refs_0_
  7.5 1.8 %collective-permute-done = f32[16,96,128]{2,1,0:T(8,128)S(1)} collective-permute-done((f32[16,96,128]{2,1,0:T(8,128)S(1)}, f32[16,96,128]{2,1,0:T(8,128)S(1)}, u32[]{:S(2)}, u32[]{:S(2)}) %collective-permute-start) | collective-permute-done | bytes 786464 | tf_op jit(solution)/shard_map/ppermute | solution.py:216
  9.4 1.0 add.184
  10.3 0.1 broadcast_in_dim.47.refs_5_
  10.4 5.1 %shard_map.69 = (f32[16,192,128]{2,1,0:T(8,128)S(1)}, f32[16,192,128]{2,1,0:T(8,128)S(1)}) custom-call(s32[1]{0:T(128)} %bitcast.core_ref, bf16[2048,768]{1,0:T(8,128)(2,1)} %desc_hbm.2, s32[1,2048]{1,0:T(1,128)} %bitcast.51), custom_call_target="tpu_custom_call" | custom-call | tf_op jit(solution)/shard_map/pallas_call | solution.py:158
  15.5 0.5 collective-permute-start.9
  16.0 5.1 %all-to-all-start = ((f32[16,96,128]{2,1,0:T(8,128)}), f32[16,96,128]{2,1,0:T(8,128)}, u32[]{:S(2)}, u32[]{:S(2)}) async-start(f32[16,96,128]{2,1,0:T(8,128)} %add.184), calls=%async_computation | async-start | bytes 1572864 | tf_op jit(solution)/shard_map/all_to_all | solution.py:170
  21.0 0.0 collective-permute-done.9
  21.0 2.7 %add.209 = f32[16,192,128]{2,1,0:T(8,128)} add(f32[16,192,128]{2,1,0:T(8,128)S(1)} %get-tuple-element.16, f32[16,192,128]{2,1,0:T(8,128)} %collective-permute-done.9) | non-fusion elementwise | flops 393216 | bytes 4718592 | tf_op jit(solution)/shard_map/add | solution.py:225
  23.8 10.0 %all-to-all-done = f32[16,96,128]{2,1,0:T(8,128)} async-done(((f32[16,96,128]{2,1,0:T(8,128)}), f32[16,96,128]{2,1,0:T(8,128)}, u32[]{:S(2)}, u32[]{:S(2)}) %all-to-all-start) | async-done | bytes 786464 | tf_op jit(solution)/shard_map/all_to_all | solution.py:170
  33.7 4.7 %all-to-all-start.2 = ((f32[16,192,128]{2,1,0:T(8,128)}), f32[16,192,128]{2,1,0:T(8,128)S(1)}, u32[]{:S(2)}, u32[]{:S(2)}) async-start(f32[16,192,128]{2,1,0:T(8,128)} %add.209), calls=%async_computation.2 | async-start | bytes 3145728 | tf_op jit(solution)/shard_map/all_to_all | solution.py:170
  38.5 1.2 %reduce_sum.18 = f32[96,128]{1,0:T(8,128)S(1)} reduce(f32[16,96,128]{2,1,0:T(8,128)} %all-to-all-done, f32[]{:T(128)} %constant.171.clone.1), dimensions={0}, to_apply=%region_0.0 | reduce | flops 184320 | bytes 835588 | tf_op jit(solution)/shard_map/reduce_sum | solution.py:226
  39.7 7.0 %collective-permute-start.1 = (f32[104,128]{1,0:T(8,128)S(1)}, f32[104,128]{1,0:T(8,128)S(1)}, u32[]{:S(2)}, u32[]{:S(2)}) collective-permute-start(f32[104,128]{1,0:T(8,128)S(1)} %pad_maximum_fusion.1), channel_id=1, source_target_pairs={{0,4},{16,20},{32,36},{48,52},{4,0},{20,16},{36,32},{52,48},{1,5},... | collective-permute-start | bytes 159752 | tf_op jit(solution)/shard_map/ppermute | solution.py:233
  46.7 1.7 %collective-permute-start.2 = (f32[104,128]{1,0:T(8,128)S(1)}, f32[104,128]{1,0:T(8,128)S(1)}, u32[]{:S(2)}, u32[]{:S(2)}) collective-permute-start(f32[104,128]{1,0:T(8,128)S(1)} %pad_maximum_fusion.1), channel_id=1, source_target_pairs={{0,48},{16,4},{32,20},{48,36},{4,52},{20,0},{36,16},{52,32},{1,49}... | collective-permute-start | bytes 159752 | tf_op jit(solution)/shard_map/ppermute | solution.py:233
  48.4 2.8 %collective-permute-start.3 = (f32[104,128]{1,0:T(8,128)S(1)}, f32[104,128]{1,0:T(8,128)S(1)}, u32[]{:S(2)}, u32[]{:S(2)}) collective-permute-start(f32[104,128]{1,0:T(8,128)S(1)} %pad_maximum_fusion.1), channel_id=1, source_target_pairs={{0,20},{16,36},{32,52},{48,0},{4,16},{20,32},{36,48},{52,4},{1,21}... | collective-permute-start | bytes 159752 | tf_op jit(solution)/shard_map/ppermute | solution.py:233
  51.2 1.2 %collective-permute-start.4 = (f32[104,128]{1,0:T(8,128)S(1)}, f32[104,128]{1,0:T(8,128)S(1)}, u32[]{:S(2)}, u32[]{:S(2)}) collective-permute-start(f32[104,128]{1,0:T(8,128)S(1)} %pad_maximum_fusion.1), channel_id=1, source_target_pairs={{0,32},{16,48},{32,4},{48,20},{4,36},{20,52},{36,0},{52,16},{1,33}... | collective-permute-start | bytes 159752 | tf_op jit(solution)/shard_map/ppermute | solution.py:233
  52.4 2.4 %collective-permute-start.5 = (f32[104,128]{1,0:T(8,128)S(1)}, f32[104,128]{1,0:T(8,128)S(1)}, u32[]{:S(2)}, u32[]{:S(2)}) collective-permute-start(f32[104,128]{1,0:T(8,128)S(1)} %pad_maximum_fusion.1), channel_id=1, source_target_pairs={{0,36},{16,52},{32,0},{48,16},{4,32},{20,48},{36,4},{52,20},{1,37}... | collective-permute-start | bytes 159752 | tf_op jit(solution)/shard_map/ppermute | solution.py:233
  54.8 0.0 collective-permute-done.1
  54.8 0.7 collective-permute-start.6
  55.5 0.0 collective-permute-done.2
  55.5 2.0 %collective-permute-start.7 = (f32[104,128]{1,0:T(8,128)S(1)}, f32[104,128]{1,0:T(8,128)S(1)}, u32[]{:S(2)}, u32[]{:S(2)}) collective-permute-start(f32[104,128]{1,0:T(8,128)S(1)} %pad_maximum_fusion.1), channel_id=1, source_target_pairs={{0,52},{16,0},{32,16},{48,32},{4,48},{20,4},{36,20},{52,36},{1,53}... | collective-permute-start | bytes 159752 | tf_op jit(solution)/shard_map/ppermute | solution.py:233
  57.5 0.0 collective-permute-done.3
  57.5 0.1 collective-permute-done.4
  57.5 0.0 collective-permute-done.5
  57.5 2.8 %collective-permute-done.6 = f32[104,128]{1,0:T(8,128)S(1)} collective-permute-done((f32[104,128]{1,0:T(8,128)S(1)}, f32[104,128]{1,0:T(8,128)S(1)}, u32[]{:S(2)}, u32[]{:S(2)}) %collective-permute-start.6) | collective-permute-done | bytes 53280 | tf_op jit(solution)/shard_map/ppermute | solution.py:233
  60.4 0.0 collective-permute-done.7
  60.4 0.0 all-to-all-done.2
  60.4 1.0 broadcast_in_dim.49
  61.4 6.3 %all-to-all-start.1 = ((f32[16,96,128]{2,1,0:T(8,128)}), f32[16,96,128]{2,1,0:T(8,128)S(1)}, u32[]{:S(2)}, u32[]{:S(2)}) async-start(f32[16,96,128]{2,1,0:T(8,128)} %broadcast_in_dim.49), calls=%async_computation.1 | async-start | bytes 1572864 | tf_op jit(solution)/shard_map/all_to_all | solution.py:170
  67.9 0.1 reduce_sum.19
  68.1 3.8 %collective-permute-start.10 = (f32[96,128]{1,0:T(8,128)S(1)}, f32[96,128]{1,0:T(8,128)S(1)}, u32[]{:S(2)}, u32[]{:S(2)}) collective-permute-start(f32[96,128]{1,0:T(8,128)S(1)} %get-tuple-element.18), channel_id=1, source_target_pairs={{0,4},{16,20},{32,36},{48,52},{4,0},{20,16},{36,32},{52,48},{1,5},... | collective-permute-start | bytes 147464 | tf_op jit(solution)/shard_map/ppermute | solution.py:233
  71.8 1.7 %collective-permute-start.11 = (f32[96,128]{1,0:T(8,128)S(1)}, f32[96,128]{1,0:T(8,128)S(1)}, u32[]{:S(2)}, u32[]{:S(2)}) collective-permute-start(f32[96,128]{1,0:T(8,128)S(1)} %get-tuple-element.24), channel_id=1, source_target_pairs={{0,48},{16,4},{32,20},{48,36},{4,52},{20,0},{36,16},{52,32},{1,49}... | collective-permute-start | bytes 147464 | tf_op jit(solution)/shard_map/ppermute | solution.py:233
  73.5 2.8 %collective-permute-start.12 = (f32[96,128]{1,0:T(8,128)S(1)}, f32[96,128]{1,0:T(8,128)S(1)}, u32[]{:S(2)}, u32[]{:S(2)}) collective-permute-start(f32[96,128]{1,0:T(8,128)S(1)} %get-tuple-element.23), channel_id=1, source_target_pairs={{0,20},{16,36},{32,52},{48,0},{4,16},{20,32},{36,48},{52,4},{1,21}... | collective-permute-start | bytes 147464 | tf_op jit(solution)/shard_map/ppermute | solution.py:233
  76.3 1.2 %collective-permute-start.13 = (f32[96,128]{1,0:T(8,128)S(1)}, f32[96,128]{1,0:T(8,128)S(1)}, u32[]{:S(2)}, u32[]{:S(2)}) collective-permute-start(f32[96,128]{1,0:T(8,128)S(1)} %get-tuple-element.22), channel_id=1, source_target_pairs={{0,32},{16,48},{32,4},{48,20},{4,36},{20,52},{36,0},{52,16},{1,33}... | collective-permute-start | bytes 147464 | tf_op jit(solution)/shard_map/ppermute | solution.py:233
  77.5 2.4 %collective-permute-start.14 = (f32[96,128]{1,0:T(8,128)S(1)}, f32[96,128]{1,0:T(8,128)S(1)}, u32[]{:S(2)}, u32[]{:S(2)}) collective-permute-start(f32[96,128]{1,0:T(8,128)S(1)} %get-tuple-element.21), channel_id=1, source_target_pairs={{0,36},{16,52},{32,0},{48,16},{4,32},{20,48},{36,4},{52,20},{1,37}... | collective-permute-start | bytes 147464 | tf_op jit(solution)/shard_map/ppermute | solution.py:233
  79.9 0.0 collective-permute-done.10
  79.9 0.7 collective-permute-start.15
  80.6 0.0 collective-permute-done.11
  80.6 2.0 %collective-permute-start.16 = (f32[96,128]{1,0:T(8,128)S(1)}, f32[96,128]{1,0:T(8,128)S(1)}, u32[]{:S(2)}, u32[]{:S(2)}) collective-permute-start(f32[96,128]{1,0:T(8,128)S(1)} %get-tuple-element.19), channel_id=1, source_target_pairs={{0,52},{16,0},{32,16},{48,32},{4,48},{20,4},{36,20},{52,36},{1,53}... | collective-permute-start | bytes 147464 | tf_op jit(solution)/shard_map/ppermute | solution.py:233
  82.5 0.0 all-to-all-done.1.refs_1_
  82.6 0.0 collective-permute-done.12
  82.6 5.5 %collective-permute-start.8 = (f32[16,96,128]{2,1,0:T(8,128)S(1)}, f32[16,96,128]{2,1,0:T(8,128)S(1)}, u32[]{:S(2)}, u32[]{:S(2)}) collective-permute-start(f32[16,96,128]{2,1,0:T(8,128)S(1)} %all-to-all-done.1.refs_1_), channel_id=1, source_target_pairs={{0,8},{8,0},{1,9},{9,1},{2,10},{10,2},{3,11},{11,3},{4,12},{12,4},... | collective-permute-start | bytes 2359304 | tf_op jit(solution)/shard_map/ppermute | solution.py:254
  88.1 0.0 collective-permute-done.13
  88.1 0.0 collective-permute-done.14
  88.1 0.0 collective-permute-done.15
  88.1 0.0 collective-permute-done.16
  88.3 14.3 %all_to_all.27.refs_3_ = f32[16,48,128]{2,1,0:T(8,128)S(1)} all-to-all(f32[16,48,128]{2,1,0:T(8,128)S(1)} %bitcast.49), channel_id=1, replica_groups=mesh['x'=4,'l'=4,'c'=2,'h'=2,'y'=4] {'x','y'}, dimensions={0} | all-to-all | bytes 786432 | tf_op jit(solution)/shard_map/all_to_all | solution.py:170
  102.6 3.4 %collective-permute-start.17 = (f32[16,48,128]{2,1,0:T(8,128)S(1)}, f32[16,48,128]{2,1,0:T(8,128)S(1)}, u32[]{:S(2)}, u32[]{:S(2)}) collective-permute-start(f32[16,48,128]{2,1,0:T(8,128)S(1)} %all_to_all.27.refs_3_), channel_id=1, source_target_pairs={{0,8},{8,0},{1,9},{9,1},{2,10},{10,2},{3,11},{11,3},{4,12},{12,4},... | collective-permute-start | bytes 1179656 | tf_op jit(solution)/shard_map/ppermute | solution.py:254
  106.0 0.0 collective-permute-done.8.refs_2_
  106.0 1.3 %collective-permute-done.17.refs_4_ = f32[16,48,128]{2,1,0:T(8,128)S(1)} collective-permute-done((f32[16,48,128]{2,1,0:T(8,128)S(1)}, f32[16,48,128]{2,1,0:T(8,128)S(1)}, u32[]{:S(2)}, u32[]{:S(2)}) %collective-permute-start.17) | collective-permute-done | bytes 393248 | tf_op jit(solution)/shard_map/ppermute | solution.py:254
  107.3 3.0 %shard_map.70 = (f32[192,1536]{1,0:T(8,128)}, f32[8,192]{1,0:T(8,128)}) custom-call(s32[4]{0:T(128)S(1)} %pad_add_fusion.refs_0_, f32[16,96,128]{2,1,0:T(8,128)S(1)} %all-to-all-done.1.refs_1_, f32[16,96,128]{2,1,0:T(8,128)S(1)} %collective-permute-done.8.refs_2_, f32[16,48,128]{2,1,0:T(8,128)S(1)} %all_to_all.27.refs_3_, ...), custom_call_target="tpu_custom_call" | custom-call | tf_op jit(solution)/shard_map/pallas_call | solution.py:158
  (15 shorter events, 0.2 us)
Async XLA Ops:
  0.6 6.8 %copy-start = (f32[8]{0:T(128)S(1)}, f32[8]{0:T(128)}, u32[]{:S(2)}) copy-start(f32[8]{0:T(128)} %param.9) | copy-start | bytes 100
  4.1 5.2 %collective-permute-start = (f32[16,96,128]{2,1,0:T(8,128)S(1)}, f32[16,96,128]{2,1,0:T(8,128)S(1)}, u32[]{:S(2)}, u32[]{:S(2)}) collective-permute-start(f32[16,96,128]{2,1,0:T(8,128)S(1)} %get-tuple-element.11), channel_id=1, source_target_pairs={{0,8},{8,0},{1,9},{9,1},{2,10},{10,2},{3,11},{11,3},{4,12},{12,4},... | collective-permute-start | bytes 2359304 | tf_op jit(solution)/shard_map/ppermute | solution.py:216
  15.5 5.5 %collective-permute-start.9 = (f32[16,192,128]{2,1,0:T(8,128)S(1)}, f32[16,192,128]{2,1,0:T(8,128)}, u32[]{:S(2)}, u32[]{:S(2)}) collective-permute-start(f32[16,192,128]{2,1,0:T(8,128)S(1)} %get-tuple-element.17), channel_id=1, source_target_pairs={{0,8},{8,0},{1,9},{9,1},{2,10},{10,2},{3,11},{11,3},{4,12},{12,4},... | collective-permute-start | bytes 4718600 | tf_op jit(solution)/shard_map/ppermute | solution.py:225
  16.0 17.8 %all-to-all-start = ((f32[16,96,128]{2,1,0:T(8,128)}), f32[16,96,128]{2,1,0:T(8,128)}, u32[]{:S(2)}, u32[]{:S(2)}) async-start(f32[16,96,128]{2,1,0:T(8,128)} %add.184), calls=%async_computation | async-start | bytes 1572864 | tf_op jit(solution)/shard_map/all_to_all | solution.py:170
  33.7 26.7 %all-to-all-start.2 = ((f32[16,192,128]{2,1,0:T(8,128)}), f32[16,192,128]{2,1,0:T(8,128)S(1)}, u32[]{:S(2)}, u32[]{:S(2)}) async-start(f32[16,192,128]{2,1,0:T(8,128)} %add.209), calls=%async_computation.2 | async-start | bytes 3145728 | tf_op jit(solution)/shard_map/all_to_all | solution.py:170
  39.7 15.1 %collective-permute-start.1 = (f32[104,128]{1,0:T(8,128)S(1)}, f32[104,128]{1,0:T(8,128)S(1)}, u32[]{:S(2)}, u32[]{:S(2)}) collective-permute-start(f32[104,128]{1,0:T(8,128)S(1)} %pad_maximum_fusion.1), channel_id=1, source_target_pairs={{0,4},{16,20},{32,36},{48,52},{4,0},{20,16},{36,32},{52,48},{1,5},... | collective-permute-start | bytes 159752 | tf_op jit(solution)/shard_map/ppermute | solution.py:233
  46.7 8.8 %collective-permute-start.2 = (f32[104,128]{1,0:T(8,128)S(1)}, f32[104,128]{1,0:T(8,128)S(1)}, u32[]{:S(2)}, u32[]{:S(2)}) collective-permute-start(f32[104,128]{1,0:T(8,128)S(1)} %pad_maximum_fusion.1), channel_id=1, source_target_pairs={{0,48},{16,4},{32,20},{48,36},{4,52},{20,0},{36,16},{52,32},{1,49}... | collective-permute-start | bytes 159752 | tf_op jit(solution)/shard_map/ppermute | solution.py:233
  48.4 9.1 %collective-permute-start.3 = (f32[104,128]{1,0:T(8,128)S(1)}, f32[104,128]{1,0:T(8,128)S(1)}, u32[]{:S(2)}, u32[]{:S(2)}) collective-permute-start(f32[104,128]{1,0:T(8,128)S(1)} %pad_maximum_fusion.1), channel_id=1, source_target_pairs={{0,20},{16,36},{32,52},{48,0},{4,16},{20,32},{36,48},{52,4},{1,21}... | collective-permute-start | bytes 159752 | tf_op jit(solution)/shard_map/ppermute | solution.py:233
  51.2 6.3 %collective-permute-start.4 = (f32[104,128]{1,0:T(8,128)S(1)}, f32[104,128]{1,0:T(8,128)S(1)}, u32[]{:S(2)}, u32[]{:S(2)}) collective-permute-start(f32[104,128]{1,0:T(8,128)S(1)} %pad_maximum_fusion.1), channel_id=1, source_target_pairs={{0,32},{16,48},{32,4},{48,20},{4,36},{20,52},{36,0},{52,16},{1,33}... | collective-permute-start | bytes 159752 | tf_op jit(solution)/shard_map/ppermute | solution.py:233
  52.4 5.2 %collective-permute-start.5 = (f32[104,128]{1,0:T(8,128)S(1)}, f32[104,128]{1,0:T(8,128)S(1)}, u32[]{:S(2)}, u32[]{:S(2)}) collective-permute-start(f32[104,128]{1,0:T(8,128)S(1)} %pad_maximum_fusion.1), channel_id=1, source_target_pairs={{0,36},{16,52},{32,0},{48,16},{4,32},{20,48},{36,4},{52,20},{1,37}... | collective-permute-start | bytes 159752 | tf_op jit(solution)/shard_map/ppermute | solution.py:233
  54.8 5.6 %collective-permute-start.6 = (f32[104,128]{1,0:T(8,128)S(1)}, f32[104,128]{1,0:T(8,128)S(1)}, u32[]{:S(2)}, u32[]{:S(2)}) collective-permute-start(f32[104,128]{1,0:T(8,128)S(1)} %pad_maximum_fusion.1), channel_id=1, source_target_pairs={{0,16},{16,32},{32,48},{48,4},{4,20},{20,36},{36,52},{52,0},{1,17}... | collective-permute-start | bytes 159752 | tf_op jit(solution)/shard_map/ppermute | solution.py:233
  55.5 4.9 %collective-permute-start.7 = (f32[104,128]{1,0:T(8,128)S(1)}, f32[104,128]{1,0:T(8,128)S(1)}, u32[]{:S(2)}, u32[]{:S(2)}) collective-permute-start(f32[104,128]{1,0:T(8,128)S(1)} %pad_maximum_fusion.1), channel_id=1, source_target_pairs={{0,52},{16,0},{32,16},{48,32},{4,48},{20,4},{36,20},{52,36},{1,53}... | collective-permute-start | bytes 159752 | tf_op jit(solution)/shard_map/ppermute | solution.py:233
  61.4 21.2 %all-to-all-start.1 = ((f32[16,96,128]{2,1,0:T(8,128)}), f32[16,96,128]{2,1,0:T(8,128)S(1)}, u32[]{:S(2)}, u32[]{:S(2)}) async-start(f32[16,96,128]{2,1,0:T(8,128)} %broadcast_in_dim.49), calls=%async_computation.1 | async-start | bytes 1572864 | tf_op jit(solution)/shard_map/all_to_all | solution.py:170
  68.1 11.8 %collective-permute-start.10 = (f32[96,128]{1,0:T(8,128)S(1)}, f32[96,128]{1,0:T(8,128)S(1)}, u32[]{:S(2)}, u32[]{:S(2)}) collective-permute-start(f32[96,128]{1,0:T(8,128)S(1)} %get-tuple-element.18), channel_id=1, source_target_pairs={{0,4},{16,20},{32,36},{48,52},{4,0},{20,16},{36,32},{52,48},{1,5},... | collective-permute-start | bytes 147464 | tf_op jit(solution)/shard_map/ppermute | solution.py:233
  71.8 8.8 %collective-permute-start.11 = (f32[96,128]{1,0:T(8,128)S(1)}, f32[96,128]{1,0:T(8,128)S(1)}, u32[]{:S(2)}, u32[]{:S(2)}) collective-permute-start(f32[96,128]{1,0:T(8,128)S(1)} %get-tuple-element.24), channel_id=1, source_target_pairs={{0,48},{16,4},{32,20},{48,36},{4,52},{20,0},{36,16},{52,32},{1,49}... | collective-permute-start | bytes 147464 | tf_op jit(solution)/shard_map/ppermute | solution.py:233
  73.5 9.1 %collective-permute-start.12 = (f32[96,128]{1,0:T(8,128)S(1)}, f32[96,128]{1,0:T(8,128)S(1)}, u32[]{:S(2)}, u32[]{:S(2)}) collective-permute-start(f32[96,128]{1,0:T(8,128)S(1)} %get-tuple-element.23), channel_id=1, source_target_pairs={{0,20},{16,36},{32,52},{48,0},{4,16},{20,32},{36,48},{52,4},{1,21}... | collective-permute-start | bytes 147464 | tf_op jit(solution)/shard_map/ppermute | solution.py:233
  76.3 11.8 %collective-permute-start.13 = (f32[96,128]{1,0:T(8,128)S(1)}, f32[96,128]{1,0:T(8,128)S(1)}, u32[]{:S(2)}, u32[]{:S(2)}) collective-permute-start(f32[96,128]{1,0:T(8,128)S(1)} %get-tuple-element.22), channel_id=1, source_target_pairs={{0,32},{16,48},{32,4},{48,20},{4,36},{20,52},{36,0},{52,16},{1,33}... | collective-permute-start | bytes 147464 | tf_op jit(solution)/shard_map/ppermute | solution.py:233
  77.5 10.6 %collective-permute-start.14 = (f32[96,128]{1,0:T(8,128)S(1)}, f32[96,128]{1,0:T(8,128)S(1)}, u32[]{:S(2)}, u32[]{:S(2)}) collective-permute-start(f32[96,128]{1,0:T(8,128)S(1)} %get-tuple-element.21), channel_id=1, source_target_pairs={{0,36},{16,52},{32,0},{48,16},{4,32},{20,48},{36,4},{52,20},{1,37}... | collective-permute-start | bytes 147464 | tf_op jit(solution)/shard_map/ppermute | solution.py:233
  79.9 8.2 %collective-permute-start.15 = (f32[96,128]{1,0:T(8,128)S(1)}, f32[96,128]{1,0:T(8,128)S(1)}, u32[]{:S(2)}, u32[]{:S(2)}) collective-permute-start(f32[96,128]{1,0:T(8,128)S(1)} %get-tuple-element.20), channel_id=1, source_target_pairs={{0,16},{16,32},{32,48},{48,4},{4,20},{20,36},{36,52},{52,0},{1,17}... | collective-permute-start | bytes 147464 | tf_op jit(solution)/shard_map/ppermute | solution.py:233
  80.6 7.5 %collective-permute-start.16 = (f32[96,128]{1,0:T(8,128)S(1)}, f32[96,128]{1,0:T(8,128)S(1)}, u32[]{:S(2)}, u32[]{:S(2)}) collective-permute-start(f32[96,128]{1,0:T(8,128)S(1)} %get-tuple-element.19), channel_id=1, source_target_pairs={{0,52},{16,0},{32,16},{48,32},{4,48},{20,4},{36,20},{52,36},{1,53}... | collective-permute-start | bytes 147464 | tf_op jit(solution)/shard_map/ppermute | solution.py:233
  82.6 23.4 %collective-permute-start.8 = (f32[16,96,128]{2,1,0:T(8,128)S(1)}, f32[16,96,128]{2,1,0:T(8,128)S(1)}, u32[]{:S(2)}, u32[]{:S(2)}) collective-permute-start(f32[16,96,128]{2,1,0:T(8,128)S(1)} %all-to-all-done.1.refs_1_), channel_id=1, source_target_pairs={{0,8},{8,0},{1,9},{9,1},{2,10},{10,2},{3,11},{11,3},{4,12},{12,4},... | collective-permute-start | bytes 2359304 | tf_op jit(solution)/shard_map/ppermute | solution.py:254
  102.6 4.8 %collective-permute-start.17 = (f32[16,48,128]{2,1,0:T(8,128)S(1)}, f32[16,48,128]{2,1,0:T(8,128)S(1)}, u32[]{:S(2)}, u32[]{:S(2)}) collective-permute-start(f32[16,48,128]{2,1,0:T(8,128)S(1)} %all_to_all.27.refs_3_), channel_id=1, source_target_pairs={{0,8},{8,0},{1,9},{9,1},{2,10},{10,2},{3,11},{11,3},{4,12},{12,4},... | collective-permute-start | bytes 1179656 | tf_op jit(solution)/shard_map/ppermute | solution.py:254

commit v6 on v5

--- a/solution.py
+++ b/solution.py
@@ -14,12 +14,12 @@
 PAIRS = ((0, 1), (0, 2), (1, 2), (0, 0), (1, 1), (2, 2))
 
 
-def put(core, block, first, keep_ref, send_ref):
+def put(core, block, first, keep_ref, send_refs):
     for half in range(block.shape[1] // LANES):
         tile = block[:, half * LANES : (half + 1) * LANES].reshape(16, 2, 8, LANES)
-        at = slice((first + half) * 8, (first + half + 1) * 8)
-        keep_ref[:, at, :] = jnp.where(core == 0, tile[:, 0], tile[:, 1])
-        send_ref[:, at, :] = jnp.where(core == 0, tile[:, 1], tile[:, 0])
+        which, at = divmod((first + half) * 8, send_refs[0].shape[1])
+        keep_ref[:, (first + half) * 8 : (first + half + 1) * 8, :] = jnp.where(core == 0, tile[:, 0], tile[:, 1])
+        send_refs[which][:, at : at + 8, :] = jnp.where(core == 0, tile[:, 1], tile[:, 0])
 
 
 def load(small, desc_hbm, desc_ref, sems):
@@ -64,10 +64,11 @@
         right = desc_ref[:, j * TILE : (j + 1) * TILE]
         for kind in range(2):
             block = jnp.dot(members[kind], right, preferred_element_type=jnp.float32)
-            put(core, block, kind * 6 + j * 2, keep_ref, send_ref)
-
-
-def gram_kernel(core_ref, desc_hbm, species_hbm, keep_ref, send_ref, desc_ref, species_ref, turned, sems):
+            put(core, block, kind * 6 + j * 2, keep_ref, [send_ref])
+
+
+def gram_kernel(core_ref, desc_hbm, species_hbm, keep_ref, *refs):
+    send_refs, (desc_ref, species_ref, turned, sems) = refs[:-4], refs[-4:]
     core = core_ref[0]
     blocks = load(((species_hbm, species_ref),), desc_hbm, desc_ref, sems)
     masks = [(species_ref[...] == kind).astype(jnp.bfloat16) for kind in range(2)]
@@ -79,24 +80,22 @@
             for kind in range(2):
                 left = turned[i * TILE : (i + 1) * TILE, :] * masks[kind]
                 block = jnp.dot(left, right, preferred_element_type=jnp.float32)
-                put(core, block, kind * 12 + PAIRS.index((i, j)) * 2, keep_ref, send_ref)
-
-
-def final_kernel(
-    norm, pos_ref, sums_ref, other_sums, gram_ref, other_gram, root_ref, normal_ref, cfg_ref, full, left, gram
-):
+                put(core, block, kind * 12 + PAIRS.index((i, j)) * 2, keep_ref, send_refs)
+
+
+def final_kernel(norm, pos_ref, mine_ref, other_ref, root_ref, normal_ref, cfg_ref, full, left, gram):
     core, kind, part, owner = pos_ref[0], pos_ref[1], pos_ref[2], pos_ref[3]
     width = gram.shape[1]
     band = left.shape[1]
 
-    def joined(tile, lo=0, hi=16, refs=(gram_ref, other_gram)):
+    def joined(tile, lo=0, hi=16):
         at = slice(tile * 8, (tile + 1) * 8)
-        a, b = [ref[lo:hi, at, :] for ref in refs]
+        a, b = mine_ref[lo:hi, at, :], other_ref[lo:hi, at, :]
         pair = [jnp.where(core == which, a, b)[:, None] for which in range(2)]
         return jnp.concatenate(pair, 1).reshape((hi - lo) * 16, LANES)
 
     for j in range(2 * width // LANES):
-        full[:, j * LANES : (j + 1) * LANES] = joined(j, refs=(sums_ref, other_sums))
+        full[:, j * LANES : (j + 1) * LANES] = joined(6 + j)
 
     def fill(row, col, piece):
         gram[row : row + piece.shape[0], col : col + piece.shape[1]] = piece
@@ -152,7 +151,7 @@
         normal_ref[:, cols] = cross * (1.0 / full.shape[0]) + extra
 
 
-def call(kernel, outs, args, scratch, space, limit):
+def call(kernel, outs, args, scratch, space, limit, flops):
     smem = pl.BlockSpec(memory_space=pltpu.SMEM)
     held = [pltpu.with_memory_space_constraint(a, space) for a in args[1:]]
     return pl.pallas_call(
@@ -162,6 +161,7 @@
         out_specs=[pl.BlockSpec(memory_space=pltpu.VMEM)] * len(outs),
         scratch_shapes=list(scratch),
         compiler_params=pltpu.CompilerParams(vmem_limit_bytes=limit),
+        cost_estimate=pl.CostEstimate(flops=flops, bytes_accessed=8 << 20, transcendentals=0),
     )(args[0], *held)
 
 
@@ -212,18 +212,21 @@
         [matrix, int_row, int_row, pltpu.VMEM((1, configs), jnp.int32), sems],
         pltpu.HBM,
         24 << 20,
+        4 * configs * atoms * width,
     )
     pair_s, desc, pos, root = lax.optimization_barrier((keep_s + lax.ppermute(send_s, "c", flip), desc, pos, root))
-    keep_g, send_g = call(
+    keep_g, *send_g = call(
         gram_kernel,
-        [tiles(24)] * 2,
+        [tiles(24)] + [tiles(6)] * 4,
         [core[None], desc, species[None]],
         [matrix, int_row, pltpu.VMEM((width, atoms), jnp.bfloat16), sems],
         pltpu.HBM,
         24 << 20,
-    )
-    pair_g = keep_g + lax.ppermute(send_g, "c", flip)
+        4 * width * width * atoms,
+    )
+    pair_g = keep_g + jnp.concatenate([lax.ppermute(part_g, "c", flip) for part_g in send_g], 1)
     plane_s = jnp.sum(exchange(pair_s, ("x", "y")), 0)
+    plane_s, pair_g = lax.optimization_barrier((plane_s, pair_g))
     plane_g = jnp.sum(exchange(pair_g, ("x", "y")), 0).reshape(2, 96, LANES)
 
     place = kind * 4 + l
@@ -238,20 +241,19 @@
     root_here = sum(jnp.where(source == part, value[96:], 0.0) for value, source in got)
     scale = 1.0 / math.sqrt(atoms * n_dev / configs)
     sums = sum(value[:96] for value, _ in got).reshape(12, 8, LANES) * (root_here * scale)
-    mine_s = exchange(jnp.broadcast_to(sums.reshape(1, 96, LANES), (16, 96, LANES)), ("x", "y"))
-
-    grams = lax.dynamic_index_in_dim(plane_g, kind, 0, False)
-    for k in far:
-        theirs = lax.dynamic_index_in_dim(plane_g, (place + k) % 8 // 4, 0, False)
-        grams = grams + along_z(theirs, k)
+    sums, plane_g = lax.optimization_barrier((sums, plane_g))
+    planes = jnp.broadcast_to(plane_g[None], (4, 2, 96, LANES)).reshape(8, 96, LANES)
+    grams = jnp.sum(exchange(planes, ("l", "h")), 0)
     bands = needed(grams, x * 4 + part)
-    mine_g = exchange(jnp.broadcast_to(bands[None], (4, 4, 48, LANES)).reshape(16, 48, LANES), ("x", "y"))
+    spread = jnp.concatenate([bands, jnp.broadcast_to(sums.reshape(1, 96, LANES), (4, 96, LANES))], 1)
+    spread = jnp.broadcast_to(spread[None], (4, 4, 144, LANES)).reshape(16, 144, LANES)
+    mine = exchange(spread, ("x", "y"))
     band = 2 * width // 8
     norm = atoms * n_dev // 8
     normal, rows = call(
         lambda *refs: final_kernel(norm, *refs),
         [jax.ShapeDtypeStruct((band, 2 * width), f32), jax.ShapeDtypeStruct((cfg_here, band), f32)],
-        [pos, mine_s, lax.ppermute(mine_s, "c", flip), mine_g, lax.ppermute(mine_g, "c", flip), root],
+        [pos, mine, lax.ppermute(mine, "c", flip), root],
         [
             pltpu.VMEM((configs, 2 * width), f32),
             pltpu.VMEM((configs, band), f32),
@@ -259,6 +261,7 @@
         ],
         pltpu.VMEM,
         24 << 20,
+        8 * band * width * configs,
     )
     return normal, rows
 

time: 111 us -> 104 us (0.937)
  the two profiles are of different devices: /device:TPU:1 before, /device:TPU:33 now
where the time goes in v6:
time: 104 us
  starting transfers between devices  38.4 us (37%)
  blocking collectives  25.2 us (24%)
  waiting for transfers between devices  24.2 us (23%)
  Pallas kernels  11.6 us (11%)
  other arithmetic  2.68 us (3%)
    all_to_all x1, blocking collectives, exchange(): return lax.all_to_all(flat, axes, 0, 0, tiled=True).reshape(values.shape)  25.2 us
    all_to_all x3, starting transfers between devices, exchange(): return lax.all_to_all(flat, axes, 0, 0, tiled=True).reshape(values.shape)  19.3 us
    ppermute x7, starting transfers between devices, along_z(): return lax.ppermute(value, ('l', 'h'), pairs)  14.4 us
    all_to_all x3, waiting for transfers between devices, exchange(): return lax.all_to_all(flat, axes, 0, 0, tiled=True).reshape(values.shape)  12.2 us
    pallas_call x3, Pallas kernels, call(): pl.pallas_call(kernel, out_shape=outs, in_specs=[smem] + [pl.BlockSpec(me...  11.6 us
    ppermute x7, waiting for transfers between devices, along_z(): return lax.ppermute(value, ('l', 'h'), pairs)  5.23 us
    ppermute x1, starting transfers between devices, shards(): lax.ppermute(mine, 'c', flip)  2.57 us
    ppermute x1, waiting for transfers between devices, shards(): lax.ppermute(mine, 'c', flip)  2.47 us
  transfers between devices with their start and end apart: 16, of which 11 were waited for; matrix products, arithmetic and copies ran while one was open for 1% of the time, Pallas kernels for 5%

profile of v6, /device:TPU:33, one launch (start us, length us, event | category | flops | bytes accessed | tf_op | source)
XLA Modules:
  0.0 103.8 jit_solution(5738820807843156309)
XLA Ops:
  0.6 0.0 copy-start
  0.6 3.5 %shard_map.68 = (f32[16,96,128]{2,1,0:T(8,128)S(1)}, f32[16,96,128]{2,1,0:T(8,128)S(1)}) custom-call(s32[1]{0:T(128)} %bitcast.core_ref, bf16[2048,768]{1,0:T(8,128)(2,1)} %desc_hbm.2, s32[1,2048]{1,0:T(1,128)} %bitcast.27, s32[1,2048]{1,0:T(1,128)} %bitcast.26, s32[1,256]{1,0:T(1,128)} %bitcast.29), custom_call_target="tpu_custom_call" | custom-call | flops 1610612736 | bytes 8388608 | tf_op jit(solution)/shard_map/pallas_call | solution.py:157
  4.1 0.8 collective-permute-start
  4.9 0.0 copy-done
  4.9 0.1 pad_add_fusion.refs_0_
  5.0 1.8 %collective-permute-done = f32[16,96,128]{2,1,0:T(8,128)S(1)} collective-permute-done((f32[16,96,128]{2,1,0:T(8,128)S(1)}, f32[16,96,128]{2,1,0:T(8,128)S(1)}, u32[]{:S(2)}, u32[]{:S(2)}) %collective-permute-start) | collective-permute-done | bytes 786464 | tf_op jit(solution)/shard_map/ppermute | solution.py:217
  6.8 1.0 add.89
  7.8 0.1 broadcast_in_dim.55.refs_3_
  7.8 6.8 %all-to-all-start = ((f32[16,96,128]{2,1,0:T(8,128)}), f32[16,96,128]{2,1,0:T(8,128)S(1)}, u32[]{:S(2)}, u32[]{:S(2)}) async-start(f32[16,96,128]{2,1,0:T(8,128)} %add.89), calls=%async_computation | async-start | bytes 1572864 | tf_op jit(solution)/shard_map/all_to_all | solution.py:170
  14.6 5.1 %shard_map.69 = (f32[16,192,128]{2,1,0:T(8,128)S(1)}, f32[16,48,128]{2,1,0:T(8,128)S(1)}, f32[16,48,128]{2,1,0:T(8,128)S(1)}, f32[16,48,128]{2,1,0:T(8,128)S(1)}, f32[16,48,128]{2,1,0:T(8,128)S(1)}) custom-call(s32[1]{0:T(128)} %bitcast.core_ref, bf16[2048,768]{1,0:T(8,128)(2,1)} %desc_hbm.2, s32[1,2048]{1,0:T(1,128)} %bitcast.28), custom_call_target="tpu_custom_call" | custom-call | flops 4831838208 | bytes 8388608 | tf_op jit(solution)/shard_map/pallas_call | solution.py:157
  19.7 0.8 collective-permute-start.4
  20.4 0.1 collective-permute-start.3
  20.5 0.4 collective-permute-start.2
  20.9 0.1 collective-permute-start.1
  21.0 0.7 collective-permute-done.4
  21.8 0.6 collective-permute-done.3
  22.4 0.6 collective-permute-done.2
  22.9 0.6 collective-permute-done.1
  23.5 1.4 %maximum_add_fusion = f32[16,192,128]{2,1,0:T(8,128)} fusion(f32[16,192,128]{2,1,0:T(8,128)S(1)} %get-tuple-element.22, f32[16,48,128]{2,1,0:T(8,128)S(1)} %collective-permute-done.4, f32[16,48,128]{2,1,0:T(8,128)S(1)} %collective-permute-done.3, f32[16,48,128]{2,1,0:T(8,128)S(1)} %collective-permute-done.2, f32[16,48,128]{2,1,0:T(8,128)S(1)} %collective-permute-done.1), kind=kLoop, calls=%fused_computation | loop fusion | flops 1572864 | bytes 4718592 | tf_op jit(solution)/shard_map/add | solution.py:227
  24.9 2.5 %all-to-all-done = f32[16,96,128]{2,1,0:T(8,128)S(1)} async-done(((f32[16,96,128]{2,1,0:T(8,128)}), f32[16,96,128]{2,1,0:T(8,128)S(1)}, u32[]{:S(2)}, u32[]{:S(2)}) %all-to-all-start) | async-done | bytes 786464 | tf_op jit(solution)/shard_map/all_to_all | solution.py:170
  27.4 4.5 %all-to-all-start.1 = ((f32[16,192,128]{2,1,0:T(8,128)}), f32[16,192,128]{2,1,0:T(8,128)S(1)}, u32[]{:S(2)}, u32[]{:S(2)}) async-start(f32[16,192,128]{2,1,0:T(8,128)} %maximum_add_fusion), calls=%async_computation.1 | async-start | bytes 3145728 | tf_op jit(solution)/shard_map/all_to_all | solution.py:170
  31.9 0.1 collective-permute-start.11
  32.0 1.7 %collective-permute-start.10 = (f32[104,128]{1,0:T(8,128)S(1)}, f32[104,128]{1,0:T(8,128)S(1)}, u32[]{:S(2)}, u32[]{:S(2)}) collective-permute-start(f32[104,128]{1,0:T(8,128)S(1)} %constant_dynamic-update-slice_fusion), channel_id=1, source_target_pairs={{0,16},{16,32},{32,48},{48,4},{4,20},{20,36},{36,52},{52,0},{1,17}... | collective-permute-start | bytes 159752 | tf_op jit(solution)/shard_map/ppermute | solution.py:236
  33.7 6.1 %collective-permute-start.9 = (f32[104,128]{1,0:T(8,128)S(1)}, f32[104,128]{1,0:T(8,128)S(1)}, u32[]{:S(2)}, u32[]{:S(2)}) collective-permute-start(f32[104,128]{1,0:T(8,128)S(1)} %constant_dynamic-update-slice_fusion), channel_id=1, source_target_pairs={{0,36},{16,52},{32,0},{48,16},{4,32},{20,48},{36,4},{52,20},{1,37}... | collective-permute-start | bytes 159752 | tf_op jit(solution)/shard_map/ppermute | solution.py:236
  39.8 0.0 collective-permute-start.8
  39.8 2.8 %collective-permute-start.7 = (f32[104,128]{1,0:T(8,128)S(1)}, f32[104,128]{1,0:T(8,128)S(1)}, u32[]{:S(2)}, u32[]{:S(2)}) collective-permute-start(f32[104,128]{1,0:T(8,128)S(1)} %constant_dynamic-update-slice_fusion), channel_id=1, source_target_pairs={{0,20},{16,36},{32,52},{48,0},{4,16},{20,32},{36,48},{52,4},{1,21}... | collective-permute-start | bytes 159752 | tf_op jit(solution)/shard_map/ppermute | solution.py:236
  42.6 0.0 collective-permute-done.11
  42.6 1.7 %collective-permute-start.6 = (f32[104,128]{1,0:T(8,128)S(1)}, f32[104,128]{1,0:T(8,128)S(1)}, u32[]{:S(2)}, u32[]{:S(2)}) collective-permute-start(f32[104,128]{1,0:T(8,128)S(1)} %constant_dynamic-update-slice_fusion), channel_id=1, source_target_pairs={{0,48},{16,4},{32,20},{48,36},{4,52},{20,0},{36,16},{52,32},{1,49}... | collective-permute-start | bytes 159752 | tf_op jit(solution)/shard_map/ppermute | solution.py:236
  44.2 0.0 collective-permute-done.10
  44.2 2.1 %collective-permute-start.5 = (f32[104,128]{1,0:T(8,128)S(1)}, f32[104,128]{1,0:T(8,128)S(1)}, u32[]{:S(2)}, u32[]{:S(2)}) collective-permute-start(f32[104,128]{1,0:T(8,128)S(1)} %constant_dynamic-update-slice_fusion), channel_id=1, source_target_pairs={{0,4},{16,20},{32,36},{48,52},{4,0},{20,16},{36,32},{52,48},{1,5},... | collective-permute-start | bytes 159752 | tf_op jit(solution)/shard_map/ppermute | solution.py:236
  46.3 0.0 collective-permute-done.9
  46.3 0.0 collective-permute-done.8
  46.3 0.0 collective-permute-done.7
  46.3 3.5 %collective-permute-done.6 = f32[104,128]{1,0:T(8,128)S(1)} collective-permute-done((f32[104,128]{1,0:T(8,128)S(1)}, f32[104,128]{1,0:T(8,128)S(1)}, u32[]{:S(2)}, u32[]{:S(2)}) %collective-permute-start.6) | collective-permute-done | bytes 53280 | tf_op jit(solution)/shard_map/ppermute | solution.py:236
  49.8 1.8 %collective-permute-done.5 = f32[104,128]{1,0:T(8,128)S(1)} collective-permute-done((f32[104,128]{1,0:T(8,128)S(1)}, f32[104,128]{1,0:T(8,128)S(1)}, u32[]{:S(2)}, u32[]{:S(2)}) %collective-permute-start.5) | collective-permute-done | bytes 53280 | tf_op jit(solution)/shard_map/ppermute | solution.py:236
  51.6 0.6 all-to-all-done.1
  52.2 0.1 reduce_sum.28
  52.3 0.8 broadcast_in_dim.57
  53.1 8.0 %all-to-all-start.2 = ((f32[8,96,128]{2,1,0:T(8,128)}), f32[8,96,128]{2,1,0:T(8,128)S(1)}, u32[]{:S(2)}, u32[]{:S(2)}) async-start(f32[8,96,128]{2,1,0:T(8,128)} %bitcast.9), calls=%async_computation.2 | async-start | bytes 786432 | tf_op jit(solution)/shard_map/all_to_all | solution.py:170
  61.1 9.2 %all-to-all-done.2 = f32[8,96,128]{2,1,0:T(8,128)S(1)} async-done(((f32[8,96,128]{2,1,0:T(8,128)}), f32[8,96,128]{2,1,0:T(8,128)S(1)}, u32[]{:S(2)}, u32[]{:S(2)}) %all-to-all-start.2) | async-done | bytes 393248 | tf_op jit(solution)/shard_map/all_to_all | solution.py:170
  70.4 0.1 broadcast_in_dim.60
  70.5 25.2 %all_to_all.30.refs_1_ = f32[16,144,128]{2,1,0:T(8,128)S(1)} all-to-all(f32[16,144,128]{2,1,0:T(8,128)S(1)} %bitcast.23), channel_id=1, replica_groups=mesh['x'=4,'l'=4,'c'=2,'h'=2,'y'=4] {'x','y'}, dimensions={0} | all-to-all | bytes 2359296 | tf_op jit(solution)/shard_map/all_to_all | solution.py:170
  95.7 2.6 %collective-permute-start.12 = (f32[16,144,128]{2,1,0:T(8,128)S(1)}, f32[16,144,128]{2,1,0:T(8,128)S(1)}, u32[]{:S(2)}, u32[]{:S(2)}) collective-permute-start(f32[16,144,128]{2,1,0:T(8,128)S(1)} %all_to_all.30.refs_1_), channel_id=1, source_target_pairs={{0,8},{8,0},{1,9},{9,1},{2,10},{10,2},{3,11},{11,3},{4,12},{12,4},... | collective-permute-start | bytes 3538952 | tf_op jit(solution)/shard_map/ppermute | solution.py:256
  98.3 2.5 %collective-permute-done.12.refs_2_ = f32[16,144,128]{2,1,0:T(8,128)S(1)} collective-permute-done((f32[16,144,128]{2,1,0:T(8,128)S(1)}, f32[16,144,128]{2,1,0:T(8,128)S(1)}, u32[]{:S(2)}, u32[]{:S(2)}) %collective-permute-start.12) | collective-permute-done | bytes 1179680 | tf_op jit(solution)/shard_map/ppermute | solution.py:256
  100.7 3.0 %shard_map.70 = (f32[192,1536]{1,0:T(8,128)}, f32[8,192]{1,0:T(8,128)}) custom-call(s32[4]{0:T(128)S(1)} %pad_add_fusion.refs_0_, f32[16,144,128]{2,1,0:T(8,128)S(1)} %all_to_all.30.refs_1_, f32[16,144,128]{2,1,0:T(8,128)S(1)} %collective-permute-done.12.refs_2_, f32[8,128]{1,0:T(8,128)S(1)} %broadcast_in_dim.55.refs_3_), custom_call_target="tpu_custom_call" | custom-call | flops 301989888 | bytes 8388608 | tf_op jit(solution)/shard_map/pallas_call | solution.py:157
  (16 shorter events, 0.2 us)
Async XLA Ops:
  0.6 4.2 %copy-start = (f32[8]{0:T(128)S(1)}, f32[8]{0:T(128)}, u32[]{:S(2)}) copy-start(f32[8]{0:T(128)} %param.9) | copy-start | bytes 100
  4.1 2.7 %collective-permute-start = (f32[16,96,128]{2,1,0:T(8,128)S(1)}, f32[16,96,128]{2,1,0:T(8,128)S(1)}, u32[]{:S(2)}, u32[]{:S(2)}) collective-permute-start(f32[16,96,128]{2,1,0:T(8,128)S(1)} %get-tuple-element.18), channel_id=1, source_target_pairs={{0,8},{8,0},{1,9},{9,1},{2,10},{10,2},{3,11},{11,3},{4,12},{12,4},... | collective-permute-start | bytes 2359304 | tf_op jit(solution)/shard_map/ppermute | solution.py:217
  7.8 19.5 %all-to-all-start = ((f32[16,96,128]{2,1,0:T(8,128)}), f32[16,96,128]{2,1,0:T(8,128)S(1)}, u32[]{:S(2)}, u32[]{:S(2)}) async-start(f32[16,96,128]{2,1,0:T(8,128)} %add.89), calls=%async_computation | async-start | bytes 1572864 | tf_op jit(solution)/shard_map/all_to_all | solution.py:170
  19.7 2.1 %collective-permute-start.4 = (f32[16,48,128]{2,1,0:T(8,128)S(1)}, f32[16,48,128]{2,1,0:T(8,128)S(1)}, u32[]{:S(2)}, u32[]{:S(2)}) collective-permute-start(f32[16,48,128]{2,1,0:T(8,128)S(1)} %get-tuple-element.26), channel_id=1, source_target_pairs={{0,8},{8,0},{1,9},{9,1},{2,10},{10,2},{3,11},{11,3},{4,12},{12,4},... | collective-permute-start | bytes 1179656 | tf_op jit(solution)/shard_map/ppermute | solution.py:227
  20.4 1.9 %collective-permute-start.3 = (f32[16,48,128]{2,1,0:T(8,128)S(1)}, f32[16,48,128]{2,1,0:T(8,128)S(1)}, u32[]{:S(2)}, u32[]{:S(2)}) collective-permute-start(f32[16,48,128]{2,1,0:T(8,128)S(1)} %get-tuple-element.25), channel_id=1, source_target_pairs={{0,8},{8,0},{1,9},{9,1},{2,10},{10,2},{3,11},{11,3},{4,12},{12,4},... | collective-permute-start | bytes 1179656 | tf_op jit(solution)/shard_map/ppermute | solution.py:227
  20.5 2.4 %collective-permute-start.2 = (f32[16,48,128]{2,1,0:T(8,128)S(1)}, f32[16,48,128]{2,1,0:T(8,128)S(1)}, u32[]{:S(2)}, u32[]{:S(2)}) collective-permute-start(f32[16,48,128]{2,1,0:T(8,128)S(1)} %get-tuple-element.24), channel_id=1, source_target_pairs={{0,8},{8,0},{1,9},{9,1},{2,10},{10,2},{3,11},{11,3},{4,12},{12,4},... | collective-permute-start | bytes 1179656 | tf_op jit(solution)/shard_map/ppermute | solution.py:227
  20.9 2.5 %collective-permute-start.1 = (f32[16,48,128]{2,1,0:T(8,128)S(1)}, f32[16,48,128]{2,1,0:T(8,128)S(1)}, u32[]{:S(2)}, u32[]{:S(2)}) collective-permute-start(f32[16,48,128]{2,1,0:T(8,128)S(1)} %get-tuple-element.23), channel_id=1, source_target_pairs={{0,8},{8,0},{1,9},{9,1},{2,10},{10,2},{3,11},{11,3},{4,12},{12,4},... | collective-permute-start | bytes 1179656 | tf_op jit(solution)/shard_map/ppermute | solution.py:227
  27.4 24.9 %all-to-all-start.1 = ((f32[16,192,128]{2,1,0:T(8,128)}), f32[16,192,128]{2,1,0:T(8,128)S(1)}, u32[]{:S(2)}, u32[]{:S(2)}) async-start(f32[16,192,128]{2,1,0:T(8,128)} %maximum_add_fusion), calls=%async_computation.1 | async-start | bytes 3145728 | tf_op jit(solution)/shard_map/all_to_all | solution.py:170
  31.9 10.7 %collective-permute-start.11 = (f32[104,128]{1,0:T(8,128)S(1)}, f32[104,128]{1,0:T(8,128)S(1)}, u32[]{:S(2)}, u32[]{:S(2)}) collective-permute-start(f32[104,128]{1,0:T(8,128)S(1)} %constant_dynamic-update-slice_fusion), channel_id=1, source_target_pairs={{0,52},{16,0},{32,16},{48,32},{4,48},{20,4},{36,20},{52,36},{1,53}... | collective-permute-start | bytes 159752 | tf_op jit(solution)/shard_map/ppermute | solution.py:236
  32.0 12.3 %collective-permute-start.10 = (f32[104,128]{1,0:T(8,128)S(1)}, f32[104,128]{1,0:T(8,128)S(1)}, u32[]{:S(2)}, u32[]{:S(2)}) collective-permute-start(f32[104,128]{1,0:T(8,128)S(1)} %constant_dynamic-update-slice_fusion), channel_id=1, source_target_pairs={{0,16},{16,32},{32,48},{48,4},{4,20},{20,36},{36,52},{52,0},{1,17}... | collective-permute-start | bytes 159752 | tf_op jit(solution)/shard_map/ppermute | solution.py:236
  33.7 12.6 %collective-permute-start.9 = (f32[104,128]{1,0:T(8,128)S(1)}, f32[104,128]{1,0:T(8,128)S(1)}, u32[]{:S(2)}, u32[]{:S(2)}) collective-permute-start(f32[104,128]{1,0:T(8,128)S(1)} %constant_dynamic-update-slice_fusion), channel_id=1, source_target_pairs={{0,36},{16,52},{32,0},{48,16},{4,32},{20,48},{36,4},{52,20},{1,37}... | collective-permute-start | bytes 159752 | tf_op jit(solution)/shard_map/ppermute | solution.py:236
  39.8 6.6 %collective-permute-start.8 = (f32[104,128]{1,0:T(8,128)S(1)}, f32[104,128]{1,0:T(8,128)S(1)}, u32[]{:S(2)}, u32[]{:S(2)}) collective-permute-start(f32[104,128]{1,0:T(8,128)S(1)} %constant_dynamic-update-slice_fusion), channel_id=1, source_target_pairs={{0,32},{16,48},{32,4},{48,20},{4,36},{20,52},{36,0},{52,16},{1,33}... | collective-permute-start | bytes 159752 | tf_op jit(solution)/shard_map/ppermute | solution.py:236
  39.8 6.6 %collective-permute-start.7 = (f32[104,128]{1,0:T(8,128)S(1)}, f32[104,128]{1,0:T(8,128)S(1)}, u32[]{:S(2)}, u32[]{:S(2)}) collective-permute-start(f32[104,128]{1,0:T(8,128)S(1)} %constant_dynamic-update-slice_fusion), channel_id=1, source_target_pairs={{0,20},{16,36},{32,52},{48,0},{4,16},{20,32},{36,48},{52,4},{1,21}... | collective-permute-start | bytes 159752 | tf_op jit(solution)/shard_map/ppermute | solution.py:236
  42.6 7.2 %collective-permute-start.6 = (f32[104,128]{1,0:T(8,128)S(1)}, f32[104,128]{1,0:T(8,128)S(1)}, u32[]{:S(2)}, u32[]{:S(2)}) collective-permute-start(f32[104,128]{1,0:T(8,128)S(1)} %constant_dynamic-update-slice_fusion), channel_id=1, source_target_pairs={{0,48},{16,4},{32,20},{48,36},{4,52},{20,0},{36,16},{52,32},{1,49}... | collective-permute-start | bytes 159752 | tf_op jit(solution)/shard_map/ppermute | solution.py:236
  44.2 7.3 %collective-permute-start.5 = (f32[104,128]{1,0:T(8,128)S(1)}, f32[104,128]{1,0:T(8,128)S(1)}, u32[]{:S(2)}, u32[]{:S(2)}) collective-permute-start(f32[104,128]{1,0:T(8,128)S(1)} %constant_dynamic-update-slice_fusion), channel_id=1, source_target_pairs={{0,4},{16,20},{32,36},{48,52},{4,0},{20,16},{36,32},{52,48},{1,5},... | collective-permute-start | bytes 159752 | tf_op jit(solution)/shard_map/ppermute | solution.py:236
  53.1 17.2 %all-to-all-start.2 = ((f32[8,96,128]{2,1,0:T(8,128)}), f32[8,96,128]{2,1,0:T(8,128)S(1)}, u32[]{:S(2)}, u32[]{:S(2)}) async-start(f32[8,96,128]{2,1,0:T(8,128)} %bitcast.9), calls=%async_computation.2 | async-start | bytes 786432 | tf_op jit(solution)/shard_map/all_to_all | solution.py:170
  95.7 5.0 %collective-permute-start.12 = (f32[16,144,128]{2,1,0:T(8,128)S(1)}, f32[16,144,128]{2,1,0:T(8,128)S(1)}, u32[]{:S(2)}, u32[]{:S(2)}) collective-permute-start(f32[16,144,128]{2,1,0:T(8,128)S(1)} %all_to_all.30.refs_1_), channel_id=1, source_target_pairs={{0,8},{8,0},{1,9},{9,1},{2,10},{10,2},{3,11},{11,3},{4,12},{12,4},... | collective-permute-start | bytes 3538952 | tf_op jit(solution)/shard_map/ppermute | solution.py:256

commit v7 on v6

--- a/solution.py
+++ b/solution.py
@@ -229,15 +229,11 @@
     plane_s, pair_g = lax.optimization_barrier((plane_s, pair_g))
     plane_g = jnp.sum(exchange(pair_g, ("x", "y")), 0).reshape(2, 96, LANES)
 
-    place = kind * 4 + l
-
-    def along_z(value, k):
-        pairs = [((z % 4) * 2 + z // 4, ((z + k) % 8 % 4) * 2 + (z + k) % 8 // 4) for z in range(8)]
-        return lax.ppermute(value, ("l", "h"), pairs)
-
-    far = (4, 3, 5, 2, 6, 1, 7)
+    plane_s = plane_s + lax.ppermute(plane_s, "h", flip)
     rooted = jnp.concatenate([plane_s, root])
-    got = [(rooted, place)] + [(along_z(rooted, k), (place - k) % 8) for k in far]
+    got = [(rooted, l)]
+    for k in (2, 1, 3):
+        got.append((lax.ppermute(rooted, "l", [(i, (i + k) % 4) for i in range(4)]), (l - k) % 4))
     root_here = sum(jnp.where(source == part, value[96:], 0.0) for value, source in got)
     scale = 1.0 / math.sqrt(atoms * n_dev / configs)
     sums = sum(value[:96] for value, _ in got).reshape(12, 8, LANES) * (root_here * scale)

time: 104 us -> 104 us (level)
  starting transfers between devices: 38.4 us -> 35.7 us
  waiting for transfers between devices: 24.2 us -> 26.8 us
    all_to_all x3, waiting for transfers between devices: 12.2 us -> 15.9 us  [exchange(): return lax.all_to_all(flat, axes, 0, 0, tiled=True).reshape(values.shape)]
    ppermute x7 -> x4, starting transfers between devices: 14.4 us -> 11.8 us  [the longest x1 6.11 us: shards(): plane_s = plane_s + lax.ppermute(plane_s, 'h', flip)]
    ppermute x7 -> x4, waiting for transfers between devices: 5.23 us -> 4.26 us  [the longest x3 2.78 us: shards(): lax.ppermute(rooted, 'l', [(i, (i + k) % 4) for i in range(4)])]
  transfers between devices with their start and end apart: 16 -> 13, of which waited for: 11 -> 12; matrix products, arithmetic and copies ran while one was open for 1% -> 1% of each run, Pallas kernels for 5% -> 5%
where the time goes in v7:
time: 104 us
  starting transfers between devices  35.7 us (34%)
  waiting for transfers between devices  26.8 us (26%)
  blocking collectives  25.3 us (24%)
  Pallas kernels  11.6 us (11%)
  other arithmetic  2.67 us (3%)
    all_to_all x1, blocking collectives, exchange(): return lax.all_to_all(flat, axes, 0, 0, tiled=True).reshape(values.shape)  25.3 us
    all_to_all x3, starting transfers between devices, exchange(): return lax.all_to_all(flat, axes, 0, 0, tiled=True).reshape(values.shape)  19.2 us
    all_to_all x3, waiting for transfers between devices, exchange(): return lax.all_to_all(flat, axes, 0, 0, tiled=True).reshape(values.shape)  15.9 us
    pallas_call x3, Pallas kernels, call(): pl.pallas_call(kernel, out_shape=outs, in_specs=[smem] + [pl.BlockSpec(me...  11.6 us
    ppermute x1, starting transfers between devices, shards(): plane_s = plane_s + lax.ppermute(plane_s, 'h', flip)  6.11 us
    ppermute x3, starting transfers between devices, shards(): lax.ppermute(rooted, 'l', [(i, (i + k) % 4) for i in range(4)])  5.72 us
    ppermute x3, waiting for transfers between devices, shards(): lax.ppermute(rooted, 'l', [(i, (i + k) % 4) for i in range(4)])  2.78 us
    ppermute x1, starting transfers between devices, shards(): lax.ppermute(mine, 'c', flip)  2.5 us
  transfers between devices with their start and end apart: 13, of which 12 were waited for; matrix products, arithmetic and copies ran while one was open for 1% of the time, Pallas kernels for 5%

profile of v7, /device:TPU:33, one launch (start us, length us, event | category | flops | bytes accessed | tf_op | source)
XLA Modules:
  0.0 103.8 jit_solution(4800623795696994278)
XLA Ops:
  0.6 0.0 copy-start
  0.6 3.5 %shard_map.68 = (f32[16,96,128]{2,1,0:T(8,128)S(1)}, f32[16,96,128]{2,1,0:T(8,128)S(1)}) custom-call(s32[1]{0:T(128)} %bitcast.core_ref, bf16[2048,768]{1,0:T(8,128)(2,1)} %desc_hbm.2, s32[1,2048]{1,0:T(1,128)} %bitcast.27, s32[1,2048]{1,0:T(1,128)} %bitcast.26, s32[1,256]{1,0:T(1,128)} %bitcast.29), custom_call_target="tpu_custom_call" | custom-call | flops 1610612736 | bytes 8388608 | tf_op jit(solution)/shard_map/pallas_call | solution.py:157
  4.1 0.8 collective-permute-start
  4.9 0.0 copy-done
  4.9 0.1 pad_add_fusion.refs_0_
  5.0 1.8 %collective-permute-done = f32[16,96,128]{2,1,0:T(8,128)S(1)} collective-permute-done((f32[16,96,128]{2,1,0:T(8,128)S(1)}, f32[16,96,128]{2,1,0:T(8,128)S(1)}, u32[]{:S(2)}, u32[]{:S(2)}) %collective-permute-start) | collective-permute-done | bytes 786464 | tf_op jit(solution)/shard_map/ppermute | solution.py:217
  6.8 1.0 add.49
  7.8 0.1 broadcast_in_dim.51.refs_3_
  7.8 6.8 %all-to-all-start = ((f32[16,96,128]{2,1,0:T(8,128)}), f32[16,96,128]{2,1,0:T(8,128)S(1)}, u32[]{:S(2)}, u32[]{:S(2)}) async-start(f32[16,96,128]{2,1,0:T(8,128)} %add.49), calls=%async_computation | async-start | bytes 1572864 | tf_op jit(solution)/shard_map/all_to_all | solution.py:170
  14.6 5.1 %shard_map.69 = (f32[16,192,128]{2,1,0:T(8,128)S(1)}, f32[16,48,128]{2,1,0:T(8,128)S(1)}, f32[16,48,128]{2,1,0:T(8,128)S(1)}, f32[16,48,128]{2,1,0:T(8,128)S(1)}, f32[16,48,128]{2,1,0:T(8,128)S(1)}) custom-call(s32[1]{0:T(128)} %bitcast.core_ref, bf16[2048,768]{1,0:T(8,128)(2,1)} %desc_hbm.2, s32[1,2048]{1,0:T(1,128)} %bitcast.28), custom_call_target="tpu_custom_call" | custom-call | flops 4831838208 | bytes 8388608 | tf_op jit(solution)/shard_map/pallas_call | solution.py:157
  19.7 0.7 collective-permute-start.4
  20.4 0.1 collective-permute-start.3
  20.5 0.4 collective-permute-start.2
  20.9 0.1 collective-permute-start.1
  21.0 0.7 collective-permute-done.4
  21.8 0.6 collective-permute-done.3
  22.3 0.6 collective-permute-done.2
  22.9 0.6 collective-permute-done.1
  23.5 1.4 %maximum_add_fusion = f32[16,192,128]{2,1,0:T(8,128)} fusion(f32[16,192,128]{2,1,0:T(8,128)S(1)} %get-tuple-element.22, f32[16,48,128]{2,1,0:T(8,128)S(1)} %collective-permute-done.4, f32[16,48,128]{2,1,0:T(8,128)S(1)} %collective-permute-done.3, f32[16,48,128]{2,1,0:T(8,128)S(1)} %collective-permute-done.2, f32[16,48,128]{2,1,0:T(8,128)S(1)} %collective-permute-done.1), kind=kLoop, calls=%fused_computation | loop fusion | flops 1572864 | bytes 4718592 | tf_op jit(solution)/shard_map/add | solution.py:227
  24.9 2.5 %all-to-all-done = f32[16,96,128]{2,1,0:T(8,128)S(1)} async-done(((f32[16,96,128]{2,1,0:T(8,128)}), f32[16,96,128]{2,1,0:T(8,128)S(1)}, u32[]{:S(2)}, u32[]{:S(2)}) %all-to-all-start) | async-done | bytes 786464 | tf_op jit(solution)/shard_map/all_to_all | solution.py:170
  27.4 4.5 %all-to-all-start.1 = ((f32[16,192,128]{2,1,0:T(8,128)}), f32[16,192,128]{2,1,0:T(8,128)S(1)}, u32[]{:S(2)}, u32[]{:S(2)}) async-start(f32[16,192,128]{2,1,0:T(8,128)} %maximum_add_fusion), calls=%async_computation.1 | async-start | bytes 3145728 | tf_op jit(solution)/shard_map/all_to_all | solution.py:170
  31.9 6.1 %collective-permute-start.5 = (f32[96,128]{1,0:T(8,128)S(1)}, f32[96,128]{1,0:T(8,128)S(1)}, u32[]{:S(2)}, u32[]{:S(2)}) collective-permute-start(f32[96,128]{1,0:T(8,128)S(1)} %reduce_sum.27), channel_id=1, source_target_pairs={{0,4},{4,0},{1,5},{5,1},{2,6},{6,2},{3,7},{7,3},{8,12},{12,8},{9,1... | collective-permute-start | bytes 147464 | tf_op jit(solution)/shard_map/ppermute | solution.py:232
  38.0 1.5 %collective-permute-done.5 = f32[96,128]{1,0:T(8,128)S(1)} collective-permute-done((f32[96,128]{1,0:T(8,128)S(1)}, f32[96,128]{1,0:T(8,128)S(1)}, u32[]{:S(2)}, u32[]{:S(2)}) %collective-permute-start.5) | collective-permute-done | bytes 49184 | tf_op jit(solution)/shard_map/ppermute | solution.py:232
  39.5 0.8 collective-permute-start.8
  40.3 0.7 collective-permute-start.7
  41.0 4.2 %collective-permute-start.6 = (f32[104,128]{1,0:T(8,128)S(1)}, f32[104,128]{1,0:T(8,128)S(1)}, u32[]{:S(2)}, u32[]{:S(2)}) collective-permute-start(f32[104,128]{1,0:T(8,128)S(1)} %pad_maximum_fusion.1), channel_id=1, source_target_pairs={{0,32},{16,48},{32,0},{48,16},{1,33},{17,49},{33,1},{49,17},{2,34}... | collective-permute-start | bytes 159752 | tf_op jit(solution)/shard_map/ppermute | solution.py:236
  45.2 0.0 collective-permute-done.8
  45.2 0.3 collective-permute-done.7
  45.5 2.5 %collective-permute-done.6 = f32[104,128]{1,0:T(8,128)S(1)} collective-permute-done((f32[104,128]{1,0:T(8,128)S(1)}, f32[104,128]{1,0:T(8,128)S(1)}, u32[]{:S(2)}, u32[]{:S(2)}) %collective-permute-start.6) | collective-permute-done | bytes 53280 | tf_op jit(solution)/shard_map/ppermute | solution.py:236
  48.0 4.2 %all-to-all-done.1 = f32[16,192,128]{2,1,0:T(8,128)S(1)} async-done(((f32[16,192,128]{2,1,0:T(8,128)}), f32[16,192,128]{2,1,0:T(8,128)S(1)}, u32[]{:S(2)}, u32[]{:S(2)}) %all-to-all-start.1) | async-done | bytes 1572896 | tf_op jit(solution)/shard_map/all_to_all | solution.py:170
  52.2 0.1 reduce_sum.28
  52.3 0.8 broadcast_in_dim.53
  53.1 8.0 %all-to-all-start.2 = ((f32[8,96,128]{2,1,0:T(8,128)}), f32[8,96,128]{2,1,0:T(8,128)S(1)}, u32[]{:S(2)}, u32[]{:S(2)}) async-start(f32[8,96,128]{2,1,0:T(8,128)} %bitcast.9), calls=%async_computation.2 | async-start | bytes 786432 | tf_op jit(solution)/shard_map/all_to_all | solution.py:170
  61.1 9.2 %all-to-all-done.2 = f32[8,96,128]{2,1,0:T(8,128)S(1)} async-done(((f32[8,96,128]{2,1,0:T(8,128)}), f32[8,96,128]{2,1,0:T(8,128)S(1)}, u32[]{:S(2)}, u32[]{:S(2)}) %all-to-all-start.2) | async-done | bytes 393248 | tf_op jit(solution)/shard_map/all_to_all | solution.py:170
  70.4 0.1 broadcast_in_dim.56
  70.5 25.3 %all_to_all.30.refs_1_ = f32[16,144,128]{2,1,0:T(8,128)S(1)} all-to-all(f32[16,144,128]{2,1,0:T(8,128)S(1)} %bitcast.23), channel_id=1, replica_groups=mesh['x'=4,'l'=4,'c'=2,'h'=2,'y'=4] {'x','y'}, dimensions={0} | all-to-all | bytes 2359296 | tf_op jit(solution)/shard_map/all_to_all | solution.py:170
  95.8 2.5 %collective-permute-start.9 = (f32[16,144,128]{2,1,0:T(8,128)S(1)}, f32[16,144,128]{2,1,0:T(8,128)S(1)}, u32[]{:S(2)}, u32[]{:S(2)}) collective-permute-start(f32[16,144,128]{2,1,0:T(8,128)S(1)} %all_to_all.30.refs_1_), channel_id=1, source_target_pairs={{0,8},{8,0},{1,9},{9,1},{2,10},{10,2},{3,11},{11,3},{4,12},{12,4},... | collective-permute-start | bytes 3538952 | tf_op jit(solution)/shard_map/ppermute | solution.py:252
  98.3 2.5 %collective-permute-done.9.refs_2_ = f32[16,144,128]{2,1,0:T(8,128)S(1)} collective-permute-done((f32[16,144,128]{2,1,0:T(8,128)S(1)}, f32[16,144,128]{2,1,0:T(8,128)S(1)}, u32[]{:S(2)}, u32[]{:S(2)}) %collective-permute-start.9) | collective-permute-done | bytes 1179680 | tf_op jit(solution)/shard_map/ppermute | solution.py:252
  100.8 3.0 %shard_map.70 = (f32[192,1536]{1,0:T(8,128)}, f32[8,192]{1,0:T(8,128)}) custom-call(s32[4]{0:T(128)S(1)} %pad_add_fusion.refs_0_, f32[16,144,128]{2,1,0:T(8,128)S(1)} %all_to_all.30.refs_1_, f32[16,144,128]{2,1,0:T(8,128)S(1)} %collective-permute-done.9.refs_2_, f32[8,128]{1,0:T(8,128)S(1)} %broadcast_in_dim.51.refs_3_), custom_call_target="tpu_custom_call" | custom-call | flops 301989888 | bytes 8388608 | tf_op jit(solution)/shard_map/pallas_call | solution.py:157
  (16 shorter events, 0.2 us)
Async XLA Ops:
  0.6 4.2 %copy-start = (f32[8]{0:T(128)S(1)}, f32[8]{0:T(128)}, u32[]{:S(2)}) copy-start(f32[8]{0:T(128)} %param.9) | copy-start | bytes 100
  4.1 2.7 %collective-permute-start = (f32[16,96,128]{2,1,0:T(8,128)S(1)}, f32[16,96,128]{2,1,0:T(8,128)S(1)}, u32[]{:S(2)}, u32[]{:S(2)}) collective-permute-start(f32[16,96,128]{2,1,0:T(8,128)S(1)} %get-tuple-element.18), channel_id=1, source_target_pairs={{0,8},{8,0},{1,9},{9,1},{2,10},{10,2},{3,11},{11,3},{4,12},{12,4},... | collective-permute-start | bytes 2359304 | tf_op jit(solution)/shard_map/ppermute | solution.py:217
  7.8 19.5 %all-to-all-start = ((f32[16,96,128]{2,1,0:T(8,128)}), f32[16,96,128]{2,1,0:T(8,128)S(1)}, u32[]{:S(2)}, u32[]{:S(2)}) async-start(f32[16,96,128]{2,1,0:T(8,128)} %add.49), calls=%async_computation | async-start | bytes 1572864 | tf_op jit(solution)/shard_map/all_to_all | solution.py:170
  19.7 2.1 %collective-permute-start.4 = (f32[16,48,128]{2,1,0:T(8,128)S(1)}, f32[16,48,128]{2,1,0:T(8,128)S(1)}, u32[]{:S(2)}, u32[]{:S(2)}) collective-permute-start(f32[16,48,128]{2,1,0:T(8,128)S(1)} %get-tuple-element.26), channel_id=1, source_target_pairs={{0,8},{8,0},{1,9},{9,1},{2,10},{10,2},{3,11},{11,3},{4,12},{12,4},... | collective-permute-start | bytes 1179656 | tf_op jit(solution)/shard_map/ppermute | solution.py:227
  20.4 1.9 %collective-permute-start.3 = (f32[16,48,128]{2,1,0:T(8,128)S(1)}, f32[16,48,128]{2,1,0:T(8,128)S(1)}, u32[]{:S(2)}, u32[]{:S(2)}) collective-permute-start(f32[16,48,128]{2,1,0:T(8,128)S(1)} %get-tuple-element.25), channel_id=1, source_target_pairs={{0,8},{8,0},{1,9},{9,1},{2,10},{10,2},{3,11},{11,3},{4,12},{12,4},... | collective-permute-start | bytes 1179656 | tf_op jit(solution)/shard_map/ppermute | solution.py:227
  20.5 2.4 %collective-permute-start.2 = (f32[16,48,128]{2,1,0:T(8,128)S(1)}, f32[16,48,128]{2,1,0:T(8,128)S(1)}, u32[]{:S(2)}, u32[]{:S(2)}) collective-permute-start(f32[16,48,128]{2,1,0:T(8,128)S(1)} %get-tuple-element.24), channel_id=1, source_target_pairs={{0,8},{8,0},{1,9},{9,1},{2,10},{10,2},{3,11},{11,3},{4,12},{12,4},... | collective-permute-start | bytes 1179656 | tf_op jit(solution)/shard_map/ppermute | solution.py:227
  20.9 2.5 %collective-permute-start.1 = (f32[16,48,128]{2,1,0:T(8,128)S(1)}, f32[16,48,128]{2,1,0:T(8,128)S(1)}, u32[]{:S(2)}, u32[]{:S(2)}) collective-permute-start(f32[16,48,128]{2,1,0:T(8,128)S(1)} %get-tuple-element.23), channel_id=1, source_target_pairs={{0,8},{8,0},{1,9},{9,1},{2,10},{10,2},{3,11},{11,3},{4,12},{12,4},... | collective-permute-start | bytes 1179656 | tf_op jit(solution)/shard_map/ppermute | solution.py:227
  27.4 24.8 %all-to-all-start.1 = ((f32[16,192,128]{2,1,0:T(8,128)}), f32[16,192,128]{2,1,0:T(8,128)S(1)}, u32[]{:S(2)}, u32[]{:S(2)}) async-start(f32[16,192,128]{2,1,0:T(8,128)} %maximum_add_fusion), calls=%async_computation.1 | async-start | bytes 3145728 | tf_op jit(solution)/shard_map/all_to_all | solution.py:170
  31.9 7.6 %collective-permute-start.5 = (f32[96,128]{1,0:T(8,128)S(1)}, f32[96,128]{1,0:T(8,128)S(1)}, u32[]{:S(2)}, u32[]{:S(2)}) collective-permute-start(f32[96,128]{1,0:T(8,128)S(1)} %reduce_sum.27), channel_id=1, source_target_pairs={{0,4},{4,0},{1,5},{5,1},{2,6},{6,2},{3,7},{7,3},{8,12},{12,8},{9,1... | collective-permute-start | bytes 147464 | tf_op jit(solution)/shard_map/ppermute | solution.py:232
  39.5 5.7 %collective-permute-start.8 = (f32[104,128]{1,0:T(8,128)S(1)}, f32[104,128]{1,0:T(8,128)S(1)}, u32[]{:S(2)}, u32[]{:S(2)}) collective-permute-start(f32[104,128]{1,0:T(8,128)S(1)} %pad_maximum_fusion.1), channel_id=1, source_target_pairs={{0,48},{16,0},{32,16},{48,32},{1,49},{17,1},{33,17},{49,33},{2,50}... | collective-permute-start | bytes 159752 | tf_op jit(solution)/shard_map/ppermute | solution.py:236
  40.3 5.2 %collective-permute-start.7 = (f32[104,128]{1,0:T(8,128)S(1)}, f32[104,128]{1,0:T(8,128)S(1)}, u32[]{:S(2)}, u32[]{:S(2)}) collective-permute-start(f32[104,128]{1,0:T(8,128)S(1)} %pad_maximum_fusion.1), channel_id=1, source_target_pairs={{0,16},{16,32},{32,48},{48,0},{1,17},{17,33},{33,49},{49,1},{2,18}... | collective-permute-start | bytes 159752 | tf_op jit(solution)/shard_map/ppermute | solution.py:236
  41.0 7.0 %collective-permute-start.6 = (f32[104,128]{1,0:T(8,128)S(1)}, f32[104,128]{1,0:T(8,128)S(1)}, u32[]{:S(2)}, u32[]{:S(2)}) collective-permute-start(f32[104,128]{1,0:T(8,128)S(1)} %pad_maximum_fusion.1), channel_id=1, source_target_pairs={{0,32},{16,48},{32,0},{48,16},{1,33},{17,49},{33,1},{49,17},{2,34}... | collective-permute-start | bytes 159752 | tf_op jit(solution)/shard_map/ppermute | solution.py:236
  53.1 17.2 %all-to-all-start.2 = ((f32[8,96,128]{2,1,0:T(8,128)}), f32[8,96,128]{2,1,0:T(8,128)S(1)}, u32[]{:S(2)}, u32[]{:S(2)}) async-start(f32[8,96,128]{2,1,0:T(8,128)} %bitcast.9), calls=%async_computation.2 | async-start | bytes 786432 | tf_op jit(solution)/shard_map/all_to_all | solution.py:170
  95.8 5.0 %collective-permute-start.9 = (f32[16,144,128]{2,1,0:T(8,128)S(1)}, f32[16,144,128]{2,1,0:T(8,128)S(1)}, u32[]{:S(2)}, u32[]{:S(2)}) collective-permute-start(f32[16,144,128]{2,1,0:T(8,128)S(1)} %all_to_all.30.refs_1_), channel_id=1, source_target_pairs={{0,8},{8,0},{1,9},{9,1},{2,10},{10,2},{3,11},{11,3},{4,12},{12,4},... | collective-permute-start | bytes 3538952 | tf_op jit(solution)/shard_map/ppermute | solution.py:252

commit v8 on v7

--- a/solution.py
+++ b/solution.py
@@ -11,15 +11,15 @@
 SIZES = (4, 4, 2, 2, 4)
 TILE = 256
 LANES = 128
-PAIRS = ((0, 1), (0, 2), (1, 2), (0, 0), (1, 1), (2, 2))
-
-
-def put(core, block, first, keep_ref, send_refs):
-    for half in range(block.shape[1] // LANES):
-        tile = block[:, half * LANES : (half + 1) * LANES].reshape(16, 2, 8, LANES)
-        which, at = divmod((first + half) * 8, send_refs[0].shape[1])
-        keep_ref[:, (first + half) * 8 : (first + half + 1) * 8, :] = jnp.where(core == 0, tile[:, 0], tile[:, 1])
-        send_refs[which][:, at : at + 8, :] = jnp.where(core == 0, tile[:, 1], tile[:, 0])
+PAIRS = ((0, 1), (0, 2), (1, 2))
+
+
+def put(core, tile, index, keep_ref, send_refs, owner=0):
+    tile = tile.reshape(-1, 2, 8, LANES)
+    owners = slice(owner, owner + tile.shape[0])
+    which, at = divmod(index * 8, send_refs[0].shape[1])
+    keep_ref[owners, index * 8 : index * 8 + 8, :] = jnp.where(core == 0, tile[:, 0], tile[:, 1])
+    send_refs[which][owners, at : at + 8, :] = jnp.where(core == 0, tile[:, 1], tile[:, 0])
 
 
 def load(small, desc_hbm, desc_ref, sems):
@@ -64,7 +64,9 @@
         right = desc_ref[:, j * TILE : (j + 1) * TILE]
         for kind in range(2):
             block = jnp.dot(members[kind], right, preferred_element_type=jnp.float32)
-            put(core, block, kind * 6 + j * 2, keep_ref, [send_ref])
+            for half in range(2):
+                tile = block[:, half * LANES : (half + 1) * LANES]
+                put(core, tile, kind * 6 + j * 2 + half, keep_ref, [send_ref])
 
 
 def gram_kernel(core_ref, desc_hbm, species_hbm, keep_ref, *refs):
@@ -80,7 +82,13 @@
             for kind in range(2):
                 left = turned[i * TILE : (i + 1) * TILE, :] * masks[kind]
                 block = jnp.dot(left, right, preferred_element_type=jnp.float32)
-                put(core, block, kind * 12 + PAIRS.index((i, j)) * 2, keep_ref, send_refs)
+                if i == j:
+                    put(core, block[:LANES, :LANES], 18 + i, keep_ref, send_refs, 8 * kind)
+                    put(core, block[:, LANES:], kind * 9 + 6 + i, keep_ref, send_refs)
+                else:
+                    first = kind * 9 + PAIRS.index((i, j)) * 2
+                    put(core, block[:, :LANES], first, keep_ref, send_refs)
+                    put(core, block[:, LANES:], first + 1, keep_ref, send_refs)
 
 
 def final_kernel(norm, pos_ref, mine_ref, other_ref, root_ref, normal_ref, cfg_ref, full, left, gram):
@@ -104,27 +112,38 @@
         for k, tile in enumerate(tiles):
             fill(row, col + k * LANES, joined(tile, lo, hi))
 
+    def corner():
+        return jnp.where(kind == 0, joined(5, 0, 8), joined(5, 8, 16))
+
     def band_0():
-        straight((4, 5, 0, 1, 2, 3), 0, 12, 0, 0)
+        fill(0, 0, corner())
+        fill(128, 0, joined(4, 0, 8).T[:64])
+        straight((4, 0, 1, 2, 3), 0, 12, 0, LANES)
 
     def band_1():
-        straight((2, 3, 0, 1, 4, 5), 12, 16, 0, 0)
+        fill(0, 0, joined(4, 0, 8).T[64:])
+        straight((4, 0, 1, 2, 3), 12, 16, 0, LANES)
         fill(64, 0, joined(0).T)
-        straight((1, 2, 3, 4), 0, 8, 64, TILE)
+        fill(64, TILE, corner())
+        straight((1, 2, 3), 0, 8, 64, TILE + LANES)
 
     def band_2():
         fill(0, 0, joined(0).T)
-        straight((4, 5, 2, 3), 8, 16, 0, TILE)
+        fill(0, TILE, joined(3, 0, 8).T)
+        straight((3, 2, 4), 8, 16, 0, TILE + LANES)
         fill(128, 0, joined(1).T[:64])
         fill(128, TILE, joined(2).T[:64])
-        straight((3, 4), 0, 4, 128, 2 * TILE)
+        fill(128, 2 * TILE, corner()[:64])
+        straight((4,), 0, 4, 128, 2 * TILE + LANES)
 
     def band_3():
         fill(0, 0, joined(0).T[64:])
         fill(64, 0, joined(1).T)
         fill(0, TILE, joined(2).T[64:])
         fill(64, TILE, joined(3).T)
-        straight((4, 5), 4, 16, 0, 2 * TILE)
+        fill(0, 2 * TILE, corner()[64:])
+        fill(64, 2 * TILE, joined(4, 0, 8).T)
+        straight((4,), 4, 16, 0, 2 * TILE + LANES)
 
     for k, body in enumerate((band_0, band_1, band_2, band_3)):
 
@@ -174,14 +193,14 @@
     def pick(*tiles):
         return jnp.concatenate([grams[8 * k : 8 * k + 8] for k in tiles])
 
-    band_1 = jnp.where(owner >= 12, pick(1, 6, 7, 2, 3), pick(8, 9, 4, 5, 5))
-    band_2 = jnp.where(owner >= 8, pick(5, 8, 9), pick(10, 11, 11))
+    band_1 = jnp.where(owner >= 12, pick(1, 2, 3), pick(7, 4, 5))
+    band_2 = jnp.where(owner >= 8, pick(5), pick(8))
     return jnp.stack(
         [
-            pick(0, 1, 2, 3, 6, 7),
-            jnp.concatenate([pick(0), band_1]),
-            jnp.concatenate([pick(1, 2, 4), band_2]),
-            pick(2, 3, 4, 5, 10, 11),
+            pick(0, 1, 2, 3, 6, 9),
+            jnp.concatenate([pick(0), band_1, pick(6, 10)]),
+            jnp.concatenate([pick(1, 2, 4, 7), band_2, pick(11)]),
+            pick(2, 3, 4, 5, 8, 11),
         ]
     )
 
@@ -217,7 +236,7 @@
     pair_s, desc, pos, root = lax.optimization_barrier((keep_s + lax.ppermute(send_s, "c", flip), desc, pos, root))
     keep_g, *send_g = call(
         gram_kernel,
-        [tiles(24)] + [tiles(6)] * 4,
+        [tiles(21)] + [tiles(6)] * 3 + [tiles(3)],
         [core[None], desc, species[None]],
         [matrix, int_row, pltpu.VMEM((width, atoms), jnp.bfloat16), sems],
         pltpu.HBM,
@@ -227,7 +246,7 @@
     pair_g = keep_g + jnp.concatenate([lax.ppermute(part_g, "c", flip) for part_g in send_g], 1)
     plane_s = jnp.sum(exchange(pair_s, ("x", "y")), 0)
     plane_s, pair_g = lax.optimization_barrier((plane_s, pair_g))
-    plane_g = jnp.sum(exchange(pair_g, ("x", "y")), 0).reshape(2, 96, LANES)
+    plane_g = jnp.sum(exchange(pair_g, ("x", "y")), 0)
 
     plane_s = plane_s + lax.ppermute(plane_s, "h", flip)
     rooted = jnp.concatenate([plane_s, root])
@@ -238,7 +257,9 @@
     scale = 1.0 / math.sqrt(atoms * n_dev / configs)
     sums = sum(value[:96] for value, _ in got).reshape(12, 8, LANES) * (root_here * scale)
     sums, plane_g = lax.optimization_barrier((sums, plane_g))
-    planes = jnp.broadcast_to(plane_g[None], (4, 2, 96, LANES)).reshape(8, 96, LANES)
+    corner = jnp.broadcast_to(plane_g[None, 144:], (2, 24, LANES))
+    planes = jnp.concatenate([plane_g[:144].reshape(2, 72, LANES), corner], 1)
+    planes = jnp.broadcast_to(planes[None], (4, 2, 96, LANES)).reshape(8, 96, LANES)
     grams = jnp.sum(exchange(planes, ("l", "h")), 0)
     bands = needed(grams, x * 4 + part)
     spread = jnp.concatenate([bands, jnp.broadcast_to(sums.reshape(1, 96, LANES), (4, 96, LANES))], 1)

time: 104 us -> 102 us (0.981)
  waiting for transfers between devices: 26.8 us -> 24.9 us
    all_to_all x3, waiting for transfers between devices: 15.9 us -> 14.5 us  [exchange(): return lax.all_to_all(flat, axes, 0, 0, tiled=True).reshape(values.shape)]
  transfers between devices with their start and end apart: 13 -> 13, of which waited for: 12 -> 9; matrix products, arithmetic and copies ran while one was open for 1% -> 1% of each run, Pallas kernels for 5% -> 5%
where the time goes in v8:
time: 102 us
  starting transfers between devices  35.1 us (34%)
  blocking collectives  25.8 us (25%)
  waiting for transfers between devices  24.9 us (24%)
  Pallas kernels  11.6 us (11%)
  other arithmetic  2.54 us (2%)
    all_to_all x1, blocking collectives, exchange(): return lax.all_to_all(flat, axes, 0, 0, tiled=True).reshape(values.shape)  25.8 us
    all_to_all x3, starting transfers between devices, exchange(): return lax.all_to_all(flat, axes, 0, 0, tiled=True).reshape(values.shape)  19 us
    all_to_all x3, waiting for transfers between devices, exchange(): return lax.all_to_all(flat, axes, 0, 0, tiled=True).reshape(values.shape)  14.5 us
    pallas_call x3, Pallas kernels, call(): pl.pallas_call(kernel, out_shape=outs, in_specs=[smem] + [pl.BlockSpec(me...  11.6 us
    ppermute x1, starting transfers between devices, shards(): plane_s = plane_s + lax.ppermute(plane_s, 'h', flip)  6.1 us
    ppermute x3, starting transfers between devices, shards(): lax.ppermute(rooted, 'l', [(i, (i + k) % 4) for i in range(4)])  5.7 us
    ppermute x3, waiting for transfers between devices, shards(): lax.ppermute(rooted, 'l', [(i, (i + k) % 4) for i in range(4)])  2.52 us
    ppermute x1, waiting for transfers between devices, shards(): lax.ppermute(mine, 'c', flip)  2.47 us
  transfers between devices with their start and end apart: 13, of which 9 were waited for; matrix products, arithmetic and copies ran while one was open for 1% of the time, Pallas kernels for 5%

profile of v8, /device:TPU:33, one launch (start us, length us, event | category | flops | bytes accessed | tf_op | source)
XLA Modules:
  0.0 101.8 jit_solution(12682879464450908889)
XLA Ops:
  0.6 0.0 copy-start
  0.6 3.5 %shard_map.68 = (f32[16,96,128]{2,1,0:T(8,128)S(1)}, f32[16,96,128]{2,1,0:T(8,128)S(1)}) custom-call(s32[1]{0:T(128)} %bitcast.core_ref, bf16[2048,768]{1,0:T(8,128)(2,1)} %desc_hbm.2, s32[1,2048]{1,0:T(1,128)} %bitcast.27, s32[1,2048]{1,0:T(1,128)} %bitcast.26, s32[1,256]{1,0:T(1,128)} %bitcast.29), custom_call_target="tpu_custom_call" | custom-call | flops 1610612736 | bytes 8388608 | tf_op jit(solution)/shard_map/pallas_call | solution.py:176
  4.1 0.8 collective-permute-start
  4.9 0.0 copy-done
  4.9 0.1 pad_add_fusion.refs_0_
  5.0 1.8 %collective-permute-done = f32[16,96,128]{2,1,0:T(8,128)S(1)} collective-permute-done((f32[16,96,128]{2,1,0:T(8,128)S(1)}, f32[16,96,128]{2,1,0:T(8,128)S(1)}, u32[]{:S(2)}, u32[]{:S(2)}) %collective-permute-start) | collective-permute-done | bytes 786464 | tf_op jit(solution)/shard_map/ppermute | solution.py:236
  6.8 1.0 add.49
  7.8 0.1 broadcast_in_dim.57.refs_3_
  7.8 6.8 %all-to-all-start = ((f32[16,96,128]{2,1,0:T(8,128)}), f32[16,96,128]{2,1,0:T(8,128)S(1)}, u32[]{:S(2)}, u32[]{:S(2)}) async-start(f32[16,96,128]{2,1,0:T(8,128)} %add.49), calls=%async_computation | async-start | bytes 1572864 | tf_op jit(solution)/shard_map/all_to_all | solution.py:189
  14.6 5.1 %shard_map.69 = (f32[16,168,128]{2,1,0:T(8,128)S(1)}, f32[16,48,128]{2,1,0:T(8,128)S(1)}, f32[16,48,128]{2,1,0:T(8,128)S(1)}, f32[16,48,128]{2,1,0:T(8,128)S(1)}, f32[16,24,128]{2,1,0:T(8,128)S(1)}) custom-call(s32[1]{0:T(128)} %bitcast.core_ref, bf16[2048,768]{1,0:T(8,128)(2,1)} %desc_hbm.2, s32[1,2048]{1,0:T(1,128)} %bitcast.28), custom_call_target="tpu_custom_call" | custom-call | flops 4831838208 | bytes 8388608 | tf_op jit(solution)/shard_map/pallas_call | solution.py:176
  19.7 0.7 collective-permute-start.3
  20.4 0.1 collective-permute-start.2
  20.5 0.4 collective-permute-start.1
  21.0 0.1 collective-permute-start.4
  21.1 2.1 %collective-permute-done.4 = f32[16,24,128]{2,1,0:T(8,128)S(1)} collective-permute-done((f32[16,24,128]{2,1,0:T(8,128)S(1)}, f32[16,24,128]{2,1,0:T(8,128)S(1)}, u32[]{:S(2)}, u32[]{:S(2)}) %collective-permute-start.4) | collective-permute-done | bytes 196640 | tf_op jit(solution)/shard_map/ppermute | solution.py:246
  23.2 0.0 collective-permute-done.3
  23.2 0.0 collective-permute-done.2
  23.2 0.0 collective-permute-done.1
  23.2 1.2 %maximum_add_fusion = f32[16,168,128]{2,1,0:T(8,128)} fusion(f32[16,168,128]{2,1,0:T(8,128)S(1)} %get-tuple-element.22, f32[16,24,128]{2,1,0:T(8,128)S(1)} %collective-permute-done.4, f32[16,48,128]{2,1,0:T(8,128)S(1)} %collective-permute-done.3, f32[16,48,128]{2,1,0:T(8,128)S(1)} %collective-permute-done.2, f32[16,48,128]{2,1,0:T(8,128)S(1)} %collective-permute-done.1), kind=kLoop, calls=%fused_computation | loop fusion | flops 1376256 | bytes 4128768 | tf_op jit(solution)/shard_map/add | solution.py:246
  24.5 2.9 %all-to-all-done = f32[16,96,128]{2,1,0:T(8,128)S(1)} async-done(((f32[16,96,128]{2,1,0:T(8,128)}), f32[16,96,128]{2,1,0:T(8,128)S(1)}, u32[]{:S(2)}, u32[]{:S(2)}) %all-to-all-start) | async-done | bytes 786464 | tf_op jit(solution)/shard_map/all_to_all | solution.py:189
  27.4 4.3 %all-to-all-start.1 = ((f32[16,168,128]{2,1,0:T(8,128)}), f32[16,168,128]{2,1,0:T(8,128)S(1)}, u32[]{:S(2)}, u32[]{:S(2)}) async-start(f32[16,168,128]{2,1,0:T(8,128)} %maximum_add_fusion), calls=%async_computation.1 | async-start | bytes 2752512 | tf_op jit(solution)/shard_map/all_to_all | solution.py:189
  31.7 6.1 %collective-permute-start.5 = (f32[96,128]{1,0:T(8,128)S(1)}, f32[96,128]{1,0:T(8,128)S(1)}, u32[]{:S(2)}, u32[]{:S(2)}) collective-permute-start(f32[96,128]{1,0:T(8,128)S(1)} %reduce_sum.27), channel_id=1, source_target_pairs={{0,4},{4,0},{1,5},{5,1},{2,6},{6,2},{3,7},{7,3},{8,12},{12,8},{9,1... | collective-permute-start | bytes 147464 | tf_op jit(solution)/shard_map/ppermute | solution.py:251
  37.8 1.5 %collective-permute-done.5 = f32[96,128]{1,0:T(8,128)S(1)} collective-permute-done((f32[96,128]{1,0:T(8,128)S(1)}, f32[96,128]{1,0:T(8,128)S(1)}, u32[]{:S(2)}, u32[]{:S(2)}) %collective-permute-start.5) | collective-permute-done | bytes 49184 | tf_op jit(solution)/shard_map/ppermute | solution.py:251
  39.3 0.8 collective-permute-start.8
  40.1 0.7 collective-permute-start.7
  40.8 4.2 %collective-permute-start.6 = (f32[104,128]{1,0:T(8,128)S(1)}, f32[104,128]{1,0:T(8,128)S(1)}, u32[]{:S(2)}, u32[]{:S(2)}) collective-permute-start(f32[104,128]{1,0:T(8,128)S(1)} %pad_maximum_fusion.2), channel_id=1, source_target_pairs={{0,32},{16,48},{32,0},{48,16},{1,33},{17,49},{33,1},{49,17},{2,34}... | collective-permute-start | bytes 159752 | tf_op jit(solution)/shard_map/ppermute | solution.py:255
  45.0 0.0 collective-permute-done.8
  45.0 0.3 collective-permute-done.7
  45.3 2.2 %collective-permute-done.6 = f32[104,128]{1,0:T(8,128)S(1)} collective-permute-done((f32[104,128]{1,0:T(8,128)S(1)}, f32[104,128]{1,0:T(8,128)S(1)}, u32[]{:S(2)}, u32[]{:S(2)}) %collective-permute-start.6) | collective-permute-done | bytes 53280 | tf_op jit(solution)/shard_map/ppermute | solution.py:255
  47.5 2.4 %all-to-all-done.1 = f32[16,168,128]{2,1,0:T(8,128)S(1)} async-done(((f32[16,168,128]{2,1,0:T(8,128)}), f32[16,168,128]{2,1,0:T(8,128)S(1)}, u32[]{:S(2)}, u32[]{:S(2)}) %all-to-all-start.1) | async-done | bytes 1376288 | tf_op jit(solution)/shard_map/all_to_all | solution.py:189
  49.9 0.1 reduce_sum.28
  50.1 0.8 broadcast_in_dim.60
  50.8 8.0 %all-to-all-start.2 = ((f32[8,96,128]{2,1,0:T(8,128)}), f32[8,96,128]{2,1,0:T(8,128)S(1)}, u32[]{:S(2)}, u32[]{:S(2)}) async-start(f32[8,96,128]{2,1,0:T(8,128)} %bitcast.9), calls=%async_computation.2 | async-start | bytes 786432 | tf_op jit(solution)/shard_map/all_to_all | solution.py:189
  58.8 9.2 %all-to-all-done.2 = f32[8,96,128]{2,1,0:T(8,128)S(1)} async-done(((f32[8,96,128]{2,1,0:T(8,128)}), f32[8,96,128]{2,1,0:T(8,128)S(1)}, u32[]{:S(2)}, u32[]{:S(2)}) %all-to-all-start.2) | async-done | bytes 393248 | tf_op jit(solution)/shard_map/all_to_all | solution.py:189
  68.2 0.1 broadcast_in_dim.63
  68.3 25.8 %all_to_all.30.refs_1_ = f32[16,144,128]{2,1,0:T(8,128)S(1)} all-to-all(f32[16,144,128]{2,1,0:T(8,128)S(1)} %bitcast.22), channel_id=1, replica_groups=mesh['x'=4,'l'=4,'c'=2,'h'=2,'y'=4] {'x','y'}, dimensions={0} | all-to-all | bytes 2359296 | tf_op jit(solution)/shard_map/all_to_all | solution.py:189
  94.1 2.2 %collective-permute-start.9 = (f32[16,144,128]{2,1,0:T(8,128)S(1)}, f32[16,144,128]{2,1,0:T(8,128)S(1)}, u32[]{:S(2)}, u32[]{:S(2)}) collective-permute-start(f32[16,144,128]{2,1,0:T(8,128)S(1)} %all_to_all.30.refs_1_), channel_id=1, source_target_pairs={{0,8},{8,0},{1,9},{9,1},{2,10},{10,2},{3,11},{11,3},{4,12},{12,4},... | collective-permute-start | bytes 3538952 | tf_op jit(solution)/shard_map/ppermute | solution.py:273
  96.2 2.5 %collective-permute-done.9.refs_2_ = f32[16,144,128]{2,1,0:T(8,128)S(1)} collective-permute-done((f32[16,144,128]{2,1,0:T(8,128)S(1)}, f32[16,144,128]{2,1,0:T(8,128)S(1)}, u32[]{:S(2)}, u32[]{:S(2)}) %collective-permute-start.9) | collective-permute-done | bytes 1179680 | tf_op jit(solution)/shard_map/ppermute | solution.py:273
  98.7 3.1 %shard_map.70 = (f32[192,1536]{1,0:T(8,128)}, f32[8,192]{1,0:T(8,128)}) custom-call(s32[4]{0:T(128)S(1)} %pad_add_fusion.refs_0_, f32[16,144,128]{2,1,0:T(8,128)S(1)} %all_to_all.30.refs_1_, f32[16,144,128]{2,1,0:T(8,128)S(1)} %collective-permute-done.9.refs_2_, f32[8,128]{1,0:T(8,128)S(1)} %broadcast_in_dim.57.refs_3_), custom_call_target="tpu_custom_call" | custom-call | flops 301989888 | bytes 8388608 | tf_op jit(solution)/shard_map/pallas_call | solution.py:176
  (21 shorter events, 0.2 us)
Async XLA Ops:
  0.6 4.2 %copy-start = (f32[8]{0:T(128)S(1)}, f32[8]{0:T(128)}, u32[]{:S(2)}) copy-start(f32[8]{0:T(128)} %param.9) | copy-start | bytes 100
  4.1 2.7 %collective-permute-start = (f32[16,96,128]{2,1,0:T(8,128)S(1)}, f32[16,96,128]{2,1,0:T(8,128)S(1)}, u32[]{:S(2)}, u32[]{:S(2)}) collective-permute-start(f32[16,96,128]{2,1,0:T(8,128)S(1)} %get-tuple-element.18), channel_id=1, source_target_pairs={{0,8},{8,0},{1,9},{9,1},{2,10},{10,2},{3,11},{11,3},{4,12},{12,4},... | collective-permute-start | bytes 2359304 | tf_op jit(solution)/shard_map/ppermute | solution.py:236
  7.8 19.5 %all-to-all-start = ((f32[16,96,128]{2,1,0:T(8,128)}), f32[16,96,128]{2,1,0:T(8,128)S(1)}, u32[]{:S(2)}, u32[]{:S(2)}) async-start(f32[16,96,128]{2,1,0:T(8,128)} %add.49), calls=%async_computation | async-start | bytes 1572864 | tf_op jit(solution)/shard_map/all_to_all | solution.py:189
  19.7 3.5 %collective-permute-start.3 = (f32[16,48,128]{2,1,0:T(8,128)S(1)}, f32[16,48,128]{2,1,0:T(8,128)S(1)}, u32[]{:S(2)}, u32[]{:S(2)}) collective-permute-start(f32[16,48,128]{2,1,0:T(8,128)S(1)} %get-tuple-element.25), channel_id=1, source_target_pairs={{0,8},{8,0},{1,9},{9,1},{2,10},{10,2},{3,11},{11,3},{4,12},{12,4},... | collective-permute-start | bytes 1179656 | tf_op jit(solution)/shard_map/ppermute | solution.py:246
  20.4 2.8 %collective-permute-start.2 = (f32[16,48,128]{2,1,0:T(8,128)S(1)}, f32[16,48,128]{2,1,0:T(8,128)S(1)}, u32[]{:S(2)}, u32[]{:S(2)}) collective-permute-start(f32[16,48,128]{2,1,0:T(8,128)S(1)} %get-tuple-element.24), channel_id=1, source_target_pairs={{0,8},{8,0},{1,9},{9,1},{2,10},{10,2},{3,11},{11,3},{4,12},{12,4},... | collective-permute-start | bytes 1179656 | tf_op jit(solution)/shard_map/ppermute | solution.py:246
  20.5 2.7 %collective-permute-start.1 = (f32[16,48,128]{2,1,0:T(8,128)S(1)}, f32[16,48,128]{2,1,0:T(8,128)S(1)}, u32[]{:S(2)}, u32[]{:S(2)}) collective-permute-start(f32[16,48,128]{2,1,0:T(8,128)S(1)} %get-tuple-element.23), channel_id=1, source_target_pairs={{0,8},{8,0},{1,9},{9,1},{2,10},{10,2},{3,11},{11,3},{4,12},{12,4},... | collective-permute-start | bytes 1179656 | tf_op jit(solution)/shard_map/ppermute | solution.py:246
  21.0 2.2 %collective-permute-start.4 = (f32[16,24,128]{2,1,0:T(8,128)S(1)}, f32[16,24,128]{2,1,0:T(8,128)S(1)}, u32[]{:S(2)}, u32[]{:S(2)}) collective-permute-start(f32[16,24,128]{2,1,0:T(8,128)S(1)} %get-tuple-element.26), channel_id=1, source_target_pairs={{0,8},{8,0},{1,9},{9,1},{2,10},{10,2},{3,11},{11,3},{4,12},{12,4},... | collective-permute-start | bytes 589832 | tf_op jit(solution)/shard_map/ppermute | solution.py:246
  27.4 22.5 %all-to-all-start.1 = ((f32[16,168,128]{2,1,0:T(8,128)}), f32[16,168,128]{2,1,0:T(8,128)S(1)}, u32[]{:S(2)}, u32[]{:S(2)}) async-start(f32[16,168,128]{2,1,0:T(8,128)} %maximum_add_fusion), calls=%async_computation.1 | async-start | bytes 2752512 | tf_op jit(solution)/shard_map/all_to_all | solution.py:189
  31.7 7.6 %collective-permute-start.5 = (f32[96,128]{1,0:T(8,128)S(1)}, f32[96,128]{1,0:T(8,128)S(1)}, u32[]{:S(2)}, u32[]{:S(2)}) collective-permute-start(f32[96,128]{1,0:T(8,128)S(1)} %reduce_sum.27), channel_id=1, source_target_pairs={{0,4},{4,0},{1,5},{5,1},{2,6},{6,2},{3,7},{7,3},{8,12},{12,8},{9,1... | collective-permute-start | bytes 147464 | tf_op jit(solution)/shard_map/ppermute | solution.py:251
  39.3 5.7 %collective-permute-start.8 = (f32[104,128]{1,0:T(8,128)S(1)}, f32[104,128]{1,0:T(8,128)S(1)}, u32[]{:S(2)}, u32[]{:S(2)}) collective-permute-start(f32[104,128]{1,0:T(8,128)S(1)} %pad_maximum_fusion.2), channel_id=1, source_target_pairs={{0,48},{16,0},{32,16},{48,32},{1,49},{17,1},{33,17},{49,33},{2,50}... | collective-permute-start | bytes 159752 | tf_op jit(solution)/shard_map/ppermute | solution.py:255
  40.1 5.2 %collective-permute-start.7 = (f32[104,128]{1,0:T(8,128)S(1)}, f32[104,128]{1,0:T(8,128)S(1)}, u32[]{:S(2)}, u32[]{:S(2)}) collective-permute-start(f32[104,128]{1,0:T(8,128)S(1)} %pad_maximum_fusion.2), channel_id=1, source_target_pairs={{0,16},{16,32},{32,48},{48,0},{1,17},{17,33},{33,49},{49,1},{2,18}... | collective-permute-start | bytes 159752 | tf_op jit(solution)/shard_map/ppermute | solution.py:255
  40.8 6.7 %collective-permute-start.6 = (f32[104,128]{1,0:T(8,128)S(1)}, f32[104,128]{1,0:T(8,128)S(1)}, u32[]{:S(2)}, u32[]{:S(2)}) collective-permute-start(f32[104,128]{1,0:T(8,128)S(1)} %pad_maximum_fusion.2), channel_id=1, source_target_pairs={{0,32},{16,48},{32,0},{48,16},{1,33},{17,49},{33,1},{49,17},{2,34}... | collective-permute-start | bytes 159752 | tf_op jit(solution)/shard_map/ppermute | solution.py:255
  50.8 17.2 %all-to-all-start.2 = ((f32[8,96,128]{2,1,0:T(8,128)}), f32[8,96,128]{2,1,0:T(8,128)S(1)}, u32[]{:S(2)}, u32[]{:S(2)}) async-start(f32[8,96,128]{2,1,0:T(8,128)} %bitcast.9), calls=%async_computation.2 | async-start | bytes 786432 | tf_op jit(solution)/shard_map/all_to_all | solution.py:189
  94.1 4.6 %collective-permute-start.9 = (f32[16,144,128]{2,1,0:T(8,128)S(1)}, f32[16,144,128]{2,1,0:T(8,128)S(1)}, u32[]{:S(2)}, u32[]{:S(2)}) collective-permute-start(f32[16,144,128]{2,1,0:T(8,128)S(1)} %all_to_all.30.refs_1_), channel_id=1, source_target_pairs={{0,8},{8,0},{1,9},{9,1},{2,10},{10,2},{3,11},{11,3},{4,12},{12,4},... | collective-permute-start | bytes 3538952 | tf_op jit(solution)/shard_map/ppermute | solution.py:273

commit v9 on v8

--- a/solution.py
+++ b/solution.py
@@ -1,3 +1,4 @@
+import functools
 import math
 
 import jax
@@ -91,19 +92,46 @@
                     put(core, block[:, LANES:], first + 1, keep_ref, send_refs)
 
 
-def final_kernel(norm, pos_ref, mine_ref, other_ref, root_ref, normal_ref, cfg_ref, full, left, gram):
+def joined_rows(core, refs, tile, lo=0, hi=16):
+    at = slice(tile * 8, (tile + 1) * 8)
+    a, b = [ref[lo:hi, at, :] for ref in refs]
+    pair = [jnp.where(core == which, a, b)[:, None] for which in range(2)]
+    return jnp.concatenate(pair, 1).reshape((hi - lo) * 16, LANES)
+
+
+def product_kernel(pos_ref, mine_ref, other_ref, root_ref, cross_ref, cfg_ref, full, left):
     core, kind, part, owner = pos_ref[0], pos_ref[1], pos_ref[2], pos_ref[3]
+    width = full.shape[1] // 2
+    band = left.shape[1]
+    for j in range(2 * width // LANES):
+        full[:, j * LANES : (j + 1) * LANES] = joined_rows(core, (mine_ref, other_ref), j)
+    for k in range(4):
+
+        @pl.when(part == k)
+        def _():
+            cols = slice(k * band, (k + 1) * band)
+            shifted = slice(width + k * band, width + (k + 1) * band)
+            left[...] = jnp.where(kind == 0, full[:, cols], full[:, shifted])
+            own = pl.ds(pl.multiple_of(owner * 8, 8), 8)
+            tile = jnp.where(kind == 0, full[own, cols], full[own, shifted])
+            cfg_ref[...] = tile / root_ref[:, :1]
+
+    cross = lax.dot_general(
+        left[...],
+        full[...],
+        (((0,), (0,)), ((), ())),
+        precision=lax.Precision.HIGHEST,
+        preferred_element_type=jnp.float32,
+    )
+    cross_ref[...] = cross * (1.0 / full.shape[0])
+
+
+def final_kernel(norm, pos_ref, mine_ref, other_ref, cross_ref, normal_ref, gram):
+    core, kind, part = pos_ref[0], pos_ref[1], pos_ref[2]
     width = gram.shape[1]
-    band = left.shape[1]
 
     def joined(tile, lo=0, hi=16):
-        at = slice(tile * 8, (tile + 1) * 8)
-        a, b = mine_ref[lo:hi, at, :], other_ref[lo:hi, at, :]
-        pair = [jnp.where(core == which, a, b)[:, None] for which in range(2)]
-        return jnp.concatenate(pair, 1).reshape((hi - lo) * 16, LANES)
-
-    for j in range(2 * width // LANES):
-        full[:, j * LANES : (j + 1) * LANES] = joined(6 + j)
+        return joined_rows(core, (mine_ref, other_ref), tile, lo, hi)
 
     def fill(row, col, piece):
         gram[row : row + piece.shape[0], col : col + piece.shape[1]] = piece
@@ -146,28 +174,12 @@
         straight((4,), 4, 16, 0, 2 * TILE + LANES)
 
     for k, body in enumerate((band_0, band_1, band_2, band_3)):
-
-        @pl.when(part == k)
-        def _():
-            cols = slice(k * band, (k + 1) * band)
-            shifted = slice(width + k * band, width + (k + 1) * band)
-            left[...] = jnp.where(kind == 0, full[:, cols], full[:, shifted])
-            own = pl.ds(pl.multiple_of(owner * 8, 8), 8)
-            tile = jnp.where(kind == 0, full[own, cols], full[own, shifted])
-            cfg_ref[...] = tile / root_ref[:, :1]
-            body()
-
-    for s in range(2):
-        cols = slice(s * width, (s + 1) * width)
-        cross = lax.dot_general(
-            left[...],
-            full[:, cols],
-            (((0,), (0,)), ((), ())),
-            precision=lax.Precision.HIGHEST,
-            preferred_element_type=jnp.float32,
-        )
-        extra = jnp.where(kind == s, gram[...] * (1.0 / norm), 0.0)
-        normal_ref[:, cols] = cross * (1.0 / full.shape[0]) + extra
+        pl.when(part == k)(body)
+
+    for which in range(2):
+        cols = slice(which * width, (which + 1) * width)
+        extra = jnp.where(kind == which, gram[...] * (1.0 / norm), 0.0)
+        normal_ref[:, cols] = cross_ref[:, cols] + extra
 
 
 def call(kernel, outs, args, scratch, space, limit, flops):
@@ -180,7 +192,7 @@
         out_specs=[pl.BlockSpec(memory_space=pltpu.VMEM)] * len(outs),
         scratch_shapes=list(scratch),
         compiler_params=pltpu.CompilerParams(vmem_limit_bytes=limit),
-        cost_estimate=pl.CostEstimate(flops=flops, bytes_accessed=8 << 20, transcendentals=0),
+        cost_estimate=pl.CostEstimate(flops=flops, bytes_accessed=flops >> 9, transcendentals=0),
     )(args[0], *held)
 
 
@@ -189,20 +201,27 @@
     return lax.all_to_all(flat, axes, 0, 0, tiled=True).reshape(values.shape)
 
 
-def needed(grams, owner):
-    def pick(*tiles):
-        return jnp.concatenate([grams[8 * k : 8 * k + 8] for k in tiles])
-
-    band_1 = jnp.where(owner >= 12, pick(1, 2, 3), pick(7, 4, 5))
-    band_2 = jnp.where(owner >= 8, pick(5), pick(8))
-    return jnp.stack(
-        [
-            pick(0, 1, 2, 3, 6, 9),
-            jnp.concatenate([pick(0), band_1, pick(6, 10)]),
-            jnp.concatenate([pick(1, 2, 4, 7), band_2, pick(11)]),
-            pick(2, 3, 4, 5, 8, 11),
-        ]
-    )
+def bands_kernel(owner_ref, *refs):
+    owner, out_ref = owner_ref[0], refs[-1]
+    total = refs[0][...]
+    for ref in refs[1:-1]:
+        total = total + ref[...]
+
+    def tile(k):
+        return total[8 * k : 8 * k + 8]
+
+    def either(first, a, b):
+        return jnp.where(owner >= first, tile(a), tile(b))
+
+    bands = (
+        [tile(k) for k in (0, 1, 2, 3, 6, 9)],
+        [tile(0), either(12, 1, 7), either(12, 2, 4), either(12, 3, 5), tile(6), tile(10)],
+        [tile(1), tile(2), tile(4), tile(7), either(8, 5, 8), tile(11)],
+        [tile(k) for k in (2, 3, 4, 5, 8, 11)],
+    )
+    for k in range(16):
+        for at, piece in enumerate(bands[k % 4]):
+            out_ref[k, at * 8 : at * 8 + 8, :] = piece
 
 
 def shards(desc, species, atom_cfg, slot, weights):
@@ -248,37 +267,53 @@
     plane_s, pair_g = lax.optimization_barrier((plane_s, pair_g))
     plane_g = jnp.sum(exchange(pair_g, ("x", "y")), 0)
 
+    def along_l(value, k):
+        return lax.ppermute(value, "l", [(i, (i + k) % 4) for i in range(4)])
+
     plane_s = plane_s + lax.ppermute(plane_s, "h", flip)
     rooted = jnp.concatenate([plane_s, root])
     got = [(rooted, l)]
     for k in (2, 1, 3):
-        got.append((lax.ppermute(rooted, "l", [(i, (i + k) % 4) for i in range(4)]), (l - k) % 4))
+        got.append((along_l(rooted, k), (l - k) % 4))
     root_here = sum(jnp.where(source == part, value[96:], 0.0) for value, source in got)
     scale = 1.0 / math.sqrt(atoms * n_dev / configs)
     sums = sum(value[:96] for value, _ in got).reshape(12, 8, LANES) * (root_here * scale)
     sums, plane_g = lax.optimization_barrier((sums, plane_g))
-    corner = jnp.broadcast_to(plane_g[None, 144:], (2, 24, LANES))
-    planes = jnp.concatenate([plane_g[:144].reshape(2, 72, LANES), corner], 1)
-    planes = jnp.broadcast_to(planes[None], (4, 2, 96, LANES)).reshape(8, 96, LANES)
-    grams = jnp.sum(exchange(planes, ("l", "h")), 0)
-    bands = needed(grams, x * 4 + part)
-    spread = jnp.concatenate([bands, jnp.broadcast_to(sums.reshape(1, 96, LANES), (4, 96, LANES))], 1)
-    spread = jnp.broadcast_to(spread[None], (4, 4, 144, LANES)).reshape(16, 144, LANES)
-    mine = exchange(spread, ("x", "y"))
+    def of_species(which):
+        return jnp.concatenate([lax.dynamic_slice_in_dim(plane_g, which * 72, 72), plane_g[144:]])
+
+    mine_s = exchange(jnp.broadcast_to(sums.reshape(1, 96, LANES), (16, 96, LANES)), ("x", "y"))
+    grams = of_species(kind) + lax.ppermute(of_species(1 - kind), "h", flip)
+    (spread,) = call(
+        bands_kernel,
+        [tiles(6)],
+        [(x * 4 + part)[None], grams] + [along_l(grams, k) for k in (2, 1, 3)],
+        (),
+        pltpu.VMEM,
+        8 << 20,
+        1,
+    )
+    spread, mine_s = lax.optimization_barrier((spread, mine_s))
+    mine_g = exchange(spread, ("x", "y"))
     band = 2 * width // 8
     norm = atoms * n_dev // 8
-    normal, rows = call(
-        lambda *refs: final_kernel(norm, *refs),
-        [jax.ShapeDtypeStruct((band, 2 * width), f32), jax.ShapeDtypeStruct((cfg_here, band), f32)],
-        [pos, mine, lax.ppermute(mine, "c", flip), root],
-        [
-            pltpu.VMEM((configs, 2 * width), f32),
-            pltpu.VMEM((configs, band), f32),
-            pltpu.VMEM((band, width), f32),
-        ],
+    cross, rows = call(
+        product_kernel,
+        [pltpu.VMEM((band, 2 * width), f32), jax.ShapeDtypeStruct((cfg_here, band), f32)],
+        [pos, mine_s, lax.ppermute(mine_s, "c", flip), root],
+        [pltpu.VMEM((configs, 2 * width), f32), pltpu.VMEM((configs, band), f32)],
         pltpu.VMEM,
         24 << 20,
-        8 * band * width * configs,
+        24 * band * width * configs,
+    )
+    (normal,) = call(
+        functools.partial(final_kernel, norm),
+        [jax.ShapeDtypeStruct((band, 2 * width), f32)],
+        [pos, mine_g, lax.ppermute(mine_g, "c", flip), cross],
+        [pltpu.VMEM((band, width), f32)],
+        pltpu.VMEM,
+        24 << 20,
+        band * width,
     )
     return normal, rows
 

time: 102 us -> 99.9 us (0.979)
  the two profiles are of different devices: /device:TPU:33 before, /device:TPU:1 now
where the time goes in v9:
time: 99.9 us; the launch traced here: 99.6 us
  starting transfers between devices  48.4 us (48%)
  waiting for transfers between devices  18.7 us (19%)
  blocking collectives  15.8 us (16%)
  Pallas kernels  12.4 us (12%)
  other arithmetic  2.47 us (2%)
  local copies, waits for them, and re-layouts  1.06 us (1%)
    all_to_all x1, blocking collectives, exchange(): return lax.all_to_all(flat, axes, 0, 0, tiled=True).reshape(values.shape)  15.8 us
    all_to_all x3, starting transfers between devices, exchange(): return lax.all_to_all(flat, axes, 0, 0, tiled=True).reshape(values.shape)  14.1 us
    pallas_call x5, Pallas kernels, call(): pl.pallas_call(kernel, out_shape=outs, in_specs=[smem] + [pl.BlockSpec(me...  12.4 us
    ppermute x6, starting transfers between devices, along_l(): return lax.ppermute(value, 'l', [(i, (i + k) % 4) for i in range(4)])  8.24 us
    ppermute x6, waiting for transfers between devices, along_l(): return lax.ppermute(value, 'l', [(i, (i + k) % 4) for i in range(4)])  7.13 us
    ppermute x1, starting transfers between devices, shards(): plane_s = plane_s + lax.ppermute(plane_s, 'h', flip)  7 us
    ppermute x1, starting transfers between devices, shards(): grams = of_species(kind) + lax.ppermute(of_species(1 - kind), 'h', flip)  6.76 us
    ppermute x1, starting transfers between devices, shards(): lax.ppermute(mine_s, 'c', flip)  5.87 us
  transfers between devices with their start and end apart: 18, of which 10 were waited for; matrix products, arithmetic and copies ran while one was open for 1% of the time, Pallas kernels for 7%

profile of v9, /device:TPU:1, one launch (start us, length us, event | category | flops | bytes accessed | tf_op | source)
XLA Modules:
  0.0 99.6 jit_solution(16701210053511271521)
XLA Ops:
  0.6 0.0 copy-start
  0.6 3.5 %shard_map.68 = (f32[16,96,128]{2,1,0:T(8,128)S(1)}, f32[16,96,128]{2,1,0:T(8,128)S(1)}) custom-call(s32[1]{0:T(128)} %bitcast.core_ref, bf16[2048,768]{1,0:T(8,128)(2,1)} %desc_hbm.2, s32[1,2048]{1,0:T(1,128)} %bitcast.15, s32[1,2048]{1,0:T(1,128)} %bitcast.14, s32[1,256]{1,0:T(1,128)} %bitcast.17), custom_call_target="tpu_custom_call" | custom-call | flops 1610612736 | bytes 3145728 | tf_op jit(solution)/shard_map/pallas_call | solution.py:188
  4.1 3.3 %collective-permute-start = (f32[16,96,128]{2,1,0:T(8,128)S(1)}, f32[16,96,128]{2,1,0:T(8,128)S(1)}, u32[]{:S(2)}, u32[]{:S(2)}) collective-permute-start(f32[16,96,128]{2,1,0:T(8,128)S(1)} %get-tuple-element.22), channel_id=1, source_target_pairs={{0,8},{8,0},{1,9},{9,1},{2,10},{10,2},{3,11},{11,3},{4,12},{12,4},... | collective-permute-start | bytes 2359304 | tf_op jit(solution)/shard_map/ppermute | solution.py:255
  7.4 0.0 copy-done
  7.4 0.1 pad_add_fusion.pos_ref
  7.5 1.8 %collective-permute-done = f32[16,96,128]{2,1,0:T(8,128)S(1)} collective-permute-done((f32[16,96,128]{2,1,0:T(8,128)S(1)}, f32[16,96,128]{2,1,0:T(8,128)S(1)}, u32[]{:S(2)}, u32[]{:S(2)}) %collective-permute-start) | collective-permute-done | bytes 786464 | tf_op jit(solution)/shard_map/ppermute | solution.py:255
  9.4 1.0 add.58
  10.3 0.1 broadcast_in_dim.42.root_ref
  10.4 5.0 %all-to-all-start = ((f32[16,96,128]{2,1,0:T(8,128)}), f32[16,96,128]{2,1,0:T(8,128)S(1)}, u32[]{:S(2)}, u32[]{:S(2)}) async-start(f32[16,96,128]{2,1,0:T(8,128)} %add.58), calls=%async_computation | async-start | bytes 1572864 | tf_op jit(solution)/shard_map/all_to_all | solution.py:201
  15.4 5.1 %shard_map.69 = (f32[16,168,128]{2,1,0:T(8,128)S(1)}, f32[16,48,128]{2,1,0:T(8,128)S(1)}, f32[16,48,128]{2,1,0:T(8,128)S(1)}, f32[16,48,128]{2,1,0:T(8,128)S(1)}, f32[16,24,128]{2,1,0:T(8,128)S(1)}) custom-call(s32[1]{0:T(128)} %bitcast.core_ref, bf16[2048,768]{1,0:T(8,128)(2,1)} %desc_hbm.2, s32[1,2048]{1,0:T(1,128)} %bitcast.16), custom_call_target="tpu_custom_call" | custom-call | flops 4831838208 | bytes 9437184 | tf_op jit(solution)/shard_map/pallas_call | solution.py:188
  20.5 0.7 collective-permute-start.3
  21.3 0.1 collective-permute-start.2
  21.4 0.4 collective-permute-start.1
  21.8 0.1 collective-permute-start.4
  21.9 2.1 %collective-permute-done.4 = f32[16,24,128]{2,1,0:T(8,128)S(1)} collective-permute-done((f32[16,24,128]{2,1,0:T(8,128)S(1)}, f32[16,24,128]{2,1,0:T(8,128)S(1)}, u32[]{:S(2)}, u32[]{:S(2)}) %collective-permute-start.4) | collective-permute-done | bytes 196640 | tf_op jit(solution)/shard_map/ppermute | solution.py:265
  24.0 0.0 collective-permute-done.3
  24.0 0.0 collective-permute-done.2
  24.0 0.0 collective-permute-done.1
  24.1 1.2 %maximum_add_fusion = f32[16,168,128]{2,1,0:T(8,128)} fusion(f32[16,168,128]{2,1,0:T(8,128)S(1)} %get-tuple-element.26, f32[16,24,128]{2,1,0:T(8,128)S(1)} %collective-permute-done.4, f32[16,48,128]{2,1,0:T(8,128)S(1)} %collective-permute-done.3, f32[16,48,128]{2,1,0:T(8,128)S(1)} %collective-permute-done.2, f32[16,48,128]{2,1,0:T(8,128)S(1)} %collective-permute-done.1), kind=kLoop, calls=%fused_computation | loop fusion | flops 1376256 | bytes 4128768 | tf_op jit(solution)/shard_map/add | solution.py:265
  25.3 2.9 %all-to-all-done = f32[16,96,128]{2,1,0:T(8,128)S(1)} async-done(((f32[16,96,128]{2,1,0:T(8,128)}), f32[16,96,128]{2,1,0:T(8,128)S(1)}, u32[]{:S(2)}, u32[]{:S(2)}) %all-to-all-start) | async-done | bytes 786464 | tf_op jit(solution)/shard_map/all_to_all | solution.py:201
  28.2 4.3 %all-to-all-start.1 = ((f32[16,168,128]{2,1,0:T(8,128)}), f32[16,168,128]{2,1,0:T(8,128)S(1)}, u32[]{:S(2)}, u32[]{:S(2)}) async-start(f32[16,168,128]{2,1,0:T(8,128)} %maximum_add_fusion), calls=%async_computation.1 | async-start | bytes 2752512 | tf_op jit(solution)/shard_map/all_to_all | solution.py:201
  32.5 7.0 %collective-permute-start.5 = (f32[96,128]{1,0:T(8,128)S(1)}, f32[96,128]{1,0:T(8,128)S(1)}, u32[]{:S(2)}, u32[]{:S(2)}) collective-permute-start(f32[96,128]{1,0:T(8,128)S(1)} %reduce_sum.18), channel_id=1, source_target_pairs={{0,4},{4,0},{1,5},{5,1},{2,6},{6,2},{3,7},{7,3},{8,12},{12,8},{9,1... | collective-permute-start | bytes 147464 | tf_op jit(solution)/shard_map/ppermute | solution.py:273
  39.5 1.5 %collective-permute-done.5 = f32[96,128]{1,0:T(8,128)S(1)} collective-permute-done((f32[96,128]{1,0:T(8,128)S(1)}, f32[96,128]{1,0:T(8,128)S(1)}, u32[]{:S(2)}, u32[]{:S(2)}) %collective-permute-start.5) | collective-permute-done | bytes 49184 | tf_op jit(solution)/shard_map/ppermute | solution.py:273
  41.0 2.9 %collective-permute-start.8 = (f32[104,128]{1,0:T(8,128)S(1)}, f32[104,128]{1,0:T(8,128)S(1)}, u32[]{:S(2)}, u32[]{:S(2)}) collective-permute-start(f32[104,128]{1,0:T(8,128)S(1)} %pad_maximum_fusion.2), channel_id=1, source_target_pairs={{0,48},{16,0},{32,16},{48,32},{1,49},{17,1},{33,17},{49,33},{2,50}... | collective-permute-start | bytes 159752 | tf_op jit(solution)/shard_map/ppermute | solution.py:271
  43.9 0.0 collective-permute-start.7
  43.9 0.4 collective-permute-start.6
  44.3 0.8 collective-permute-done.8
  45.1 3.9 %collective-permute-done.7 = f32[104,128]{1,0:T(8,128)S(1)} collective-permute-done((f32[104,128]{1,0:T(8,128)S(1)}, f32[104,128]{1,0:T(8,128)S(1)}, u32[]{:S(2)}, u32[]{:S(2)}) %collective-permute-start.7) | collective-permute-done | bytes 53280 | tf_op jit(solution)/shard_map/ppermute | solution.py:271
  49.0 0.0 collective-permute-done.6
  49.0 1.7 %all-to-all-done.1 = f32[16,168,128]{2,1,0:T(8,128)S(1)} async-done(((f32[16,168,128]{2,1,0:T(8,128)}), f32[16,168,128]{2,1,0:T(8,128)S(1)}, u32[]{:S(2)}, u32[]{:S(2)}) %all-to-all-start.1) | async-done | bytes 1376288 | tf_op jit(solution)/shard_map/all_to_all | solution.py:201
  50.8 0.1 reduce_sum.19
  50.8 1.0 broadcast_in_dim.46
  51.8 4.8 %all-to-all-start.2 = ((f32[16,96,128]{2,1,0:T(8,128)}), f32[16,96,128]{2,1,0:T(8,128)S(1)}, u32[]{:S(2)}, u32[]{:S(2)}) async-start(f32[16,96,128]{2,1,0:T(8,128)} %broadcast_in_dim.46), calls=%async_computation.2 | async-start | bytes 1572864 | tf_op jit(solution)/shard_map/all_to_all | solution.py:201
  56.7 6.8 %collective-permute-start.9 = (f32[96,128]{1,0:T(8,128)S(1)}, f32[96,128]{1,0:T(8,128)S(1)}, u32[]{:S(2)}, u32[]{:S(2)}) collective-permute-start(f32[96,128]{1,0:T(8,128)S(1)} %pad_maximum_fusion), channel_id=1, source_target_pairs={{0,4},{4,0},{1,5},{5,1},{2,6},{6,2},{3,7},{7,3},{8,12},{12,8},{9,1... | collective-permute-start | bytes 147464 | tf_op jit(solution)/shard_map/ppermute | solution.py:286
  63.4 1.5 %collective-permute-done.9 = f32[96,128]{1,0:T(8,128)S(1)} collective-permute-done((f32[96,128]{1,0:T(8,128)S(1)}, f32[96,128]{1,0:T(8,128)S(1)}, u32[]{:S(2)}, u32[]{:S(2)}) %collective-permute-start.9) | collective-permute-done | bytes 49184 | tf_op jit(solution)/shard_map/ppermute | solution.py:286
  64.9 1.7 %collective-permute-start.10 = (f32[96,128]{1,0:T(8,128)S(1)}, f32[96,128]{1,0:T(8,128)S(1)}, u32[]{:S(2)}, u32[]{:S(2)}) collective-permute-start(f32[96,128]{1,0:T(8,128)S(1)} %fusion.refs_0_), channel_id=1, source_target_pairs={{0,32},{16,48},{32,0},{48,16},{1,33},{17,49},{33,1},{49,17},{2,34}... | collective-permute-start | bytes 147464 | tf_op jit(solution)/shard_map/ppermute | solution.py:271
  66.6 1.6 %collective-permute-start.11 = (f32[96,128]{1,0:T(8,128)S(1)}, f32[96,128]{1,0:T(8,128)S(1)}, u32[]{:S(2)}, u32[]{:S(2)}) collective-permute-start(f32[96,128]{1,0:T(8,128)S(1)} %fusion.refs_0_), channel_id=1, source_target_pairs={{0,16},{16,32},{32,48},{48,0},{1,17},{17,33},{33,49},{49,1},{2,18}... | collective-permute-start | bytes 147464 | tf_op jit(solution)/shard_map/ppermute | solution.py:271
  68.3 1.6 %collective-permute-start.12 = (f32[96,128]{1,0:T(8,128)S(1)}, f32[96,128]{1,0:T(8,128)S(1)}, u32[]{:S(2)}, u32[]{:S(2)}) collective-permute-start(f32[96,128]{1,0:T(8,128)S(1)} %fusion.refs_0_), channel_id=1, source_target_pairs={{0,48},{16,0},{32,16},{48,32},{1,49},{17,1},{33,17},{49,33},{2,50}... | collective-permute-start | bytes 147464 | tf_op jit(solution)/shard_map/ppermute | solution.py:271
  69.9 0.0 collective-permute-done.10.refs_1_
  69.9 1.9 %collective-permute-done.11.refs_2_ = f32[96,128]{1,0:T(8,128)S(1)} collective-permute-done((f32[96,128]{1,0:T(8,128)S(1)}, f32[96,128]{1,0:T(8,128)S(1)}, u32[]{:S(2)}, u32[]{:S(2)}) %collective-permute-start.11) | collective-permute-done | bytes 49184 | tf_op jit(solution)/shard_map/ppermute | solution.py:271
  71.8 0.6 collective-permute-done.12.refs_3_
  72.4 0.0 all-to-all-done.2.mine_ref
  72.4 5.9 %collective-permute-start.14 = (f32[16,96,128]{2,1,0:T(8,128)S(1)}, f32[16,96,128]{2,1,0:T(8,128)S(1)}, u32[]{:S(2)}, u32[]{:S(2)}) collective-permute-start(f32[16,96,128]{2,1,0:T(8,128)S(1)} %all-to-all-done.2.mine_ref), channel_id=1, source_target_pairs={{0,8},{8,0},{1,9},{9,1},{2,10},{10,2},{3,11},{11,3},{4,12},{12,4},... | collective-permute-start | bytes 2359304 | tf_op jit(solution)/shard_map/ppermute | solution.py:303
  78.2 15.8 %all_to_all.24.mine_ref = f32[16,48,128]{2,1,0:T(8,128)S(1)} all-to-all(f32[16,48,128]{2,1,0:T(8,128)S(1)} %shard_map.70), channel_id=1, replica_groups=mesh['x'=4,'l'=4,'c'=2,'h'=2,'y'=4] {'x','y'}, dimensions={0} | all-to-all | bytes 786432 | tf_op jit(solution)/shard_map/all_to_all | solution.py:201
  94.1 1.7 %collective-permute-start.13 = (f32[16,48,128]{2,1,0:T(8,128)S(1)}, f32[16,48,128]{2,1,0:T(8,128)S(1)}, u32[]{:S(2)}, u32[]{:S(2)}) collective-permute-start(f32[16,48,128]{2,1,0:T(8,128)S(1)} %all_to_all.24.mine_ref), channel_id=1, source_target_pairs={{0,8},{8,0},{1,9},{9,1},{2,10},{10,2},{3,11},{11,3},{4,12},{12,4},... | collective-permute-start | bytes 1179656 | tf_op jit(solution)/shard_map/ppermute | solution.py:312
  95.7 0.0 collective-permute-done.14.other_ref
  95.7 2.0 %shard_map.71 = (f32[192,1536]{1,0:T(8,128)S(1)}, f32[8,192]{1,0:T(8,128)}) custom-call(s32[4]{0:T(128)S(1)} %pad_add_fusion.pos_ref, f32[16,96,128]{2,1,0:T(8,128)S(1)} %all-to-all-done.2.mine_ref, f32[16,96,128]{2,1,0:T(8,128)S(1)} %collective-permute-done.14.other_ref, f32[8,128]{1,0:T(8,128)S(1)} %broadcast_in_dim.42.root_ref), custom_call_target="tpu_custom_call" | custom-call | flops 905969664 | bytes 1769472 | tf_op jit(solution)/shard_map/pallas_call | solution.py:188
  97.7 0.0 collective-permute-done.13.other_ref
  97.7 1.8 %shard_map.72 = f32[192,1536]{1,0:T(8,128)} custom-call(s32[4]{0:T(128)S(1)} %pad_add_fusion.pos_ref, f32[16,48,128]{2,1,0:T(8,128)S(1)} %all_to_all.24.mine_ref, f32[16,48,128]{2,1,0:T(8,128)S(1)} %collective-permute-done.13.other_ref, f32[192,1536]{1,0:T(8,128)S(1)} %get-tuple-element.38.cross_ref), custom_call_target="tpu_custom_call" | custom-call | flops 147456 | bytes 288 | tf_op jit(solution)/shard_map/pallas_call | solution.py:188
  (11 shorter events, 0.2 us)
Async XLA Ops:
  0.6 6.8 %copy-start = (f32[8]{0:T(128)S(1)}, f32[8]{0:T(128)}, u32[]{:S(2)}) copy-start(f32[8]{0:T(128)} %param.9) | copy-start | bytes 100
  4.1 5.2 %collective-permute-start = (f32[16,96,128]{2,1,0:T(8,128)S(1)}, f32[16,96,128]{2,1,0:T(8,128)S(1)}, u32[]{:S(2)}, u32[]{:S(2)}) collective-permute-start(f32[16,96,128]{2,1,0:T(8,128)S(1)} %get-tuple-element.22), channel_id=1, source_target_pairs={{0,8},{8,0},{1,9},{9,1},{2,10},{10,2},{3,11},{11,3},{4,12},{12,4},... | collective-permute-start | bytes 2359304 | tf_op jit(solution)/shard_map/ppermute | solution.py:255
  10.4 17.8 %all-to-all-start = ((f32[16,96,128]{2,1,0:T(8,128)}), f32[16,96,128]{2,1,0:T(8,128)S(1)}, u32[]{:S(2)}, u32[]{:S(2)}) async-start(f32[16,96,128]{2,1,0:T(8,128)} %add.58), calls=%async_computation | async-start | bytes 1572864 | tf_op jit(solution)/shard_map/all_to_all | solution.py:201
  20.5 3.5 %collective-permute-start.3 = (f32[16,48,128]{2,1,0:T(8,128)S(1)}, f32[16,48,128]{2,1,0:T(8,128)S(1)}, u32[]{:S(2)}, u32[]{:S(2)}) collective-permute-start(f32[16,48,128]{2,1,0:T(8,128)S(1)} %get-tuple-element.29), channel_id=1, source_target_pairs={{0,8},{8,0},{1,9},{9,1},{2,10},{10,2},{3,11},{11,3},{4,12},{12,4},... | collective-permute-start | bytes 1179656 | tf_op jit(solution)/shard_map/ppermute | solution.py:265
  21.3 2.8 %collective-permute-start.2 = (f32[16,48,128]{2,1,0:T(8,128)S(1)}, f32[16,48,128]{2,1,0:T(8,128)S(1)}, u32[]{:S(2)}, u32[]{:S(2)}) collective-permute-start(f32[16,48,128]{2,1,0:T(8,128)S(1)} %get-tuple-element.28), channel_id=1, source_target_pairs={{0,8},{8,0},{1,9},{9,1},{2,10},{10,2},{3,11},{11,3},{4,12},{12,4},... | collective-permute-start | bytes 1179656 | tf_op jit(solution)/shard_map/ppermute | solution.py:265
  21.4 2.7 %collective-permute-start.1 = (f32[16,48,128]{2,1,0:T(8,128)S(1)}, f32[16,48,128]{2,1,0:T(8,128)S(1)}, u32[]{:S(2)}, u32[]{:S(2)}) collective-permute-start(f32[16,48,128]{2,1,0:T(8,128)S(1)} %get-tuple-element.27), channel_id=1, source_target_pairs={{0,8},{8,0},{1,9},{9,1},{2,10},{10,2},{3,11},{11,3},{4,12},{12,4},... | collective-permute-start | bytes 1179656 | tf_op jit(solution)/shard_map/ppermute | solution.py:265
  21.8 2.2 %collective-permute-start.4 = (f32[16,24,128]{2,1,0:T(8,128)S(1)}, f32[16,24,128]{2,1,0:T(8,128)S(1)}, u32[]{:S(2)}, u32[]{:S(2)}) collective-permute-start(f32[16,24,128]{2,1,0:T(8,128)S(1)} %get-tuple-element.30), channel_id=1, source_target_pairs={{0,8},{8,0},{1,9},{9,1},{2,10},{10,2},{3,11},{11,3},{4,12},{12,4},... | collective-permute-start | bytes 589832 | tf_op jit(solution)/shard_map/ppermute | solution.py:265
  28.2 22.5 %all-to-all-start.1 = ((f32[16,168,128]{2,1,0:T(8,128)}), f32[16,168,128]{2,1,0:T(8,128)S(1)}, u32[]{:S(2)}, u32[]{:S(2)}) async-start(f32[16,168,128]{2,1,0:T(8,128)} %maximum_add_fusion), calls=%async_computation.1 | async-start | bytes 2752512 | tf_op jit(solution)/shard_map/all_to_all | solution.py:201
  32.5 8.5 %collective-permute-start.5 = (f32[96,128]{1,0:T(8,128)S(1)}, f32[96,128]{1,0:T(8,128)S(1)}, u32[]{:S(2)}, u32[]{:S(2)}) collective-permute-start(f32[96,128]{1,0:T(8,128)S(1)} %reduce_sum.18), channel_id=1, source_target_pairs={{0,4},{4,0},{1,5},{5,1},{2,6},{6,2},{3,7},{7,3},{8,12},{12,8},{9,1... | collective-permute-start | bytes 147464 | tf_op jit(solution)/shard_map/ppermute | solution.py:273
  41.0 4.1 %collective-permute-start.8 = (f32[104,128]{1,0:T(8,128)S(1)}, f32[104,128]{1,0:T(8,128)S(1)}, u32[]{:S(2)}, u32[]{:S(2)}) collective-permute-start(f32[104,128]{1,0:T(8,128)S(1)} %pad_maximum_fusion.2), channel_id=1, source_target_pairs={{0,48},{16,0},{32,16},{48,32},{1,49},{17,1},{33,17},{49,33},{2,50}... | collective-permute-start | bytes 159752 | tf_op jit(solution)/shard_map/ppermute | solution.py:271
  43.9 5.1 %collective-permute-start.7 = (f32[104,128]{1,0:T(8,128)S(1)}, f32[104,128]{1,0:T(8,128)S(1)}, u32[]{:S(2)}, u32[]{:S(2)}) collective-permute-start(f32[104,128]{1,0:T(8,128)S(1)} %pad_maximum_fusion.2), channel_id=1, source_target_pairs={{0,16},{16,32},{32,48},{48,0},{1,17},{17,33},{33,49},{49,1},{2,18}... | collective-permute-start | bytes 159752 | tf_op jit(solution)/shard_map/ppermute | solution.py:271
  43.9 5.1 %collective-permute-start.6 = (f32[104,128]{1,0:T(8,128)S(1)}, f32[104,128]{1,0:T(8,128)S(1)}, u32[]{:S(2)}, u32[]{:S(2)}) collective-permute-start(f32[104,128]{1,0:T(8,128)S(1)} %pad_maximum_fusion.2), channel_id=1, source_target_pairs={{0,32},{16,48},{32,0},{48,16},{1,33},{17,49},{33,1},{49,17},{2,34}... | collective-permute-start | bytes 159752 | tf_op jit(solution)/shard_map/ppermute | solution.py:271
  51.8 20.6 %all-to-all-start.2 = ((f32[16,96,128]{2,1,0:T(8,128)}), f32[16,96,128]{2,1,0:T(8,128)S(1)}, u32[]{:S(2)}, u32[]{:S(2)}) async-start(f32[16,96,128]{2,1,0:T(8,128)} %broadcast_in_dim.46), calls=%async_computation.2 | async-start | bytes 1572864 | tf_op jit(solution)/shard_map/all_to_all | solution.py:201
  56.7 8.2 %collective-permute-start.9 = (f32[96,128]{1,0:T(8,128)S(1)}, f32[96,128]{1,0:T(8,128)S(1)}, u32[]{:S(2)}, u32[]{:S(2)}) collective-permute-start(f32[96,128]{1,0:T(8,128)S(1)} %pad_maximum_fusion), channel_id=1, source_target_pairs={{0,4},{4,0},{1,5},{5,1},{2,6},{6,2},{3,7},{7,3},{8,12},{12,8},{9,1... | collective-permute-start | bytes 147464 | tf_op jit(solution)/shard_map/ppermute | solution.py:286
  64.9 5.0 %collective-permute-start.10 = (f32[96,128]{1,0:T(8,128)S(1)}, f32[96,128]{1,0:T(8,128)S(1)}, u32[]{:S(2)}, u32[]{:S(2)}) collective-permute-start(f32[96,128]{1,0:T(8,128)S(1)} %fusion.refs_0_), channel_id=1, source_target_pairs={{0,32},{16,48},{32,0},{48,16},{1,33},{17,49},{33,1},{49,17},{2,34}... | collective-permute-start | bytes 147464 | tf_op jit(solution)/shard_map/ppermute | solution.py:271
  66.6 5.1 %collective-permute-start.11 = (f32[96,128]{1,0:T(8,128)S(1)}, f32[96,128]{1,0:T(8,128)S(1)}, u32[]{:S(2)}, u32[]{:S(2)}) collective-permute-start(f32[96,128]{1,0:T(8,128)S(1)} %fusion.refs_0_), channel_id=1, source_target_pairs={{0,16},{16,32},{32,48},{48,0},{1,17},{17,33},{33,49},{49,1},{2,18}... | collective-permute-start | bytes 147464 | tf_op jit(solution)/shard_map/ppermute | solution.py:271
  68.3 4.1 %collective-permute-start.12 = (f32[96,128]{1,0:T(8,128)S(1)}, f32[96,128]{1,0:T(8,128)S(1)}, u32[]{:S(2)}, u32[]{:S(2)}) collective-permute-start(f32[96,128]{1,0:T(8,128)S(1)} %fusion.refs_0_), channel_id=1, source_target_pairs={{0,48},{16,0},{32,16},{48,32},{1,49},{17,1},{33,17},{49,33},{2,50}... | collective-permute-start | bytes 147464 | tf_op jit(solution)/shard_map/ppermute | solution.py:271
  72.4 23.4 %collective-permute-start.14 = (f32[16,96,128]{2,1,0:T(8,128)S(1)}, f32[16,96,128]{2,1,0:T(8,128)S(1)}, u32[]{:S(2)}, u32[]{:S(2)}) collective-permute-start(f32[16,96,128]{2,1,0:T(8,128)S(1)} %all-to-all-done.2.mine_ref), channel_id=1, source_target_pairs={{0,8},{8,0},{1,9},{9,1},{2,10},{10,2},{3,11},{11,3},{4,12},{12,4},... | collective-permute-start | bytes 2359304 | tf_op jit(solution)/shard_map/ppermute | solution.py:303
  94.1 3.6 %collective-permute-start.13 = (f32[16,48,128]{2,1,0:T(8,128)S(1)}, f32[16,48,128]{2,1,0:T(8,128)S(1)}, u32[]{:S(2)}, u32[]{:S(2)}) collective-permute-start(f32[16,48,128]{2,1,0:T(8,128)S(1)} %all_to_all.24.mine_ref), channel_id=1, source_target_pairs={{0,8},{8,0},{1,9},{9,1},{2,10},{10,2},{3,11},{11,3},{4,12},{12,4},... | collective-permute-start | bytes 1179656 | tf_op jit(solution)/shard_map/ppermute | solution.py:312

commit v10 on v9

--- a/solution.py
+++ b/solution.py
@@ -291,7 +291,7 @@
         (),
         pltpu.VMEM,
         8 << 20,
-        1,
+        5500000000,
     )
     spread, mine_s = lax.optimization_barrier((spread, mine_s))
     mine_g = exchange(spread, ("x", "y"))
@@ -306,6 +306,7 @@
         24 << 20,
         24 * band * width * configs,
     )
+    mine_g, cross = lax.optimization_barrier((mine_g, cross))
     (normal,) = call(
         functools.partial(final_kernel, norm),
         [jax.ShapeDtypeStruct((band, 2 * width), f32)],

time: 99.9 us -> 96.9 us (0.970)
  blocking collectives: 15.8 us -> 0 us
  waiting for transfers between devices: 18.7 us -> 28.4 us
  starting transfers between devices: 48.4 us -> 50.7 us
    all_to_all x1 -> x0, blocking collectives: 15.8 us -> none  [exchange(): return lax.all_to_all(flat, axes, 0, 0, tiled=True).reshape(values.shape)]
    all_to_all x3 -> x4, waiting for transfers between devices: 4.63 us -> 15.4 us  [exchange(): return lax.all_to_all(flat, axes, 0, 0, tiled=True).reshape(values.shape)]
    all_to_all x3 -> x4, starting transfers between devices: 14.1 us -> 17.8 us  [exchange(): return lax.all_to_all(flat, axes, 0, 0, tiled=True).reshape(values.shape)]
    ppermute x1, waiting for transfers between devices: 1.48 us -> 0.01 us  [shards(): grams = of_species(kind) + lax.ppermute(of_species(1 - kind), 'h', flip)]
    ppermute x1, waiting for transfers between devices: 0.01 us -> 1.35 us  [shards(): lax.ppermute(mine_g, 'c', flip)]
    ppermute x1, starting transfers between devices: 5.87 us -> 4.57 us  [shards(): lax.ppermute(mine_s, 'c', flip)]
  transfers between devices with their start and end apart: 18 -> 19, of which waited for: 10 -> 11; matrix products, arithmetic and copies ran while one was open for 1% -> 2% of each run, Pallas kernels for 7% -> 8%
where the time goes in v10:
time: 96.9 us; the launch traced here: 96.5 us
  starting transfers between devices  50.7 us (52%)
  waiting for transfers between devices  28.4 us (29%)
  Pallas kernels  13.1 us (14%)
  other arithmetic  2.45 us (3%)
  local copies, waits for them, and re-layouts  1.06 us (1%)
    all_to_all x4, starting transfers between devices, exchange(): return lax.all_to_all(flat, axes, 0, 0, tiled=True).reshape(values.shape)  17.8 us
    all_to_all x4, waiting for transfers between devices, exchange(): return lax.all_to_all(flat, axes, 0, 0, tiled=True).reshape(values.shape)  15.4 us
    pallas_call x5, Pallas kernels, call(): pl.pallas_call(kernel, out_shape=outs, in_specs=[smem] + [pl.BlockSpec(me...  13.1 us
    ppermute x6, starting transfers between devices, along_l(): return lax.ppermute(value, 'l', [(i, (i + k) % 4) for i in range(4)])  7.99 us
    ppermute x1, starting transfers between devices, shards(): plane_s = plane_s + lax.ppermute(plane_s, 'h', flip)  7 us
    ppermute x1, starting transfers between devices, shards(): grams = of_species(kind) + lax.ppermute(of_species(1 - kind), 'h', flip)  7 us
    ppermute x6, waiting for transfers between devices, along_l(): return lax.ppermute(value, 'l', [(i, (i + k) % 4) for i in range(4)])  6.18 us
    ppermute x1, starting transfers between devices, shards(): lax.ppermute(mine_s, 'c', flip)  4.57 us
  transfers between devices with their start and end apart: 19, of which 11 were waited for; matrix products, arithmetic and copies ran while one was open for 2% of the time, Pallas kernels for 8%

profile of v10, /device:TPU:1, one launch (start us, length us, event | category | flops | bytes accessed | tf_op | source)
XLA Modules:
  0.0 96.5 jit_solution(8595788586722276881)
XLA Ops:
  0.6 0.0 copy-start
  0.6 3.5 %shard_map.68 = (f32[16,96,128]{2,1,0:T(8,128)S(1)}, f32[16,96,128]{2,1,0:T(8,128)S(1)}) custom-call(s32[1]{0:T(128)} %bitcast.core_ref, bf16[2048,768]{1,0:T(8,128)(2,1)} %desc_hbm.2, s32[1,2048]{1,0:T(1,128)} %bitcast.15, s32[1,2048]{1,0:T(1,128)} %bitcast.14, s32[1,256]{1,0:T(1,128)} %bitcast.17), custom_call_target="tpu_custom_call" | custom-call | flops 1610612736 | bytes 3145728 | tf_op jit(solution)/shard_map/pallas_call | solution.py:188
  4.1 3.3 %collective-permute-start = (f32[16,96,128]{2,1,0:T(8,128)S(1)}, f32[16,96,128]{2,1,0:T(8,128)S(1)}, u32[]{:S(2)}, u32[]{:S(2)}) collective-permute-start(f32[16,96,128]{2,1,0:T(8,128)S(1)} %get-tuple-element.24), channel_id=1, source_target_pairs={{0,8},{8,0},{1,9},{9,1},{2,10},{10,2},{3,11},{11,3},{4,12},{12,4},... | collective-permute-start | bytes 2359304 | tf_op jit(solution)/shard_map/ppermute | solution.py:255
  7.4 0.0 copy-done
  7.4 0.1 pad_add_fusion.pos_ref
  7.5 1.8 %collective-permute-done = f32[16,96,128]{2,1,0:T(8,128)S(1)} collective-permute-done((f32[16,96,128]{2,1,0:T(8,128)S(1)}, f32[16,96,128]{2,1,0:T(8,128)S(1)}, u32[]{:S(2)}, u32[]{:S(2)}) %collective-permute-start) | collective-permute-done | bytes 786464 | tf_op jit(solution)/shard_map/ppermute | solution.py:255
  9.4 1.0 %add.58 = f32[16,96,128]{2,1,0:T(8,128)} add(f32[16,96,128]{2,1,0:T(8,128)S(1)} %get-tuple-element.23, f32[16,96,128]{2,1,0:T(8,128)S(1)} %collective-permute-done) | non-fusion elementwise | flops 196608 | bytes 2359296 | tf_op jit(solution)/shard_map/add | solution.py:255
  10.3 0.1 broadcast_in_dim.42.root_ref
  10.4 5.0 %all-to-all-start = ((f32[16,96,128]{2,1,0:T(8,128)}), f32[16,96,128]{2,1,0:T(8,128)S(1)}, u32[]{:S(2)}, u32[]{:S(2)}) async-start(f32[16,96,128]{2,1,0:T(8,128)} %add.58), calls=%async_computation | async-start | bytes 1572864 | tf_op jit(solution)/shard_map/all_to_all | solution.py:201
  15.4 5.1 %shard_map.69 = (f32[16,168,128]{2,1,0:T(8,128)S(1)}, f32[16,48,128]{2,1,0:T(8,128)S(1)}, f32[16,48,128]{2,1,0:T(8,128)S(1)}, f32[16,48,128]{2,1,0:T(8,128)S(1)}, f32[16,24,128]{2,1,0:T(8,128)S(1)}) custom-call(s32[1]{0:T(128)} %bitcast.core_ref, bf16[2048,768]{1,0:T(8,128)(2,1)} %desc_hbm.2, s32[1,2048]{1,0:T(1,128)} %bitcast.16), custom_call_target="tpu_custom_call" | custom-call | flops 4831838208 | bytes 9437184 | tf_op jit(solution)/shard_map/pallas_call | solution.py:188
  20.5 0.7 collective-permute-start.3
  21.3 0.1 collective-permute-start.2
  21.4 0.4 collective-permute-start.1
  21.8 0.1 collective-permute-start.4
  21.9 2.1 %collective-permute-done.4 = f32[16,24,128]{2,1,0:T(8,128)S(1)} collective-permute-done((f32[16,24,128]{2,1,0:T(8,128)S(1)}, f32[16,24,128]{2,1,0:T(8,128)S(1)}, u32[]{:S(2)}, u32[]{:S(2)}) %collective-permute-start.4) | collective-permute-done | bytes 196640 | tf_op jit(solution)/shard_map/ppermute | solution.py:265
  24.0 0.0 collective-permute-done.3
  24.0 0.0 collective-permute-done.2
  24.0 0.0 collective-permute-done.1
  24.0 1.2 %maximum_add_fusion = f32[16,168,128]{2,1,0:T(8,128)} fusion(f32[16,168,128]{2,1,0:T(8,128)S(1)} %get-tuple-element.28, f32[16,24,128]{2,1,0:T(8,128)S(1)} %collective-permute-done.4, f32[16,48,128]{2,1,0:T(8,128)S(1)} %collective-permute-done.3, f32[16,48,128]{2,1,0:T(8,128)S(1)} %collective-permute-done.2, f32[16,48,128]{2,1,0:T(8,128)S(1)} %collective-permute-done.1), kind=kLoop, calls=%fused_computation | loop fusion | flops 1376256 | bytes 4128768 | tf_op jit(solution)/shard_map/add | solution.py:265
  25.3 2.9 %all-to-all-done = f32[16,96,128]{2,1,0:T(8,128)S(1)} async-done(((f32[16,96,128]{2,1,0:T(8,128)}), f32[16,96,128]{2,1,0:T(8,128)S(1)}, u32[]{:S(2)}, u32[]{:S(2)}) %all-to-all-start) | async-done | bytes 786464 | tf_op jit(solution)/shard_map/all_to_all | solution.py:201
  28.2 4.3 %all-to-all-start.1 = ((f32[16,168,128]{2,1,0:T(8,128)}), f32[16,168,128]{2,1,0:T(8,128)S(1)}, u32[]{:S(2)}, u32[]{:S(2)}) async-start(f32[16,168,128]{2,1,0:T(8,128)} %maximum_add_fusion), calls=%async_computation.1 | async-start | bytes 2752512 | tf_op jit(solution)/shard_map/all_to_all | solution.py:201
  32.5 7.0 %collective-permute-start.5 = (f32[96,128]{1,0:T(8,128)S(1)}, f32[96,128]{1,0:T(8,128)S(1)}, u32[]{:S(2)}, u32[]{:S(2)}) collective-permute-start(f32[96,128]{1,0:T(8,128)S(1)} %reduce_sum.18), channel_id=1, source_target_pairs={{0,4},{4,0},{1,5},{5,1},{2,6},{6,2},{3,7},{7,3},{8,12},{12,8},{9,1... | collective-permute-start | bytes 147464 | tf_op jit(solution)/shard_map/ppermute | solution.py:273
  39.5 1.5 %collective-permute-done.5 = f32[96,128]{1,0:T(8,128)S(1)} collective-permute-done((f32[96,128]{1,0:T(8,128)S(1)}, f32[96,128]{1,0:T(8,128)S(1)}, u32[]{:S(2)}, u32[]{:S(2)}) %collective-permute-start.5) | collective-permute-done | bytes 49184 | tf_op jit(solution)/shard_map/ppermute | solution.py:273
  41.0 2.9 %collective-permute-start.8 = (f32[104,128]{1,0:T(8,128)S(1)}, f32[104,128]{1,0:T(8,128)S(1)}, u32[]{:S(2)}, u32[]{:S(2)}) collective-permute-start(f32[104,128]{1,0:T(8,128)S(1)} %pad_maximum_fusion.2), channel_id=1, source_target_pairs={{0,48},{16,0},{32,16},{48,32},{1,49},{17,1},{33,17},{49,33},{2,50}... | collective-permute-start | bytes 159752 | tf_op jit(solution)/shard_map/ppermute | solution.py:271
  43.9 0.0 collective-permute-start.7
  43.9 0.4 collective-permute-start.6
  44.3 0.8 collective-permute-done.8
  45.1 3.9 %collective-permute-done.7 = f32[104,128]{1,0:T(8,128)S(1)} collective-permute-done((f32[104,128]{1,0:T(8,128)S(1)}, f32[104,128]{1,0:T(8,128)S(1)}, u32[]{:S(2)}, u32[]{:S(2)}) %collective-permute-start.7) | collective-permute-done | bytes 53280 | tf_op jit(solution)/shard_map/ppermute | solution.py:271
  49.0 0.0 collective-permute-done.6
  49.0 1.7 %all-to-all-done.1 = f32[16,168,128]{2,1,0:T(8,128)S(1)} async-done(((f32[16,168,128]{2,1,0:T(8,128)}), f32[16,168,128]{2,1,0:T(8,128)S(1)}, u32[]{:S(2)}, u32[]{:S(2)}) %all-to-all-start.1) | async-done | bytes 1376288 | tf_op jit(solution)/shard_map/all_to_all | solution.py:201
  50.7 0.1 reduce_sum.19
  50.9 7.0 %collective-permute-start.9 = (f32[96,128]{1,0:T(8,128)S(1)}, f32[96,128]{1,0:T(8,128)S(1)}, u32[]{:S(2)}, u32[]{:S(2)}) collective-permute-start(f32[96,128]{1,0:T(8,128)S(1)} %pad_maximum_fusion), channel_id=1, source_target_pairs={{0,4},{4,0},{1,5},{5,1},{2,6},{6,2},{3,7},{7,3},{8,12},{12,8},{9,1... | collective-permute-start | bytes 147464 | tf_op jit(solution)/shard_map/ppermute | solution.py:286
  57.9 1.0 broadcast_in_dim.46
  58.8 4.6 %all-to-all-start.2 = ((f32[16,96,128]{2,1,0:T(8,128)}), f32[16,96,128]{2,1,0:T(8,128)S(1)}, u32[]{:S(2)}, u32[]{:S(2)}) async-start(f32[16,96,128]{2,1,0:T(8,128)} %broadcast_in_dim.46), calls=%async_computation.2 | async-start | bytes 1572864 | tf_op jit(solution)/shard_map/all_to_all | solution.py:201
  63.4 0.0 collective-permute-done.9
  63.4 1.5 %collective-permute-start.10 = (f32[96,128]{1,0:T(8,128)S(1)}, f32[96,128]{1,0:T(8,128)S(1)}, u32[]{:S(2)}, u32[]{:S(2)}) collective-permute-start(f32[96,128]{1,0:T(8,128)S(1)} %fusion.refs_0_), channel_id=1, source_target_pairs={{0,32},{16,48},{32,0},{48,16},{1,33},{17,49},{33,1},{49,17},{2,34}... | collective-permute-start | bytes 147464 | tf_op jit(solution)/shard_map/ppermute | solution.py:271
  64.9 0.7 collective-permute-start.11
  65.6 2.5 %collective-permute-start.12 = (f32[96,128]{1,0:T(8,128)S(1)}, f32[96,128]{1,0:T(8,128)S(1)}, u32[]{:S(2)}, u32[]{:S(2)}) collective-permute-start(f32[96,128]{1,0:T(8,128)S(1)} %fusion.refs_0_), channel_id=1, source_target_pairs={{0,48},{16,0},{32,16},{48,32},{1,49},{17,1},{33,17},{49,33},{2,50}... | collective-permute-start | bytes 147464 | tf_op jit(solution)/shard_map/ppermute | solution.py:271
  68.2 0.0 collective-permute-done.10.refs_1_
  68.2 1.5 %collective-permute-done.11.refs_2_ = f32[96,128]{1,0:T(8,128)S(1)} collective-permute-done((f32[96,128]{1,0:T(8,128)S(1)}, f32[96,128]{1,0:T(8,128)S(1)}, u32[]{:S(2)}, u32[]{:S(2)}) %collective-permute-start.11) | collective-permute-done | bytes 49184 | tf_op jit(solution)/shard_map/ppermute | solution.py:271
  69.6 0.0 collective-permute-done.12.refs_3_
  69.7 0.8 shard_map.70
  70.4 3.7 %all-to-all-done.2.mine_ref = f32[16,96,128]{2,1,0:T(8,128)S(1)} async-done(((f32[16,96,128]{2,1,0:T(8,128)}), f32[16,96,128]{2,1,0:T(8,128)S(1)}, u32[]{:S(2)}, u32[]{:S(2)}) %all-to-all-start.2) | async-done | bytes 786464 | tf_op jit(solution)/shard_map/all_to_all | solution.py:201
  74.1 4.6 %collective-permute-start.13 = (f32[16,96,128]{2,1,0:T(8,128)S(1)}, f32[16,96,128]{2,1,0:T(8,128)S(1)}, u32[]{:S(2)}, u32[]{:S(2)}) collective-permute-start(f32[16,96,128]{2,1,0:T(8,128)S(1)} %all-to-all-done.2.mine_ref), channel_id=1, source_target_pairs={{0,8},{8,0},{1,9},{9,1},{2,10},{10,2},{3,11},{11,3},{4,12},{12,4},... | collective-permute-start | bytes 2359304 | tf_op jit(solution)/shard_map/ppermute | solution.py:303
  78.7 3.9 %all-to-all-start.3 = ((f32[16,48,128]{2,1,0:T(8,128)}), f32[16,48,128]{2,1,0:T(8,128)S(1)}, u32[]{:S(2)}, u32[]{:S(2)}) async-start(f32[16,48,128]{2,1,0:T(8,128)} %shard_map.70), calls=%async_computation.3 | async-start | bytes 786432 | tf_op jit(solution)/shard_map/all_to_all | solution.py:201
  82.6 0.0 collective-permute-done.13.other_ref
  82.6 2.0 %shard_map.71 = (f32[192,1536]{1,0:T(8,128)S(1)}, f32[8,192]{1,0:T(8,128)}) custom-call(s32[4]{0:T(128)S(1)} %pad_add_fusion.pos_ref, f32[16,96,128]{2,1,0:T(8,128)S(1)} %all-to-all-done.2.mine_ref, f32[16,96,128]{2,1,0:T(8,128)S(1)} %collective-permute-done.13.other_ref, f32[8,128]{1,0:T(8,128)S(1)} %broadcast_in_dim.42.root_ref), custom_call_target="tpu_custom_call" | custom-call | flops 905969664 | bytes 1769472 | tf_op jit(solution)/shard_map/pallas_call | solution.py:188
  84.5 7.1 %all-to-all-done.3.mine_ref = f32[16,48,128]{2,1,0:T(8,128)S(1)} async-done(((f32[16,48,128]{2,1,0:T(8,128)}), f32[16,48,128]{2,1,0:T(8,128)S(1)}, u32[]{:S(2)}, u32[]{:S(2)}) %all-to-all-start.3) | async-done | bytes 393248 | tf_op jit(solution)/shard_map/all_to_all | solution.py:201
  91.6 1.7 %collective-permute-start.14 = (f32[16,48,128]{2,1,0:T(8,128)S(1)}, f32[16,48,128]{2,1,0:T(8,128)S(1)}, u32[]{:S(2)}, u32[]{:S(2)}) collective-permute-start(f32[16,48,128]{2,1,0:T(8,128)S(1)} %all-to-all-done.3.mine_ref), channel_id=1, source_target_pairs={{0,8},{8,0},{1,9},{9,1},{2,10},{10,2},{3,11},{11,3},{4,12},{12,4},... | collective-permute-start | bytes 1179656 | tf_op jit(solution)/shard_map/ppermute | solution.py:313
  93.3 1.3 %collective-permute-done.14.other_ref = f32[16,48,128]{2,1,0:T(8,128)S(1)} collective-permute-done((f32[16,48,128]{2,1,0:T(8,128)S(1)}, f32[16,48,128]{2,1,0:T(8,128)S(1)}, u32[]{:S(2)}, u32[]{:S(2)}) %collective-permute-start.14) | collective-permute-done | bytes 393248 | tf_op jit(solution)/shard_map/ppermute | solution.py:313
  94.7 1.8 %shard_map.72 = f32[192,1536]{1,0:T(8,128)} custom-call(s32[4]{0:T(128)S(1)} %pad_add_fusion.pos_ref, f32[16,48,128]{2,1,0:T(8,128)S(1)} %all-to-all-done.3.mine_ref, f32[16,48,128]{2,1,0:T(8,128)S(1)} %collective-permute-done.14.other_ref, f32[192,1536]{1,0:T(8,128)S(1)} %get-tuple-element.42.cross_ref), custom_call_target="tpu_custom_call" | custom-call | flops 147456 | bytes 288 | tf_op jit(solution)/shard_map/pallas_call | solution.py:188
  (10 shorter events, 0.1 us)
Async XLA Ops:
  0.6 6.8 %copy-start = (f32[8]{0:T(128)S(1)}, f32[8]{0:T(128)}, u32[]{:S(2)}) copy-start(f32[8]{0:T(128)} %param.9) | copy-start | bytes 100
  4.1 5.2 %collective-permute-start = (f32[16,96,128]{2,1,0:T(8,128)S(1)}, f32[16,96,128]{2,1,0:T(8,128)S(1)}, u32[]{:S(2)}, u32[]{:S(2)}) collective-permute-start(f32[16,96,128]{2,1,0:T(8,128)S(1)} %get-tuple-element.24), channel_id=1, source_target_pairs={{0,8},{8,0},{1,9},{9,1},{2,10},{10,2},{3,11},{11,3},{4,12},{12,4},... | collective-permute-start | bytes 2359304 | tf_op jit(solution)/shard_map/ppermute | solution.py:255
  10.4 17.8 %all-to-all-start = ((f32[16,96,128]{2,1,0:T(8,128)}), f32[16,96,128]{2,1,0:T(8,128)S(1)}, u32[]{:S(2)}, u32[]{:S(2)}) async-start(f32[16,96,128]{2,1,0:T(8,128)} %add.58), calls=%async_computation | async-start | bytes 1572864 | tf_op jit(solution)/shard_map/all_to_all | solution.py:201
  20.5 3.5 %collective-permute-start.3 = (f32[16,48,128]{2,1,0:T(8,128)S(1)}, f32[16,48,128]{2,1,0:T(8,128)S(1)}, u32[]{:S(2)}, u32[]{:S(2)}) collective-permute-start(f32[16,48,128]{2,1,0:T(8,128)S(1)} %get-tuple-element.31), channel_id=1, source_target_pairs={{0,8},{8,0},{1,9},{9,1},{2,10},{10,2},{3,11},{11,3},{4,12},{12,4},... | collective-permute-start | bytes 1179656 | tf_op jit(solution)/shard_map/ppermute | solution.py:265
  21.3 2.8 %collective-permute-start.2 = (f32[16,48,128]{2,1,0:T(8,128)S(1)}, f32[16,48,128]{2,1,0:T(8,128)S(1)}, u32[]{:S(2)}, u32[]{:S(2)}) collective-permute-start(f32[16,48,128]{2,1,0:T(8,128)S(1)} %get-tuple-element.30), channel_id=1, source_target_pairs={{0,8},{8,0},{1,9},{9,1},{2,10},{10,2},{3,11},{11,3},{4,12},{12,4},... | collective-permute-start | bytes 1179656 | tf_op jit(solution)/shard_map/ppermute | solution.py:265
  21.4 2.7 %collective-permute-start.1 = (f32[16,48,128]{2,1,0:T(8,128)S(1)}, f32[16,48,128]{2,1,0:T(8,128)S(1)}, u32[]{:S(2)}, u32[]{:S(2)}) collective-permute-start(f32[16,48,128]{2,1,0:T(8,128)S(1)} %get-tuple-element.29), channel_id=1, source_target_pairs={{0,8},{8,0},{1,9},{9,1},{2,10},{10,2},{3,11},{11,3},{4,12},{12,4},... | collective-permute-start | bytes 1179656 | tf_op jit(solution)/shard_map/ppermute | solution.py:265
  21.8 2.2 %collective-permute-start.4 = (f32[16,24,128]{2,1,0:T(8,128)S(1)}, f32[16,24,128]{2,1,0:T(8,128)S(1)}, u32[]{:S(2)}, u32[]{:S(2)}) collective-permute-start(f32[16,24,128]{2,1,0:T(8,128)S(1)} %get-tuple-element.32), channel_id=1, source_target_pairs={{0,8},{8,0},{1,9},{9,1},{2,10},{10,2},{3,11},{11,3},{4,12},{12,4},... | collective-permute-start | bytes 589832 | tf_op jit(solution)/shard_map/ppermute | solution.py:265
  28.2 22.5 %all-to-all-start.1 = ((f32[16,168,128]{2,1,0:T(8,128)}), f32[16,168,128]{2,1,0:T(8,128)S(1)}, u32[]{:S(2)}, u32[]{:S(2)}) async-start(f32[16,168,128]{2,1,0:T(8,128)} %maximum_add_fusion), calls=%async_computation.1 | async-start | bytes 2752512 | tf_op jit(solution)/shard_map/all_to_all | solution.py:201
  32.5 8.5 %collective-permute-start.5 = (f32[96,128]{1,0:T(8,128)S(1)}, f32[96,128]{1,0:T(8,128)S(1)}, u32[]{:S(2)}, u32[]{:S(2)}) collective-permute-start(f32[96,128]{1,0:T(8,128)S(1)} %reduce_sum.18), channel_id=1, source_target_pairs={{0,4},{4,0},{1,5},{5,1},{2,6},{6,2},{3,7},{7,3},{8,12},{12,8},{9,1... | collective-permute-start | bytes 147464 | tf_op jit(solution)/shard_map/ppermute | solution.py:273
  41.0 4.1 %collective-permute-start.8 = (f32[104,128]{1,0:T(8,128)S(1)}, f32[104,128]{1,0:T(8,128)S(1)}, u32[]{:S(2)}, u32[]{:S(2)}) collective-permute-start(f32[104,128]{1,0:T(8,128)S(1)} %pad_maximum_fusion.2), channel_id=1, source_target_pairs={{0,48},{16,0},{32,16},{48,32},{1,49},{17,1},{33,17},{49,33},{2,50}... | collective-permute-start | bytes 159752 | tf_op jit(solution)/shard_map/ppermute | solution.py:271
  43.9 5.1 %collective-permute-start.7 = (f32[104,128]{1,0:T(8,128)S(1)}, f32[104,128]{1,0:T(8,128)S(1)}, u32[]{:S(2)}, u32[]{:S(2)}) collective-permute-start(f32[104,128]{1,0:T(8,128)S(1)} %pad_maximum_fusion.2), channel_id=1, source_target_pairs={{0,16},{16,32},{32,48},{48,0},{1,17},{17,33},{33,49},{49,1},{2,18}... | collective-permute-start | bytes 159752 | tf_op jit(solution)/shard_map/ppermute | solution.py:271
  43.9 5.1 %collective-permute-start.6 = (f32[104,128]{1,0:T(8,128)S(1)}, f32[104,128]{1,0:T(8,128)S(1)}, u32[]{:S(2)}, u32[]{:S(2)}) collective-permute-start(f32[104,128]{1,0:T(8,128)S(1)} %pad_maximum_fusion.2), channel_id=1, source_target_pairs={{0,32},{16,48},{32,0},{48,16},{1,33},{17,49},{33,1},{49,17},{2,34}... | collective-permute-start | bytes 159752 | tf_op jit(solution)/shard_map/ppermute | solution.py:271
  50.9 12.6 %collective-permute-start.9 = (f32[96,128]{1,0:T(8,128)S(1)}, f32[96,128]{1,0:T(8,128)S(1)}, u32[]{:S(2)}, u32[]{:S(2)}) collective-permute-start(f32[96,128]{1,0:T(8,128)S(1)} %pad_maximum_fusion), channel_id=1, source_target_pairs={{0,4},{4,0},{1,5},{5,1},{2,6},{6,2},{3,7},{7,3},{8,12},{12,8},{9,1... | collective-permute-start | bytes 147464 | tf_op jit(solution)/shard_map/ppermute | solution.py:286
  58.8 15.3 %all-to-all-start.2 = ((f32[16,96,128]{2,1,0:T(8,128)}), f32[16,96,128]{2,1,0:T(8,128)S(1)}, u32[]{:S(2)}, u32[]{:S(2)}) async-start(f32[16,96,128]{2,1,0:T(8,128)} %broadcast_in_dim.46), calls=%async_computation.2 | async-start | bytes 1572864 | tf_op jit(solution)/shard_map/all_to_all | solution.py:201
  63.4 4.7 %collective-permute-start.10 = (f32[96,128]{1,0:T(8,128)S(1)}, f32[96,128]{1,0:T(8,128)S(1)}, u32[]{:S(2)}, u32[]{:S(2)}) collective-permute-start(f32[96,128]{1,0:T(8,128)S(1)} %fusion.refs_0_), channel_id=1, source_target_pairs={{0,32},{16,48},{32,0},{48,16},{1,33},{17,49},{33,1},{49,17},{2,34}... | collective-permute-start | bytes 147464 | tf_op jit(solution)/shard_map/ppermute | solution.py:271
  64.9 4.7 %collective-permute-start.11 = (f32[96,128]{1,0:T(8,128)S(1)}, f32[96,128]{1,0:T(8,128)S(1)}, u32[]{:S(2)}, u32[]{:S(2)}) collective-permute-start(f32[96,128]{1,0:T(8,128)S(1)} %fusion.refs_0_), channel_id=1, source_target_pairs={{0,16},{16,32},{32,48},{48,0},{1,17},{17,33},{33,49},{49,1},{2,18}... | collective-permute-start | bytes 147464 | tf_op jit(solution)/shard_map/ppermute | solution.py:271
  65.6 4.0 %collective-permute-start.12 = (f32[96,128]{1,0:T(8,128)S(1)}, f32[96,128]{1,0:T(8,128)S(1)}, u32[]{:S(2)}, u32[]{:S(2)}) collective-permute-start(f32[96,128]{1,0:T(8,128)S(1)} %fusion.refs_0_), channel_id=1, source_target_pairs={{0,48},{16,0},{32,16},{48,32},{1,49},{17,1},{33,17},{49,33},{2,50}... | collective-permute-start | bytes 147464 | tf_op jit(solution)/shard_map/ppermute | solution.py:271
  74.1 8.5 %collective-permute-start.13 = (f32[16,96,128]{2,1,0:T(8,128)S(1)}, f32[16,96,128]{2,1,0:T(8,128)S(1)}, u32[]{:S(2)}, u32[]{:S(2)}) collective-permute-start(f32[16,96,128]{2,1,0:T(8,128)S(1)} %all-to-all-done.2.mine_ref), channel_id=1, source_target_pairs={{0,8},{8,0},{1,9},{9,1},{2,10},{10,2},{3,11},{11,3},{4,12},{12,4},... | collective-permute-start | bytes 2359304 | tf_op jit(solution)/shard_map/ppermute | solution.py:303
  78.7 13.0 %all-to-all-start.3 = ((f32[16,48,128]{2,1,0:T(8,128)}), f32[16,48,128]{2,1,0:T(8,128)S(1)}, u32[]{:S(2)}, u32[]{:S(2)}) async-start(f32[16,48,128]{2,1,0:T(8,128)} %shard_map.70), calls=%async_computation.3 | async-start | bytes 786432 | tf_op jit(solution)/shard_map/all_to_all | solution.py:201
  91.6 3.1 %collective-permute-start.14 = (f32[16,48,128]{2,1,0:T(8,128)S(1)}, f32[16,48,128]{2,1,0:T(8,128)S(1)}, u32[]{:S(2)}, u32[]{:S(2)}) collective-permute-start(f32[16,48,128]{2,1,0:T(8,128)S(1)} %all-to-all-done.3.mine_ref), channel_id=1, source_target_pairs={{0,8},{8,0},{1,9},{9,1},{2,10},{10,2},{3,11},{11,3},{4,12},{12,4},... | collective-permute-start | bytes 1179656 | tf_op jit(solution)/shard_map/ppermute | solution.py:313

commit v11 on v10

--- a/solution.py
+++ b/solution.py
@@ -201,6 +201,17 @@
     return lax.all_to_all(flat, axes, 0, 0, tiled=True).reshape(values.shape)
 
 
+def rows_kernel(scale, from_ref, *refs):
+    out_ref = refs[-1]
+    total, root = 0.0, 0.0
+    for k, ref in enumerate(refs[:-1]):
+        total = total + ref[:96]
+        root = root + jnp.where(from_ref[k] == 1, ref[96:], 0.0)
+    rows = (total.reshape(12, 8, LANES) * (root * scale)).reshape(96, LANES)
+    for k in range(16):
+        out_ref[k] = rows
+
+
 def bands_kernel(owner_ref, *refs):
     owner, out_ref = owner_ref[0], refs[-1]
     total = refs[0][...]
@@ -275,14 +286,21 @@
     got = [(rooted, l)]
     for k in (2, 1, 3):
         got.append((along_l(rooted, k), (l - k) % 4))
-    root_here = sum(jnp.where(source == part, value[96:], 0.0) for value, source in got)
     scale = 1.0 / math.sqrt(atoms * n_dev / configs)
-    sums = sum(value[:96] for value, _ in got).reshape(12, 8, LANES) * (root_here * scale)
+    (sums,) = call(
+        functools.partial(rows_kernel, scale),
+        [tiles(12)],
+        [jnp.stack([source == part for _, source in got]).astype(jnp.int32)] + [value for value, _ in got],
+        (),
+        pltpu.VMEM,
+        8 << 20,
+        1 << 20,
+    )
     sums, plane_g = lax.optimization_barrier((sums, plane_g))
     def of_species(which):
         return jnp.concatenate([lax.dynamic_slice_in_dim(plane_g, which * 72, 72), plane_g[144:]])
 
-    mine_s = exchange(jnp.broadcast_to(sums.reshape(1, 96, LANES), (16, 96, LANES)), ("x", "y"))
+    mine_s = exchange(sums, ("x", "y"))
     grams = of_species(kind) + lax.ppermute(of_species(1 - kind), "h", flip)
     (spread,) = call(
         bands_kernel,

time: 96.9 us -> 97.4 us (level)
  waiting for transfers between devices: 28.4 us -> 25.1 us
  starting transfers between devices: 50.7 us -> 53.9 us
  Pallas kernels: 13.1 us -> 14.6 us
    ppermute x6, waiting for transfers between devices: 6.18 us -> 3.63 us  [along_l(): return lax.ppermute(value, 'l', [(i, (i + k) % 4) for i in range(4)])]
    ppermute x6, starting transfers between devices: 7.99 us -> 9.52 us  [along_l(): return lax.ppermute(value, 'l', [(i, (i + k) % 4) for i in range(4)])]
    pallas_call x5 -> x6, Pallas kernels: 13.1 us -> 14.6 us  [call(): pl.pallas_call(kernel, out_shape=outs, in_specs=[smem] + [pl.BlockSpec(me...]
  transfers between devices with their start and end apart: 19 -> 19, of which waited for: 11 -> 12; matrix products, arithmetic and copies ran while one was open for 2% -> 1% of each run, Pallas kernels for 8% -> 10%
where the time goes in v11:
time: 97.4 us; the launch traced here: 96.9 us
  starting transfers between devices  53.9 us (55%)
  waiting for transfers between devices  25.1 us (26%)
  Pallas kernels  14.6 us (15%)
  other arithmetic  2.5 us (3%)
    all_to_all x4, starting transfers between devices, exchange(): return lax.all_to_all(flat, axes, 0, 0, tiled=True).reshape(values.shape)  18.5 us
    all_to_all x4, waiting for transfers between devices, exchange(): return lax.all_to_all(flat, axes, 0, 0, tiled=True).reshape(values.shape)  14.6 us
    pallas_call x6, Pallas kernels, call(): pl.pallas_call(kernel, out_shape=outs, in_specs=[smem] + [pl.BlockSpec(me...  14.6 us
    ppermute x6, starting transfers between devices, along_l(): return lax.ppermute(value, 'l', [(i, (i + k) % 4) for i in range(4)])  9.52 us
    ppermute x1, starting transfers between devices, shards(): plane_s = plane_s + lax.ppermute(plane_s, 'h', flip)  7 us
    ppermute x1, starting transfers between devices, shards(): grams = of_species(kind) + lax.ppermute(of_species(1 - kind), 'h', flip)  7 us
    ppermute x1, starting transfers between devices, shards(): lax.ppermute(mine_s, 'c', flip)  5.42 us
    ppermute x6, waiting for transfers between devices, along_l(): return lax.ppermute(value, 'l', [(i, (i + k) % 4) for i in range(4)])  3.63 us
  transfers between devices with their start and end apart: 19, of which 12 were waited for; matrix products, arithmetic and copies ran while one was open for 1% of the time, Pallas kernels for 10%

profile of v11, /device:TPU:1, one launch (start us, length us, event | category | flops | bytes accessed | tf_op | source)
XLA Modules:
  0.0 96.9 jit_solution(5177464471760262697)
XLA Ops:
  0.6 0.0 copy-start
  0.6 3.5 %shard_map.68 = (f32[16,96,128]{2,1,0:T(8,128)S(1)}, f32[16,96,128]{2,1,0:T(8,128)S(1)}) custom-call(s32[1]{0:T(128)} %bitcast.core_ref, bf16[2048,768]{1,0:T(8,128)(2,1)} %desc_hbm.2, s32[1,2048]{1,0:T(1,128)} %bitcast.13, s32[1,2048]{1,0:T(1,128)} %bitcast.12, s32[1,256]{1,0:T(1,128)} %bitcast.15), custom_call_target="tpu_custom_call" | custom-call | flops 1610612736 | bytes 3145728 | tf_op jit(solution)/shard_map/pallas_call | solution.py:188
  4.1 3.3 %collective-permute-start = (f32[16,96,128]{2,1,0:T(8,128)S(1)}, f32[16,96,128]{2,1,0:T(8,128)S(1)}, u32[]{:S(2)}, u32[]{:S(2)}) collective-permute-start(f32[16,96,128]{2,1,0:T(8,128)S(1)} %get-tuple-element.24), channel_id=1, source_target_pairs={{0,8},{8,0},{1,9},{9,1},{2,10},{10,2},{3,11},{11,3},{4,12},{12,4},... | collective-permute-start | bytes 2359304 | tf_op jit(solution)/shard_map/ppermute | solution.py:266
  7.4 0.0 copy-done
  7.4 0.1 pad_add_fusion.pos_ref
  7.5 1.8 %collective-permute-done = f32[16,96,128]{2,1,0:T(8,128)S(1)} collective-permute-done((f32[16,96,128]{2,1,0:T(8,128)S(1)}, f32[16,96,128]{2,1,0:T(8,128)S(1)}, u32[]{:S(2)}, u32[]{:S(2)}) %collective-permute-start) | collective-permute-done | bytes 786464 | tf_op jit(solution)/shard_map/ppermute | solution.py:266
  9.4 1.0 add.40
  10.3 0.1 broadcast_in_dim.27.root_ref
  10.4 5.0 %all-to-all-start = ((f32[16,96,128]{2,1,0:T(8,128)}), f32[16,96,128]{2,1,0:T(8,128)S(1)}, u32[]{:S(2)}, u32[]{:S(2)}) async-start(f32[16,96,128]{2,1,0:T(8,128)} %add.40), calls=%async_computation | async-start | bytes 1572864 | tf_op jit(solution)/shard_map/all_to_all | solution.py:201
  15.4 5.1 %shard_map.69 = (f32[16,168,128]{2,1,0:T(8,128)S(1)}, f32[16,48,128]{2,1,0:T(8,128)S(1)}, f32[16,48,128]{2,1,0:T(8,128)S(1)}, f32[16,48,128]{2,1,0:T(8,128)S(1)}, f32[16,24,128]{2,1,0:T(8,128)S(1)}) custom-call(s32[1]{0:T(128)} %bitcast.core_ref, bf16[2048,768]{1,0:T(8,128)(2,1)} %desc_hbm.2, s32[1,2048]{1,0:T(1,128)} %bitcast.14), custom_call_target="tpu_custom_call" | custom-call | flops 4831838208 | bytes 9437184 | tf_op jit(solution)/shard_map/pallas_call | solution.py:188
  20.5 0.7 collective-permute-start.3
  21.3 0.1 collective-permute-start.2
  21.4 0.4 collective-permute-start.1
  21.8 0.1 collective-permute-start.4
  21.9 2.1 %collective-permute-done.4 = f32[16,24,128]{2,1,0:T(8,128)S(1)} collective-permute-done((f32[16,24,128]{2,1,0:T(8,128)S(1)}, f32[16,24,128]{2,1,0:T(8,128)S(1)}, u32[]{:S(2)}, u32[]{:S(2)}) %collective-permute-start.4) | collective-permute-done | bytes 196640 | tf_op jit(solution)/shard_map/ppermute | solution.py:276
  24.0 0.0 collective-permute-done.3
  24.0 0.0 collective-permute-done.2
  24.0 0.0 collective-permute-done.1
  24.0 1.2 %maximum_add_fusion = f32[16,168,128]{2,1,0:T(8,128)} fusion(f32[16,168,128]{2,1,0:T(8,128)S(1)} %get-tuple-element.28, f32[16,24,128]{2,1,0:T(8,128)S(1)} %collective-permute-done.4, f32[16,48,128]{2,1,0:T(8,128)S(1)} %collective-permute-done.3, f32[16,48,128]{2,1,0:T(8,128)S(1)} %collective-permute-done.2, f32[16,48,128]{2,1,0:T(8,128)S(1)} %collective-permute-done.1), kind=kLoop, calls=%fused_computation | loop fusion | flops 1376256 | bytes 4128768 | tf_op jit(solution)/shard_map/add | solution.py:276
  25.3 2.9 %all-to-all-done = f32[16,96,128]{2,1,0:T(8,128)S(1)} async-done(((f32[16,96,128]{2,1,0:T(8,128)}), f32[16,96,128]{2,1,0:T(8,128)S(1)}, u32[]{:S(2)}, u32[]{:S(2)}) %all-to-all-start) | async-done | bytes 786464 | tf_op jit(solution)/shard_map/all_to_all | solution.py:201
  28.2 4.3 %all-to-all-start.1 = ((f32[16,168,128]{2,1,0:T(8,128)}), f32[16,168,128]{2,1,0:T(8,128)S(1)}, u32[]{:S(2)}, u32[]{:S(2)}) async-start(f32[16,168,128]{2,1,0:T(8,128)} %maximum_add_fusion), calls=%async_computation.1 | async-start | bytes 2752512 | tf_op jit(solution)/shard_map/all_to_all | solution.py:201
  32.5 7.0 %collective-permute-start.5 = (f32[96,128]{1,0:T(8,128)S(1)}, f32[96,128]{1,0:T(8,128)S(1)}, u32[]{:S(2)}, u32[]{:S(2)}) collective-permute-start(f32[96,128]{1,0:T(8,128)S(1)} %reduce_sum.18), channel_id=1, source_target_pairs={{0,4},{4,0},{1,5},{5,1},{2,6},{6,2},{3,7},{7,3},{8,12},{12,8},{9,1... | collective-permute-start | bytes 147464 | tf_op jit(solution)/shard_map/ppermute | solution.py:284
  39.5 1.5 %collective-permute-done.5 = f32[96,128]{1,0:T(8,128)S(1)} collective-permute-done((f32[96,128]{1,0:T(8,128)S(1)}, f32[96,128]{1,0:T(8,128)S(1)}, u32[]{:S(2)}, u32[]{:S(2)}) %collective-permute-start.5) | collective-permute-done | bytes 49184 | tf_op jit(solution)/shard_map/ppermute | solution.py:284
  41.0 1.5 %collective-permute-start.6 = (f32[104,128]{1,0:T(8,128)S(1)}, f32[104,128]{1,0:T(8,128)S(1)}, u32[]{:S(2)}, u32[]{:S(2)}) collective-permute-start(f32[104,128]{1,0:T(8,128)S(1)} %pad_maximum_fusion.2.refs_0_), channel_id=1, source_target_pairs={{0,32},{16,48},{32,0},{48,16},{1,33},{17,49},{33,1},{49,17},{2,34}... | collective-permute-start | bytes 159752 | tf_op jit(solution)/shard_map/ppermute | solution.py:282
  42.5 1.7 %collective-permute-start.7 = (f32[104,128]{1,0:T(8,128)S(1)}, f32[104,128]{1,0:T(8,128)S(1)}, u32[]{:S(2)}, u32[]{:S(2)}) collective-permute-start(f32[104,128]{1,0:T(8,128)S(1)} %pad_maximum_fusion.2.refs_0_), channel_id=1, source_target_pairs={{0,16},{16,32},{32,48},{48,0},{1,17},{17,33},{33,49},{49,1},{2,18}... | collective-permute-start | bytes 159752 | tf_op jit(solution)/shard_map/ppermute | solution.py:282
  44.2 1.6 %collective-permute-start.8 = (f32[104,128]{1,0:T(8,128)S(1)}, f32[104,128]{1,0:T(8,128)S(1)}, u32[]{:S(2)}, u32[]{:S(2)}) collective-permute-start(f32[104,128]{1,0:T(8,128)S(1)} %pad_maximum_fusion.2.refs_0_), channel_id=1, source_target_pairs={{0,48},{16,0},{32,16},{48,32},{1,49},{17,1},{33,17},{49,33},{2,50}... | collective-permute-start | bytes 159752 | tf_op jit(solution)/shard_map/ppermute | solution.py:282
  45.8 0.1 add_convert_fusion.from_ref
  45.9 0.5 collective-permute-done.6.refs_1_
  46.3 1.3 %collective-permute-done.7.refs_2_ = f32[104,128]{1,0:T(8,128)S(1)} collective-permute-done((f32[104,128]{1,0:T(8,128)S(1)}, f32[104,128]{1,0:T(8,128)S(1)}, u32[]{:S(2)}, u32[]{:S(2)}) %collective-permute-start.7) | collective-permute-done | bytes 53280 | tf_op jit(solution)/shard_map/ppermute | solution.py:282
  47.6 0.4 collective-permute-done.8.refs_3_
  48.0 1.5 %shard_map.70 = f32[16,96,128]{2,1,0:T(8,128)} custom-call(s32[4]{0:T(128)S(1)} %add_convert_fusion.from_ref, f32[104,128]{1,0:T(8,128)S(1)} %pad_maximum_fusion.2.refs_0_, f32[104,128]{1,0:T(8,128)S(1)} %collective-permute-done.6.refs_1_, f32[104,128]{1,0:T(8,128)S(1)} %collective-permute-done.7.refs_2_, f32[104,128]{1,0:T(8,128)S(1)} %collective-permute-done.8.refs_3_), custom_call_target="tpu_custom_call" | custom-call | flops 1048576 | bytes 2048 | tf_op jit(solution)/shard_map/pallas_call | solution.py:188
  49.5 1.2 %all-to-all-done.1 = f32[16,168,128]{2,1,0:T(8,128)S(1)} async-done(((f32[16,168,128]{2,1,0:T(8,128)}), f32[16,168,128]{2,1,0:T(8,128)S(1)}, u32[]{:S(2)}, u32[]{:S(2)}) %all-to-all-start.1) | async-done | bytes 1376288 | tf_op jit(solution)/shard_map/all_to_all | solution.py:201
  50.7 0.1 reduce_sum.19
  50.9 7.0 %collective-permute-start.9 = (f32[96,128]{1,0:T(8,128)S(1)}, f32[96,128]{1,0:T(8,128)S(1)}, u32[]{:S(2)}, u32[]{:S(2)}) collective-permute-start(f32[96,128]{1,0:T(8,128)S(1)} %pad_maximum_fusion), channel_id=1, source_target_pairs={{0,4},{4,0},{1,5},{5,1},{2,6},{6,2},{3,7},{7,3},{8,12},{12,8},{9,1... | collective-permute-start | bytes 147464 | tf_op jit(solution)/shard_map/ppermute | solution.py:304
  57.9 4.6 %all-to-all-start.2 = ((f32[16,96,128]{2,1,0:T(8,128)}), f32[16,96,128]{2,1,0:T(8,128)S(1)}, u32[]{:S(2)}, u32[]{:S(2)}) async-start(f32[16,96,128]{2,1,0:T(8,128)} %shard_map.70), calls=%async_computation.2 | async-start | bytes 1572864 | tf_op jit(solution)/shard_map/all_to_all | solution.py:201
  62.5 0.0 collective-permute-done.9
  62.5 1.5 %collective-permute-start.10 = (f32[96,128]{1,0:T(8,128)S(1)}, f32[96,128]{1,0:T(8,128)S(1)}, u32[]{:S(2)}, u32[]{:S(2)}) collective-permute-start(f32[96,128]{1,0:T(8,128)S(1)} %fusion.refs_0_), channel_id=1, source_target_pairs={{0,32},{16,48},{32,0},{48,16},{1,33},{17,49},{33,1},{49,17},{2,34}... | collective-permute-start | bytes 147464 | tf_op jit(solution)/shard_map/ppermute | solution.py:282
  64.0 1.1 %collective-permute-start.11 = (f32[96,128]{1,0:T(8,128)S(1)}, f32[96,128]{1,0:T(8,128)S(1)}, u32[]{:S(2)}, u32[]{:S(2)}) collective-permute-start(f32[96,128]{1,0:T(8,128)S(1)} %fusion.refs_0_), channel_id=1, source_target_pairs={{0,16},{16,32},{32,48},{48,0},{1,17},{17,33},{33,49},{49,1},{2,18}... | collective-permute-start | bytes 147464 | tf_op jit(solution)/shard_map/ppermute | solution.py:282
  65.0 2.2 %collective-permute-start.12 = (f32[96,128]{1,0:T(8,128)S(1)}, f32[96,128]{1,0:T(8,128)S(1)}, u32[]{:S(2)}, u32[]{:S(2)}) collective-permute-start(f32[96,128]{1,0:T(8,128)S(1)} %fusion.refs_0_), channel_id=1, source_target_pairs={{0,48},{16,0},{32,16},{48,32},{1,49},{17,1},{33,17},{49,33},{2,50}... | collective-permute-start | bytes 147464 | tf_op jit(solution)/shard_map/ppermute | solution.py:282
  67.2 0.0 collective-permute-done.10.refs_1_
  67.2 1.5 %collective-permute-done.11.refs_2_ = f32[96,128]{1,0:T(8,128)S(1)} collective-permute-done((f32[96,128]{1,0:T(8,128)S(1)}, f32[96,128]{1,0:T(8,128)S(1)}, u32[]{:S(2)}, u32[]{:S(2)}) %collective-permute-start.11) | collective-permute-done | bytes 49184 | tf_op jit(solution)/shard_map/ppermute | solution.py:282
  68.7 0.0 collective-permute-done.12.refs_3_
  68.7 0.8 shard_map.71
  69.5 3.4 %all-to-all-done.2.mine_ref = f32[16,96,128]{2,1,0:T(8,128)S(1)} async-done(((f32[16,96,128]{2,1,0:T(8,128)}), f32[16,96,128]{2,1,0:T(8,128)S(1)}, u32[]{:S(2)}, u32[]{:S(2)}) %all-to-all-start.2) | async-done | bytes 786464 | tf_op jit(solution)/shard_map/all_to_all | solution.py:201
  72.9 5.4 %collective-permute-start.13 = (f32[16,96,128]{2,1,0:T(8,128)S(1)}, f32[16,96,128]{2,1,0:T(8,128)S(1)}, u32[]{:S(2)}, u32[]{:S(2)}) collective-permute-start(f32[16,96,128]{2,1,0:T(8,128)S(1)} %all-to-all-done.2.mine_ref), channel_id=1, source_target_pairs={{0,8},{8,0},{1,9},{9,1},{2,10},{10,2},{3,11},{11,3},{4,12},{12,4},... | collective-permute-start | bytes 2359304 | tf_op jit(solution)/shard_map/ppermute | solution.py:321
  78.3 4.6 %all-to-all-start.3 = ((f32[16,48,128]{2,1,0:T(8,128)}), f32[16,48,128]{2,1,0:T(8,128)S(1)}, u32[]{:S(2)}, u32[]{:S(2)}) async-start(f32[16,48,128]{2,1,0:T(8,128)} %shard_map.71), calls=%async_computation.3 | async-start | bytes 786432 | tf_op jit(solution)/shard_map/all_to_all | solution.py:201
  83.0 0.0 collective-permute-done.13.other_ref
  83.0 2.0 %shard_map.72 = (f32[192,1536]{1,0:T(8,128)S(1)}, f32[8,192]{1,0:T(8,128)}) custom-call(s32[4]{0:T(128)S(1)} %pad_add_fusion.pos_ref, f32[16,96,128]{2,1,0:T(8,128)S(1)} %all-to-all-done.2.mine_ref, f32[16,96,128]{2,1,0:T(8,128)S(1)} %collective-permute-done.13.other_ref, f32[8,128]{1,0:T(8,128)S(1)} %broadcast_in_dim.27.root_ref), custom_call_target="tpu_custom_call" | custom-call | flops 905969664 | bytes 1769472 | tf_op jit(solution)/shard_map/pallas_call | solution.py:188
  85.0 7.1 %all-to-all-done.3.mine_ref = f32[16,48,128]{2,1,0:T(8,128)S(1)} async-done(((f32[16,48,128]{2,1,0:T(8,128)}), f32[16,48,128]{2,1,0:T(8,128)S(1)}, u32[]{:S(2)}, u32[]{:S(2)}) %all-to-all-start.3) | async-done | bytes 393248 | tf_op jit(solution)/shard_map/all_to_all | solution.py:201
  92.1 1.7 %collective-permute-start.14 = (f32[16,48,128]{2,1,0:T(8,128)S(1)}, f32[16,48,128]{2,1,0:T(8,128)S(1)}, u32[]{:S(2)}, u32[]{:S(2)}) collective-permute-start(f32[16,48,128]{2,1,0:T(8,128)S(1)} %all-to-all-done.3.mine_ref), channel_id=1, source_target_pairs={{0,8},{8,0},{1,9},{9,1},{2,10},{10,2},{3,11},{11,3},{4,12},{12,4},... | collective-permute-start | bytes 1179656 | tf_op jit(solution)/shard_map/ppermute | solution.py:331
  93.8 1.3 %collective-permute-done.14.other_ref = f32[16,48,128]{2,1,0:T(8,128)S(1)} collective-permute-done((f32[16,48,128]{2,1,0:T(8,128)S(1)}, f32[16,48,128]{2,1,0:T(8,128)S(1)}, u32[]{:S(2)}, u32[]{:S(2)}) %collective-permute-start.14) | collective-permute-done | bytes 393248 | tf_op jit(solution)/shard_map/ppermute | solution.py:331
  95.1 1.8 %shard_map.73 = f32[192,1536]{1,0:T(8,128)} custom-call(s32[4]{0:T(128)S(1)} %pad_add_fusion.pos_ref, f32[16,48,128]{2,1,0:T(8,128)S(1)} %all-to-all-done.3.mine_ref, f32[16,48,128]{2,1,0:T(8,128)S(1)} %collective-permute-done.14.other_ref, f32[192,1536]{1,0:T(8,128)S(1)} %get-tuple-element.42.cross_ref), custom_call_target="tpu_custom_call" | custom-call | flops 147456 | bytes 288 | tf_op jit(solution)/shard_map/pallas_call | solution.py:188
  (8 shorter events, 0.1 us)
Async XLA Ops:
  0.6 6.8 %copy-start = (f32[8]{0:T(128)S(1)}, f32[8]{0:T(128)}, u32[]{:S(2)}) copy-start(f32[8]{0:T(128)} %param.9) | copy-start | bytes 100
  4.1 5.2 %collective-permute-start = (f32[16,96,128]{2,1,0:T(8,128)S(1)}, f32[16,96,128]{2,1,0:T(8,128)S(1)}, u32[]{:S(2)}, u32[]{:S(2)}) collective-permute-start(f32[16,96,128]{2,1,0:T(8,128)S(1)} %get-tuple-element.24), channel_id=1, source_target_pairs={{0,8},{8,0},{1,9},{9,1},{2,10},{10,2},{3,11},{11,3},{4,12},{12,4},... | collective-permute-start | bytes 2359304 | tf_op jit(solution)/shard_map/ppermute | solution.py:266
  10.4 17.8 %all-to-all-start = ((f32[16,96,128]{2,1,0:T(8,128)}), f32[16,96,128]{2,1,0:T(8,128)S(1)}, u32[]{:S(2)}, u32[]{:S(2)}) async-start(f32[16,96,128]{2,1,0:T(8,128)} %add.40), calls=%async_computation | async-start | bytes 1572864 | tf_op jit(solution)/shard_map/all_to_all | solution.py:201
  20.5 3.5 %collective-permute-start.3 = (f32[16,48,128]{2,1,0:T(8,128)S(1)}, f32[16,48,128]{2,1,0:T(8,128)S(1)}, u32[]{:S(2)}, u32[]{:S(2)}) collective-permute-start(f32[16,48,128]{2,1,0:T(8,128)S(1)} %get-tuple-element.31), channel_id=1, source_target_pairs={{0,8},{8,0},{1,9},{9,1},{2,10},{10,2},{3,11},{11,3},{4,12},{12,4},... | collective-permute-start | bytes 1179656 | tf_op jit(solution)/shard_map/ppermute | solution.py:276
  21.3 2.8 %collective-permute-start.2 = (f32[16,48,128]{2,1,0:T(8,128)S(1)}, f32[16,48,128]{2,1,0:T(8,128)S(1)}, u32[]{:S(2)}, u32[]{:S(2)}) collective-permute-start(f32[16,48,128]{2,1,0:T(8,128)S(1)} %get-tuple-element.30), channel_id=1, source_target_pairs={{0,8},{8,0},{1,9},{9,1},{2,10},{10,2},{3,11},{11,3},{4,12},{12,4},... | collective-permute-start | bytes 1179656 | tf_op jit(solution)/shard_map/ppermute | solution.py:276
  21.4 2.7 %collective-permute-start.1 = (f32[16,48,128]{2,1,0:T(8,128)S(1)}, f32[16,48,128]{2,1,0:T(8,128)S(1)}, u32[]{:S(2)}, u32[]{:S(2)}) collective-permute-start(f32[16,48,128]{2,1,0:T(8,128)S(1)} %get-tuple-element.29), channel_id=1, source_target_pairs={{0,8},{8,0},{1,9},{9,1},{2,10},{10,2},{3,11},{11,3},{4,12},{12,4},... | collective-permute-start | bytes 1179656 | tf_op jit(solution)/shard_map/ppermute | solution.py:276
  21.8 2.2 %collective-permute-start.4 = (f32[16,24,128]{2,1,0:T(8,128)S(1)}, f32[16,24,128]{2,1,0:T(8,128)S(1)}, u32[]{:S(2)}, u32[]{:S(2)}) collective-permute-start(f32[16,24,128]{2,1,0:T(8,128)S(1)} %get-tuple-element.32), channel_id=1, source_target_pairs={{0,8},{8,0},{1,9},{9,1},{2,10},{10,2},{3,11},{11,3},{4,12},{12,4},... | collective-permute-start | bytes 589832 | tf_op jit(solution)/shard_map/ppermute | solution.py:276
  28.2 22.5 %all-to-all-start.1 = ((f32[16,168,128]{2,1,0:T(8,128)}), f32[16,168,128]{2,1,0:T(8,128)S(1)}, u32[]{:S(2)}, u32[]{:S(2)}) async-start(f32[16,168,128]{2,1,0:T(8,128)} %maximum_add_fusion), calls=%async_computation.1 | async-start | bytes 2752512 | tf_op jit(solution)/shard_map/all_to_all | solution.py:201
  32.5 8.5 %collective-permute-start.5 = (f32[96,128]{1,0:T(8,128)S(1)}, f32[96,128]{1,0:T(8,128)S(1)}, u32[]{:S(2)}, u32[]{:S(2)}) collective-permute-start(f32[96,128]{1,0:T(8,128)S(1)} %reduce_sum.18), channel_id=1, source_target_pairs={{0,4},{4,0},{1,5},{5,1},{2,6},{6,2},{3,7},{7,3},{8,12},{12,8},{9,1... | collective-permute-start | bytes 147464 | tf_op jit(solution)/shard_map/ppermute | solution.py:284
  41.0 5.4 %collective-permute-start.6 = (f32[104,128]{1,0:T(8,128)S(1)}, f32[104,128]{1,0:T(8,128)S(1)}, u32[]{:S(2)}, u32[]{:S(2)}) collective-permute-start(f32[104,128]{1,0:T(8,128)S(1)} %pad_maximum_fusion.2.refs_0_), channel_id=1, source_target_pairs={{0,32},{16,48},{32,0},{48,16},{1,33},{17,49},{33,1},{49,17},{2,34}... | collective-permute-start | bytes 159752 | tf_op jit(solution)/shard_map/ppermute | solution.py:282
  42.5 5.1 %collective-permute-start.7 = (f32[104,128]{1,0:T(8,128)S(1)}, f32[104,128]{1,0:T(8,128)S(1)}, u32[]{:S(2)}, u32[]{:S(2)}) collective-permute-start(f32[104,128]{1,0:T(8,128)S(1)} %pad_maximum_fusion.2.refs_0_), channel_id=1, source_target_pairs={{0,16},{16,32},{32,48},{48,0},{1,17},{17,33},{33,49},{49,1},{2,18}... | collective-permute-start | bytes 159752 | tf_op jit(solution)/shard_map/ppermute | solution.py:282
  44.2 3.9 %collective-permute-start.8 = (f32[104,128]{1,0:T(8,128)S(1)}, f32[104,128]{1,0:T(8,128)S(1)}, u32[]{:S(2)}, u32[]{:S(2)}) collective-permute-start(f32[104,128]{1,0:T(8,128)S(1)} %pad_maximum_fusion.2.refs_0_), channel_id=1, source_target_pairs={{0,48},{16,0},{32,16},{48,32},{1,49},{17,1},{33,17},{49,33},{2,50}... | collective-permute-start | bytes 159752 | tf_op jit(solution)/shard_map/ppermute | solution.py:282
  50.9 11.6 %collective-permute-start.9 = (f32[96,128]{1,0:T(8,128)S(1)}, f32[96,128]{1,0:T(8,128)S(1)}, u32[]{:S(2)}, u32[]{:S(2)}) collective-permute-start(f32[96,128]{1,0:T(8,128)S(1)} %pad_maximum_fusion), channel_id=1, source_target_pairs={{0,4},{4,0},{1,5},{5,1},{2,6},{6,2},{3,7},{7,3},{8,12},{12,8},{9,1... | collective-permute-start | bytes 147464 | tf_op jit(solution)/shard_map/ppermute | solution.py:304
  57.9 15.1 %all-to-all-start.2 = ((f32[16,96,128]{2,1,0:T(8,128)}), f32[16,96,128]{2,1,0:T(8,128)S(1)}, u32[]{:S(2)}, u32[]{:S(2)}) async-start(f32[16,96,128]{2,1,0:T(8,128)} %shard_map.70), calls=%async_computation.2 | async-start | bytes 1572864 | tf_op jit(solution)/shard_map/all_to_all | solution.py:201
  62.5 4.7 %collective-permute-start.10 = (f32[96,128]{1,0:T(8,128)S(1)}, f32[96,128]{1,0:T(8,128)S(1)}, u32[]{:S(2)}, u32[]{:S(2)}) collective-permute-start(f32[96,128]{1,0:T(8,128)S(1)} %fusion.refs_0_), channel_id=1, source_target_pairs={{0,32},{16,48},{32,0},{48,16},{1,33},{17,49},{33,1},{49,17},{2,34}... | collective-permute-start | bytes 147464 | tf_op jit(solution)/shard_map/ppermute | solution.py:282
  64.0 4.7 %collective-permute-start.11 = (f32[96,128]{1,0:T(8,128)S(1)}, f32[96,128]{1,0:T(8,128)S(1)}, u32[]{:S(2)}, u32[]{:S(2)}) collective-permute-start(f32[96,128]{1,0:T(8,128)S(1)} %fusion.refs_0_), channel_id=1, source_target_pairs={{0,16},{16,32},{32,48},{48,0},{1,17},{17,33},{33,49},{49,1},{2,18}... | collective-permute-start | bytes 147464 | tf_op jit(solution)/shard_map/ppermute | solution.py:282
  65.0 3.7 %collective-permute-start.12 = (f32[96,128]{1,0:T(8,128)S(1)}, f32[96,128]{1,0:T(8,128)S(1)}, u32[]{:S(2)}, u32[]{:S(2)}) collective-permute-start(f32[96,128]{1,0:T(8,128)S(1)} %fusion.refs_0_), channel_id=1, source_target_pairs={{0,48},{16,0},{32,16},{48,32},{1,49},{17,1},{33,17},{49,33},{2,50}... | collective-permute-start | bytes 147464 | tf_op jit(solution)/shard_map/ppermute | solution.py:282
  72.9 10.1 %collective-permute-start.13 = (f32[16,96,128]{2,1,0:T(8,128)S(1)}, f32[16,96,128]{2,1,0:T(8,128)S(1)}, u32[]{:S(2)}, u32[]{:S(2)}) collective-permute-start(f32[16,96,128]{2,1,0:T(8,128)S(1)} %all-to-all-done.2.mine_ref), channel_id=1, source_target_pairs={{0,8},{8,0},{1,9},{9,1},{2,10},{10,2},{3,11},{11,3},{4,12},{12,4},... | collective-permute-start | bytes 2359304 | tf_op jit(solution)/shard_map/ppermute | solution.py:321
  78.3 13.7 %all-to-all-start.3 = ((f32[16,48,128]{2,1,0:T(8,128)}), f32[16,48,128]{2,1,0:T(8,128)S(1)}, u32[]{:S(2)}, u32[]{:S(2)}) async-start(f32[16,48,128]{2,1,0:T(8,128)} %shard_map.71), calls=%async_computation.3 | async-start | bytes 786432 | tf_op jit(solution)/shard_map/all_to_all | solution.py:201
  92.1 3.1 %collective-permute-start.14 = (f32[16,48,128]{2,1,0:T(8,128)S(1)}, f32[16,48,128]{2,1,0:T(8,128)S(1)}, u32[]{:S(2)}, u32[]{:S(2)}) collective-permute-start(f32[16,48,128]{2,1,0:T(8,128)S(1)} %all-to-all-done.3.mine_ref), channel_id=1, source_target_pairs={{0,8},{8,0},{1,9},{9,1},{2,10},{10,2},{3,11},{11,3},{4,12},{12,4},... | collective-permute-start | bytes 1179656 | tf_op jit(solution)/shard_map/ppermute | solution.py:331

commit v12 on v10

--- a/solution.py
+++ b/solution.py
@@ -99,12 +99,17 @@
     return jnp.concatenate(pair, 1).reshape((hi - lo) * 16, LANES)
 
 
-def product_kernel(pos_ref, mine_ref, other_ref, root_ref, cross_ref, cfg_ref, full, left):
+def product_kernel(pos_ref, mine_ref, *refs):
+    other_refs, (root_ref, cross_ref, cfg_ref, full, left) = refs[:-5], refs[-5:]
     core, kind, part, owner = pos_ref[0], pos_ref[1], pos_ref[2], pos_ref[3]
     width = full.shape[1] // 2
     band = left.shape[1]
-    for j in range(2 * width // LANES):
-        full[:, j * LANES : (j + 1) * LANES] = joined_rows(core, (mine_ref, other_ref), j)
+    owners = other_refs[0].shape[0]
+    for k, other_ref in enumerate(other_refs):
+        for j in range(2 * width // LANES):
+            part_refs = (mine_ref.at[k * owners : (k + 1) * owners], other_ref)
+            piece = joined_rows(core, part_refs, j, 0, owners)
+            full[k * owners * 16 : (k + 1) * owners * 16, j * LANES : (j + 1) * LANES] = piece
     for k in range(4):
 
         @pl.when(part == k)
@@ -300,7 +305,7 @@
     cross, rows = call(
         product_kernel,
         [pltpu.VMEM((band, 2 * width), f32), jax.ShapeDtypeStruct((cfg_here, band), f32)],
-        [pos, mine_s, lax.ppermute(mine_s, "c", flip), root],
+        [pos, mine_s] + [lax.ppermute(mine_s[k : k + 4], "c", flip) for k in range(0, 16, 4)] + [root],
         [pltpu.VMEM((configs, 2 * width), f32), pltpu.VMEM((configs, band), f32)],
         pltpu.VMEM,
         24 << 20,

time: 96.9 us -> 95.6 us (0.987)
  waiting for transfers between devices: 28.4 us -> 22.7 us
  starting transfers between devices: 50.7 us -> 55.1 us
    all_to_all x4, waiting for transfers between devices: 15.4 us -> 8.29 us  [exchange(): return lax.all_to_all(flat, axes, 0, 0, tiled=True).reshape(values.shape)]
    ppermute x1, starting transfers between devices: 1.7 us -> 5.07 us  [shards(): lax.ppermute(mine_g, 'c', flip)]
    ppermute x1 -> x4, waiting for transfers between devices: 0.01 us -> 1.39 us  [shards(): lax.ppermute(mine_s[k:k + 4], 'c', flip)]
    ppermute x1 -> x4, starting transfers between devices: 4.57 us -> 5.76 us  [shards(): lax.ppermute(mine_s[k:k + 4], 'c', flip)]
  transfers between devices with their start and end apart: 19 -> 22, of which waited for: 11 -> 14; matrix products, arithmetic and copies ran while one was open for 2% -> 3% of each run, Pallas kernels for 8% -> 8%
where the time goes in v12:
time: 95.6 us; the launch traced here: 95.1 us
  starting transfers between devices  55.1 us (58%)
  waiting for transfers between devices  22.7 us (24%)
  Pallas kernels  13 us (14%)
  other arithmetic  2.47 us (3%)
  local copies, waits for them, and re-layouts  1.11 us (1%)
    all_to_all x4, starting transfers between devices, exchange(): return lax.all_to_all(flat, axes, 0, 0, tiled=True).reshape(values.shape)  17.6 us
    pallas_call x5, Pallas kernels, call(): pl.pallas_call(kernel, out_shape=outs, in_specs=[smem] + [pl.BlockSpec(me...  13 us
    all_to_all x4, waiting for transfers between devices, exchange(): return lax.all_to_all(flat, axes, 0, 0, tiled=True).reshape(values.shape)  8.29 us
    ppermute x6, starting transfers between devices, along_l(): return lax.ppermute(value, 'l', [(i, (i + k) % 4) for i in range(4)])  7.99 us
    ppermute x1, starting transfers between devices, shards(): plane_s = plane_s + lax.ppermute(plane_s, 'h', flip)  7 us
    ppermute x1, starting transfers between devices, shards(): grams = of_species(kind) + lax.ppermute(of_species(1 - kind), 'h', flip)  7 us
    ppermute x6, waiting for transfers between devices, along_l(): return lax.ppermute(value, 'l', [(i, (i + k) % 4) for i in range(4)])  6.18 us
    ppermute x4, starting transfers between devices, shards(): lax.ppermute(mine_s[k:k + 4], 'c', flip)  5.76 us
  transfers between devices with their start and end apart: 22, of which 14 were waited for; matrix products, arithmetic and copies ran while one was open for 3% of the time, Pallas kernels for 8%

profile of v12, /device:TPU:1, one launch (start us, length us, event | category | flops | bytes accessed | tf_op | source)
XLA Modules:
  0.0 95.1 jit_solution(7865708859787216279)
XLA Ops:
  0.6 0.0 copy-start
  0.6 3.5 %shard_map.68 = (f32[16,96,128]{2,1,0:T(8,128)S(1)}, f32[16,96,128]{2,1,0:T(8,128)S(1)}) custom-call(s32[1]{0:T(128)} %bitcast.core_ref, bf16[2048,768]{1,0:T(8,128)(2,1)} %desc_hbm.2, s32[1,2048]{1,0:T(1,128)} %bitcast.15, s32[1,2048]{1,0:T(1,128)} %bitcast.14, s32[1,256]{1,0:T(1,128)} %bitcast.17), custom_call_target="tpu_custom_call" | custom-call | flops 1610612736 | bytes 3145728 | tf_op jit(solution)/shard_map/pallas_call | solution.py:193
  4.1 3.3 %collective-permute-start = (f32[16,96,128]{2,1,0:T(8,128)S(1)}, f32[16,96,128]{2,1,0:T(8,128)S(1)}, u32[]{:S(2)}, u32[]{:S(2)}) collective-permute-start(f32[16,96,128]{2,1,0:T(8,128)S(1)} %get-tuple-element.24), channel_id=1, source_target_pairs={{0,8},{8,0},{1,9},{9,1},{2,10},{10,2},{3,11},{11,3},{4,12},{12,4},... | collective-permute-start | bytes 2359304 | tf_op jit(solution)/shard_map/ppermute | solution.py:260
  7.4 0.0 copy-done
  7.4 0.1 pad_add_fusion.pos_ref
  7.5 1.8 %collective-permute-done = f32[16,96,128]{2,1,0:T(8,128)S(1)} collective-permute-done((f32[16,96,128]{2,1,0:T(8,128)S(1)}, f32[16,96,128]{2,1,0:T(8,128)S(1)}, u32[]{:S(2)}, u32[]{:S(2)}) %collective-permute-start) | collective-permute-done | bytes 786464 | tf_op jit(solution)/shard_map/ppermute | solution.py:260
  9.4 1.0 %add.58 = f32[16,96,128]{2,1,0:T(8,128)} add(f32[16,96,128]{2,1,0:T(8,128)S(1)} %get-tuple-element.23, f32[16,96,128]{2,1,0:T(8,128)S(1)} %collective-permute-done) | non-fusion elementwise | flops 196608 | bytes 2359296 | tf_op jit(solution)/shard_map/add | solution.py:260
  10.3 0.1 broadcast_in_dim.42.refs_4_
  10.4 5.0 %all-to-all-start = ((f32[16,96,128]{2,1,0:T(8,128)}), f32[16,96,128]{2,1,0:T(8,128)S(1)}, u32[]{:S(2)}, u32[]{:S(2)}) async-start(f32[16,96,128]{2,1,0:T(8,128)} %add.58), calls=%async_computation | async-start | bytes 1572864 | tf_op jit(solution)/shard_map/all_to_all | solution.py:206
  15.4 5.1 %shard_map.69 = (f32[16,168,128]{2,1,0:T(8,128)S(1)}, f32[16,48,128]{2,1,0:T(8,128)S(1)}, f32[16,48,128]{2,1,0:T(8,128)S(1)}, f32[16,48,128]{2,1,0:T(8,128)S(1)}, f32[16,24,128]{2,1,0:T(8,128)S(1)}) custom-call(s32[1]{0:T(128)} %bitcast.core_ref, bf16[2048,768]{1,0:T(8,128)(2,1)} %desc_hbm.2, s32[1,2048]{1,0:T(1,128)} %bitcast.16), custom_call_target="tpu_custom_call" | custom-call | flops 4831838208 | bytes 9437184 | tf_op jit(solution)/shard_map/pallas_call | solution.py:193
  20.5 0.7 collective-permute-start.3
  21.3 0.1 collective-permute-start.2
  21.4 0.4 collective-permute-start.1
  21.8 0.1 collective-permute-start.4
  21.9 2.1 %collective-permute-done.4 = f32[16,24,128]{2,1,0:T(8,128)S(1)} collective-permute-done((f32[16,24,128]{2,1,0:T(8,128)S(1)}, f32[16,24,128]{2,1,0:T(8,128)S(1)}, u32[]{:S(2)}, u32[]{:S(2)}) %collective-permute-start.4) | collective-permute-done | bytes 196640 | tf_op jit(solution)/shard_map/ppermute | solution.py:270
  24.0 0.0 collective-permute-done.3
  24.0 0.0 collective-permute-done.2
  24.0 0.0 collective-permute-done.1
  24.0 1.3 %maximum_add_fusion = f32[16,168,128]{2,1,0:T(8,128)} fusion(f32[16,168,128]{2,1,0:T(8,128)S(1)} %get-tuple-element.28, f32[16,24,128]{2,1,0:T(8,128)S(1)} %collective-permute-done.4, f32[16,48,128]{2,1,0:T(8,128)S(1)} %collective-permute-done.3, f32[16,48,128]{2,1,0:T(8,128)S(1)} %collective-permute-done.2, f32[16,48,128]{2,1,0:T(8,128)S(1)} %collective-permute-done.1), kind=kLoop, calls=%fused_computation | loop fusion | flops 1376256 | bytes 4128768 | tf_op jit(solution)/shard_map/add | solution.py:270
  25.3 2.9 %all-to-all-done = f32[16,96,128]{2,1,0:T(8,128)S(1)} async-done(((f32[16,96,128]{2,1,0:T(8,128)}), f32[16,96,128]{2,1,0:T(8,128)S(1)}, u32[]{:S(2)}, u32[]{:S(2)}) %all-to-all-start) | async-done | bytes 786464 | tf_op jit(solution)/shard_map/all_to_all | solution.py:206
  28.2 4.3 %all-to-all-start.1 = ((f32[16,168,128]{2,1,0:T(8,128)}), f32[16,168,128]{2,1,0:T(8,128)S(1)}, u32[]{:S(2)}, u32[]{:S(2)}) async-start(f32[16,168,128]{2,1,0:T(8,128)} %maximum_add_fusion), calls=%async_computation.1 | async-start | bytes 2752512 | tf_op jit(solution)/shard_map/all_to_all | solution.py:206
  32.5 7.0 %collective-permute-start.5 = (f32[96,128]{1,0:T(8,128)S(1)}, f32[96,128]{1,0:T(8,128)S(1)}, u32[]{:S(2)}, u32[]{:S(2)}) collective-permute-start(f32[96,128]{1,0:T(8,128)S(1)} %reduce_sum.18), channel_id=1, source_target_pairs={{0,4},{4,0},{1,5},{5,1},{2,6},{6,2},{3,7},{7,3},{8,12},{12,8},{9,1... | collective-permute-start | bytes 147464 | tf_op jit(solution)/shard_map/ppermute | solution.py:278
  39.5 1.5 %collective-permute-done.5 = f32[96,128]{1,0:T(8,128)S(1)} collective-permute-done((f32[96,128]{1,0:T(8,128)S(1)}, f32[96,128]{1,0:T(8,128)S(1)}, u32[]{:S(2)}, u32[]{:S(2)}) %collective-permute-start.5) | collective-permute-done | bytes 49184 | tf_op jit(solution)/shard_map/ppermute | solution.py:278
  41.0 2.9 %collective-permute-start.8 = (f32[104,128]{1,0:T(8,128)S(1)}, f32[104,128]{1,0:T(8,128)S(1)}, u32[]{:S(2)}, u32[]{:S(2)}) collective-permute-start(f32[104,128]{1,0:T(8,128)S(1)} %pad_maximum_fusion.2), channel_id=1, source_target_pairs={{0,48},{16,0},{32,16},{48,32},{1,49},{17,1},{33,17},{49,33},{2,50}... | collective-permute-start | bytes 159752 | tf_op jit(solution)/shard_map/ppermute | solution.py:276
  43.9 0.0 collective-permute-start.7
  43.9 0.4 collective-permute-start.6
  44.3 0.8 collective-permute-done.8
  45.1 3.9 %collective-permute-done.7 = f32[104,128]{1,0:T(8,128)S(1)} collective-permute-done((f32[104,128]{1,0:T(8,128)S(1)}, f32[104,128]{1,0:T(8,128)S(1)}, u32[]{:S(2)}, u32[]{:S(2)}) %collective-permute-start.7) | collective-permute-done | bytes 53280 | tf_op jit(solution)/shard_map/ppermute | solution.py:276
  49.0 0.0 collective-permute-done.6
  49.0 1.7 %all-to-all-done.1 = f32[16,168,128]{2,1,0:T(8,128)S(1)} async-done(((f32[16,168,128]{2,1,0:T(8,128)}), f32[16,168,128]{2,1,0:T(8,128)S(1)}, u32[]{:S(2)}, u32[]{:S(2)}) %all-to-all-start.1) | async-done | bytes 1376288 | tf_op jit(solution)/shard_map/all_to_all | solution.py:206
  50.7 0.1 reduce_sum.19
  50.9 7.0 %collective-permute-start.9 = (f32[96,128]{1,0:T(8,128)S(1)}, f32[96,128]{1,0:T(8,128)S(1)}, u32[]{:S(2)}, u32[]{:S(2)}) collective-permute-start(f32[96,128]{1,0:T(8,128)S(1)} %pad_maximum_fusion), channel_id=1, source_target_pairs={{0,4},{4,0},{1,5},{5,1},{2,6},{6,2},{3,7},{7,3},{8,12},{12,8},{9,1... | collective-permute-start | bytes 147464 | tf_op jit(solution)/shard_map/ppermute | solution.py:291
  57.9 1.0 %broadcast_in_dim.46 = f32[16,96,128]{2,1,0:T(8,128)} broadcast(f32[96,128]{1,0:T(8,128)S(1)} %bitcast.13), dimensions={1,2} | broadcast | bytes 835584 | tf_op jit(solution)/shard_map/broadcast_in_dim | solution.py:290
  58.8 4.6 %all-to-all-start.2 = ((f32[16,96,128]{2,1,0:T(8,128)}), f32[16,96,128]{2,1,0:T(8,128)S(1)}, u32[]{:S(2)}, u32[]{:S(2)}) async-start(f32[16,96,128]{2,1,0:T(8,128)} %broadcast_in_dim.46), calls=%async_computation.2 | async-start | bytes 1572864 | tf_op jit(solution)/shard_map/all_to_all | solution.py:206
  63.4 0.0 collective-permute-done.9
  63.4 1.5 %collective-permute-start.10 = (f32[96,128]{1,0:T(8,128)S(1)}, f32[96,128]{1,0:T(8,128)S(1)}, u32[]{:S(2)}, u32[]{:S(2)}) collective-permute-start(f32[96,128]{1,0:T(8,128)S(1)} %fusion.refs_0_), channel_id=1, source_target_pairs={{0,32},{16,48},{32,0},{48,16},{1,33},{17,49},{33,1},{49,17},{2,34}... | collective-permute-start | bytes 147464 | tf_op jit(solution)/shard_map/ppermute | solution.py:276
  64.9 0.7 collective-permute-start.11
  65.6 2.5 %collective-permute-start.12 = (f32[96,128]{1,0:T(8,128)S(1)}, f32[96,128]{1,0:T(8,128)S(1)}, u32[]{:S(2)}, u32[]{:S(2)}) collective-permute-start(f32[96,128]{1,0:T(8,128)S(1)} %fusion.refs_0_), channel_id=1, source_target_pairs={{0,48},{16,0},{32,16},{48,32},{1,49},{17,1},{33,17},{49,33},{2,50}... | collective-permute-start | bytes 147464 | tf_op jit(solution)/shard_map/ppermute | solution.py:276
  68.2 0.0 collective-permute-done.10.refs_1_
  68.2 1.5 %collective-permute-done.11.refs_2_ = f32[96,128]{1,0:T(8,128)S(1)} collective-permute-done((f32[96,128]{1,0:T(8,128)S(1)}, f32[96,128]{1,0:T(8,128)S(1)}, u32[]{:S(2)}, u32[]{:S(2)}) %collective-permute-start.11) | collective-permute-done | bytes 49184 | tf_op jit(solution)/shard_map/ppermute | solution.py:276
  69.6 0.0 collective-permute-done.12.refs_3_
  69.7 0.8 shard_map.70
  70.4 3.7 %all-to-all-done.2.mine_ref = f32[16,96,128]{2,1,0:T(8,128)S(1)} async-done(((f32[16,96,128]{2,1,0:T(8,128)}), f32[16,96,128]{2,1,0:T(8,128)S(1)}, u32[]{:S(2)}, u32[]{:S(2)}) %all-to-all-start.2) | async-done | bytes 786464 | tf_op jit(solution)/shard_map/all_to_all | solution.py:206
  74.1 3.7 %all-to-all-start.3 = ((f32[16,48,128]{2,1,0:T(8,128)}), f32[16,48,128]{2,1,0:T(8,128)S(1)}, u32[]{:S(2)}, u32[]{:S(2)}) async-start(f32[16,48,128]{2,1,0:T(8,128)} %shard_map.70), calls=%async_computation.3 | async-start | bytes 786432 | tf_op jit(solution)/shard_map/all_to_all | solution.py:206
  77.8 0.1 fusion.7
  77.8 5.2 %collective-permute-start.13 = (f32[4,96,128]{2,1,0:T(8,128)S(1)}, f32[4,96,128]{2,1,0:T(8,128)S(1)}, u32[]{:S(2)}, u32[]{:S(2)}) collective-permute-start(f32[4,96,128]{2,1,0:T(8,128)S(1)} %get-tuple-element.47), channel_id=1, source_target_pairs={{0,8},{8,0},{1,9},{9,1},{2,10},{10,2},{3,11},{11,3},{4,12},{12,4},... | collective-permute-start | bytes 589832 | tf_op jit(solution)/shard_map/ppermute | solution.py:308
  83.0 0.1 collective-permute-start.14
  83.1 0.4 collective-permute-start.15
  83.5 0.1 collective-permute-start.16
  83.6 0.5 collective-permute-done.13.refs_0_
  84.1 0.4 collective-permute-done.14.refs_1_
  84.4 0.3 collective-permute-done.15.refs_2_
  84.7 0.3 collective-permute-done.16.refs_3_
  85.0 1.9 %shard_map.71 = (f32[192,1536]{1,0:T(8,128)S(1)}, f32[8,192]{1,0:T(8,128)}) custom-call(s32[4]{0:T(128)S(1)} %pad_add_fusion.pos_ref, f32[16,96,128]{2,1,0:T(8,128)S(1)} %all-to-all-done.2.mine_ref, f32[4,96,128]{2,1,0:T(8,128)S(1)} %collective-permute-done.13.refs_0_, f32[4,96,128]{2,1,0:T(8,128)S(1)} %collective-permute-done.14.refs_1_, ...), custom_call_target="tpu_custom_call" | custom-call | flops 905969664 | bytes 1769472 | tf_op jit(solution)/shard_map/pallas_call | solution.py:193
  86.9 0.0 all-to-all-done.3.mine_ref
  86.9 5.1 %collective-permute-start.17 = (f32[16,48,128]{2,1,0:T(8,128)S(1)}, f32[16,48,128]{2,1,0:T(8,128)S(1)}, u32[]{:S(2)}, u32[]{:S(2)}) collective-permute-start(f32[16,48,128]{2,1,0:T(8,128)S(1)} %all-to-all-done.3.mine_ref), channel_id=1, source_target_pairs={{0,8},{8,0},{1,9},{9,1},{2,10},{10,2},{3,11},{11,3},{4,12},{12,4},... | collective-permute-start | bytes 1179656 | tf_op jit(solution)/shard_map/ppermute | solution.py:318
  92.0 1.3 %collective-permute-done.17.other_ref = f32[16,48,128]{2,1,0:T(8,128)S(1)} collective-permute-done((f32[16,48,128]{2,1,0:T(8,128)S(1)}, f32[16,48,128]{2,1,0:T(8,128)S(1)}, u32[]{:S(2)}, u32[]{:S(2)}) %collective-permute-start.17) | collective-permute-done | bytes 393248 | tf_op jit(solution)/shard_map/ppermute | solution.py:318
  93.3 1.8 %shard_map.72 = f32[192,1536]{1,0:T(8,128)} custom-call(s32[4]{0:T(128)S(1)} %pad_add_fusion.pos_ref, f32[16,48,128]{2,1,0:T(8,128)S(1)} %all-to-all-done.3.mine_ref, f32[16,48,128]{2,1,0:T(8,128)S(1)} %collective-permute-done.17.other_ref, f32[192,1536]{1,0:T(8,128)S(1)} %get-tuple-element.42.cross_ref), custom_call_target="tpu_custom_call" | custom-call | flops 147456 | bytes 288 | tf_op jit(solution)/shard_map/pallas_call | solution.py:193
  (10 shorter events, 0.1 us)
Async XLA Ops:
  0.6 6.8 %copy-start = (f32[8]{0:T(128)S(1)}, f32[8]{0:T(128)}, u32[]{:S(2)}) copy-start(f32[8]{0:T(128)} %param.9) | copy-start | bytes 100
  4.1 5.2 %collective-permute-start = (f32[16,96,128]{2,1,0:T(8,128)S(1)}, f32[16,96,128]{2,1,0:T(8,128)S(1)}, u32[]{:S(2)}, u32[]{:S(2)}) collective-permute-start(f32[16,96,128]{2,1,0:T(8,128)S(1)} %get-tuple-element.24), channel_id=1, source_target_pairs={{0,8},{8,0},{1,9},{9,1},{2,10},{10,2},{3,11},{11,3},{4,12},{12,4},... | collective-permute-start | bytes 2359304 | tf_op jit(solution)/shard_map/ppermute | solution.py:260
  10.4 17.8 %all-to-all-start = ((f32[16,96,128]{2,1,0:T(8,128)}), f32[16,96,128]{2,1,0:T(8,128)S(1)}, u32[]{:S(2)}, u32[]{:S(2)}) async-start(f32[16,96,128]{2,1,0:T(8,128)} %add.58), calls=%async_computation | async-start | bytes 1572864 | tf_op jit(solution)/shard_map/all_to_all | solution.py:206
  20.5 3.5 %collective-permute-start.3 = (f32[16,48,128]{2,1,0:T(8,128)S(1)}, f32[16,48,128]{2,1,0:T(8,128)S(1)}, u32[]{:S(2)}, u32[]{:S(2)}) collective-permute-start(f32[16,48,128]{2,1,0:T(8,128)S(1)} %get-tuple-element.31), channel_id=1, source_target_pairs={{0,8},{8,0},{1,9},{9,1},{2,10},{10,2},{3,11},{11,3},{4,12},{12,4},... | collective-permute-start | bytes 1179656 | tf_op jit(solution)/shard_map/ppermute | solution.py:270
  21.3 2.8 %collective-permute-start.2 = (f32[16,48,128]{2,1,0:T(8,128)S(1)}, f32[16,48,128]{2,1,0:T(8,128)S(1)}, u32[]{:S(2)}, u32[]{:S(2)}) collective-permute-start(f32[16,48,128]{2,1,0:T(8,128)S(1)} %get-tuple-element.30), channel_id=1, source_target_pairs={{0,8},{8,0},{1,9},{9,1},{2,10},{10,2},{3,11},{11,3},{4,12},{12,4},... | collective-permute-start | bytes 1179656 | tf_op jit(solution)/shard_map/ppermute | solution.py:270
  21.4 2.7 %collective-permute-start.1 = (f32[16,48,128]{2,1,0:T(8,128)S(1)}, f32[16,48,128]{2,1,0:T(8,128)S(1)}, u32[]{:S(2)}, u32[]{:S(2)}) collective-permute-start(f32[16,48,128]{2,1,0:T(8,128)S(1)} %get-tuple-element.29), channel_id=1, source_target_pairs={{0,8},{8,0},{1,9},{9,1},{2,10},{10,2},{3,11},{11,3},{4,12},{12,4},... | collective-permute-start | bytes 1179656 | tf_op jit(solution)/shard_map/ppermute | solution.py:270
  21.8 2.2 %collective-permute-start.4 = (f32[16,24,128]{2,1,0:T(8,128)S(1)}, f32[16,24,128]{2,1,0:T(8,128)S(1)}, u32[]{:S(2)}, u32[]{:S(2)}) collective-permute-start(f32[16,24,128]{2,1,0:T(8,128)S(1)} %get-tuple-element.32), channel_id=1, source_target_pairs={{0,8},{8,0},{1,9},{9,1},{2,10},{10,2},{3,11},{11,3},{4,12},{12,4},... | collective-permute-start | bytes 589832 | tf_op jit(solution)/shard_map/ppermute | solution.py:270
  28.2 22.5 %all-to-all-start.1 = ((f32[16,168,128]{2,1,0:T(8,128)}), f32[16,168,128]{2,1,0:T(8,128)S(1)}, u32[]{:S(2)}, u32[]{:S(2)}) async-start(f32[16,168,128]{2,1,0:T(8,128)} %maximum_add_fusion), calls=%async_computation.1 | async-start | bytes 2752512 | tf_op jit(solution)/shard_map/all_to_all | solution.py:206
  32.5 8.5 %collective-permute-start.5 = (f32[96,128]{1,0:T(8,128)S(1)}, f32[96,128]{1,0:T(8,128)S(1)}, u32[]{:S(2)}, u32[]{:S(2)}) collective-permute-start(f32[96,128]{1,0:T(8,128)S(1)} %reduce_sum.18), channel_id=1, source_target_pairs={{0,4},{4,0},{1,5},{5,1},{2,6},{6,2},{3,7},{7,3},{8,12},{12,8},{9,1... | collective-permute-start | bytes 147464 | tf_op jit(solution)/shard_map/ppermute | solution.py:278
  41.0 4.1 %collective-permute-start.8 = (f32[104,128]{1,0:T(8,128)S(1)}, f32[104,128]{1,0:T(8,128)S(1)}, u32[]{:S(2)}, u32[]{:S(2)}) collective-permute-start(f32[104,128]{1,0:T(8,128)S(1)} %pad_maximum_fusion.2), channel_id=1, source_target_pairs={{0,48},{16,0},{32,16},{48,32},{1,49},{17,1},{33,17},{49,33},{2,50}... | collective-permute-start | bytes 159752 | tf_op jit(solution)/shard_map/ppermute | solution.py:276
  43.9 5.1 %collective-permute-start.7 = (f32[104,128]{1,0:T(8,128)S(1)}, f32[104,128]{1,0:T(8,128)S(1)}, u32[]{:S(2)}, u32[]{:S(2)}) collective-permute-start(f32[104,128]{1,0:T(8,128)S(1)} %pad_maximum_fusion.2), channel_id=1, source_target_pairs={{0,16},{16,32},{32,48},{48,0},{1,17},{17,33},{33,49},{49,1},{2,18}... | collective-permute-start | bytes 159752 | tf_op jit(solution)/shard_map/ppermute | solution.py:276
  43.9 5.1 %collective-permute-start.6 = (f32[104,128]{1,0:T(8,128)S(1)}, f32[104,128]{1,0:T(8,128)S(1)}, u32[]{:S(2)}, u32[]{:S(2)}) collective-permute-start(f32[104,128]{1,0:T(8,128)S(1)} %pad_maximum_fusion.2), channel_id=1, source_target_pairs={{0,32},{16,48},{32,0},{48,16},{1,33},{17,49},{33,1},{49,17},{2,34}... | collective-permute-start | bytes 159752 | tf_op jit(solution)/shard_map/ppermute | solution.py:276
  50.9 12.6 %collective-permute-start.9 = (f32[96,128]{1,0:T(8,128)S(1)}, f32[96,128]{1,0:T(8,128)S(1)}, u32[]{:S(2)}, u32[]{:S(2)}) collective-permute-start(f32[96,128]{1,0:T(8,128)S(1)} %pad_maximum_fusion), channel_id=1, source_target_pairs={{0,4},{4,0},{1,5},{5,1},{2,6},{6,2},{3,7},{7,3},{8,12},{12,8},{9,1... | collective-permute-start | bytes 147464 | tf_op jit(solution)/shard_map/ppermute | solution.py:291
  58.8 15.3 %all-to-all-start.2 = ((f32[16,96,128]{2,1,0:T(8,128)}), f32[16,96,128]{2,1,0:T(8,128)S(1)}, u32[]{:S(2)}, u32[]{:S(2)}) async-start(f32[16,96,128]{2,1,0:T(8,128)} %broadcast_in_dim.46), calls=%async_computation.2 | async-start | bytes 1572864 | tf_op jit(solution)/shard_map/all_to_all | solution.py:206
  63.4 4.7 %collective-permute-start.10 = (f32[96,128]{1,0:T(8,128)S(1)}, f32[96,128]{1,0:T(8,128)S(1)}, u32[]{:S(2)}, u32[]{:S(2)}) collective-permute-start(f32[96,128]{1,0:T(8,128)S(1)} %fusion.refs_0_), channel_id=1, source_target_pairs={{0,32},{16,48},{32,0},{48,16},{1,33},{17,49},{33,1},{49,17},{2,34}... | collective-permute-start | bytes 147464 | tf_op jit(solution)/shard_map/ppermute | solution.py:276
  64.9 4.7 %collective-permute-start.11 = (f32[96,128]{1,0:T(8,128)S(1)}, f32[96,128]{1,0:T(8,128)S(1)}, u32[]{:S(2)}, u32[]{:S(2)}) collective-permute-start(f32[96,128]{1,0:T(8,128)S(1)} %fusion.refs_0_), channel_id=1, source_target_pairs={{0,16},{16,32},{32,48},{48,0},{1,17},{17,33},{33,49},{49,1},{2,18}... | collective-permute-start | bytes 147464 | tf_op jit(solution)/shard_map/ppermute | solution.py:276
  65.6 4.0 %collective-permute-start.12 = (f32[96,128]{1,0:T(8,128)S(1)}, f32[96,128]{1,0:T(8,128)S(1)}, u32[]{:S(2)}, u32[]{:S(2)}) collective-permute-start(f32[96,128]{1,0:T(8,128)S(1)} %fusion.refs_0_), channel_id=1, source_target_pairs={{0,48},{16,0},{32,16},{48,32},{1,49},{17,1},{33,17},{49,33},{2,50}... | collective-permute-start | bytes 147464 | tf_op jit(solution)/shard_map/ppermute | solution.py:276
  74.1 12.8 %all-to-all-start.3 = ((f32[16,48,128]{2,1,0:T(8,128)}), f32[16,48,128]{2,1,0:T(8,128)S(1)}, u32[]{:S(2)}, u32[]{:S(2)}) async-start(f32[16,48,128]{2,1,0:T(8,128)} %shard_map.70), calls=%async_computation.3 | async-start | bytes 786432 | tf_op jit(solution)/shard_map/all_to_all | solution.py:206
  77.8 6.2 %collective-permute-start.13 = (f32[4,96,128]{2,1,0:T(8,128)S(1)}, f32[4,96,128]{2,1,0:T(8,128)S(1)}, u32[]{:S(2)}, u32[]{:S(2)}) collective-permute-start(f32[4,96,128]{2,1,0:T(8,128)S(1)} %get-tuple-element.47), channel_id=1, source_target_pairs={{0,8},{8,0},{1,9},{9,1},{2,10},{10,2},{3,11},{11,3},{4,12},{12,4},... | collective-permute-start | bytes 589832 | tf_op jit(solution)/shard_map/ppermute | solution.py:308
  83.0 1.4 %collective-permute-start.14 = (f32[4,96,128]{2,1,0:T(8,128)S(1)}, f32[4,96,128]{2,1,0:T(8,128)S(1)}, u32[]{:S(2)}, u32[]{:S(2)}) collective-permute-start(f32[4,96,128]{2,1,0:T(8,128)S(1)} %get-tuple-element.46), channel_id=1, source_target_pairs={{0,8},{8,0},{1,9},{9,1},{2,10},{10,2},{3,11},{11,3},{4,12},{12,4},... | collective-permute-start | bytes 589832 | tf_op jit(solution)/shard_map/ppermute | solution.py:308
  83.1 1.6 %collective-permute-start.15 = (f32[4,96,128]{2,1,0:T(8,128)S(1)}, f32[4,96,128]{2,1,0:T(8,128)S(1)}, u32[]{:S(2)}, u32[]{:S(2)}) collective-permute-start(f32[4,96,128]{2,1,0:T(8,128)S(1)} %get-tuple-element.45), channel_id=1, source_target_pairs={{0,8},{8,0},{1,9},{9,1},{2,10},{10,2},{3,11},{11,3},{4,12},{12,4},... | collective-permute-start | bytes 589832 | tf_op jit(solution)/shard_map/ppermute | solution.py:308
  83.5 1.5 %collective-permute-start.16 = (f32[4,96,128]{2,1,0:T(8,128)S(1)}, f32[4,96,128]{2,1,0:T(8,128)S(1)}, u32[]{:S(2)}, u32[]{:S(2)}) collective-permute-start(f32[4,96,128]{2,1,0:T(8,128)S(1)} %get-tuple-element.44), channel_id=1, source_target_pairs={{0,8},{8,0},{1,9},{9,1},{2,10},{10,2},{3,11},{11,3},{4,12},{12,4},... | collective-permute-start | bytes 589832 | tf_op jit(solution)/shard_map/ppermute | solution.py:308
  86.9 6.4 %collective-permute-start.17 = (f32[16,48,128]{2,1,0:T(8,128)S(1)}, f32[16,48,128]{2,1,0:T(8,128)S(1)}, u32[]{:S(2)}, u32[]{:S(2)}) collective-permute-start(f32[16,48,128]{2,1,0:T(8,128)S(1)} %all-to-all-done.3.mine_ref), channel_id=1, source_target_pairs={{0,8},{8,0},{1,9},{9,1},{2,10},{10,2},{3,11},{11,3},{4,12},{12,4},... | collective-permute-start | bytes 1179656 | tf_op jit(solution)/shard_map/ppermute | solution.py:318

commit v13 on v11

--- a/solution.py
+++ b/solution.py
@@ -99,12 +99,17 @@
     return jnp.concatenate(pair, 1).reshape((hi - lo) * 16, LANES)
 
 
-def product_kernel(pos_ref, mine_ref, other_ref, root_ref, cross_ref, cfg_ref, full, left):
+def product_kernel(pos_ref, mine_ref, *refs):
+    other_refs, (root_ref, cross_ref, cfg_ref, full, left) = refs[:-5], refs[-5:]
     core, kind, part, owner = pos_ref[0], pos_ref[1], pos_ref[2], pos_ref[3]
     width = full.shape[1] // 2
     band = left.shape[1]
-    for j in range(2 * width // LANES):
-        full[:, j * LANES : (j + 1) * LANES] = joined_rows(core, (mine_ref, other_ref), j)
+    owners = other_refs[0].shape[0]
+    for k, other_ref in enumerate(other_refs):
+        for j in range(2 * width // LANES):
+            part_refs = (mine_ref.at[k * owners : (k + 1) * owners], other_ref)
+            piece = joined_rows(core, part_refs, j, 0, owners)
+            full[k * owners * 16 : (k + 1) * owners * 16, j * LANES : (j + 1) * LANES] = piece
     for k in range(4):
 
         @pl.when(part == k)
@@ -318,7 +323,7 @@
     cross, rows = call(
         product_kernel,
         [pltpu.VMEM((band, 2 * width), f32), jax.ShapeDtypeStruct((cfg_here, band), f32)],
-        [pos, mine_s, lax.ppermute(mine_s, "c", flip), root],
+        [pos, mine_s] + [lax.ppermute(mine_s[k : k + 4], "c", flip) for k in range(0, 16, 4)] + [root],
         [pltpu.VMEM((configs, 2 * width), f32), pltpu.VMEM((configs, band), f32)],
         pltpu.VMEM,
         24 << 20,

time: 97.4 us -> 96 us (0.986)
  waiting for transfers between devices: 25.1 us -> 19.4 us
  starting transfers between devices: 53.9 us -> 58.2 us
    all_to_all x4, waiting for transfers between devices: 14.6 us -> 7.52 us  [exchange(): return lax.all_to_all(flat, axes, 0, 0, tiled=True).reshape(values.shape)]
    ppermute x1, starting transfers between devices: 1.7 us -> 5.07 us  [shards(): lax.ppermute(mine_g, 'c', flip)]
    ppermute x1 -> x4, starting transfers between devices: 5.42 us -> 7.48 us  [shards(): lax.ppermute(mine_s[k:k + 4], 'c', flip)]
    ppermute x1 -> x4, waiting for transfers between devices: 0.01 us -> 1.39 us  [shards(): lax.ppermute(mine_s[k:k + 4], 'c', flip)]
    all_to_all x4, starting transfers between devices: 18.5 us -> 17.4 us  [exchange(): return lax.all_to_all(flat, axes, 0, 0, tiled=True).reshape(values.shape)]
  transfers between devices with their start and end apart: 19 -> 22, of which waited for: 12 -> 15; matrix products, arithmetic and copies ran while one was open for 1% -> 2% of each run, Pallas kernels for 10% -> 10%
where the time goes in v13:
time: 96 us; the launch traced here: 95.6 us
  starting transfers between devices  58.2 us (61%)
  waiting for transfers between devices  19.4 us (20%)
  Pallas kernels  14.5 us (15%)
  other arithmetic  2.52 us (3%)
    all_to_all x4, starting transfers between devices, exchange(): return lax.all_to_all(flat, axes, 0, 0, tiled=True).reshape(values.shape)  17.4 us
    pallas_call x6, Pallas kernels, call(): pl.pallas_call(kernel, out_shape=outs, in_specs=[smem] + [pl.BlockSpec(me...  14.5 us
    ppermute x6, starting transfers between devices, along_l(): return lax.ppermute(value, 'l', [(i, (i + k) % 4) for i in range(4)])  9.52 us
    all_to_all x4, waiting for transfers between devices, exchange(): return lax.all_to_all(flat, axes, 0, 0, tiled=True).reshape(values.shape)  7.52 us
    ppermute x4, starting transfers between devices, shards(): lax.ppermute(mine_s[k:k + 4], 'c', flip)  7.48 us
    ppermute x1, starting transfers between devices, shards(): plane_s = plane_s + lax.ppermute(plane_s, 'h', flip)  7 us
    ppermute x1, starting transfers between devices, shards(): grams = of_species(kind) + lax.ppermute(of_species(1 - kind), 'h', flip)  7 us
    ppermute x1, starting transfers between devices, shards(): lax.ppermute(mine_g, 'c', flip)  5.07 us
  transfers between devices with their start and end apart: 22, of which 15 were waited for; matrix products, arithmetic and copies ran while one was open for 2% of the time, Pallas kernels for 10%

profile of v13, /device:TPU:1, one launch (start us, length us, event | category | flops | bytes accessed | tf_op | source)
XLA Modules:
  0.0 95.6 jit_solution(16648328789898995783)
XLA Ops:
  0.6 0.0 copy-start
  0.6 3.5 %shard_map.68 = (f32[16,96,128]{2,1,0:T(8,128)S(1)}, f32[16,96,128]{2,1,0:T(8,128)S(1)}) custom-call(s32[1]{0:T(128)} %bitcast.core_ref, bf16[2048,768]{1,0:T(8,128)(2,1)} %desc_hbm.2, s32[1,2048]{1,0:T(1,128)} %bitcast.13, s32[1,2048]{1,0:T(1,128)} %bitcast.12, s32[1,256]{1,0:T(1,128)} %bitcast.15), custom_call_target="tpu_custom_call" | custom-call | flops 1610612736 | bytes 3145728 | tf_op jit(solution)/shard_map/pallas_call | solution.py:193
  4.1 3.3 %collective-permute-start = (f32[16,96,128]{2,1,0:T(8,128)S(1)}, f32[16,96,128]{2,1,0:T(8,128)S(1)}, u32[]{:S(2)}, u32[]{:S(2)}) collective-permute-start(f32[16,96,128]{2,1,0:T(8,128)S(1)} %get-tuple-element.24), channel_id=1, source_target_pairs={{0,8},{8,0},{1,9},{9,1},{2,10},{10,2},{3,11},{11,3},{4,12},{12,4},... | collective-permute-start | bytes 2359304 | tf_op jit(solution)/shard_map/ppermute | solution.py:271
  7.4 0.0 copy-done
  7.4 0.1 pad_add_fusion.pos_ref
  7.5 1.8 %collective-permute-done = f32[16,96,128]{2,1,0:T(8,128)S(1)} collective-permute-done((f32[16,96,128]{2,1,0:T(8,128)S(1)}, f32[16,96,128]{2,1,0:T(8,128)S(1)}, u32[]{:S(2)}, u32[]{:S(2)}) %collective-permute-start) | collective-permute-done | bytes 786464 | tf_op jit(solution)/shard_map/ppermute | solution.py:271
  9.4 1.0 %add.40 = f32[16,96,128]{2,1,0:T(8,128)} add(f32[16,96,128]{2,1,0:T(8,128)S(1)} %get-tuple-element.23, f32[16,96,128]{2,1,0:T(8,128)S(1)} %collective-permute-done) | non-fusion elementwise | flops 196608 | bytes 2359296 | tf_op jit(solution)/shard_map/add | solution.py:271
  10.3 0.1 broadcast_in_dim.27.refs_4_
  10.4 5.0 %all-to-all-start = ((f32[16,96,128]{2,1,0:T(8,128)}), f32[16,96,128]{2,1,0:T(8,128)S(1)}, u32[]{:S(2)}, u32[]{:S(2)}) async-start(f32[16,96,128]{2,1,0:T(8,128)} %add.40), calls=%async_computation | async-start | bytes 1572864 | tf_op jit(solution)/shard_map/all_to_all | solution.py:206
  15.4 5.1 %shard_map.69 = (f32[16,168,128]{2,1,0:T(8,128)S(1)}, f32[16,48,128]{2,1,0:T(8,128)S(1)}, f32[16,48,128]{2,1,0:T(8,128)S(1)}, f32[16,48,128]{2,1,0:T(8,128)S(1)}, f32[16,24,128]{2,1,0:T(8,128)S(1)}) custom-call(s32[1]{0:T(128)} %bitcast.core_ref, bf16[2048,768]{1,0:T(8,128)(2,1)} %desc_hbm.2, s32[1,2048]{1,0:T(1,128)} %bitcast.14), custom_call_target="tpu_custom_call" | custom-call | flops 4831838208 | bytes 9437184 | tf_op jit(solution)/shard_map/pallas_call | solution.py:193
  20.5 0.7 collective-permute-start.3
  21.3 0.1 collective-permute-start.2
  21.4 0.4 collective-permute-start.1
  21.8 0.1 collective-permute-start.4
  21.9 2.1 %collective-permute-done.4 = f32[16,24,128]{2,1,0:T(8,128)S(1)} collective-permute-done((f32[16,24,128]{2,1,0:T(8,128)S(1)}, f32[16,24,128]{2,1,0:T(8,128)S(1)}, u32[]{:S(2)}, u32[]{:S(2)}) %collective-permute-start.4) | collective-permute-done | bytes 196640 | tf_op jit(solution)/shard_map/ppermute | solution.py:281
  24.0 0.0 collective-permute-done.3
  24.0 0.0 collective-permute-done.2
  24.0 0.0 collective-permute-done.1
  24.0 1.3 %maximum_add_fusion = f32[16,168,128]{2,1,0:T(8,128)} fusion(f32[16,168,128]{2,1,0:T(8,128)S(1)} %get-tuple-element.28, f32[16,24,128]{2,1,0:T(8,128)S(1)} %collective-permute-done.4, f32[16,48,128]{2,1,0:T(8,128)S(1)} %collective-permute-done.3, f32[16,48,128]{2,1,0:T(8,128)S(1)} %collective-permute-done.2, f32[16,48,128]{2,1,0:T(8,128)S(1)} %collective-permute-done.1), kind=kLoop, calls=%fused_computation | loop fusion | flops 1376256 | bytes 4128768 | tf_op jit(solution)/shard_map/add | solution.py:281
  25.3 2.9 %all-to-all-done = f32[16,96,128]{2,1,0:T(8,128)S(1)} async-done(((f32[16,96,128]{2,1,0:T(8,128)}), f32[16,96,128]{2,1,0:T(8,128)S(1)}, u32[]{:S(2)}, u32[]{:S(2)}) %all-to-all-start) | async-done | bytes 786464 | tf_op jit(solution)/shard_map/all_to_all | solution.py:206
  28.2 4.3 %all-to-all-start.1 = ((f32[16,168,128]{2,1,0:T(8,128)}), f32[16,168,128]{2,1,0:T(8,128)S(1)}, u32[]{:S(2)}, u32[]{:S(2)}) async-start(f32[16,168,128]{2,1,0:T(8,128)} %maximum_add_fusion), calls=%async_computation.1 | async-start | bytes 2752512 | tf_op jit(solution)/shard_map/all_to_all | solution.py:206
  32.5 7.0 %collective-permute-start.5 = (f32[96,128]{1,0:T(8,128)S(1)}, f32[96,128]{1,0:T(8,128)S(1)}, u32[]{:S(2)}, u32[]{:S(2)}) collective-permute-start(f32[96,128]{1,0:T(8,128)S(1)} %reduce_sum.18), channel_id=1, source_target_pairs={{0,4},{4,0},{1,5},{5,1},{2,6},{6,2},{3,7},{7,3},{8,12},{12,8},{9,1... | collective-permute-start | bytes 147464 | tf_op jit(solution)/shard_map/ppermute | solution.py:289
  39.5 1.5 %collective-permute-done.5 = f32[96,128]{1,0:T(8,128)S(1)} collective-permute-done((f32[96,128]{1,0:T(8,128)S(1)}, f32[96,128]{1,0:T(8,128)S(1)}, u32[]{:S(2)}, u32[]{:S(2)}) %collective-permute-start.5) | collective-permute-done | bytes 49184 | tf_op jit(solution)/shard_map/ppermute | solution.py:289
  41.0 1.5 %collective-permute-start.6 = (f32[104,128]{1,0:T(8,128)S(1)}, f32[104,128]{1,0:T(8,128)S(1)}, u32[]{:S(2)}, u32[]{:S(2)}) collective-permute-start(f32[104,128]{1,0:T(8,128)S(1)} %pad_maximum_fusion.2.refs_0_), channel_id=1, source_target_pairs={{0,32},{16,48},{32,0},{48,16},{1,33},{17,49},{33,1},{49,17},{2,34}... | collective-permute-start | bytes 159752 | tf_op jit(solution)/shard_map/ppermute | solution.py:287
  42.5 1.7 %collective-permute-start.7 = (f32[104,128]{1,0:T(8,128)S(1)}, f32[104,128]{1,0:T(8,128)S(1)}, u32[]{:S(2)}, u32[]{:S(2)}) collective-permute-start(f32[104,128]{1,0:T(8,128)S(1)} %pad_maximum_fusion.2.refs_0_), channel_id=1, source_target_pairs={{0,16},{16,32},{32,48},{48,0},{1,17},{17,33},{33,49},{49,1},{2,18}... | collective-permute-start | bytes 159752 | tf_op jit(solution)/shard_map/ppermute | solution.py:287
  44.2 1.6 %collective-permute-start.8 = (f32[104,128]{1,0:T(8,128)S(1)}, f32[104,128]{1,0:T(8,128)S(1)}, u32[]{:S(2)}, u32[]{:S(2)}) collective-permute-start(f32[104,128]{1,0:T(8,128)S(1)} %pad_maximum_fusion.2.refs_0_), channel_id=1, source_target_pairs={{0,48},{16,0},{32,16},{48,32},{1,49},{17,1},{33,17},{49,33},{2,50}... | collective-permute-start | bytes 159752 | tf_op jit(solution)/shard_map/ppermute | solution.py:287
  45.8 0.1 add_convert_fusion.from_ref
  45.9 0.5 collective-permute-done.6.refs_1_
  46.3 1.3 %collective-permute-done.7.refs_2_ = f32[104,128]{1,0:T(8,128)S(1)} collective-permute-done((f32[104,128]{1,0:T(8,128)S(1)}, f32[104,128]{1,0:T(8,128)S(1)}, u32[]{:S(2)}, u32[]{:S(2)}) %collective-permute-start.7) | collective-permute-done | bytes 53280 | tf_op jit(solution)/shard_map/ppermute | solution.py:287
  47.6 0.4 collective-permute-done.8.refs_3_
  48.0 1.5 %shard_map.70 = f32[16,96,128]{2,1,0:T(8,128)} custom-call(s32[4]{0:T(128)S(1)} %add_convert_fusion.from_ref, f32[104,128]{1,0:T(8,128)S(1)} %pad_maximum_fusion.2.refs_0_, f32[104,128]{1,0:T(8,128)S(1)} %collective-permute-done.6.refs_1_, f32[104,128]{1,0:T(8,128)S(1)} %collective-permute-done.7.refs_2_, f32[104,128]{1,0:T(8,128)S(1)} %collective-permute-done.8.refs_3_), custom_call_target="tpu_custom_call" | custom-call | flops 1048576 | bytes 2048 | tf_op jit(solution)/shard_map/pallas_call | solution.py:193
  49.5 1.2 %all-to-all-done.1 = f32[16,168,128]{2,1,0:T(8,128)S(1)} async-done(((f32[16,168,128]{2,1,0:T(8,128)}), f32[16,168,128]{2,1,0:T(8,128)S(1)}, u32[]{:S(2)}, u32[]{:S(2)}) %all-to-all-start.1) | async-done | bytes 1376288 | tf_op jit(solution)/shard_map/all_to_all | solution.py:206
  50.7 0.1 reduce_sum.19
  50.9 7.0 %collective-permute-start.9 = (f32[96,128]{1,0:T(8,128)S(1)}, f32[96,128]{1,0:T(8,128)S(1)}, u32[]{:S(2)}, u32[]{:S(2)}) collective-permute-start(f32[96,128]{1,0:T(8,128)S(1)} %pad_maximum_fusion), channel_id=1, source_target_pairs={{0,4},{4,0},{1,5},{5,1},{2,6},{6,2},{3,7},{7,3},{8,12},{12,8},{9,1... | collective-permute-start | bytes 147464 | tf_op jit(solution)/shard_map/ppermute | solution.py:309
  57.9 4.6 %all-to-all-start.2 = ((f32[16,96,128]{2,1,0:T(8,128)}), f32[16,96,128]{2,1,0:T(8,128)S(1)}, u32[]{:S(2)}, u32[]{:S(2)}) async-start(f32[16,96,128]{2,1,0:T(8,128)} %shard_map.70), calls=%async_computation.2 | async-start | bytes 1572864 | tf_op jit(solution)/shard_map/all_to_all | solution.py:206
  62.5 0.0 collective-permute-done.9
  62.5 1.5 %collective-permute-start.10 = (f32[96,128]{1,0:T(8,128)S(1)}, f32[96,128]{1,0:T(8,128)S(1)}, u32[]{:S(2)}, u32[]{:S(2)}) collective-permute-start(f32[96,128]{1,0:T(8,128)S(1)} %fusion.refs_0_), channel_id=1, source_target_pairs={{0,32},{16,48},{32,0},{48,16},{1,33},{17,49},{33,1},{49,17},{2,34}... | collective-permute-start | bytes 147464 | tf_op jit(solution)/shard_map/ppermute | solution.py:287
  64.0 1.1 %collective-permute-start.11 = (f32[96,128]{1,0:T(8,128)S(1)}, f32[96,128]{1,0:T(8,128)S(1)}, u32[]{:S(2)}, u32[]{:S(2)}) collective-permute-start(f32[96,128]{1,0:T(8,128)S(1)} %fusion.refs_0_), channel_id=1, source_target_pairs={{0,16},{16,32},{32,48},{48,0},{1,17},{17,33},{33,49},{49,1},{2,18}... | collective-permute-start | bytes 147464 | tf_op jit(solution)/shard_map/ppermute | solution.py:287
  65.0 2.2 %collective-permute-start.12 = (f32[96,128]{1,0:T(8,128)S(1)}, f32[96,128]{1,0:T(8,128)S(1)}, u32[]{:S(2)}, u32[]{:S(2)}) collective-permute-start(f32[96,128]{1,0:T(8,128)S(1)} %fusion.refs_0_), channel_id=1, source_target_pairs={{0,48},{16,0},{32,16},{48,32},{1,49},{17,1},{33,17},{49,33},{2,50}... | collective-permute-start | bytes 147464 | tf_op jit(solution)/shard_map/ppermute | solution.py:287
  67.2 0.0 collective-permute-done.10.refs_1_
  67.2 1.5 %collective-permute-done.11.refs_2_ = f32[96,128]{1,0:T(8,128)S(1)} collective-permute-done((f32[96,128]{1,0:T(8,128)S(1)}, f32[96,128]{1,0:T(8,128)S(1)}, u32[]{:S(2)}, u32[]{:S(2)}) %collective-permute-start.11) | collective-permute-done | bytes 49184 | tf_op jit(solution)/shard_map/ppermute | solution.py:287
  68.7 0.0 collective-permute-done.12.refs_3_
  68.7 0.8 shard_map.71
  69.5 3.4 %all-to-all-done.2.mine_ref = f32[16,96,128]{2,1,0:T(8,128)S(1)} async-done(((f32[16,96,128]{2,1,0:T(8,128)}), f32[16,96,128]{2,1,0:T(8,128)S(1)}, u32[]{:S(2)}, u32[]{:S(2)}) %all-to-all-start.2) | async-done | bytes 786464 | tf_op jit(solution)/shard_map/all_to_all | solution.py:206
  72.9 3.6 %all-to-all-start.3 = ((f32[16,48,128]{2,1,0:T(8,128)}), f32[16,48,128]{2,1,0:T(8,128)S(1)}, u32[]{:S(2)}, u32[]{:S(2)}) async-start(f32[16,48,128]{2,1,0:T(8,128)} %shard_map.71), calls=%async_computation.3 | async-start | bytes 786432 | tf_op jit(solution)/shard_map/all_to_all | solution.py:206
  76.5 0.1 fusion.1
  76.5 6.9 %collective-permute-start.13 = (f32[4,96,128]{2,1,0:T(8,128)S(1)}, f32[4,96,128]{2,1,0:T(8,128)S(1)}, u32[]{:S(2)}, u32[]{:S(2)}) collective-permute-start(f32[4,96,128]{2,1,0:T(8,128)S(1)} %get-tuple-element.47), channel_id=1, source_target_pairs={{0,8},{8,0},{1,9},{9,1},{2,10},{10,2},{3,11},{11,3},{4,12},{12,4},... | collective-permute-start | bytes 589832 | tf_op jit(solution)/shard_map/ppermute | solution.py:326
  83.4 0.1 collective-permute-start.14
  83.5 0.4 collective-permute-start.15
  83.9 0.1 collective-permute-start.16
  84.0 0.5 collective-permute-done.13.refs_0_
  84.5 0.4 collective-permute-done.14.refs_1_
  84.9 0.3 collective-permute-done.15.refs_2_
  85.1 0.3 collective-permute-done.16.refs_3_
  85.4 1.9 %shard_map.72 = (f32[192,1536]{1,0:T(8,128)S(1)}, f32[8,192]{1,0:T(8,128)}) custom-call(s32[4]{0:T(128)S(1)} %pad_add_fusion.pos_ref, f32[16,96,128]{2,1,0:T(8,128)S(1)} %all-to-all-done.2.mine_ref, f32[4,96,128]{2,1,0:T(8,128)S(1)} %collective-permute-done.13.refs_0_, f32[4,96,128]{2,1,0:T(8,128)S(1)} %collective-permute-done.14.refs_1_, ...), custom_call_target="tpu_custom_call" | custom-call | flops 905969664 | bytes 1769472 | tf_op jit(solution)/shard_map/pallas_call | solution.py:193
  87.3 0.0 all-to-all-done.3.mine_ref
  87.3 5.1 %collective-permute-start.17 = (f32[16,48,128]{2,1,0:T(8,128)S(1)}, f32[16,48,128]{2,1,0:T(8,128)S(1)}, u32[]{:S(2)}, u32[]{:S(2)}) collective-permute-start(f32[16,48,128]{2,1,0:T(8,128)S(1)} %all-to-all-done.3.mine_ref), channel_id=1, source_target_pairs={{0,8},{8,0},{1,9},{9,1},{2,10},{10,2},{3,11},{11,3},{4,12},{12,4},... | collective-permute-start | bytes 1179656 | tf_op jit(solution)/shard_map/ppermute | solution.py:336
  92.4 1.3 %collective-permute-done.17.other_ref = f32[16,48,128]{2,1,0:T(8,128)S(1)} collective-permute-done((f32[16,48,128]{2,1,0:T(8,128)S(1)}, f32[16,48,128]{2,1,0:T(8,128)S(1)}, u32[]{:S(2)}, u32[]{:S(2)}) %collective-permute-start.17) | collective-permute-done | bytes 393248 | tf_op jit(solution)/shard_map/ppermute | solution.py:336
  93.7 1.8 %shard_map.73 = f32[192,1536]{1,0:T(8,128)} custom-call(s32[4]{0:T(128)S(1)} %pad_add_fusion.pos_ref, f32[16,48,128]{2,1,0:T(8,128)S(1)} %all-to-all-done.3.mine_ref, f32[16,48,128]{2,1,0:T(8,128)S(1)} %collective-permute-done.17.other_ref, f32[192,1536]{1,0:T(8,128)S(1)} %get-tuple-element.42.cross_ref), custom_call_target="tpu_custom_call" | custom-call | flops 147456 | bytes 288 | tf_op jit(solution)/shard_map/pallas_call | solution.py:193
  (8 shorter events, 0.1 us)
Async XLA Ops:
  0.6 6.8 %copy-start = (f32[8]{0:T(128)S(1)}, f32[8]{0:T(128)}, u32[]{:S(2)}) copy-start(f32[8]{0:T(128)} %param.9) | copy-start | bytes 100
  4.1 5.2 %collective-permute-start = (f32[16,96,128]{2,1,0:T(8,128)S(1)}, f32[16,96,128]{2,1,0:T(8,128)S(1)}, u32[]{:S(2)}, u32[]{:S(2)}) collective-permute-start(f32[16,96,128]{2,1,0:T(8,128)S(1)} %get-tuple-element.24), channel_id=1, source_target_pairs={{0,8},{8,0},{1,9},{9,1},{2,10},{10,2},{3,11},{11,3},{4,12},{12,4},... | collective-permute-start | bytes 2359304 | tf_op jit(solution)/shard_map/ppermute | solution.py:271
  10.4 17.8 %all-to-all-start = ((f32[16,96,128]{2,1,0:T(8,128)}), f32[16,96,128]{2,1,0:T(8,128)S(1)}, u32[]{:S(2)}, u32[]{:S(2)}) async-start(f32[16,96,128]{2,1,0:T(8,128)} %add.40), calls=%async_computation | async-start | bytes 1572864 | tf_op jit(solution)/shard_map/all_to_all | solution.py:206
  20.5 3.5 %collective-permute-start.3 = (f32[16,48,128]{2,1,0:T(8,128)S(1)}, f32[16,48,128]{2,1,0:T(8,128)S(1)}, u32[]{:S(2)}, u32[]{:S(2)}) collective-permute-start(f32[16,48,128]{2,1,0:T(8,128)S(1)} %get-tuple-element.31), channel_id=1, source_target_pairs={{0,8},{8,0},{1,9},{9,1},{2,10},{10,2},{3,11},{11,3},{4,12},{12,4},... | collective-permute-start | bytes 1179656 | tf_op jit(solution)/shard_map/ppermute | solution.py:281
  21.3 2.8 %collective-permute-start.2 = (f32[16,48,128]{2,1,0:T(8,128)S(1)}, f32[16,48,128]{2,1,0:T(8,128)S(1)}, u32[]{:S(2)}, u32[]{:S(2)}) collective-permute-start(f32[16,48,128]{2,1,0:T(8,128)S(1)} %get-tuple-element.30), channel_id=1, source_target_pairs={{0,8},{8,0},{1,9},{9,1},{2,10},{10,2},{3,11},{11,3},{4,12},{12,4},... | collective-permute-start | bytes 1179656 | tf_op jit(solution)/shard_map/ppermute | solution.py:281
  21.4 2.7 %collective-permute-start.1 = (f32[16,48,128]{2,1,0:T(8,128)S(1)}, f32[16,48,128]{2,1,0:T(8,128)S(1)}, u32[]{:S(2)}, u32[]{:S(2)}) collective-permute-start(f32[16,48,128]{2,1,0:T(8,128)S(1)} %get-tuple-element.29), channel_id=1, source_target_pairs={{0,8},{8,0},{1,9},{9,1},{2,10},{10,2},{3,11},{11,3},{4,12},{12,4},... | collective-permute-start | bytes 1179656 | tf_op jit(solution)/shard_map/ppermute | solution.py:281
  21.8 2.2 %collective-permute-start.4 = (f32[16,24,128]{2,1,0:T(8,128)S(1)}, f32[16,24,128]{2,1,0:T(8,128)S(1)}, u32[]{:S(2)}, u32[]{:S(2)}) collective-permute-start(f32[16,24,128]{2,1,0:T(8,128)S(1)} %get-tuple-element.32), channel_id=1, source_target_pairs={{0,8},{8,0},{1,9},{9,1},{2,10},{10,2},{3,11},{11,3},{4,12},{12,4},... | collective-permute-start | bytes 589832 | tf_op jit(solution)/shard_map/ppermute | solution.py:281
  28.2 22.5 %all-to-all-start.1 = ((f32[16,168,128]{2,1,0:T(8,128)}), f32[16,168,128]{2,1,0:T(8,128)S(1)}, u32[]{:S(2)}, u32[]{:S(2)}) async-start(f32[16,168,128]{2,1,0:T(8,128)} %maximum_add_fusion), calls=%async_computation.1 | async-start | bytes 2752512 | tf_op jit(solution)/shard_map/all_to_all | solution.py:206
  32.5 8.5 %collective-permute-start.5 = (f32[96,128]{1,0:T(8,128)S(1)}, f32[96,128]{1,0:T(8,128)S(1)}, u32[]{:S(2)}, u32[]{:S(2)}) collective-permute-start(f32[96,128]{1,0:T(8,128)S(1)} %reduce_sum.18), channel_id=1, source_target_pairs={{0,4},{4,0},{1,5},{5,1},{2,6},{6,2},{3,7},{7,3},{8,12},{12,8},{9,1... | collective-permute-start | bytes 147464 | tf_op jit(solution)/shard_map/ppermute | solution.py:289
  41.0 5.4 %collective-permute-start.6 = (f32[104,128]{1,0:T(8,128)S(1)}, f32[104,128]{1,0:T(8,128)S(1)}, u32[]{:S(2)}, u32[]{:S(2)}) collective-permute-start(f32[104,128]{1,0:T(8,128)S(1)} %pad_maximum_fusion.2.refs_0_), channel_id=1, source_target_pairs={{0,32},{16,48},{32,0},{48,16},{1,33},{17,49},{33,1},{49,17},{2,34}... | collective-permute-start | bytes 159752 | tf_op jit(solution)/shard_map/ppermute | solution.py:287
  42.5 5.1 %collective-permute-start.7 = (f32[104,128]{1,0:T(8,128)S(1)}, f32[104,128]{1,0:T(8,128)S(1)}, u32[]{:S(2)}, u32[]{:S(2)}) collective-permute-start(f32[104,128]{1,0:T(8,128)S(1)} %pad_maximum_fusion.2.refs_0_), channel_id=1, source_target_pairs={{0,16},{16,32},{32,48},{48,0},{1,17},{17,33},{33,49},{49,1},{2,18}... | collective-permute-start | bytes 159752 | tf_op jit(solution)/shard_map/ppermute | solution.py:287
  44.2 3.9 %collective-permute-start.8 = (f32[104,128]{1,0:T(8,128)S(1)}, f32[104,128]{1,0:T(8,128)S(1)}, u32[]{:S(2)}, u32[]{:S(2)}) collective-permute-start(f32[104,128]{1,0:T(8,128)S(1)} %pad_maximum_fusion.2.refs_0_), channel_id=1, source_target_pairs={{0,48},{16,0},{32,16},{48,32},{1,49},{17,1},{33,17},{49,33},{2,50}... | collective-permute-start | bytes 159752 | tf_op jit(solution)/shard_map/ppermute | solution.py:287
  50.9 11.6 %collective-permute-start.9 = (f32[96,128]{1,0:T(8,128)S(1)}, f32[96,128]{1,0:T(8,128)S(1)}, u32[]{:S(2)}, u32[]{:S(2)}) collective-permute-start(f32[96,128]{1,0:T(8,128)S(1)} %pad_maximum_fusion), channel_id=1, source_target_pairs={{0,4},{4,0},{1,5},{5,1},{2,6},{6,2},{3,7},{7,3},{8,12},{12,8},{9,1... | collective-permute-start | bytes 147464 | tf_op jit(solution)/shard_map/ppermute | solution.py:309
  57.9 15.1 %all-to-all-start.2 = ((f32[16,96,128]{2,1,0:T(8,128)}), f32[16,96,128]{2,1,0:T(8,128)S(1)}, u32[]{:S(2)}, u32[]{:S(2)}) async-start(f32[16,96,128]{2,1,0:T(8,128)} %shard_map.70), calls=%async_computation.2 | async-start | bytes 1572864 | tf_op jit(solution)/shard_map/all_to_all | solution.py:206
  62.5 4.7 %collective-permute-start.10 = (f32[96,128]{1,0:T(8,128)S(1)}, f32[96,128]{1,0:T(8,128)S(1)}, u32[]{:S(2)}, u32[]{:S(2)}) collective-permute-start(f32[96,128]{1,0:T(8,128)S(1)} %fusion.refs_0_), channel_id=1, source_target_pairs={{0,32},{16,48},{32,0},{48,16},{1,33},{17,49},{33,1},{49,17},{2,34}... | collective-permute-start | bytes 147464 | tf_op jit(solution)/shard_map/ppermute | solution.py:287
  64.0 4.7 %collective-permute-start.11 = (f32[96,128]{1,0:T(8,128)S(1)}, f32[96,128]{1,0:T(8,128)S(1)}, u32[]{:S(2)}, u32[]{:S(2)}) collective-permute-start(f32[96,128]{1,0:T(8,128)S(1)} %fusion.refs_0_), channel_id=1, source_target_pairs={{0,16},{16,32},{32,48},{48,0},{1,17},{17,33},{33,49},{49,1},{2,18}... | collective-permute-start | bytes 147464 | tf_op jit(solution)/shard_map/ppermute | solution.py:287
  65.0 3.7 %collective-permute-start.12 = (f32[96,128]{1,0:T(8,128)S(1)}, f32[96,128]{1,0:T(8,128)S(1)}, u32[]{:S(2)}, u32[]{:S(2)}) collective-permute-start(f32[96,128]{1,0:T(8,128)S(1)} %fusion.refs_0_), channel_id=1, source_target_pairs={{0,48},{16,0},{32,16},{48,32},{1,49},{17,1},{33,17},{49,33},{2,50}... | collective-permute-start | bytes 147464 | tf_op jit(solution)/shard_map/ppermute | solution.py:287
  72.9 14.4 %all-to-all-start.3 = ((f32[16,48,128]{2,1,0:T(8,128)}), f32[16,48,128]{2,1,0:T(8,128)S(1)}, u32[]{:S(2)}, u32[]{:S(2)}) async-start(f32[16,48,128]{2,1,0:T(8,128)} %shard_map.71), calls=%async_computation.3 | async-start | bytes 786432 | tf_op jit(solution)/shard_map/all_to_all | solution.py:206
  76.5 7.9 %collective-permute-start.13 = (f32[4,96,128]{2,1,0:T(8,128)S(1)}, f32[4,96,128]{2,1,0:T(8,128)S(1)}, u32[]{:S(2)}, u32[]{:S(2)}) collective-permute-start(f32[4,96,128]{2,1,0:T(8,128)S(1)} %get-tuple-element.47), channel_id=1, source_target_pairs={{0,8},{8,0},{1,9},{9,1},{2,10},{10,2},{3,11},{11,3},{4,12},{12,4},... | collective-permute-start | bytes 589832 | tf_op jit(solution)/shard_map/ppermute | solution.py:326
  83.4 1.4 %collective-permute-start.14 = (f32[4,96,128]{2,1,0:T(8,128)S(1)}, f32[4,96,128]{2,1,0:T(8,128)S(1)}, u32[]{:S(2)}, u32[]{:S(2)}) collective-permute-start(f32[4,96,128]{2,1,0:T(8,128)S(1)} %get-tuple-element.46), channel_id=1, source_target_pairs={{0,8},{8,0},{1,9},{9,1},{2,10},{10,2},{3,11},{11,3},{4,12},{12,4},... | collective-permute-start | bytes 589832 | tf_op jit(solution)/shard_map/ppermute | solution.py:326
  83.5 1.6 %collective-permute-start.15 = (f32[4,96,128]{2,1,0:T(8,128)S(1)}, f32[4,96,128]{2,1,0:T(8,128)S(1)}, u32[]{:S(2)}, u32[]{:S(2)}) collective-permute-start(f32[4,96,128]{2,1,0:T(8,128)S(1)} %get-tuple-element.45), channel_id=1, source_target_pairs={{0,8},{8,0},{1,9},{9,1},{2,10},{10,2},{3,11},{11,3},{4,12},{12,4},... | collective-permute-start | bytes 589832 | tf_op jit(solution)/shard_map/ppermute | solution.py:326
  83.9 1.5 %collective-permute-start.16 = (f32[4,96,128]{2,1,0:T(8,128)S(1)}, f32[4,96,128]{2,1,0:T(8,128)S(1)}, u32[]{:S(2)}, u32[]{:S(2)}) collective-permute-start(f32[4,96,128]{2,1,0:T(8,128)S(1)} %get-tuple-element.44), channel_id=1, source_target_pairs={{0,8},{8,0},{1,9},{9,1},{2,10},{10,2},{3,11},{11,3},{4,12},{12,4},... | collective-permute-start | bytes 589832 | tf_op jit(solution)/shard_map/ppermute | solution.py:326
  87.3 6.4 %collective-permute-start.17 = (f32[16,48,128]{2,1,0:T(8,128)S(1)}, f32[16,48,128]{2,1,0:T(8,128)S(1)}, u32[]{:S(2)}, u32[]{:S(2)}) collective-permute-start(f32[16,48,128]{2,1,0:T(8,128)S(1)} %all-to-all-done.3.mine_ref), channel_id=1, source_target_pairs={{0,8},{8,0},{1,9},{9,1},{2,10},{10,2},{3,11},{11,3},{4,12},{12,4},... | collective-permute-start | bytes 1179656 | tf_op jit(solution)/shard_map/ppermute | solution.py:336

commit v14 on v12

--- a/solution.py
+++ b/solution.py
@@ -278,7 +278,7 @@
     plane_s = plane_s + lax.ppermute(plane_s, "h", flip)
     rooted = jnp.concatenate([plane_s, root])
     got = [(rooted, l)]
-    for k in (2, 1, 3):
+    for k in (1, 3, 2):
         got.append((along_l(rooted, k), (l - k) % 4))
     root_here = sum(jnp.where(source == part, value[96:], 0.0) for value, source in got)
     scale = 1.0 / math.sqrt(atoms * n_dev / configs)
@@ -292,7 +292,7 @@
     (spread,) = call(
         bands_kernel,
         [tiles(6)],
-        [(x * 4 + part)[None], grams] + [along_l(grams, k) for k in (2, 1, 3)],
+        [(x * 4 + part)[None], grams] + [along_l(grams, k) for k in (1, 3, 2)],
         (),
         pltpu.VMEM,
         8 << 20,

time: 95.6 us -> 98.7 us (1.032)
  starting transfers between devices: 55.1 us -> 57.1 us
  waiting for transfers between devices: 22.7 us -> 23.7 us
    ppermute x4, starting transfers between devices: 5.76 us -> 8.37 us  [shards(): lax.ppermute(mine_s[k:k + 4], 'c', flip)]
    ppermute x6, waiting for transfers between devices: 6.18 us -> 8.71 us  [along_l(): return lax.ppermute(value, 'l', [(i, (i + k) % 4) for i in range(4)])]
    all_to_all x4, waiting for transfers between devices: 8.29 us -> 6.78 us  [exchange(): return lax.all_to_all(flat, axes, 0, 0, tiled=True).reshape(values.shape)]
    ppermute x6, starting transfers between devices: 7.99 us -> 6.72 us  [along_l(): return lax.ppermute(value, 'l', [(i, (i + k) % 4) for i in range(4)])]
  transfers between devices with their start and end apart: 22 -> 22, of which waited for: 14 -> 15; matrix products, arithmetic and copies ran while one was open for 3% -> 2% of each run, Pallas kernels for 8% -> 8%
where the time goes in v14:
time: 98.7 us; the launch traced here: 98.2 us
  starting transfers between devices  57.1 us (58%)
  waiting for transfers between devices  23.7 us (24%)
  Pallas kernels  13 us (13%)
  other arithmetic  2.47 us (3%)
  local copies, waits for them, and re-layouts  1.11 us (1%)
    all_to_all x4, starting transfers between devices, exchange(): return lax.all_to_all(flat, axes, 0, 0, tiled=True).reshape(values.shape)  18.3 us
    pallas_call x5, Pallas kernels, call(): pl.pallas_call(kernel, out_shape=outs, in_specs=[smem] + [pl.BlockSpec(me...  13 us
    ppermute x6, waiting for transfers between devices, along_l(): return lax.ppermute(value, 'l', [(i, (i + k) % 4) for i in range(4)])  8.71 us
    ppermute x4, starting transfers between devices, shards(): lax.ppermute(mine_s[k:k + 4], 'c', flip)  8.37 us
    ppermute x1, starting transfers between devices, shards(): plane_s = plane_s + lax.ppermute(plane_s, 'h', flip)  7 us
    ppermute x1, starting transfers between devices, shards(): grams = of_species(kind) + lax.ppermute(of_species(1 - kind), 'h', flip)  7 us
    all_to_all x4, waiting for transfers between devices, exchange(): return lax.all_to_all(flat, axes, 0, 0, tiled=True).reshape(values.shape)  6.78 us
    ppermute x6, starting transfers between devices, along_l(): return lax.ppermute(value, 'l', [(i, (i + k) % 4) for i in range(4)])  6.72 us
  transfers between devices with their start and end apart: 22, of which 15 were waited for; matrix products, arithmetic and copies ran while one was open for 2% of the time, Pallas kernels for 8%

profile of v14, /device:TPU:1, one launch (start us, length us, event | category | flops | bytes accessed | tf_op | source)
XLA Modules:
  0.0 98.2 jit_solution(10127061667029092077)
XLA Ops:
  0.6 0.0 copy-start
  0.6 3.5 %shard_map.68 = (f32[16,96,128]{2,1,0:T(8,128)S(1)}, f32[16,96,128]{2,1,0:T(8,128)S(1)}) custom-call(s32[1]{0:T(128)} %bitcast.core_ref, bf16[2048,768]{1,0:T(8,128)(2,1)} %desc_hbm.2, s32[1,2048]{1,0:T(1,128)} %bitcast.15, s32[1,2048]{1,0:T(1,128)} %bitcast.14, s32[1,256]{1,0:T(1,128)} %bitcast.17), custom_call_target="tpu_custom_call" | custom-call | flops 1610612736 | bytes 3145728 | tf_op jit(solution)/shard_map/pallas_call | solution.py:193
  4.1 3.3 %collective-permute-start = (f32[16,96,128]{2,1,0:T(8,128)S(1)}, f32[16,96,128]{2,1,0:T(8,128)S(1)}, u32[]{:S(2)}, u32[]{:S(2)}) collective-permute-start(f32[16,96,128]{2,1,0:T(8,128)S(1)} %get-tuple-element.24), channel_id=1, source_target_pairs={{0,8},{8,0},{1,9},{9,1},{2,10},{10,2},{3,11},{11,3},{4,12},{12,4},... | collective-permute-start | bytes 2359304 | tf_op jit(solution)/shard_map/ppermute | solution.py:260
  7.4 0.0 copy-done
  7.4 0.1 pad_add_fusion.pos_ref
  7.5 1.8 %collective-permute-done = f32[16,96,128]{2,1,0:T(8,128)S(1)} collective-permute-done((f32[16,96,128]{2,1,0:T(8,128)S(1)}, f32[16,96,128]{2,1,0:T(8,128)S(1)}, u32[]{:S(2)}, u32[]{:S(2)}) %collective-permute-start) | collective-permute-done | bytes 786464 | tf_op jit(solution)/shard_map/ppermute | solution.py:260
  9.4 1.0 add.58
  10.3 0.1 broadcast_in_dim.42.refs_4_
  10.4 5.0 %all-to-all-start = ((f32[16,96,128]{2,1,0:T(8,128)}), f32[16,96,128]{2,1,0:T(8,128)S(1)}, u32[]{:S(2)}, u32[]{:S(2)}) async-start(f32[16,96,128]{2,1,0:T(8,128)} %add.58), calls=%async_computation | async-start | bytes 1572864 | tf_op jit(solution)/shard_map/all_to_all | solution.py:206
  15.4 5.1 %shard_map.69 = (f32[16,168,128]{2,1,0:T(8,128)S(1)}, f32[16,48,128]{2,1,0:T(8,128)S(1)}, f32[16,48,128]{2,1,0:T(8,128)S(1)}, f32[16,48,128]{2,1,0:T(8,128)S(1)}, f32[16,24,128]{2,1,0:T(8,128)S(1)}) custom-call(s32[1]{0:T(128)} %bitcast.core_ref, bf16[2048,768]{1,0:T(8,128)(2,1)} %desc_hbm.2, s32[1,2048]{1,0:T(1,128)} %bitcast.16), custom_call_target="tpu_custom_call" | custom-call | flops 4831838208 | bytes 9437184 | tf_op jit(solution)/shard_map/pallas_call | solution.py:193
  20.5 0.7 collective-permute-start.3
  21.3 0.1 collective-permute-start.2
  21.4 0.4 collective-permute-start.1
  21.8 0.1 collective-permute-start.4
  21.9 2.1 %collective-permute-done.4 = f32[16,24,128]{2,1,0:T(8,128)S(1)} collective-permute-done((f32[16,24,128]{2,1,0:T(8,128)S(1)}, f32[16,24,128]{2,1,0:T(8,128)S(1)}, u32[]{:S(2)}, u32[]{:S(2)}) %collective-permute-start.4) | collective-permute-done | bytes 196640 | tf_op jit(solution)/shard_map/ppermute | solution.py:270
  24.0 0.0 collective-permute-done.3
  24.0 0.0 collective-permute-done.2
  24.0 0.0 collective-permute-done.1
  24.0 1.3 %maximum_add_fusion = f32[16,168,128]{2,1,0:T(8,128)} fusion(f32[16,168,128]{2,1,0:T(8,128)S(1)} %get-tuple-element.28, f32[16,24,128]{2,1,0:T(8,128)S(1)} %collective-permute-done.4, f32[16,48,128]{2,1,0:T(8,128)S(1)} %collective-permute-done.3, f32[16,48,128]{2,1,0:T(8,128)S(1)} %collective-permute-done.2, f32[16,48,128]{2,1,0:T(8,128)S(1)} %collective-permute-done.1), kind=kLoop, calls=%fused_computation | loop fusion | flops 1376256 | bytes 4128768 | tf_op jit(solution)/shard_map/add | solution.py:270
  25.3 2.9 %all-to-all-done = f32[16,96,128]{2,1,0:T(8,128)S(1)} async-done(((f32[16,96,128]{2,1,0:T(8,128)}), f32[16,96,128]{2,1,0:T(8,128)S(1)}, u32[]{:S(2)}, u32[]{:S(2)}) %all-to-all-start) | async-done | bytes 786464 | tf_op jit(solution)/shard_map/all_to_all | solution.py:206
  28.2 4.3 %all-to-all-start.1 = ((f32[16,168,128]{2,1,0:T(8,128)}), f32[16,168,128]{2,1,0:T(8,128)S(1)}, u32[]{:S(2)}, u32[]{:S(2)}) async-start(f32[16,168,128]{2,1,0:T(8,128)} %maximum_add_fusion), calls=%async_computation.1 | async-start | bytes 2752512 | tf_op jit(solution)/shard_map/all_to_all | solution.py:206
  32.5 7.0 %collective-permute-start.5 = (f32[96,128]{1,0:T(8,128)S(1)}, f32[96,128]{1,0:T(8,128)S(1)}, u32[]{:S(2)}, u32[]{:S(2)}) collective-permute-start(f32[96,128]{1,0:T(8,128)S(1)} %reduce_sum.18), channel_id=1, source_target_pairs={{0,4},{4,0},{1,5},{5,1},{2,6},{6,2},{3,7},{7,3},{8,12},{12,8},{9,1... | collective-permute-start | bytes 147464 | tf_op jit(solution)/shard_map/ppermute | solution.py:278
  39.5 1.5 %collective-permute-done.5 = f32[96,128]{1,0:T(8,128)S(1)} collective-permute-done((f32[96,128]{1,0:T(8,128)S(1)}, f32[96,128]{1,0:T(8,128)S(1)}, u32[]{:S(2)}, u32[]{:S(2)}) %collective-permute-start.5) | collective-permute-done | bytes 49184 | tf_op jit(solution)/shard_map/ppermute | solution.py:278
  41.0 1.5 %collective-permute-start.8 = (f32[104,128]{1,0:T(8,128)S(1)}, f32[104,128]{1,0:T(8,128)S(1)}, u32[]{:S(2)}, u32[]{:S(2)}) collective-permute-start(f32[104,128]{1,0:T(8,128)S(1)} %pad_maximum_fusion.2), channel_id=1, source_target_pairs={{0,32},{16,48},{32,0},{48,16},{1,33},{17,49},{33,1},{49,17},{2,34}... | collective-permute-start | bytes 159752 | tf_op jit(solution)/shard_map/ppermute | solution.py:276
  42.5 1.5 %collective-permute-start.7 = (f32[104,128]{1,0:T(8,128)S(1)}, f32[104,128]{1,0:T(8,128)S(1)}, u32[]{:S(2)}, u32[]{:S(2)}) collective-permute-start(f32[104,128]{1,0:T(8,128)S(1)} %pad_maximum_fusion.2), channel_id=1, source_target_pairs={{0,48},{16,0},{32,16},{48,32},{1,49},{17,1},{33,17},{49,33},{2,50}... | collective-permute-start | bytes 159752 | tf_op jit(solution)/shard_map/ppermute | solution.py:276
  44.0 0.2 collective-permute-start.6
  44.2 2.2 %collective-permute-done.8 = f32[104,128]{1,0:T(8,128)S(1)} collective-permute-done((f32[104,128]{1,0:T(8,128)S(1)}, f32[104,128]{1,0:T(8,128)S(1)}, u32[]{:S(2)}, u32[]{:S(2)}) %collective-permute-start.8) | collective-permute-done | bytes 53280 | tf_op jit(solution)/shard_map/ppermute | solution.py:276
  46.3 0.0 collective-permute-done.7
  46.4 2.7 %collective-permute-done.6 = f32[104,128]{1,0:T(8,128)S(1)} collective-permute-done((f32[104,128]{1,0:T(8,128)S(1)}, f32[104,128]{1,0:T(8,128)S(1)}, u32[]{:S(2)}, u32[]{:S(2)}) %collective-permute-start.6) | collective-permute-done | bytes 53280 | tf_op jit(solution)/shard_map/ppermute | solution.py:276
  49.1 1.7 %all-to-all-done.1 = f32[16,168,128]{2,1,0:T(8,128)S(1)} async-done(((f32[16,168,128]{2,1,0:T(8,128)}), f32[16,168,128]{2,1,0:T(8,128)S(1)}, u32[]{:S(2)}, u32[]{:S(2)}) %all-to-all-start.1) | async-done | bytes 1376288 | tf_op jit(solution)/shard_map/all_to_all | solution.py:206
  50.7 0.1 reduce_sum.19
  50.9 7.0 %collective-permute-start.9 = (f32[96,128]{1,0:T(8,128)S(1)}, f32[96,128]{1,0:T(8,128)S(1)}, u32[]{:S(2)}, u32[]{:S(2)}) collective-permute-start(f32[96,128]{1,0:T(8,128)S(1)} %pad_maximum_fusion), channel_id=1, source_target_pairs={{0,4},{4,0},{1,5},{5,1},{2,6},{6,2},{3,7},{7,3},{8,12},{12,8},{9,1... | collective-permute-start | bytes 147464 | tf_op jit(solution)/shard_map/ppermute | solution.py:291
  57.9 1.0 broadcast_in_dim.46
  58.8 4.6 %all-to-all-start.2 = ((f32[16,96,128]{2,1,0:T(8,128)}), f32[16,96,128]{2,1,0:T(8,128)S(1)}, u32[]{:S(2)}, u32[]{:S(2)}) async-start(f32[16,96,128]{2,1,0:T(8,128)} %broadcast_in_dim.46), calls=%async_computation.2 | async-start | bytes 1572864 | tf_op jit(solution)/shard_map/all_to_all | solution.py:206
  63.4 0.0 collective-permute-done.9
  63.4 1.0 %collective-permute-start.10 = (f32[96,128]{1,0:T(8,128)S(1)}, f32[96,128]{1,0:T(8,128)S(1)}, u32[]{:S(2)}, u32[]{:S(2)}) collective-permute-start(f32[96,128]{1,0:T(8,128)S(1)} %fusion.refs_0_), channel_id=1, source_target_pairs={{0,16},{16,32},{32,48},{48,0},{1,17},{17,33},{33,49},{49,1},{2,18}... | collective-permute-start | bytes 147464 | tf_op jit(solution)/shard_map/ppermute | solution.py:276
  64.4 2.5 %collective-permute-start.11 = (f32[96,128]{1,0:T(8,128)S(1)}, f32[96,128]{1,0:T(8,128)S(1)}, u32[]{:S(2)}, u32[]{:S(2)}) collective-permute-start(f32[96,128]{1,0:T(8,128)S(1)} %fusion.refs_0_), channel_id=1, source_target_pairs={{0,48},{16,0},{32,16},{48,32},{1,49},{17,1},{33,17},{49,33},{2,50}... | collective-permute-start | bytes 147464 | tf_op jit(solution)/shard_map/ppermute | solution.py:276
  67.0 0.0 collective-permute-start.12
  67.0 1.5 %collective-permute-done.10.refs_1_ = f32[96,128]{1,0:T(8,128)S(1)} collective-permute-done((f32[96,128]{1,0:T(8,128)S(1)}, f32[96,128]{1,0:T(8,128)S(1)}, u32[]{:S(2)}, u32[]{:S(2)}) %collective-permute-start.10) | collective-permute-done | bytes 49184 | tf_op jit(solution)/shard_map/ppermute | solution.py:276
  68.4 0.0 collective-permute-done.11.refs_2_
  68.4 2.4 %collective-permute-done.12.refs_3_ = f32[96,128]{1,0:T(8,128)S(1)} collective-permute-done((f32[96,128]{1,0:T(8,128)S(1)}, f32[96,128]{1,0:T(8,128)S(1)}, u32[]{:S(2)}, u32[]{:S(2)}) %collective-permute-start.12) | collective-permute-done | bytes 49184 | tf_op jit(solution)/shard_map/ppermute | solution.py:276
  70.8 0.8 shard_map.70
  71.6 2.3 %all-to-all-done.2.mine_ref = f32[16,96,128]{2,1,0:T(8,128)S(1)} async-done(((f32[16,96,128]{2,1,0:T(8,128)}), f32[16,96,128]{2,1,0:T(8,128)S(1)}, u32[]{:S(2)}, u32[]{:S(2)}) %all-to-all-start.2) | async-done | bytes 786464 | tf_op jit(solution)/shard_map/all_to_all | solution.py:206
  73.8 4.4 %all-to-all-start.3 = ((f32[16,48,128]{2,1,0:T(8,128)}), f32[16,48,128]{2,1,0:T(8,128)S(1)}, u32[]{:S(2)}, u32[]{:S(2)}) async-start(f32[16,48,128]{2,1,0:T(8,128)} %shard_map.70), calls=%async_computation.3 | async-start | bytes 786432 | tf_op jit(solution)/shard_map/all_to_all | solution.py:206
  78.3 0.1 fusion.7
  78.3 7.8 %collective-permute-start.13 = (f32[4,96,128]{2,1,0:T(8,128)S(1)}, f32[4,96,128]{2,1,0:T(8,128)S(1)}, u32[]{:S(2)}, u32[]{:S(2)}) collective-permute-start(f32[4,96,128]{2,1,0:T(8,128)S(1)} %get-tuple-element.47), channel_id=1, source_target_pairs={{0,8},{8,0},{1,9},{9,1},{2,10},{10,2},{3,11},{11,3},{4,12},{12,4},... | collective-permute-start | bytes 589832 | tf_op jit(solution)/shard_map/ppermute | solution.py:308
  86.1 0.1 collective-permute-start.14
  86.2 0.4 collective-permute-start.15
  86.6 0.1 collective-permute-start.16
  86.7 0.5 collective-permute-done.13.refs_0_
  87.2 0.4 collective-permute-done.14.refs_1_
  87.5 0.3 collective-permute-done.15.refs_2_
  87.8 0.3 collective-permute-done.16.refs_3_
  88.1 1.9 %shard_map.71 = (f32[192,1536]{1,0:T(8,128)S(1)}, f32[8,192]{1,0:T(8,128)}) custom-call(s32[4]{0:T(128)S(1)} %pad_add_fusion.pos_ref, f32[16,96,128]{2,1,0:T(8,128)S(1)} %all-to-all-done.2.mine_ref, f32[4,96,128]{2,1,0:T(8,128)S(1)} %collective-permute-done.13.refs_0_, f32[4,96,128]{2,1,0:T(8,128)S(1)} %collective-permute-done.14.refs_1_, ...), custom_call_target="tpu_custom_call" | custom-call | flops 905969664 | bytes 1769472 | tf_op jit(solution)/shard_map/pallas_call | solution.py:193
  90.0 0.0 all-to-all-done.3.mine_ref
  90.0 5.1 %collective-permute-start.17 = (f32[16,48,128]{2,1,0:T(8,128)S(1)}, f32[16,48,128]{2,1,0:T(8,128)S(1)}, u32[]{:S(2)}, u32[]{:S(2)}) collective-permute-start(f32[16,48,128]{2,1,0:T(8,128)S(1)} %all-to-all-done.3.mine_ref), channel_id=1, source_target_pairs={{0,8},{8,0},{1,9},{9,1},{2,10},{10,2},{3,11},{11,3},{4,12},{12,4},... | collective-permute-start | bytes 1179656 | tf_op jit(solution)/shard_map/ppermute | solution.py:318
  95.1 1.3 %collective-permute-done.17.other_ref = f32[16,48,128]{2,1,0:T(8,128)S(1)} collective-permute-done((f32[16,48,128]{2,1,0:T(8,128)S(1)}, f32[16,48,128]{2,1,0:T(8,128)S(1)}, u32[]{:S(2)}, u32[]{:S(2)}) %collective-permute-start.17) | collective-permute-done | bytes 393248 | tf_op jit(solution)/shard_map/ppermute | solution.py:318
  96.4 1.8 %shard_map.72 = f32[192,1536]{1,0:T(8,128)} custom-call(s32[4]{0:T(128)S(1)} %pad_add_fusion.pos_ref, f32[16,48,128]{2,1,0:T(8,128)S(1)} %all-to-all-done.3.mine_ref, f32[16,48,128]{2,1,0:T(8,128)S(1)} %collective-permute-done.17.other_ref, f32[192,1536]{1,0:T(8,128)S(1)} %get-tuple-element.42.cross_ref), custom_call_target="tpu_custom_call" | custom-call | flops 147456 | bytes 288 | tf_op jit(solution)/shard_map/pallas_call | solution.py:193
  (10 shorter events, 0.1 us)
Async XLA Ops:
  0.6 6.8 %copy-start = (f32[8]{0:T(128)S(1)}, f32[8]{0:T(128)}, u32[]{:S(2)}) copy-start(f32[8]{0:T(128)} %param.9) | copy-start | bytes 100
  4.1 5.2 %collective-permute-start = (f32[16,96,128]{2,1,0:T(8,128)S(1)}, f32[16,96,128]{2,1,0:T(8,128)S(1)}, u32[]{:S(2)}, u32[]{:S(2)}) collective-permute-start(f32[16,96,128]{2,1,0:T(8,128)S(1)} %get-tuple-element.24), channel_id=1, source_target_pairs={{0,8},{8,0},{1,9},{9,1},{2,10},{10,2},{3,11},{11,3},{4,12},{12,4},... | collective-permute-start | bytes 2359304 | tf_op jit(solution)/shard_map/ppermute | solution.py:260
  10.4 17.8 %all-to-all-start = ((f32[16,96,128]{2,1,0:T(8,128)}), f32[16,96,128]{2,1,0:T(8,128)S(1)}, u32[]{:S(2)}, u32[]{:S(2)}) async-start(f32[16,96,128]{2,1,0:T(8,128)} %add.58), calls=%async_computation | async-start | bytes 1572864 | tf_op jit(solution)/shard_map/all_to_all | solution.py:206
  20.5 3.5 %collective-permute-start.3 = (f32[16,48,128]{2,1,0:T(8,128)S(1)}, f32[16,48,128]{2,1,0:T(8,128)S(1)}, u32[]{:S(2)}, u32[]{:S(2)}) collective-permute-start(f32[16,48,128]{2,1,0:T(8,128)S(1)} %get-tuple-element.31), channel_id=1, source_target_pairs={{0,8},{8,0},{1,9},{9,1},{2,10},{10,2},{3,11},{11,3},{4,12},{12,4},... | collective-permute-start | bytes 1179656 | tf_op jit(solution)/shard_map/ppermute | solution.py:270
  21.3 2.8 %collective-permute-start.2 = (f32[16,48,128]{2,1,0:T(8,128)S(1)}, f32[16,48,128]{2,1,0:T(8,128)S(1)}, u32[]{:S(2)}, u32[]{:S(2)}) collective-permute-start(f32[16,48,128]{2,1,0:T(8,128)S(1)} %get-tuple-element.30), channel_id=1, source_target_pairs={{0,8},{8,0},{1,9},{9,1},{2,10},{10,2},{3,11},{11,3},{4,12},{12,4},... | collective-permute-start | bytes 1179656 | tf_op jit(solution)/shard_map/ppermute | solution.py:270
  21.4 2.7 %collective-permute-start.1 = (f32[16,48,128]{2,1,0:T(8,128)S(1)}, f32[16,48,128]{2,1,0:T(8,128)S(1)}, u32[]{:S(2)}, u32[]{:S(2)}) collective-permute-start(f32[16,48,128]{2,1,0:T(8,128)S(1)} %get-tuple-element.29), channel_id=1, source_target_pairs={{0,8},{8,0},{1,9},{9,1},{2,10},{10,2},{3,11},{11,3},{4,12},{12,4},... | collective-permute-start | bytes 1179656 | tf_op jit(solution)/shard_map/ppermute | solution.py:270
  21.8 2.2 %collective-permute-start.4 = (f32[16,24,128]{2,1,0:T(8,128)S(1)}, f32[16,24,128]{2,1,0:T(8,128)S(1)}, u32[]{:S(2)}, u32[]{:S(2)}) collective-permute-start(f32[16,24,128]{2,1,0:T(8,128)S(1)} %get-tuple-element.32), channel_id=1, source_target_pairs={{0,8},{8,0},{1,9},{9,1},{2,10},{10,2},{3,11},{11,3},{4,12},{12,4},... | collective-permute-start | bytes 589832 | tf_op jit(solution)/shard_map/ppermute | solution.py:270
  28.2 22.5 %all-to-all-start.1 = ((f32[16,168,128]{2,1,0:T(8,128)}), f32[16,168,128]{2,1,0:T(8,128)S(1)}, u32[]{:S(2)}, u32[]{:S(2)}) async-start(f32[16,168,128]{2,1,0:T(8,128)} %maximum_add_fusion), calls=%async_computation.1 | async-start | bytes 2752512 | tf_op jit(solution)/shard_map/all_to_all | solution.py:206
  32.5 8.5 %collective-permute-start.5 = (f32[96,128]{1,0:T(8,128)S(1)}, f32[96,128]{1,0:T(8,128)S(1)}, u32[]{:S(2)}, u32[]{:S(2)}) collective-permute-start(f32[96,128]{1,0:T(8,128)S(1)} %reduce_sum.18), channel_id=1, source_target_pairs={{0,4},{4,0},{1,5},{5,1},{2,6},{6,2},{3,7},{7,3},{8,12},{12,8},{9,1... | collective-permute-start | bytes 147464 | tf_op jit(solution)/shard_map/ppermute | solution.py:278
  41.0 5.4 %collective-permute-start.8 = (f32[104,128]{1,0:T(8,128)S(1)}, f32[104,128]{1,0:T(8,128)S(1)}, u32[]{:S(2)}, u32[]{:S(2)}) collective-permute-start(f32[104,128]{1,0:T(8,128)S(1)} %pad_maximum_fusion.2), channel_id=1, source_target_pairs={{0,32},{16,48},{32,0},{48,16},{1,33},{17,49},{33,1},{49,17},{2,34}... | collective-permute-start | bytes 159752 | tf_op jit(solution)/shard_map/ppermute | solution.py:276
  42.5 3.8 %collective-permute-start.7 = (f32[104,128]{1,0:T(8,128)S(1)}, f32[104,128]{1,0:T(8,128)S(1)}, u32[]{:S(2)}, u32[]{:S(2)}) collective-permute-start(f32[104,128]{1,0:T(8,128)S(1)} %pad_maximum_fusion.2), channel_id=1, source_target_pairs={{0,48},{16,0},{32,16},{48,32},{1,49},{17,1},{33,17},{49,33},{2,50}... | collective-permute-start | bytes 159752 | tf_op jit(solution)/shard_map/ppermute | solution.py:276
  44.0 5.1 %collective-permute-start.6 = (f32[104,128]{1,0:T(8,128)S(1)}, f32[104,128]{1,0:T(8,128)S(1)}, u32[]{:S(2)}, u32[]{:S(2)}) collective-permute-start(f32[104,128]{1,0:T(8,128)S(1)} %pad_maximum_fusion.2), channel_id=1, source_target_pairs={{0,16},{16,32},{32,48},{48,0},{1,17},{17,33},{33,49},{49,1},{2,18}... | collective-permute-start | bytes 159752 | tf_op jit(solution)/shard_map/ppermute | solution.py:276
  50.9 12.6 %collective-permute-start.9 = (f32[96,128]{1,0:T(8,128)S(1)}, f32[96,128]{1,0:T(8,128)S(1)}, u32[]{:S(2)}, u32[]{:S(2)}) collective-permute-start(f32[96,128]{1,0:T(8,128)S(1)} %pad_maximum_fusion), channel_id=1, source_target_pairs={{0,4},{4,0},{1,5},{5,1},{2,6},{6,2},{3,7},{7,3},{8,12},{12,8},{9,1... | collective-permute-start | bytes 147464 | tf_op jit(solution)/shard_map/ppermute | solution.py:291
  58.8 15.0 %all-to-all-start.2 = ((f32[16,96,128]{2,1,0:T(8,128)}), f32[16,96,128]{2,1,0:T(8,128)S(1)}, u32[]{:S(2)}, u32[]{:S(2)}) async-start(f32[16,96,128]{2,1,0:T(8,128)} %broadcast_in_dim.46), calls=%async_computation.2 | async-start | bytes 1572864 | tf_op jit(solution)/shard_map/all_to_all | solution.py:206
  63.4 5.0 %collective-permute-start.10 = (f32[96,128]{1,0:T(8,128)S(1)}, f32[96,128]{1,0:T(8,128)S(1)}, u32[]{:S(2)}, u32[]{:S(2)}) collective-permute-start(f32[96,128]{1,0:T(8,128)S(1)} %fusion.refs_0_), channel_id=1, source_target_pairs={{0,16},{16,32},{32,48},{48,0},{1,17},{17,33},{33,49},{49,1},{2,18}... | collective-permute-start | bytes 147464 | tf_op jit(solution)/shard_map/ppermute | solution.py:276
  64.4 4.0 %collective-permute-start.11 = (f32[96,128]{1,0:T(8,128)S(1)}, f32[96,128]{1,0:T(8,128)S(1)}, u32[]{:S(2)}, u32[]{:S(2)}) collective-permute-start(f32[96,128]{1,0:T(8,128)S(1)} %fusion.refs_0_), channel_id=1, source_target_pairs={{0,48},{16,0},{32,16},{48,32},{1,49},{17,1},{33,17},{49,33},{2,50}... | collective-permute-start | bytes 147464 | tf_op jit(solution)/shard_map/ppermute | solution.py:276
  67.0 3.8 %collective-permute-start.12 = (f32[96,128]{1,0:T(8,128)S(1)}, f32[96,128]{1,0:T(8,128)S(1)}, u32[]{:S(2)}, u32[]{:S(2)}) collective-permute-start(f32[96,128]{1,0:T(8,128)S(1)} %fusion.refs_0_), channel_id=1, source_target_pairs={{0,32},{16,48},{32,0},{48,16},{1,33},{17,49},{33,1},{49,17},{2,34}... | collective-permute-start | bytes 147464 | tf_op jit(solution)/shard_map/ppermute | solution.py:276
  73.8 16.1 %all-to-all-start.3 = ((f32[16,48,128]{2,1,0:T(8,128)}), f32[16,48,128]{2,1,0:T(8,128)S(1)}, u32[]{:S(2)}, u32[]{:S(2)}) async-start(f32[16,48,128]{2,1,0:T(8,128)} %shard_map.70), calls=%async_computation.3 | async-start | bytes 786432 | tf_op jit(solution)/shard_map/all_to_all | solution.py:206
  78.3 8.8 %collective-permute-start.13 = (f32[4,96,128]{2,1,0:T(8,128)S(1)}, f32[4,96,128]{2,1,0:T(8,128)S(1)}, u32[]{:S(2)}, u32[]{:S(2)}) collective-permute-start(f32[4,96,128]{2,1,0:T(8,128)S(1)} %get-tuple-element.47), channel_id=1, source_target_pairs={{0,8},{8,0},{1,9},{9,1},{2,10},{10,2},{3,11},{11,3},{4,12},{12,4},... | collective-permute-start | bytes 589832 | tf_op jit(solution)/shard_map/ppermute | solution.py:308
  86.1 1.4 %collective-permute-start.14 = (f32[4,96,128]{2,1,0:T(8,128)S(1)}, f32[4,96,128]{2,1,0:T(8,128)S(1)}, u32[]{:S(2)}, u32[]{:S(2)}) collective-permute-start(f32[4,96,128]{2,1,0:T(8,128)S(1)} %get-tuple-element.46), channel_id=1, source_target_pairs={{0,8},{8,0},{1,9},{9,1},{2,10},{10,2},{3,11},{11,3},{4,12},{12,4},... | collective-permute-start | bytes 589832 | tf_op jit(solution)/shard_map/ppermute | solution.py:308
  86.2 1.6 %collective-permute-start.15 = (f32[4,96,128]{2,1,0:T(8,128)S(1)}, f32[4,96,128]{2,1,0:T(8,128)S(1)}, u32[]{:S(2)}, u32[]{:S(2)}) collective-permute-start(f32[4,96,128]{2,1,0:T(8,128)S(1)} %get-tuple-element.45), channel_id=1, source_target_pairs={{0,8},{8,0},{1,9},{9,1},{2,10},{10,2},{3,11},{11,3},{4,12},{12,4},... | collective-permute-start | bytes 589832 | tf_op jit(solution)/shard_map/ppermute | solution.py:308
  86.6 1.5 %collective-permute-start.16 = (f32[4,96,128]{2,1,0:T(8,128)S(1)}, f32[4,96,128]{2,1,0:T(8,128)S(1)}, u32[]{:S(2)}, u32[]{:S(2)}) collective-permute-start(f32[4,96,128]{2,1,0:T(8,128)S(1)} %get-tuple-element.44), channel_id=1, source_target_pairs={{0,8},{8,0},{1,9},{9,1},{2,10},{10,2},{3,11},{11,3},{4,12},{12,4},... | collective-permute-start | bytes 589832 | tf_op jit(solution)/shard_map/ppermute | solution.py:308
  90.0 6.4 %collective-permute-start.17 = (f32[16,48,128]{2,1,0:T(8,128)S(1)}, f32[16,48,128]{2,1,0:T(8,128)S(1)}, u32[]{:S(2)}, u32[]{:S(2)}) collective-permute-start(f32[16,48,128]{2,1,0:T(8,128)S(1)} %all-to-all-done.3.mine_ref), channel_id=1, source_target_pairs={{0,8},{8,0},{1,9},{9,1},{2,10},{10,2},{3,11},{11,3},{4,12},{12,4},... | collective-permute-start | bytes 1179656 | tf_op jit(solution)/shard_map/ppermute | solution.py:318
